TPU v7x, 256 devices: a whole 4x4x8 slice. The times are simulated.
256 devices in a mesh: seq: 32 (over y, x, core), head: 8 (over z).
Axes of the slice: x: 4, y: 4, z: 8, core: 2. Of those that a mesh axis runs over, the one named last changes fastest.
Arguments:
- frames: bfloat16 [8192, 4096], P('seq'), may hold values from -6 to 6
- norm_gain: float32 [4096], replicated, may hold values from 0.5 to 1.5
- qkv_weight: bfloat16 [4096, 3, 2048], P(None, None, 'head'), may hold values from -0.09375 to 0.09375
- gate_weight: bfloat16 [4096, 2, 8], P(None, None, 'head'), may hold values from -0.09375 to 0.09375
- beta_scale: float32 [8], P('head'), may hold values from 0.2 to 1
- decay_rate: float32 [8], P('head'), may hold values from 1e-06 to 0.05
- resets: int32 [8192], P('seq'), may hold values 0 or 1
- out_gain: float32 [2048], P('head'), may hold values from 0.5 to 1.5
- out_weight: bfloat16 [2048, 4096], P('head'), may hold values from -0.125 to 0.125
Outputs:
- mixed: bfloat16 [8192, 4096], P(('seq', 'head'))
Inputs may be any that keep to these rules, and one draw needn't show every extreme that they name: `resets`: reset flags are 0 or 1.
All inputs are finite; a program needn't handle non-finite values. No bound on the sum of `resets` on one device may be relied on, other than what follows from the above.
Results may differ from a plain program's by a relative error of at most 0.017.
Values may be sent and summed in bfloat16 or wider, within the bound.
No kernel may reach another device: no remote copies, remote signals or barrier semaphores. Data moves between devices by JAX's collectives and lax.ppermute only.
A program may use at most 64 MiB of HBM per device.

v0:
```python
import jax
import jax.numpy as jnp
from jax import lax
from jax.sharding import PartitionSpec as P

D = 4096
SPAN = 256


HIGH_ACCURACY = lax.Precision.HIGHEST


def carried_in(value, axis, join, neutral):
    place = lax.axis_index(axis)
    gathered = jax.tree.map(
        lambda a, kind: lax.all_gather(a.astype(kind), axis), value, (jnp.bfloat16, jnp.bfloat16)
    )
    state = jax.tree.map(lambda a, e: jnp.zeros_like(a) + jnp.asarray(e, a.dtype), value, neutral)

    def one(turn, state):
        return join(
            state,
            jax.tree.map(
                lambda a, own: lax.dynamic_index_in_dim(a, turn, 0, False).astype(own.dtype),
                gathered,
                value,
            ),
        )

    return lax.fori_loop(0, place, one, state)


def unit_rows(vectors):
    return vectors * lax.rsqrt(jnp.sum(vectors * vectors, axis=-1, keepdims=True) + 1e-06)


def matmul(left, right):
    return jnp.einsum("hij,hjk->hik", left, right, precision=HIGH_ACCURACY)


def per_device(
    frames, norm_gain, qkv_weight, gate_weight, beta_scale, decay_rate, resets, out_gain, out_weight
):
    frame_rows = frames.shape[0]
    head_count = beta_scale.shape[0]
    local_width = qkv_weight.shape[2]
    head_size = local_width // head_count
    span_count = frame_rows // SPAN
    expanded_input = frames.astype(jnp.float32)
    normed = (
        expanded_input
        * lax.rsqrt(jnp.mean(expanded_input * expanded_input, axis=-1, keepdims=True) + 1e-06)
        * norm_gain
    ).astype(jnp.bfloat16)
    projected = jnp.dot(
        normed, qkv_weight.reshape(D, 3 * local_width), preferred_element_type=jnp.float32
    ).reshape(frame_rows, 3, head_count, head_size)

    def blocked(values):
        return values.reshape(span_count, SPAN, head_count, head_size).transpose(2, 0, 1, 3)

    def blocked_scalar(values):
        return values.reshape(span_count, SPAN, head_count).transpose(2, 0, 1)

    query_vec = blocked(unit_rows(projected[:, 0]))
    key_vec = blocked(unit_rows(projected[:, 1]))
    value_vec = blocked(projected[:, 2])
    gating = jnp.dot(
        normed, gate_weight.reshape(D, 2 * head_count), preferred_element_type=jnp.float32
    ).reshape(frame_rows, 2, head_count)
    strength = blocked_scalar(beta_scale * jax.nn.sigmoid(gating[:, 0]))
    log_forget = blocked_scalar(-decay_rate * jax.nn.softplus(gating[:, 1]))
    cumulative = jnp.cumsum(log_forget, axis=-1)
    segment = jnp.cumsum(resets.reshape(span_count, SPAN), axis=-1)
    position = jnp.arange(SPAN)
    causal = position[:, None] >= position[None, :]
    same = (segment[:, :, None] == segment[:, None, :]) & causal
    gap = cumulative[..., :, None] - cumulative[..., None, :]
    decay = jnp.where(same, jnp.exp(jnp.where(same, gap, 0.0)), 0.0)
    gamma = jnp.exp(cumulative) * (segment == 0).astype(jnp.float32)
    tail = decay[..., SPAN - 1, :]
    key_gram = jnp.einsum("hntk,hnsk->hnts", key_vec, key_vec, precision=HIGH_ACCURACY)
    strict = position[:, None] > position[None, :]
    system = jnp.where(strict, strength[..., :, None] * decay * key_gram, 0.0) + jnp.eye(
        SPAN, dtype=jnp.float32
    )
    corrected = lax.linalg.triangular_solve(
        system, strength[..., None] * value_vec, left_side=True, lower=True, unit_diagonal=True
    )
    leaked = lax.linalg.triangular_solve(
        system,
        (strength * gamma)[..., None] * key_vec,
        left_side=True,
        lower=True,
        unit_diagonal=True,
    )
    weighted_keys = key_vec * tail[..., None]
    identity_mat = jnp.eye(head_size, dtype=jnp.float32)
    transition = gamma[..., SPAN - 1][..., None, None] * identity_mat - jnp.einsum(
        "hnsk,hnsj->hnkj", weighted_keys, leaked, precision=HIGH_ACCURACY
    )
    offset = jnp.einsum("hnsk,hnsj->hnkj", weighted_keys, corrected, precision=HIGH_ACCURACY)
    carry_mat = transition[:, 0]
    carry_add = offset[:, 0]
    empty_state = jnp.zeros((head_count, head_size, head_size), jnp.float32)

    def combine(earlier, later):
        return (matmul(later[0], earlier[0]), matmul(later[0], earlier[1]) + later[1])

    unit_pair = (jnp.broadcast_to(identity_mat, (head_count, head_size, head_size)), empty_state)
    prefix = carried_in((carry_mat, carry_add), "seq", combine, unit_pair)
    incoming = prefix[1]
    starts = [incoming]
    state_stack = jnp.stack(starts, axis=1)
    attention_scores = (
        jnp.einsum("hntk,hnsk->hnts", query_vec, key_vec, precision=HIGH_ACCURACY) * decay
    )
    carried_query = gamma[..., None] * query_vec - jnp.einsum(
        "hnts,hnsk->hntk", attention_scores, leaked, precision=HIGH_ACCURACY
    )
    read_out = jnp.einsum(
        "hnts,hnsj->hntj", attention_scores, corrected, precision=HIGH_ACCURACY
    ) + jnp.einsum("hntk,hnkj->hntj", carried_query, state_stack, precision=HIGH_ACCURACY)
    read_out = read_out.transpose(1, 2, 0, 3).reshape(frame_rows, head_count, head_size)
    normalized = (
        read_out
        * lax.rsqrt(jnp.mean(read_out * read_out, axis=-1, keepdims=True) + 1e-06)
        * out_gain.reshape(head_count, head_size)
    )
    flat = normalized.reshape(frame_rows, local_width).astype(jnp.bfloat16)
    mixed = lax.psum_scatter(
        jnp.dot(flat, out_weight, preferred_element_type=jnp.float32).astype(jnp.bfloat16),
        "head",
        scatter_dimension=0,
        tiled=True,
    )
    return mixed


def solution(mesh):
    in_specs = (
        P("seq", None),
        P(),
        P(None, None, "head"),
        P(None, None, "head"),
        P("head"),
        P("head"),
        P("seq"),
        P("head"),
        P("head", None),
    )
    out_specs = P(("seq", "head"), None)
    return jax.shard_map(
        per_device, mesh=mesh, in_specs=in_specs, out_specs=out_specs, check_vma=False
    )
```

profile of v0, /device:TPU:1, one launch (start us, length us, event | category | flops | bytes accessed | tf_op | source)
XLA Modules:
  0.0 262.2 jit_solution(9179630053066560905)
XLA Ops:
  6.5 0.0 copy-start
  6.5 0.0 all-gather.5.cloned.1.call-start
  8.0 1.0 reduce-window.14
  9.0 0.2 slice_reduce_fusion.1
  9.2 0.6 slice.103
  9.8 0.2 reduce-window.15
  10.0 0.1 broadcast.439
  10.1 0.6 slice.104
  10.7 2.1 fusion.7
  12.8 2.3 convolution_bitcast_fusion.4
  15.2 0.3 reduce-window.16
  15.5 0.2 slice_reduce_fusion
  15.7 0.6 slice.105
  16.2 0.2 reduce-window.19
  16.4 0.1 broadcast.440
  16.5 0.7 slice.106
  18.5 0.0 copy-start.5
  18.5 8.8 %copy.14 = bf16[4096,3,256]{0,2,1:T(8,128)(2,1)} copy(bf16[4096,3,256]{2,0,1:T(8,128)(2,1)} %param.15) | data formatting | bytes 12582912 | tf_op args[2]
  27.3 0.0 copy-done.5
  27.3 5.3 %fusion.11 = f32[256,3,1,256]{0,3,1,2:T(8,128)S(1)} fusion(bf16[4096,3,256]{0,2,1:T(8,128)(2,1)} %copy.14, bf16[256,4096]{1,0:T(8,128)(2,1)} %param.13, f32[4096]{0:T(1024)S(1)} %copy-done.5, f32[256]{0:T(256)S(1)} %add_rsqrt_fusion.3), kind=kOutput, calls=%fused_computation.17 | convolution fusion | flops 1614807040 | bytes 9192448 | tf_op jit(solution)/shard_map/dot_general | solution.py:55
  32.7 0.1 multiply_reduce_fusion.2
  32.7 0.6 fusion.71
  33.3 0.6 slice.108
  34.0 0.6 slice.107
  34.6 0.7 fusion.21
  35.3 0.1 broadcast.473
  35.4 4.1 %while.17 = (s32[]{:T(128)}, f32[1,1,256,256]{3,2,1,0:T(8,128)S(1)}, s32[2,2]{1,0:T(2,128)S(1)}, f32[2,1,1,128,128]{4,3,2,1,0:T(8,128)S(1)}, s32[]{:T(128)}) while((s32[]{:T(128)}, f32[1,1,256,256]{3,2,1,0:T(8,128)S(1)}, s32[2,2]{1,0:T(2,128)S(1)}, f32[2,1,1,128,128]{4,3,2,1,0:T(8,128)S(1)}, s32[]{:T(128)}) %tuple.50), condition=%wide.while_cond, body=%wide.while_body.sunk | while | flops 2 | bytes 131189 | solution.py:87
  35.4 0.6 fusion.89
  36.0 1.4 bitcast_dynamic-update-slice_fusion.2
  37.4 0.6 fusion.89
  38.0 1.4 bitcast_dynamic-update-slice_fusion.2
  39.5 0.0 copy-start.1
  39.5 20.3 %custom-call.4 = f32[1,1,2,128,128]{3,4,2,1,0:T(8,128)} custom-call(f32[1,1,2,128,128]{4,3,2,1,0:T(8,128)S(1)} %bitcast.215), custom_call_target="InvertDiagBlocksLowerTriangular" | custom-call | tf_op jit(solution)/shard_map/triangular_solve/custom-call.1 | solution.py:87
  59.8 1.2 fusion.50
  61.0 0.4 fusion.25
  61.4 1.2 convolution_bitcast_fusion
  62.5 0.0 copy-start.2
  63.8 0.0 copy-done.4
  63.8 1.9 exponential_select_fusion.1
  65.8 0.0 copy-done.2
  65.8 1.0 fusion.19
  66.8 0.0 all-gather.5.cloned.1.call-update
  66.8 0.0 all-gather.7.cloned.1.call-start
  66.9 0.0 copy-done.1
  66.9 1.1 fusion.51
  68.0 1.2 fusion.23
  69.3 1.2 convolution_bitcast_fusion.2
  70.4 1.1 convolution_convert_fusion.1
  71.5 0.0 all-gather.7.cloned.1.call-update
  71.5 0.0 reduce-scatter.2.cloned.1.call-start
  71.6 1.3 convolution_multiply_fusion.1
  72.9 0.6 fusion.45
  73.5 1.5 convolution_subtract_fusion.1
  75.0 0.0 copy-start.3
  75.0 47.3 %all-gather.5.cloned.1.call-done = bf16[8192,256]{1,0:T(8,128)(2,1)} async-done(((bf16[256,256]{1,0:T(8,128)(2,1)}), bf16[8192,256]{1,0:T(8,128)(2,1)}) %all-gather.5.cloned.1.call-update) | async-done | bytes 4194320 | tf_op jit(solution)/shard_map/all_gather | solution.py:16
  122.3 53.1 %all-gather.7.cloned.1.call-done = bf16[8192,256]{1,0:T(8,128)(2,1)} async-done(((bf16[256,256]{1,0:T(8,128)(2,1)}), bf16[8192,256]{1,0:T(8,128)(2,1)}) %all-gather.7.cloned.1.call-update) | async-done | bytes 4194320 | tf_op jit(solution)/shard_map/all_gather | solution.py:16
  175.4 1.3 while.16
  175.5 1.3 fusion.88
  176.8 0.6 multiply_reduce_fusion
  177.4 0.0 copy-done
  177.4 0.0 copy-done.3
  177.4 2.2 convolution_convert_fusion
  179.6 0.0 reduce-scatter.2.cloned.1.call-update
  179.6 76.1 %reduce-scatter.2.cloned.1.call-done = bf16[32,4096]{1,0:T(8,128)(2,1)} async-done(((bf16[256,4096]{1,0:T(8,128)(2,1)}), bf16[32,4096]{1,0:T(8,128)(2,1)}) %reduce-scatter.2.cloned.1.call-update) | async-done | bytes 262160 | tf_op jit(solution)/shard_map/reduce_scatter | solution.py:131
  (16 shorter events, 0.2 us)
Async XLA Ops:
  6.5 170.9 %copy-start = (bf16[256,4096]{1,0:T(8,128)(2,1)S(1)}, bf16[256,4096]{1,0:T(8,128)(2,1)}, u32[]{:S(2)}) copy-start(bf16[256,4096]{1,0:T(8,128)(2,1)} %param.21) | copy-start | bytes 6291460
  6.5 115.8 %all-gather.5.cloned.1.call-start = ((), (), s32[]{:S(2)}) async-start(), calls=%async_computation.2 | async-start | bytes 4325376 | tf_op jit(solution)/shard_map/all_gather | solution.py:16
  18.5 8.8 %copy-start.5 = (f32[4096]{0:T(1024)S(1)}, f32[4096]{0:T(1024)}, u32[]{:S(2)}) copy-start(f32[4096]{0:T(1024)} %param.14) | copy-start | bytes 49156
  33.3 30.5 %copy-start.4 = (f32[256]{0:T(256)}, f32[256]{0:T(256)S(1)}, u32[]{:S(2)}) copy-start(f32[256]{0:T(256)S(1)} %get-tuple-element.100) | copy-start | bytes 3076
  39.5 27.4 %copy-start.1 = (f32[1,1,256,256]{3,2,1,0:T(8,128)}, f32[1,1,256,256]{3,2,1,0:T(8,128)S(1)}, u32[]{:S(2)}) copy-start(f32[1,1,256,256]{3,2,1,0:T(8,128)S(1)} %get-tuple-element.215) | copy-start | bytes 786436
  62.5 3.3 %copy-start.2 = (f32[1,1,128,256]{3,2,1,0:T(8,128)}, f32[1,1,128,256]{3,2,1,0:T(8,128)S(1)}, u32[]{:S(2)}) copy-start(f32[1,1,128,256]{3,2,1,0:T(8,128)S(1)} %convolution_bitcast_fusion) | copy-start | bytes 393220
  66.8 108.6 %all-gather.7.cloned.1.call-start = ((), (), s32[]{:S(2)}) async-start(), calls=%async_computation.3 | async-start | bytes 4325376 | tf_op jit(solution)/shard_map/all_gather | solution.py:16
  71.5 184.2 %reduce-scatter.2.cloned.1.call-start = ((), (), s32[]{:S(2)}) async-start(), calls=%async_computation.1 | async-start | bytes 2359296 | tf_op jit(solution)/shard_map/reduce_scatter | solution.py:131
  75.0 102.4 %copy-start.3 = (f32[256]{0:T(256)S(1)}, f32[256]{0:T(256)}, u32[]{:S(2)}) copy-start(f32[256]{0:T(256)} %param.20) | copy-start | bytes 3076
Sparse Core Ops, SparseCore 0:
  67.0 55.2 all-gather.4
  124.9 50.5 all-gather.6
  179.7 75.9 reduce-scatter.1
where the time goes:
time: 267 us; the launch traced here: 262 us
  waiting for transfers between devices  176 us (66%)
  other arithmetic  26.7 us (10%)
  matrix products  24.1 us (9%)
  between operations  17.5 us (7%)
  local copies, waits for them, and re-layouts  17.3 us (6%)
    all_gather x2, waiting for transfers between devices, carried_in(): lax.all_gather(a.astype(kind), axis)  100 us
    reduce_scatter x1, waiting for transfers between devices, per_device(): lax.psum_scatter(jnp.dot(flat, out_weight, preferred_element_type=jnp.flo...  76.1 us
    another operation x4, other arithmetic, per_device(): lax.linalg.triangular_solve(system, strength[..., None] * value_vec, left...  20.3 us
    unnamed x13, local copies, waits for them, and re-layouts  8.83 us
  transfers between devices with their start and end apart: 3, of which 3 were waited for; matrix products, arithmetic and copies ran while one was open for 3% of the time, Pallas kernels for 0%

commit v1 on v0

v1 whole, which is shorter than its diff:
```python
import functools

import jax
import jax.numpy as jnp
from jax import lax
from jax.experimental import pallas as pl
from jax.experimental.pallas import tpu as pltpu
from jax.sharding import PartitionSpec as P

KB = 1024
F32 = jnp.float32
BF16 = jnp.bfloat16
NN = (((1,), (0,)), ((), ()))
NT = (((1,), (1,)), ((), ()))
TN = (((0,), (0,)), ((), ()))


def mm(a, b, dims=NN):
    return lax.dot_general(a, b, dims, preferred_element_type=F32)


def split(a):
    hi = a.astype(BF16)
    return hi, (a - hi.astype(F32)).astype(BF16)


def mm3(a, b, dims=NN):
    (ah, al), (bh, bl) = a, b
    return mm(ah, bh, dims) + (mm(ah, bl, dims) + mm(al, bh, dims))


def unit_rows(vectors):
    return vectors * lax.rsqrt(jnp.sum(vectors * vectors, axis=-1, keepdims=True) + 1e-06)


def chunk_kernel(
    scale_ref, x_ref, gain_ref, w_ref, gate_ref, resets_ref,
    carry_ref, local_ref, query_ref,
    xn_ref, acc_ref, gating_ref,
):
    step = pl.program_id(0)
    n = x_ref.shape[0]

    @pl.when(step == 0)
    def _():
        x = x_ref[...].astype(F32)
        rs = lax.rsqrt(jnp.mean(x * x, axis=-1, keepdims=True) + 1e-06)
        xn_ref[...] = (x * rs * gain_ref[...]).astype(BF16)

    xb = xn_ref[:, pl.ds(pl.multiple_of(step * KB, KB), KB)]
    parts = [mm(xb, w_ref[j]) for j in range(3)]
    gating = mm(gate_ref[...], xb, NT)

    @pl.when(step == 0)
    def _():
        for j in range(3):
            acc_ref[j] = parts[j]
        gating_ref[...] = gating

    @pl.when(step > 0)
    def _():
        for j in range(3):
            acc_ref[j] = acc_ref[j] + parts[j]
        gating_ref[...] = gating_ref[...] + gating

    @pl.when(step == pl.num_programs(0) - 1)
    def _():
        query = unit_rows(acc_ref[0])
        key = unit_rows(acc_ref[1])
        value = acc_ref[2]
        gating = gating_ref[...]
        beta_row = scale_ref[0] * jax.nn.sigmoid(gating[0:1])
        logf_row = -scale_ref[1] * jax.nn.softplus(gating[1:2])
        reset_row = resets_ref[...].astype(F32)
        t = lax.broadcasted_iota(jnp.int32, (n, n), 0)
        s = lax.broadcasted_iota(jnp.int32, (n, n), 1)
        causal = t >= s
        eye = t == s

        def to_col(row):
            return jnp.sum(jnp.where(eye, row, 0.0), axis=1, keepdims=True)

        def to_row(col):
            return jnp.sum(jnp.where(eye, col, 0.0), axis=0, keepdims=True)

        beta = to_col(beta_row)
        cum = jnp.sum(jnp.where(causal, logf_row, 0.0), axis=1, keepdims=True)
        seg = jnp.sum(jnp.where(causal, reset_row, 0.0), axis=1, keepdims=True)
        cum_row = to_row(cum)
        seg_row = to_row(seg)
        same = (seg == seg_row) & causal
        decay = jnp.where(same, jnp.exp(jnp.where(same, cum - cum_row, 0.0)), 0.0)
        gamma = jnp.where(seg == 0.0, jnp.exp(cum), 0.0)
        cum_last, seg_last = cum[n - 1 : n], seg[n - 1 : n]
        tail = jnp.where(seg == seg_last, jnp.exp(cum_last - cum), 0.0)
        gamma_last = gamma[n - 1 : n]

        ks = split(key)
        gram = mm3(ks, ks, NT)
        low = jnp.where(t > s, beta * decay * gram, 0.0)
        apart = t ^ s
        inv = jnp.where(eye, 1.0, jnp.where(apart == 1, -low, 0.0))
        for level in range(1, n.bit_length() - 1):
            part = jnp.where((apart >> level) == 1, low, 0.0)
            vs = split(inv)
            inv = inv - mm3(vs, split(mm3(split(part), vs)))
        rhs = jnp.concatenate([(beta * gamma) * key, beta * value], axis=1)
        solved = split(mm3(split(inv), split(rhs)))
        folded = mm3(split(key * tail), solved, TN)
        carry_ref[:, :n] = (jnp.where(eye, gamma_last, 0.0) - folded[:, :n]).astype(BF16)
        carry_ref[:, n:] = folded[:, n:].astype(BF16)
        scores = mm3(split(query), ks, NT) * decay
        seen = mm3(split(scores), solved)
        query_ref[...] = gamma * query - seen[:, :n]
        local_ref[...] = seen[:, n:]


def after(later, earlier, n):
    both = mm(later[:, :n], earlier)
    return both[:, :n], both[:, n:] + later[:, n:].astype(F32)


def pair_kernel(own_ref, other_ref, out_ref):
    n = own_ref.shape[0]
    first = lax.axis_index("seq") % 2 == 0
    own, other = own_ref[...], other_ref[...]
    earlier = jnp.where(first, own, other)
    later = jnp.where(first, other, own)
    a, b = after(later, earlier, n)
    out_ref[:, :n] = a.astype(BF16)
    out_ref[:, n:] = b.astype(BF16)


def row_kernel(own_ref, one_ref, two_ref, three_ref, total_ref, prefix_ref, held):
    n = own_ref.shape[0]
    place = (lax.axis_index("seq") // 2) % 4
    for shift, ref in enumerate((own_ref, one_ref, two_ref, three_ref)):
        held[(place + (4 - shift)) % 4] = ref[...]

    def joined(later, earlier):
        a, b = after(later, earlier, n)
        return jnp.concatenate([a, b], axis=1).astype(BF16)

    low = joined(held[1], held[0])
    high = joined(held[3], held[2])
    a, b = after(high, low, n)
    total_ref[:, :n] = a.astype(BF16)
    total_ref[:, n:] = b.astype(BF16)

    @pl.when(place == 0)
    def _():
        prefix_ref[...] = jnp.zeros_like(prefix_ref)

    @pl.when(place == 1)
    def _():
        prefix_ref[...] = held[0]

    @pl.when(place == 2)
    def _():
        prefix_ref[...] = low

    @pl.when(place == 3)
    def _():
        prefix_ref[...] = joined(held[2], low)


def read_kernel(
    one_ref, two_ref, three_ref, prefix_ref, other_ref, query_ref, local_ref, gain_ref,
    out_ref, held, state,
):
    n = query_ref.shape[0]
    index = lax.axis_index("seq")
    place = index // 8
    for shift, ref in enumerate((one_ref, two_ref, three_ref)):
        held[(place + (3 - shift)) % 4] = ref[...]

    def push(pair, value):
        hi, lo = split(value)
        return mm(pair[:, :n], hi) + mm(pair[:, :n], lo) + pair[:, n:].astype(F32)

    @pl.when(place == 0)
    def _():
        state[...] = jnp.zeros_like(state)

    @pl.when(place > 0)
    def _():
        state[...] = held[0, :, n:].astype(F32)

    for turn in (1, 2):
        @pl.when(place > turn)
        def _():
            state[...] = push(held[turn], state[...])

    @pl.when((index // 2) % 4 > 0)
    def _():
        state[...] = push(prefix_ref[...], state[...])

    @pl.when(index % 2 > 0)
    def _():
        state[...] = push(other_ref[...], state[...])

    read = local_ref[...] + mm3(split(query_ref[...]), split(state[...]))
    read = read * lax.rsqrt(jnp.mean(read * read, axis=-1, keepdims=True) + 1e-06)
    out_ref[...] = (read * gain_ref[...]).astype(BF16)


def vmem():
    return pl.BlockSpec(memory_space=pltpu.VMEM)


def per_device(
    frames, norm_gain, qkv_weight, gate_weight, beta_scale, decay_rate, resets, out_gain, out_weight
):
    rows, width = frames.shape
    n = qkv_weight.shape[2]
    weight = qkv_weight.transpose(1, 0, 2)
    gate = gate_weight.transpose(2, 1, 0).reshape(2, width)
    scales = jnp.concatenate([beta_scale, decay_rate])
    whole = lambda shape: pl.BlockSpec(shape, lambda i: (0,) * len(shape), pipeline_mode=pl.Buffered(1))
    carry, local, query = pl.pallas_call(
        chunk_kernel,
        name="chunk",
        grid=(width // KB,),
        in_specs=[
            pl.BlockSpec(memory_space=pltpu.SMEM),
            whole((rows, width)),
            whole((1, width)),
            pl.BlockSpec((3, KB, n), lambda i: (0, i, 0)),
            pl.BlockSpec((2, KB), lambda i: (0, i)),
            whole((1, rows)),
        ],
        out_specs=[whole((n, 2 * n)), whole((rows, n)), whole((rows, n))],
        out_shape=[
            jax.ShapeDtypeStruct((n, 2 * n), BF16),
            jax.ShapeDtypeStruct((rows, n), F32),
            jax.ShapeDtypeStruct((rows, n), F32),
        ],
        scratch_shapes=[
            pltpu.VMEM((rows, width), BF16),
            pltpu.VMEM((3, rows, n), F32),
            pltpu.VMEM((2, rows), F32),
        ],
    )(scales, frames, norm_gain.reshape(1, width), weight, gate, resets.reshape(1, rows))

    count = 32

    def moved(value, place_of):
        return lax.ppermute(value, "seq", [(i, place_of(i)) for i in range(count)])

    def along_x(shift):
        return lambda i: (i // 8) * 8 + (i + 2 * shift) % 8

    def along_y(shift):
        return lambda i: (i + 8 * shift) % 32

    pair_shape = jax.ShapeDtypeStruct((n, 2 * n), BF16)
    other = moved(carry, lambda i: i ^ 1)
    pair = pl.pallas_call(
        pair_kernel, name="pair", in_specs=[vmem()] * 2, out_specs=vmem(), out_shape=pair_shape
    )(carry, other)
    near = [moved(pair, along_x(s)) for s in (1, 2, 3)]
    total, prefix = pl.pallas_call(
        row_kernel,
        name="row",
        in_specs=[vmem()] * 4,
        out_specs=[vmem()] * 2,
        out_shape=[pair_shape] * 2,
        scratch_shapes=[pltpu.VMEM((4, n, 2 * n), BF16)],
    )(pair, *near)
    far = [moved(total, along_y(s)) for s in (1, 2, 3)]
    flat = pl.pallas_call(
        read_kernel,
        name="read",
        in_specs=[vmem()] * 8,
        out_specs=vmem(),
        out_shape=jax.ShapeDtypeStruct((rows, n), BF16),
        scratch_shapes=[pltpu.VMEM((4, n, 2 * n), BF16), pltpu.VMEM((n, n), F32)],
    )(*far, prefix, other, query, local, out_gain.reshape(1, n))
    return lax.psum_scatter(
        jnp.dot(flat, out_weight, preferred_element_type=F32).astype(BF16),
        "head",
        scatter_dimension=0,
        tiled=True,
    )


def solution(mesh):
    in_specs = (
        P("seq", None),
        P(),
        P(None, None, "head"),
        P(None, None, "head"),
        P("head"),
        P("head"),
        P("seq"),
        P("head"),
        P("head", None),
    )
    out_specs = P(("seq", "head"), None)
    return jax.shard_map(
        per_device, mesh=mesh, in_specs=in_specs, out_specs=out_specs, check_vma=False
    )
```

time: 267 us -> 122 us (0.46)
  the two profiles are of different devices: /device:TPU:1 before, /device:TPU:6 now
where the time goes in v1:
time: 122 us; the launch traced here: 121 us
  waiting for transfers between devices  70.2 us (58%)
  Pallas kernels  21.8 us (18%)
  between operations  14.9 us (12%)
  starting transfers between devices  8.34 us (7%)
  matrix products  2.96 us (2%)
  local copies, waits for them, and re-layouts  2.63 us (2%)
    reduce_scatter x1, waiting for transfers between devices, per_device(): lax.psum_scatter(jnp.dot(flat, out_weight, preferred_element_type=F32).as...  43.5 us
    ppermute x7, waiting for transfers between devices, moved(): return lax.ppermute(value, 'seq', [(i, place_of(i)) for i in range(count)])  26.7 us
    pallas_call x1, Pallas kernels, per_device(): pl.pallas_call(chunk_kernel, name='chunk', grid=(width // KB,), in_specs=...  14.2 us
    ppermute x7, starting transfers between devices, moved(): return lax.ppermute(value, 'seq', [(i, place_of(i)) for i in range(count)])  8.34 us
    dot_general x1, matrix products, per_device(): jnp.dot(flat, out_weight, preferred_element_type=F32).astype(BF16)  2.96 us
    pallas_call x1, Pallas kernels, per_device(): pl.pallas_call(read_kernel, name='read', in_specs=[vmem()] * 8, out_specs...  2.78 us
    pallas_call x1, Pallas kernels, per_device(): pl.pallas_call(row_kernel, name='row', in_specs=[vmem()] * 4, out_specs=[...  2.77 us
    unnamed x16, local copies, waits for them, and re-layouts  2.63 us
  transfers between devices with their start and end apart: 8, of which 7 were waited for; matrix products, arithmetic and copies ran while one was open for 0% of the time, Pallas kernels for 0%

profile of v1, /device:TPU:6, one launch (start us, length us, event | category | flops | bytes accessed | tf_op | source)
XLA Modules:
  0.0 121.4 jit_solution(1022835131748893199)
XLA Ops:
  6.5 0.0 copy-start
  6.5 0.0 reduce-scatter.2.cloned.1.call-start
  8.0 0.6 pad_maximum_fusion.scale_ref
  8.6 14.2 %chunk.1 = (bf16[256,512]{1,0:T(8,128)(2,1)}, f32[256,256]{1,0:T(8,128)}, f32[256,256]{1,0:T(8,128)}) custom-call(f32[2]{0:T(128)} %pad_maximum_fusion.scale_ref, bf16[256,4096]{1,0:T(8,128)(2,1)} %x_ref.1, f32[1,4096]{1,0:T(1,128)} %bitcast.10, bf16[3,4096,256]{2,1,0:T(8,128)(2,1)} %bitcast.9, bf16[2,4096]{1,0:T(2,128)(2,1)} %bitcast.11, s32[1,256]{1,0:T(1,128)} %bitcast.13), custom_call_target="tpu_custom_call" | custom-call | tf_op jit(solution)/shard_map/chunk/pallas_call | solution.py:220
  22.8 0.0 collective-permute-start
  22.8 1.7 %collective-permute-done.other_ref = bf16[256,512]{1,0:T(8,128)(2,1)S(1)} collective-permute-done((bf16[256,512]{1,0:T(8,128)(2,1)}, bf16[256,512]{1,0:T(8,128)(2,1)S(1)}, u32[]{:S(2)}, u32[]{:S(2)}) %collective-permute-start) | collective-permute-done | bytes 262176 | tf_op jit(solution)/shard_map/ppermute | solution.py:248
  24.6 0.0 copy-start.1
  24.6 0.7 copy-done.1
  25.3 2.0 %pair.1.own_ref = bf16[256,512]{1,0:T(8,128)(2,1)} custom-call(bf16[256,512]{1,0:T(8,128)(2,1)} %get-tuple-element.10.own_ref, bf16[256,512]{1,0:T(8,128)(2,1)} %copy-done.1), custom_call_target="tpu_custom_call" | custom-call | tf_op jit(solution)/shard_map/pair/pallas_call | solution.py:258
  27.3 0.8 collective-permute-start.3
  28.1 2.8 %collective-permute-start.2 = (bf16[256,512]{1,0:T(8,128)(2,1)}, bf16[256,512]{1,0:T(8,128)(2,1)S(1)}, u32[]{:S(2)}, u32[]{:S(2)}) collective-permute-start(bf16[256,512]{1,0:T(8,128)(2,1)} %pair.1.own_ref), channel_id=1, source_target_pairs={{0,32},{8,40},{16,48},{24,56},{32,0},{40,8},{48,16},{56,24},{64,96... | collective-permute-start | bytes 786440 | tf_op jit(solution)/shard_map/ppermute | solution.py:248
  30.9 0.4 collective-permute-start.1
  31.3 6.1 %collective-permute-done.3.three_ref = bf16[256,512]{1,0:T(8,128)(2,1)S(1)} collective-permute-done((bf16[256,512]{1,0:T(8,128)(2,1)}, bf16[256,512]{1,0:T(8,128)(2,1)S(1)}, u32[]{:S(2)}, u32[]{:S(2)}) %collective-permute-start.3) | collective-permute-done | bytes 262176 | tf_op jit(solution)/shard_map/ppermute | solution.py:248
  37.4 0.0 copy-start.5
  37.4 5.7 %collective-permute-done.2.two_ref = bf16[256,512]{1,0:T(8,128)(2,1)S(1)} collective-permute-done((bf16[256,512]{1,0:T(8,128)(2,1)}, bf16[256,512]{1,0:T(8,128)(2,1)S(1)}, u32[]{:S(2)}, u32[]{:S(2)}) %collective-permute-start.2) | collective-permute-done | bytes 262176 | tf_op jit(solution)/shard_map/ppermute | solution.py:248
  43.1 0.0 copy-start.6
  43.1 0.2 collective-permute-done.1.one_ref
  43.3 0.0 copy-done.5
  43.3 0.5 copy-done.6
  43.8 0.0 copy-start.7
  43.8 0.7 copy-done.7
  44.5 2.8 %row.1 = (bf16[256,512]{1,0:T(8,128)(2,1)}, bf16[256,512]{1,0:T(8,128)(2,1)}) custom-call(bf16[256,512]{1,0:T(8,128)(2,1)} %pair.1.own_ref, bf16[256,512]{1,0:T(8,128)(2,1)} %copy-done.7, bf16[256,512]{1,0:T(8,128)(2,1)} %copy-done.6, bf16[256,512]{1,0:T(8,128)(2,1)} %copy-done.5), custom_call_target="tpu_custom_call" | custom-call | tf_op jit(solution)/shard_map/row/pallas_call | solution.py:262
  47.3 2.7 %collective-permute-start.6 = (bf16[256,512]{1,0:T(8,128)(2,1)}, bf16[256,512]{1,0:T(8,128)(2,1)S(1)}, u32[]{:S(2)}, u32[]{:S(2)}) collective-permute-start(bf16[256,512]{1,0:T(8,128)(2,1)} %get-tuple-element.11), channel_id=1, source_target_pairs={{0,192},{8,200},{16,208},{24,216},{32,224},{40,232},{48,240},{56,2... | collective-permute-start | bytes 786440 | tf_op jit(solution)/shard_map/ppermute | solution.py:248
  50.0 0.6 collective-permute-start.5
  50.6 1.0 collective-permute-start.4
  51.6 9.4 %collective-permute-done.6.three_ref = bf16[256,512]{1,0:T(8,128)(2,1)S(1)} collective-permute-done((bf16[256,512]{1,0:T(8,128)(2,1)}, bf16[256,512]{1,0:T(8,128)(2,1)S(1)}, u32[]{:S(2)}, u32[]{:S(2)}) %collective-permute-start.6) | collective-permute-done | bytes 262176 | tf_op jit(solution)/shard_map/ppermute | solution.py:248
  61.0 0.0 copy-start.2
  61.0 0.0 collective-permute-done.5.two_ref
  61.0 0.0 copy-start.3
  61.0 3.6 %collective-permute-done.4.one_ref = bf16[256,512]{1,0:T(8,128)(2,1)S(1)} collective-permute-done((bf16[256,512]{1,0:T(8,128)(2,1)}, bf16[256,512]{1,0:T(8,128)(2,1)S(1)}, u32[]{:S(2)}, u32[]{:S(2)}) %collective-permute-start.4) | collective-permute-done | bytes 262176 | tf_op jit(solution)/shard_map/ppermute | solution.py:248
  64.5 0.0 copy-start.4
  64.5 0.0 copy-done.2
  64.5 0.0 copy-done.3
  64.5 0.7 copy-done.4
  65.2 2.8 %read.1 = bf16[256,256]{1,0:T(8,128)(2,1)} custom-call(bf16[256,512]{1,0:T(8,128)(2,1)} %copy-done.4, bf16[256,512]{1,0:T(8,128)(2,1)} %copy-done.3, bf16[256,512]{1,0:T(8,128)(2,1)} %copy-done.2, bf16[256,512]{1,0:T(8,128)(2,1)} %get-tuple-element.12.prefix_ref, bf16[256,512]{1,0:T(8,128)(2,1)} %copy-done.1, f32[256,256]{1,0:T(8,128)} %get-tuple-element.13.query_ref, ...), custom_call_target="tpu_custom_call" | custom-call | tf_op jit(solution)/shard_map/read/pallas_call | solution.py:271
  68.0 0.0 copy-done
  68.0 3.0 %convolution_convert_fusion = bf16[256,4096]{1,0:T(8,128)(2,1)} fusion(bf16[256,256]{1,0:T(8,128)(2,1)} %read.1, bf16[256,4096]{1,0:T(8,128)(2,1)S(1)} %copy-done), kind=kOutput, calls=%fused_computation | convolution fusion | flops 537919488 | bytes 4325376 | tf_op jit(solution)/shard_map/dot_general | solution.py:280
  71.0 0.0 reduce-scatter.2.cloned.1.call-update
  71.0 43.5 %reduce-scatter.2.cloned.1.call-done = bf16[32,4096]{1,0:T(8,128)(2,1)} async-done(((bf16[256,4096]{1,0:T(8,128)(2,1)}), bf16[32,4096]{1,0:T(8,128)(2,1)}) %reduce-scatter.2.cloned.1.call-update) | async-done | bytes 262160 | tf_op jit(solution)/shard_map/reduce_scatter | solution.py:279
Async XLA Ops:
  6.5 61.5 %copy-start = (bf16[256,4096]{1,0:T(8,128)(2,1)S(1)}, bf16[256,4096]{1,0:T(8,128)(2,1)}, u32[]{:S(2)}) copy-start(bf16[256,4096]{1,0:T(8,128)(2,1)} %param.17) | copy-start | bytes 6291460
  6.5 108.0 %reduce-scatter.2.cloned.1.call-start = ((), (), s32[]{:S(2)}) async-start(), calls=%async_computation.1 | async-start | bytes 2359296 | tf_op jit(solution)/shard_map/reduce_scatter | solution.py:279
  22.8 1.7 %collective-permute-start = (bf16[256,512]{1,0:T(8,128)(2,1)}, bf16[256,512]{1,0:T(8,128)(2,1)S(1)}, u32[]{:S(2)}, u32[]{:S(2)}) collective-permute-start(bf16[256,512]{1,0:T(8,128)(2,1)} %get-tuple-element.10.own_ref), channel_id=1, source_target_pairs={{0,8},{8,0},{16,24},{24,16},{32,40},{40,32},{48,56},{56,48},{64,72... | collective-permute-start | bytes 786440 | tf_op jit(solution)/shard_map/ppermute | solution.py:248
  24.6 0.7 copy-start.1
  27.3 10.1 %collective-permute-start.3 = (bf16[256,512]{1,0:T(8,128)(2,1)}, bf16[256,512]{1,0:T(8,128)(2,1)S(1)}, u32[]{:S(2)}, u32[]{:S(2)}) collective-permute-start(bf16[256,512]{1,0:T(8,128)(2,1)} %pair.1.own_ref), channel_id=1, source_target_pairs={{0,48},{8,56},{16,0},{24,8},{32,16},{40,24},{48,32},{56,40},{64,11... | collective-permute-start | bytes 786440 | tf_op jit(solution)/shard_map/ppermute | solution.py:248
  28.1 15.0 %collective-permute-start.2 = (bf16[256,512]{1,0:T(8,128)(2,1)}, bf16[256,512]{1,0:T(8,128)(2,1)S(1)}, u32[]{:S(2)}, u32[]{:S(2)}) collective-permute-start(bf16[256,512]{1,0:T(8,128)(2,1)} %pair.1.own_ref), channel_id=1, source_target_pairs={{0,32},{8,40},{16,48},{24,56},{32,0},{40,8},{48,16},{56,24},{64,96... | collective-permute-start | bytes 786440 | tf_op jit(solution)/shard_map/ppermute | solution.py:248
  30.9 12.3 %collective-permute-start.1 = (bf16[256,512]{1,0:T(8,128)(2,1)}, bf16[256,512]{1,0:T(8,128)(2,1)S(1)}, u32[]{:S(2)}, u32[]{:S(2)}) collective-permute-start(bf16[256,512]{1,0:T(8,128)(2,1)} %pair.1.own_ref), channel_id=1, source_target_pairs={{0,16},{8,24},{16,32},{24,40},{32,48},{40,56},{48,0},{56,8},{64,80... | collective-permute-start | bytes 786440 | tf_op jit(solution)/shard_map/ppermute | solution.py:248
  37.4 5.9 %copy-start.5 = (bf16[256,512]{1,0:T(8,128)(2,1)}, bf16[256,512]{1,0:T(8,128)(2,1)S(1)}, u32[]{:S(2)}) copy-start(bf16[256,512]{1,0:T(8,128)(2,1)S(1)} %collective-permute-done.3.three_ref) | copy-start | bytes 786436
  43.1 0.7 copy-start.6
  43.8 0.7 copy-start.7
  47.3 13.7 %collective-permute-start.6 = (bf16[256,512]{1,0:T(8,128)(2,1)}, bf16[256,512]{1,0:T(8,128)(2,1)S(1)}, u32[]{:S(2)}, u32[]{:S(2)}) collective-permute-start(bf16[256,512]{1,0:T(8,128)(2,1)} %get-tuple-element.11), channel_id=1, source_target_pairs={{0,192},{8,200},{16,208},{24,216},{32,224},{40,232},{48,240},{56,2... | collective-permute-start | bytes 786440 | tf_op jit(solution)/shard_map/ppermute | solution.py:248
  50.0 11.0 %collective-permute-start.5 = (bf16[256,512]{1,0:T(8,128)(2,1)}, bf16[256,512]{1,0:T(8,128)(2,1)S(1)}, u32[]{:S(2)}, u32[]{:S(2)}) collective-permute-start(bf16[256,512]{1,0:T(8,128)(2,1)} %get-tuple-element.11), channel_id=1, source_target_pairs={{0,128},{8,136},{16,144},{24,152},{32,160},{40,168},{48,176},{56,1... | collective-permute-start | bytes 786440 | tf_op jit(solution)/shard_map/ppermute | solution.py:248
  50.6 13.9 %collective-permute-start.4 = (bf16[256,512]{1,0:T(8,128)(2,1)}, bf16[256,512]{1,0:T(8,128)(2,1)S(1)}, u32[]{:S(2)}, u32[]{:S(2)}) collective-permute-start(bf16[256,512]{1,0:T(8,128)(2,1)} %get-tuple-element.11), channel_id=1, source_target_pairs={{0,64},{8,72},{16,80},{24,88},{32,96},{40,104},{48,112},{56,120},{... | collective-permute-start | bytes 786440 | tf_op jit(solution)/shard_map/ppermute | solution.py:248
  61.0 3.6 %copy-start.2 = (bf16[256,512]{1,0:T(8,128)(2,1)}, bf16[256,512]{1,0:T(8,128)(2,1)S(1)}, u32[]{:S(2)}) copy-start(bf16[256,512]{1,0:T(8,128)(2,1)S(1)} %collective-permute-done.6.three_ref) | copy-start | bytes 786436
  61.0 3.6 %copy-start.3 = (bf16[256,512]{1,0:T(8,128)(2,1)}, bf16[256,512]{1,0:T(8,128)(2,1)S(1)}, u32[]{:S(2)}) copy-start(bf16[256,512]{1,0:T(8,128)(2,1)S(1)} %collective-permute-done.5.two_ref) | copy-start | bytes 786436
  64.5 0.7 copy-start.4
Sparse Core Ops, SparseCore 0:
  71.1 43.3 reduce-scatter.1

commit v2 on v1

--- a/solution.py
+++ b/solution.py
@@ -1,10 +1,9 @@
-import functools
-
 import jax
 import jax.numpy as jnp
 from jax import lax
 from jax.experimental import pallas as pl
 from jax.experimental.pallas import tpu as pltpu
+from jax.sharding import Mesh
 from jax.sharding import PartitionSpec as P
 
 KB = 1024
@@ -13,6 +12,10 @@
 NN = (((1,), (0,)), ((), ()))
 NT = (((1,), (1,)), ((), ()))
 TN = (((0,), (0,)), ((), ()))
+SEQ = ("y", "xh", "xl", "core")
+SMALL = pltpu.CompilerParams(vmem_limit_bytes=8 << 20)
+MIDDLE = pltpu.CompilerParams(vmem_limit_bytes=16 << 20)
+LARGE = pltpu.CompilerParams(vmem_limit_bytes=58 << 20)
 
 
 def mm(a, b, dims=NN):
@@ -34,7 +37,7 @@
 
 
 def chunk_kernel(
-    scale_ref, x_ref, gain_ref, w_ref, gate_ref, resets_ref,
+    scale_ref, rate_ref, x_ref, gain_ref, w_ref, gate_ref, resets_ref,
     carry_ref, local_ref, query_ref,
     xn_ref, acc_ref, gating_ref,
 ):
@@ -69,8 +72,8 @@
         key = unit_rows(acc_ref[1])
         value = acc_ref[2]
         gating = gating_ref[...]
-        beta_row = scale_ref[0] * jax.nn.sigmoid(gating[0:1])
-        logf_row = -scale_ref[1] * jax.nn.softplus(gating[1:2])
+        beta_row = scale_ref[...] * jax.nn.sigmoid(gating[0:1])
+        logf_row = -rate_ref[...] * jax.nn.softplus(gating[1:2])
         reset_row = resets_ref[...].astype(F32)
         t = lax.broadcasted_iota(jnp.int32, (n, n), 0)
         s = lax.broadcasted_iota(jnp.int32, (n, n), 1)
@@ -122,7 +125,7 @@
 
 def pair_kernel(own_ref, other_ref, out_ref):
     n = own_ref.shape[0]
-    first = lax.axis_index("seq") % 2 == 0
+    first = lax.axis_index("core") == 0
     own, other = own_ref[...], other_ref[...]
     earlier = jnp.where(first, own, other)
     later = jnp.where(first, other, own)
@@ -133,7 +136,7 @@
 
 def row_kernel(own_ref, one_ref, two_ref, three_ref, total_ref, prefix_ref, held):
     n = own_ref.shape[0]
-    place = (lax.axis_index("seq") // 2) % 4
+    place = lax.axis_index("xh") * 2 + lax.axis_index("xl")
     for shift, ref in enumerate((own_ref, one_ref, two_ref, three_ref)):
         held[(place + (4 - shift)) % 4] = ref[...]
 
@@ -169,8 +172,7 @@
     out_ref, held, state,
 ):
     n = query_ref.shape[0]
-    index = lax.axis_index("seq")
-    place = index // 8
+    place = lax.axis_index("y")
     for shift, ref in enumerate((one_ref, two_ref, three_ref)):
         held[(place + (3 - shift)) % 4] = ref[...]
 
@@ -191,17 +193,53 @@
         def _():
             state[...] = push(held[turn], state[...])
 
-    @pl.when((index // 2) % 4 > 0)
+    @pl.when(lax.axis_index("xh") + lax.axis_index("xl") > 0)
     def _():
         state[...] = push(prefix_ref[...], state[...])
 
-    @pl.when(index % 2 > 0)
+    @pl.when(lax.axis_index("core") > 0)
     def _():
         state[...] = push(other_ref[...], state[...])
 
     read = local_ref[...] + mm3(split(query_ref[...]), split(state[...]))
     read = read * lax.rsqrt(jnp.mean(read * read, axis=-1, keepdims=True) + 1e-06)
-    out_ref[...] = (read * gain_ref[...]).astype(BF16)
+    flat = (read * gain_ref[...]).astype(BF16)
+    out_ref[0] = flat
+    out_ref[1] = flat
+
+
+def take_kernel(whole_ref, out_ref, sem):
+    width = out_ref.shape[1]
+    block = lax.axis_index("core") * 2 + lax.axis_index("xl")
+    columns = pl.ds(pl.multiple_of(block * width, width), width)
+    copy = pltpu.make_async_copy(whole_ref.at[:, columns], out_ref, sem)
+    copy.start()
+    copy.wait()
+
+
+def mix_kernel(own_ref, other_ref, *refs):
+    weights, outs = refs[:8], refs[8:]
+    core, half, head = lax.axis_index("core"), lax.axis_index("xl"), lax.axis_index("head")
+    rows = own_ref.shape[2]
+    for shift, ref in enumerate(weights):
+        source = (head + (8 - shift)) % 8
+        block = []
+        for place in (half, 1 - half):
+            for ref_x in (own_ref, other_ref):
+                block.append(ref_x[place, source])
+        part = mm(jnp.concatenate(block, axis=0), ref[...])
+        total = part if shift == 0 else total + part
+    total = total.astype(BF16)
+    for k, ref in enumerate(outs):
+        ref[...] = total[k * rows : (k + 1) * rows]
+
+
+def lay_kernel(mine_ref, core_ref, half_ref, far_ref, out_ref):
+    width = mine_ref.shape[1]
+    block = lax.axis_index("core") * 2 + lax.axis_index("xl")
+    for flip, ref in ((0, mine_ref), (2, core_ref), (1, half_ref), (3, far_ref)):
+        place = pl.multiple_of((block ^ flip) * width, width)
+        out_ref[:, pl.ds(place, width)] = ref[...]
 
 
 def vmem():
@@ -215,14 +253,14 @@
     n = qkv_weight.shape[2]
     weight = qkv_weight.transpose(1, 0, 2)
     gate = gate_weight.transpose(2, 1, 0).reshape(2, width)
-    scales = jnp.concatenate([beta_scale, decay_rate])
     whole = lambda shape: pl.BlockSpec(shape, lambda i: (0,) * len(shape), pipeline_mode=pl.Buffered(1))
     carry, local, query = pl.pallas_call(
         chunk_kernel,
         name="chunk",
         grid=(width // KB,),
         in_specs=[
-            pl.BlockSpec(memory_space=pltpu.SMEM),
+            whole((1, 1)),
+            whole((1, 1)),
             whole((rows, width)),
             whole((1, width)),
             pl.BlockSpec((3, KB, n), lambda i: (0, i, 0)),
@@ -240,12 +278,13 @@
             pltpu.VMEM((3, rows, n), F32),
             pltpu.VMEM((2, rows), F32),
         ],
-    )(scales, frames, norm_gain.reshape(1, width), weight, gate, resets.reshape(1, rows))
+        compiler_params=LARGE,
+    )(beta_scale.reshape(1, 1), decay_rate.reshape(1, 1), frames, norm_gain.reshape(1, width), weight, gate, resets.reshape(1, rows))
 
     count = 32
 
     def moved(value, place_of):
-        return lax.ppermute(value, "seq", [(i, place_of(i)) for i in range(count)])
+        return lax.ppermute(value, SEQ, [(i, place_of(i)) for i in range(count)])
 
     def along_x(shift):
         return lambda i: (i // 8) * 8 + (i + 2 * shift) % 8
@@ -253,12 +292,42 @@
     def along_y(shift):
         return lambda i: (i + 8 * shift) % 32
 
+    def flip(bits):
+        return lambda i: i ^ bits
+
+    def along_z(value, shift):
+        return lax.ppermute(value, "head", [(i, (i + shift) % 8) for i in range(8)])
+
+    def later(values, gate):
+        return lax.optimization_barrier((values, gate))[0]
+
+    quarter = out_weight.shape[1] // 4
+    mine = pl.pallas_call(
+        take_kernel,
+        name="take",
+        in_specs=[pl.BlockSpec(memory_space=pl.ANY)],
+        out_specs=vmem(),
+        out_shape=jax.ShapeDtypeStruct((n, quarter), BF16),
+        scratch_shapes=[pltpu.SemaphoreType.DMA],
+        compiler_params=LARGE,
+    )(out_weight)
+    up = [along_z(mine, 1)]
+    down = [along_z(mine, -1)]
+
     pair_shape = jax.ShapeDtypeStruct((n, 2 * n), BF16)
-    other = moved(carry, lambda i: i ^ 1)
+    other = moved(carry, flip(1))
     pair = pl.pallas_call(
-        pair_kernel, name="pair", in_specs=[vmem()] * 2, out_specs=vmem(), out_shape=pair_shape
+        pair_kernel,
+        name="pair",
+        in_specs=[vmem()] * 2,
+        out_specs=vmem(),
+        out_shape=pair_shape,
+        compiler_params=SMALL,
     )(carry, other)
     near = [moved(pair, along_x(s)) for s in (1, 2, 3)]
+    ahead, behind = later((up[-1], down[-1]), other)
+    up.append(along_z(ahead, 1))
+    down.append(along_z(behind, -1))
     total, prefix = pl.pallas_call(
         row_kernel,
         name="row",
@@ -266,37 +335,61 @@
         out_specs=[vmem()] * 2,
         out_shape=[pair_shape] * 2,
         scratch_shapes=[pltpu.VMEM((4, n, 2 * n), BF16)],
+        compiler_params=SMALL,
     )(pair, *near)
     far = [moved(total, along_y(s)) for s in (1, 2, 3)]
+    ahead, behind = later((up[-1], down[-1]), total)
+    up.append(along_z(ahead, 1))
+    down.append(along_z(behind, -1))
     flat = pl.pallas_call(
         read_kernel,
         name="read",
         in_specs=[vmem()] * 8,
         out_specs=vmem(),
-        out_shape=jax.ShapeDtypeStruct((rows, n), BF16),
+        out_shape=jax.ShapeDtypeStruct((2, rows, n), BF16),
         scratch_shapes=[pltpu.VMEM((4, n, 2 * n), BF16), pltpu.VMEM((n, n), F32)],
+        compiler_params=SMALL,
     )(*far, prefix, other, query, local, out_gain.reshape(1, n))
-    return lax.psum_scatter(
-        jnp.dot(flat, out_weight, preferred_element_type=F32).astype(BF16),
-        "head",
-        scatter_dimension=0,
-        tiled=True,
-    )
+    ahead = later(up[-1], far[-1])
+    up.append(along_z(ahead, 1))
+    part = rows // 8
+    reads = lax.all_to_all(
+        flat.reshape(16, part, n), ("xl", "head"), 0, 0, tiled=True
+    ).reshape(2, 8, part, n)
+    beside = moved(reads, flip(1))
+    piece = jax.ShapeDtypeStruct((part, quarter), BF16)
+    kept, to_core, to_half, to_far = pl.pallas_call(
+        mix_kernel,
+        name="mix",
+        in_specs=[vmem()] * 10,
+        out_specs=[vmem()] * 4,
+        out_shape=[piece] * 4,
+        compiler_params=MIDDLE,
+    )(reads, beside, mine, *up, *down[::-1])
+    return pl.pallas_call(
+        lay_kernel,
+        name="lay",
+        in_specs=[vmem()] * 4,
+        out_specs=vmem(),
+        out_shape=jax.ShapeDtypeStruct((part, 4 * quarter), BF16),
+        compiler_params=SMALL,
+    )(kept, moved(to_core, flip(1)), moved(to_half, flip(2)), moved(to_far, flip(3)))
 
 
 def solution(mesh):
+    fine = Mesh(mesh.devices.reshape(4, 2, 2, 2, 8), SEQ + ("head",))
     in_specs = (
-        P("seq", None),
+        P(SEQ, None),
         P(),
         P(None, None, "head"),
         P(None, None, "head"),
         P("head"),
         P("head"),
-        P("seq"),
+        P(SEQ),
         P("head"),
         P("head", None),
     )
-    out_specs = P(("seq", "head"), None)
+    out_specs = P(SEQ + ("head",), None)
     return jax.shard_map(
-        per_device, mesh=mesh, in_specs=in_specs, out_specs=out_specs, check_vma=False
+        per_device, mesh=fine, in_specs=in_specs, out_specs=out_specs, check_vma=False
     )

time: 122 us -> 105 us (0.86)
  the two profiles are of different devices: /device:TPU:6 before, /device:TPU:1 now
where the time goes in v2:
time: 105 us; the launch traced here: 104 us
  waiting for transfers between devices  48 us (46%)
  starting transfers between devices  31 us (30%)
  Pallas kernels  21.1 us (20%)
  local copies, waits for them, and re-layouts  2.86 us (3%)
  between operations  1.4 us (1%)
    ppermute x11, waiting for transfers between devices, moved(): return lax.ppermute(value, SEQ, [(i, place_of(i)) for i in range(count)])  34.6 us
    ppermute x11, starting transfers between devices, moved(): return lax.ppermute(value, SEQ, [(i, place_of(i)) for i in range(count)])  14.5 us
    pallas_call x1, Pallas kernels, per_device(): pl.pallas_call(chunk_kernel, name='chunk', grid=(width // KB,), in_specs=...  14.2 us
    ppermute x7, starting transfers between devices, along_z(): return lax.ppermute(value, 'head', [(i, (i + shift) % 8) for i in range(8)])  12.2 us
    ppermute x7, waiting for transfers between devices, along_z(): return lax.ppermute(value, 'head', [(i, (i + shift) % 8) for i in range(8)])  7.03 us
    all_to_all x1, waiting for transfers between devices, per_device(): lax.all_to_all(flat.reshape(16, part, n), ('xl', 'head'), 0, 0, tiled=True)  6.42 us
    all_to_all x1, starting transfers between devices, per_device(): lax.all_to_all(flat.reshape(16, part, n), ('xl', 'head'), 0, 0, tiled=True)  4.3 us
    unnamed x10, local copies, waits for them, and re-layouts  2.86 us
  transfers between devices with their start and end apart: 19, of which 12 were waited for; matrix products, arithmetic and copies ran while one was open for 0% of the time, Pallas kernels for 16%

profile of v2, /device:TPU:1, one launch (start us, length us, event | category | flops | bytes accessed | tf_op | source)
XLA Modules:
  0.0 104.4 jit_solution(7687481303922150353)
XLA Ops:
  0.0 1.9 %take.1.refs_0_ = bf16[256,1024]{1,0:T(8,128)(2,1)} custom-call(bf16[256,4096]{1,0:T(8,128)(2,1)} %whole_ref.1), custom_call_target="tpu_custom_call" | custom-call | tf_op jit(solution)/shard_map/take/pallas_call | solution.py:305
  1.9 6.5 %collective-permute-start.9 = (bf16[256,1024]{1,0:T(8,128)(2,1)}, bf16[256,1024]{1,0:T(8,128)(2,1)S(1)}, u32[]{:S(2)}, u32[]{:S(2)}) collective-permute-start(bf16[256,1024]{1,0:T(8,128)(2,1)} %take.1.refs_0_), channel_id=1, source_target_pairs={{0,7},{1,0},{2,1},{3,2},{4,3},{5,4},{6,5},{7,6},{8,15},{9,8},{10,9... | collective-permute-start | bytes 1572872 | tf_op jit(solution)/shard_map/ppermute | solution.py:299
  8.4 0.0 collective-permute-start.8
  9.7 0.0 copy-start.4
  9.7 14.2 %chunk.1 = (bf16[256,512]{1,0:T(8,128)(2,1)}, f32[256,256]{1,0:T(8,128)}, f32[256,256]{1,0:T(8,128)}) custom-call(f32[1,1]{1,0:T(1,128)} %bitcast.11.scale_ref, f32[1,1]{1,0:T(1,128)} %bitcast.12.rate_ref, bf16[256,4096]{1,0:T(8,128)(2,1)} %x_ref.1, f32[1,4096]{1,0:T(1,128)} %bitcast.17, bf16[3,4096,256]{2,1,0:T(8,128)(2,1)} %bitcast.16, ...), custom_call_target="tpu_custom_call" | custom-call | tf_op jit(solution)/shard_map/chunk/pallas_call | solution.py:257
  23.9 0.0 copy-start
  23.9 1.0 collective-permute-start
  24.9 1.4 %collective-permute-done.other_ref = bf16[256,512]{1,0:T(8,128)(2,1)S(1)} collective-permute-done((bf16[256,512]{1,0:T(8,128)(2,1)}, bf16[256,512]{1,0:T(8,128)(2,1)S(1)}, u32[]{:S(2)}, u32[]{:S(2)}) %collective-permute-start) | collective-permute-done | bytes 262176 | tf_op jit(solution)/shard_map/ppermute | solution.py:287
  26.2 0.0 collective-permute-done.9.refs_7_
  26.2 0.0 collective-permute-done.8.refs_1_
  26.2 0.0 collective-permute-start.10
  26.3 3.0 %collective-permute-start.11 = (bf16[256,1024]{1,0:T(8,128)(2,1)S(1)}, bf16[256,1024]{1,0:T(8,128)(2,1)S(1)}, u32[]{:S(2)}, u32[]{:S(2)}) collective-permute-start(bf16[256,1024]{1,0:T(8,128)(2,1)S(1)} %collective-permute-done.9.refs_7_), channel_id=1, source_target_pairs={{0,7},{1,0},{2,1},{3,2},{4,3},{5,4},{6,5},{7,6},{8,15},{9,8},{10,9... | collective-permute-start | bytes 1572872 | tf_op jit(solution)/shard_map/ppermute | solution.py:299
  29.3 0.0 copy-start.1
  29.3 0.9 copy-done.1
  30.2 0.2 pair.1.own_ref
  30.5 2.6 %collective-permute-start.3 = (bf16[256,512]{1,0:T(8,128)(2,1)S(1)}, bf16[256,512]{1,0:T(8,128)(2,1)S(1)}, u32[]{:S(2)}, u32[]{:S(2)}) collective-permute-start(bf16[256,512]{1,0:T(8,128)(2,1)S(1)} %pair.1.own_ref), channel_id=1, source_target_pairs={{0,48},{8,56},{16,0},{24,8},{32,16},{40,24},{48,32},{56,40},{64,11... | collective-permute-start | bytes 786440 | tf_op jit(solution)/shard_map/ppermute | solution.py:287
  33.0 0.5 collective-permute-start.2
  33.6 0.6 collective-permute-start.1
  34.2 4.6 %collective-permute-done.3.three_ref = bf16[256,512]{1,0:T(8,128)(2,1)S(1)} collective-permute-done((bf16[256,512]{1,0:T(8,128)(2,1)S(1)}, bf16[256,512]{1,0:T(8,128)(2,1)S(1)}, u32[]{:S(2)}, u32[]{:S(2)}) %collective-permute-start.3) | collective-permute-done | bytes 262176 | tf_op jit(solution)/shard_map/ppermute | solution.py:287
  38.8 2.6 %collective-permute-done.2.two_ref = bf16[256,512]{1,0:T(8,128)(2,1)S(1)} collective-permute-done((bf16[256,512]{1,0:T(8,128)(2,1)S(1)}, bf16[256,512]{1,0:T(8,128)(2,1)S(1)}, u32[]{:S(2)}, u32[]{:S(2)}) %collective-permute-start.2) | collective-permute-done | bytes 262176 | tf_op jit(solution)/shard_map/ppermute | solution.py:287
  41.5 6.9 %collective-permute-done.1.one_ref = bf16[256,512]{1,0:T(8,128)(2,1)S(1)} collective-permute-done((bf16[256,512]{1,0:T(8,128)(2,1)S(1)}, bf16[256,512]{1,0:T(8,128)(2,1)S(1)}, u32[]{:S(2)}, u32[]{:S(2)}) %collective-permute-start.1) | collective-permute-done | bytes 262176 | tf_op jit(solution)/shard_map/ppermute | solution.py:287
  48.4 0.7 row.1
  49.1 0.0 collective-permute-done.10.refs_2_
  49.1 0.0 collective-permute-done.11.refs_6_
  49.1 0.1 collective-permute-start.12
  49.2 2.8 %collective-permute-start.6 = (bf16[256,512]{1,0:T(8,128)(2,1)S(1)}, bf16[256,512]{1,0:T(8,128)(2,1)S(1)}, u32[]{:S(2)}, u32[]{:S(2)}) collective-permute-start(bf16[256,512]{1,0:T(8,128)(2,1)S(1)} %get-tuple-element.20), channel_id=1, source_target_pairs={{0,192},{8,200},{16,208},{24,216},{32,224},{40,232},{48,240},{56,2... | collective-permute-start | bytes 786440 | tf_op jit(solution)/shard_map/ppermute | solution.py:287
  52.1 0.3 collective-permute-start.5
  52.4 0.7 collective-permute-start.4
  53.1 9.6 %collective-permute-done.6.three_ref = bf16[256,512]{1,0:T(8,128)(2,1)S(1)} collective-permute-done((bf16[256,512]{1,0:T(8,128)(2,1)S(1)}, bf16[256,512]{1,0:T(8,128)(2,1)S(1)}, u32[]{:S(2)}, u32[]{:S(2)}) %collective-permute-start.6) | collective-permute-done | bytes 262176 | tf_op jit(solution)/shard_map/ppermute | solution.py:287
  62.7 0.0 collective-permute-done.5.two_ref
  62.7 4.7 %collective-permute-done.4.one_ref = bf16[256,512]{1,0:T(8,128)(2,1)S(1)} collective-permute-done((bf16[256,512]{1,0:T(8,128)(2,1)S(1)}, bf16[256,512]{1,0:T(8,128)(2,1)S(1)}, u32[]{:S(2)}, u32[]{:S(2)}) %collective-permute-start.4) | collective-permute-done | bytes 262176 | tf_op jit(solution)/shard_map/ppermute | solution.py:287
  67.4 0.0 copy-done.4
  67.4 0.0 copy-start.2
  67.4 0.9 copy-done.2
  68.4 0.0 copy-start.3
  68.4 0.9 copy-done.3
  69.3 1.4 %read.1 = bf16[2,256,256]{2,1,0:T(8,128)(2,1)} custom-call(bf16[256,512]{1,0:T(8,128)(2,1)S(1)} %collective-permute-done.4.one_ref, bf16[256,512]{1,0:T(8,128)(2,1)S(1)} %collective-permute-done.5.two_ref, bf16[256,512]{1,0:T(8,128)(2,1)S(1)} %collective-permute-done.6.three_ref, bf16[256,512]{1,0:T(8,128)(2,1)S(1)} %get-tuple-element.21.prefix_ref, ...), custom_call_target="tpu_custom_call" | custom-call | tf_op jit(solution)/shard_map/read/pallas_call | solution.py:344
  70.7 4.3 %all-to-all-start = ((bf16[16,32,256]{2,1,0:T(8,128)(2,1)}), bf16[16,32,256]{2,1,0:T(8,128)(2,1)S(1)}, u32[]{:S(2)}, u32[]{:S(2)}) async-start(bf16[16,32,256]{2,1,0:T(8,128)(2,1)} %bitcast.8), calls=%async_computation | async-start | bytes 524288 | tf_op jit(solution)/shard_map/all_to_all | solution.py:356
  75.0 2.6 %collective-permute-start.14 = (bf16[256,1024]{1,0:T(8,128)(2,1)S(1)}, bf16[256,1024]{1,0:T(8,128)(2,1)}, u32[]{:S(2)}, u32[]{:S(2)}) collective-permute-start(bf16[256,1024]{1,0:T(8,128)(2,1)S(1)} %collective-permute-done.11.refs_6_), channel_id=1, source_target_pairs={{0,7},{1,0},{2,1},{3,2},{4,3},{5,4},{6,5},{7,6},{8,15},{9,8},{10,9... | collective-permute-start | bytes 1572872 | tf_op jit(solution)/shard_map/ppermute | solution.py:299
  77.6 0.0 collective-permute-done.12.refs_3_
  77.6 0.0 collective-permute-start.13
  77.6 6.4 %all-to-all-done = bf16[16,32,256]{2,1,0:T(8,128)(2,1)S(1)} async-done(((bf16[16,32,256]{2,1,0:T(8,128)(2,1)}), bf16[16,32,256]{2,1,0:T(8,128)(2,1)S(1)}, u32[]{:S(2)}, u32[]{:S(2)}) %all-to-all-start) | async-done | bytes 262176 | tf_op jit(solution)/shard_map/all_to_all | solution.py:356
  84.0 3.2 %collective-permute-start.7 = (bf16[2,8,32,256]{3,2,1,0:T(8,128)(2,1)S(1)}, bf16[2,8,32,256]{3,2,1,0:T(8,128)(2,1)S(1)}, u32[]{:S(2)}, u32[]{:S(2)}) collective-permute-start(bf16[2,8,32,256]{3,2,1,0:T(8,128)(2,1)S(1)} %bitcast.13), channel_id=1, source_target_pairs={{0,8},{8,0},{16,24},{24,16},{32,40},{40,32},{48,56},{56,48},{64,72... | collective-permute-start | bytes 786440 | tf_op jit(solution)/shard_map/ppermute | solution.py:287
  87.2 1.2 %collective-permute-done.7.other_ref = bf16[2,8,32,256]{3,2,1,0:T(8,128)(2,1)S(1)} collective-permute-done((bf16[2,8,32,256]{3,2,1,0:T(8,128)(2,1)S(1)}, bf16[2,8,32,256]{3,2,1,0:T(8,128)(2,1)S(1)}, u32[]{:S(2)}, u32[]{:S(2)}) %collective-permute-start.7) | collective-permute-done | bytes 262176 | tf_op jit(solution)/shard_map/ppermute | solution.py:287
  88.4 5.4 %collective-permute-done.14.refs_5_ = bf16[256,1024]{1,0:T(8,128)(2,1)} collective-permute-done((bf16[256,1024]{1,0:T(8,128)(2,1)S(1)}, bf16[256,1024]{1,0:T(8,128)(2,1)}, u32[]{:S(2)}, u32[]{:S(2)}) %collective-permute-start.14) | collective-permute-done | bytes 524320 | tf_op jit(solution)/shard_map/ppermute | solution.py:299
  93.8 1.6 %collective-permute-done.13.refs_4_ = bf16[256,1024]{1,0:T(8,128)(2,1)} collective-permute-done((bf16[256,1024]{1,0:T(8,128)(2,1)S(1)}, bf16[256,1024]{1,0:T(8,128)(2,1)}, u32[]{:S(2)}, u32[]{:S(2)}) %collective-permute-start.13) | collective-permute-done | bytes 524320 | tf_op jit(solution)/shard_map/ppermute | solution.py:299
  95.4 0.0 copy-done
  95.4 1.9 %mix.1 = (bf16[32,1024]{1,0:T(8,128)(2,1)S(1)}, bf16[32,1024]{1,0:T(8,128)(2,1)S(1)}, bf16[32,1024]{1,0:T(8,128)(2,1)S(1)}, bf16[32,1024]{1,0:T(8,128)(2,1)S(1)}) custom-call(bf16[2,8,32,256]{3,2,1,0:T(8,128)(2,1)S(1)} %bitcast.14, bf16[2,8,32,256]{3,2,1,0:T(8,128)(2,1)S(1)} %collective-permute-done.7.other_ref, bf16[256,1024]{1,0:T(8,128)(2,1)S(1)} %copy-done, ...), custom_call_target="tpu_custom_call" | custom-call | tf_op jit(solution)/shard_map/mix/pallas_call | solution.py:361
  97.3 1.1 %collective-permute-start.15 = (bf16[32,1024]{1,0:T(8,128)(2,1)S(1)}, bf16[32,1024]{1,0:T(8,128)(2,1)S(1)}, u32[]{:S(2)}, u32[]{:S(2)}) collective-permute-start(bf16[32,1024]{1,0:T(8,128)(2,1)S(1)} %get-tuple-element.30), channel_id=1, source_target_pairs={{0,8},{8,0},{16,24},{24,16},{32,40},{40,32},{48,56},{56,48},{64,72... | collective-permute-start | bytes 196616 | tf_op jit(solution)/shard_map/ppermute | solution.py:287
  98.4 1.2 %collective-permute-start.16 = (bf16[32,1024]{1,0:T(8,128)(2,1)S(1)}, bf16[32,1024]{1,0:T(8,128)(2,1)S(1)}, u32[]{:S(2)}, u32[]{:S(2)}) collective-permute-start(bf16[32,1024]{1,0:T(8,128)(2,1)S(1)} %get-tuple-element.31), channel_id=1, source_target_pairs={{0,16},{8,24},{16,0},{24,8},{32,48},{40,56},{48,32},{56,40},{64,80... | collective-permute-start | bytes 196616 | tf_op jit(solution)/shard_map/ppermute | solution.py:287
  99.6 0.5 collective-permute-start.17
  100.2 0.0 collective-permute-done.15.core_ref
  100.2 1.9 %collective-permute-done.16.half_ref = bf16[32,1024]{1,0:T(8,128)(2,1)S(1)} collective-permute-done((bf16[32,1024]{1,0:T(8,128)(2,1)S(1)}, bf16[32,1024]{1,0:T(8,128)(2,1)S(1)}, u32[]{:S(2)}, u32[]{:S(2)}) %collective-permute-start.16) | collective-permute-done | bytes 65568 | tf_op jit(solution)/shard_map/ppermute | solution.py:287
  102.1 1.6 %collective-permute-done.17.far_ref = bf16[32,1024]{1,0:T(8,128)(2,1)S(1)} collective-permute-done((bf16[32,1024]{1,0:T(8,128)(2,1)S(1)}, bf16[32,1024]{1,0:T(8,128)(2,1)S(1)}, u32[]{:S(2)}, u32[]{:S(2)}) %collective-permute-start.17) | collective-permute-done | bytes 65568 | tf_op jit(solution)/shard_map/ppermute | solution.py:287
  103.7 0.7 lay.1
Async XLA Ops:
  1.9 24.4 %collective-permute-start.9 = (bf16[256,1024]{1,0:T(8,128)(2,1)}, bf16[256,1024]{1,0:T(8,128)(2,1)S(1)}, u32[]{:S(2)}, u32[]{:S(2)}) collective-permute-start(bf16[256,1024]{1,0:T(8,128)(2,1)} %take.1.refs_0_), channel_id=1, source_target_pairs={{0,7},{1,0},{2,1},{3,2},{4,3},{5,4},{6,5},{7,6},{8,15},{9,8},{10,9... | collective-permute-start | bytes 1572872 | tf_op jit(solution)/shard_map/ppermute | solution.py:299
  8.4 17.9 %collective-permute-start.8 = (bf16[256,1024]{1,0:T(8,128)(2,1)}, bf16[256,1024]{1,0:T(8,128)(2,1)S(1)}, u32[]{:S(2)}, u32[]{:S(2)}) collective-permute-start(bf16[256,1024]{1,0:T(8,128)(2,1)} %take.1.refs_0_), channel_id=1, source_target_pairs={{0,1},{1,2},{2,3},{3,4},{4,5},{5,6},{6,7},{7,0},{8,9},{9,10},{10,1... | collective-permute-start | bytes 1572872 | tf_op jit(solution)/shard_map/ppermute | solution.py:299
  9.7 57.8 %copy-start.4 = (f32[256]{0:T(256)S(1)}, f32[256]{0:T(256)}, u32[]{:S(2)}) copy-start(f32[256]{0:T(256)} %param.16) | copy-start | bytes 3076
  23.9 71.5 %copy-start = (bf16[256,1024]{1,0:T(8,128)(2,1)S(1)}, bf16[256,1024]{1,0:T(8,128)(2,1)}, u32[]{:S(2)}) copy-start(bf16[256,1024]{1,0:T(8,128)(2,1)} %take.1.refs_0_) | copy-start | bytes 1572868
  23.9 2.3 %collective-permute-start = (bf16[256,512]{1,0:T(8,128)(2,1)}, bf16[256,512]{1,0:T(8,128)(2,1)S(1)}, u32[]{:S(2)}, u32[]{:S(2)}) collective-permute-start(bf16[256,512]{1,0:T(8,128)(2,1)} %get-tuple-element.19.own_ref), channel_id=1, source_target_pairs={{0,8},{8,0},{16,24},{24,16},{32,40},{40,32},{48,56},{56,48},{64,72... | collective-permute-start | bytes 786440 | tf_op jit(solution)/shard_map/ppermute | solution.py:287
  26.2 22.9 %collective-permute-start.10 = (bf16[256,1024]{1,0:T(8,128)(2,1)S(1)}, bf16[256,1024]{1,0:T(8,128)(2,1)S(1)}, u32[]{:S(2)}, u32[]{:S(2)}) collective-permute-start(bf16[256,1024]{1,0:T(8,128)(2,1)S(1)} %collective-permute-done.8.refs_1_), channel_id=1, source_target_pairs={{0,1},{1,2},{2,3},{3,4},{4,5},{5,6},{6,7},{7,0},{8,9},{9,10},{10,1... | collective-permute-start | bytes 1572872 | tf_op jit(solution)/shard_map/ppermute | solution.py:299
  26.3 22.9 %collective-permute-start.11 = (bf16[256,1024]{1,0:T(8,128)(2,1)S(1)}, bf16[256,1024]{1,0:T(8,128)(2,1)S(1)}, u32[]{:S(2)}, u32[]{:S(2)}) collective-permute-start(bf16[256,1024]{1,0:T(8,128)(2,1)S(1)} %collective-permute-done.9.refs_7_), channel_id=1, source_target_pairs={{0,7},{1,0},{2,1},{3,2},{4,3},{5,4},{6,5},{7,6},{8,15},{9,8},{10,9... | collective-permute-start | bytes 1572872 | tf_op jit(solution)/shard_map/ppermute | solution.py:299
  29.3 0.9 copy-start.1
  30.5 8.3 %collective-permute-start.3 = (bf16[256,512]{1,0:T(8,128)(2,1)S(1)}, bf16[256,512]{1,0:T(8,128)(2,1)S(1)}, u32[]{:S(2)}, u32[]{:S(2)}) collective-permute-start(bf16[256,512]{1,0:T(8,128)(2,1)S(1)} %pair.1.own_ref), channel_id=1, source_target_pairs={{0,48},{8,56},{16,0},{24,8},{32,16},{40,24},{48,32},{56,40},{64,11... | collective-permute-start | bytes 786440 | tf_op jit(solution)/shard_map/ppermute | solution.py:287
  33.0 8.4 %collective-permute-start.2 = (bf16[256,512]{1,0:T(8,128)(2,1)S(1)}, bf16[256,512]{1,0:T(8,128)(2,1)S(1)}, u32[]{:S(2)}, u32[]{:S(2)}) collective-permute-start(bf16[256,512]{1,0:T(8,128)(2,1)S(1)} %pair.1.own_ref), channel_id=1, source_target_pairs={{0,32},{8,40},{16,48},{24,56},{32,0},{40,8},{48,16},{56,24},{64,96... | collective-permute-start | bytes 786440 | tf_op jit(solution)/shard_map/ppermute | solution.py:287
  33.6 14.8 %collective-permute-start.1 = (bf16[256,512]{1,0:T(8,128)(2,1)S(1)}, bf16[256,512]{1,0:T(8,128)(2,1)S(1)}, u32[]{:S(2)}, u32[]{:S(2)}) collective-permute-start(bf16[256,512]{1,0:T(8,128)(2,1)S(1)} %pair.1.own_ref), channel_id=1, source_target_pairs={{0,16},{8,24},{16,32},{24,40},{32,48},{40,56},{48,0},{56,8},{64,80... | collective-permute-start | bytes 786440 | tf_op jit(solution)/shard_map/ppermute | solution.py:287
  49.1 28.5 %collective-permute-start.12 = (bf16[256,1024]{1,0:T(8,128)(2,1)S(1)}, bf16[256,1024]{1,0:T(8,128)(2,1)S(1)}, u32[]{:S(2)}, u32[]{:S(2)}) collective-permute-start(bf16[256,1024]{1,0:T(8,128)(2,1)S(1)} %collective-permute-done.10.refs_2_), channel_id=1, source_target_pairs={{0,1},{1,2},{2,3},{3,4},{4,5},{5,6},{6,7},{7,0},{8,9},{9,10},{10,1... | collective-permute-start | bytes 1572872 | tf_op jit(solution)/shard_map/ppermute | solution.py:299
  49.2 13.5 %collective-permute-start.6 = (bf16[256,512]{1,0:T(8,128)(2,1)S(1)}, bf16[256,512]{1,0:T(8,128)(2,1)S(1)}, u32[]{:S(2)}, u32[]{:S(2)}) collective-permute-start(bf16[256,512]{1,0:T(8,128)(2,1)S(1)} %get-tuple-element.20), channel_id=1, source_target_pairs={{0,192},{8,200},{16,208},{24,216},{32,224},{40,232},{48,240},{56,2... | collective-permute-start | bytes 786440 | tf_op jit(solution)/shard_map/ppermute | solution.py:287
  52.1 10.7 %collective-permute-start.5 = (bf16[256,512]{1,0:T(8,128)(2,1)S(1)}, bf16[256,512]{1,0:T(8,128)(2,1)S(1)}, u32[]{:S(2)}, u32[]{:S(2)}) collective-permute-start(bf16[256,512]{1,0:T(8,128)(2,1)S(1)} %get-tuple-element.20), channel_id=1, source_target_pairs={{0,128},{8,136},{16,144},{24,152},{32,160},{40,168},{48,176},{56,1... | collective-permute-start | bytes 786440 | tf_op jit(solution)/shard_map/ppermute | solution.py:287
  52.4 15.0 %collective-permute-start.4 = (bf16[256,512]{1,0:T(8,128)(2,1)S(1)}, bf16[256,512]{1,0:T(8,128)(2,1)S(1)}, u32[]{:S(2)}, u32[]{:S(2)}) collective-permute-start(bf16[256,512]{1,0:T(8,128)(2,1)S(1)} %get-tuple-element.20), channel_id=1, source_target_pairs={{0,64},{8,72},{16,80},{24,88},{32,96},{40,104},{48,112},{56,120},{... | collective-permute-start | bytes 786440 | tf_op jit(solution)/shard_map/ppermute | solution.py:287
  67.4 1.0 copy-start.2
  68.4 0.9 copy-start.3
  70.7 13.3 %all-to-all-start = ((bf16[16,32,256]{2,1,0:T(8,128)(2,1)}), bf16[16,32,256]{2,1,0:T(8,128)(2,1)S(1)}, u32[]{:S(2)}, u32[]{:S(2)}) async-start(bf16[16,32,256]{2,1,0:T(8,128)(2,1)} %bitcast.8), calls=%async_computation | async-start | bytes 524288 | tf_op jit(solution)/shard_map/all_to_all | solution.py:356
  75.0 18.8 %collective-permute-start.14 = (bf16[256,1024]{1,0:T(8,128)(2,1)S(1)}, bf16[256,1024]{1,0:T(8,128)(2,1)}, u32[]{:S(2)}, u32[]{:S(2)}) collective-permute-start(bf16[256,1024]{1,0:T(8,128)(2,1)S(1)} %collective-permute-done.11.refs_6_), channel_id=1, source_target_pairs={{0,7},{1,0},{2,1},{3,2},{4,3},{5,4},{6,5},{7,6},{8,15},{9,8},{10,9... | collective-permute-start | bytes 1572872 | tf_op jit(solution)/shard_map/ppermute | solution.py:299
  77.6 17.8 %collective-permute-start.13 = (bf16[256,1024]{1,0:T(8,128)(2,1)S(1)}, bf16[256,1024]{1,0:T(8,128)(2,1)}, u32[]{:S(2)}, u32[]{:S(2)}) collective-permute-start(bf16[256,1024]{1,0:T(8,128)(2,1)S(1)} %collective-permute-done.12.refs_3_), channel_id=1, source_target_pairs={{0,1},{1,2},{2,3},{3,4},{4,5},{5,6},{6,7},{7,0},{8,9},{9,10},{10,1... | collective-permute-start | bytes 1572872 | tf_op jit(solution)/shard_map/ppermute | solution.py:299
  84.0 4.3 %collective-permute-start.7 = (bf16[2,8,32,256]{3,2,1,0:T(8,128)(2,1)S(1)}, bf16[2,8,32,256]{3,2,1,0:T(8,128)(2,1)S(1)}, u32[]{:S(2)}, u32[]{:S(2)}) collective-permute-start(bf16[2,8,32,256]{3,2,1,0:T(8,128)(2,1)S(1)} %bitcast.13), channel_id=1, source_target_pairs={{0,8},{8,0},{16,24},{24,16},{32,40},{40,32},{48,56},{56,48},{64,72... | collective-permute-start | bytes 786440 | tf_op jit(solution)/shard_map/ppermute | solution.py:287
  97.3 2.8 %collective-permute-start.15 = (bf16[32,1024]{1,0:T(8,128)(2,1)S(1)}, bf16[32,1024]{1,0:T(8,128)(2,1)S(1)}, u32[]{:S(2)}, u32[]{:S(2)}) collective-permute-start(bf16[32,1024]{1,0:T(8,128)(2,1)S(1)} %get-tuple-element.30), channel_id=1, source_target_pairs={{0,8},{8,0},{16,24},{24,16},{32,40},{40,32},{48,56},{56,48},{64,72... | collective-permute-start | bytes 196616 | tf_op jit(solution)/shard_map/ppermute | solution.py:287
  98.4 3.7 %collective-permute-start.16 = (bf16[32,1024]{1,0:T(8,128)(2,1)S(1)}, bf16[32,1024]{1,0:T(8,128)(2,1)S(1)}, u32[]{:S(2)}, u32[]{:S(2)}) collective-permute-start(bf16[32,1024]{1,0:T(8,128)(2,1)S(1)} %get-tuple-element.31), channel_id=1, source_target_pairs={{0,16},{8,24},{16,0},{24,8},{32,48},{40,56},{48,32},{56,40},{64,80... | collective-permute-start | bytes 196616 | tf_op jit(solution)/shard_map/ppermute | solution.py:287
  99.6 4.1 %collective-permute-start.17 = (bf16[32,1024]{1,0:T(8,128)(2,1)S(1)}, bf16[32,1024]{1,0:T(8,128)(2,1)S(1)}, u32[]{:S(2)}, u32[]{:S(2)}) collective-permute-start(bf16[32,1024]{1,0:T(8,128)(2,1)S(1)} %get-tuple-element.32), channel_id=1, source_target_pairs={{0,24},{8,16},{16,8},{24,0},{32,56},{40,48},{48,40},{56,32},{64,88... | collective-permute-start | bytes 196616 | tf_op jit(solution)/shard_map/ppermute | solution.py:287

commit v3 on v2

--- a/solution.py
+++ b/solution.py
@@ -15,7 +15,7 @@
 SEQ = ("y", "xh", "xl", "core")
 SMALL = pltpu.CompilerParams(vmem_limit_bytes=8 << 20)
 MIDDLE = pltpu.CompilerParams(vmem_limit_bytes=16 << 20)
-LARGE = pltpu.CompilerParams(vmem_limit_bytes=58 << 20)
+LARGE = pltpu.CompilerParams(vmem_limit_bytes=57 << 20)
 
 
 def mm(a, b, dims=NN):
@@ -123,7 +123,19 @@
     return both[:, :n], both[:, n:] + later[:, n:].astype(F32)
 
 
-def pair_kernel(own_ref, other_ref, out_ref):
+def own_half(ref):
+    half = ref.shape[0] // 2
+    return ref[pl.ds(pl.multiple_of(lax.axis_index("core") * half, half), half)]
+
+
+def hold(held, place, near_ref, swap_ref):
+    half = near_ref.shape[0]
+    core = lax.axis_index("core")
+    held[place, pl.ds(pl.multiple_of(core * half, half), half)] = near_ref[...]
+    held[place, pl.ds(pl.multiple_of((1 - core) * half, half), half)] = swap_ref[...]
+
+
+def pair_kernel(own_ref, other_ref, out_ref, half_ref):
     n = own_ref.shape[0]
     first = lax.axis_index("core") == 0
     own, other = own_ref[...], other_ref[...]
@@ -132,13 +144,16 @@
     a, b = after(later, earlier, n)
     out_ref[:, :n] = a.astype(BF16)
     out_ref[:, n:] = b.astype(BF16)
-
-
-def row_kernel(own_ref, one_ref, two_ref, three_ref, total_ref, prefix_ref, held):
+    half_ref[...] = own_half(out_ref)
+
+
+def row_kernel(own_ref, *refs):
+    near, swapped, (half_ref, prefix_ref, held, total_ref) = refs[:3], refs[3:6], refs[6:]
     n = own_ref.shape[0]
     place = lax.axis_index("xh") * 2 + lax.axis_index("xl")
-    for shift, ref in enumerate((own_ref, one_ref, two_ref, three_ref)):
-        held[(place + (4 - shift)) % 4] = ref[...]
+    held[place] = own_ref[...]
+    for shift, ref, swap in zip((1, 2, 3), near, swapped):
+        hold(held, (place + (4 - shift)) % 4, ref, swap)
 
     def joined(later, earlier):
         a, b = after(later, earlier, n)
@@ -149,6 +164,7 @@
     a, b = after(high, low, n)
     total_ref[:, :n] = a.astype(BF16)
     total_ref[:, n:] = b.astype(BF16)
+    half_ref[...] = own_half(total_ref)
 
     @pl.when(place == 0)
     def _():
@@ -167,14 +183,13 @@
         prefix_ref[...] = joined(held[2], low)
 
 
-def read_kernel(
-    one_ref, two_ref, three_ref, prefix_ref, other_ref, query_ref, local_ref, gain_ref,
-    out_ref, held, state,
-):
+def read_kernel(*refs):
+    near, swapped = refs[:3], refs[3:6]
+    prefix_ref, other_ref, query_ref, local_ref, gain_ref, out_ref, held, state = refs[6:]
     n = query_ref.shape[0]
     place = lax.axis_index("y")
-    for shift, ref in enumerate((one_ref, two_ref, three_ref)):
-        held[(place + (3 - shift)) % 4] = ref[...]
+    for shift, ref, swap in zip((1, 2, 3), near, swapped):
+        hold(held, (place + (4 - shift)) % 4, ref, swap)
 
     def push(pair, value):
         hi, lo = split(value)
@@ -208,26 +223,18 @@
     out_ref[1] = flat
 
 
-def take_kernel(whole_ref, out_ref, sem):
-    width = out_ref.shape[1]
-    block = lax.axis_index("core") * 2 + lax.axis_index("xl")
-    columns = pl.ds(pl.multiple_of(block * width, width), width)
-    copy = pltpu.make_async_copy(whole_ref.at[:, columns], out_ref, sem)
-    copy.start()
-    copy.wait()
-
-
 def mix_kernel(own_ref, other_ref, *refs):
-    weights, outs = refs[:8], refs[8:]
+    weights, across, outs = refs[:7], refs[7:9], refs[9:]
     core, half, head = lax.axis_index("core"), lax.axis_index("xl"), lax.axis_index("head")
     rows = own_ref.shape[2]
-    for shift, ref in enumerate(weights):
+    for shift, refs in zip((0, 1, 2, 3, 5, 6, 7, 4), [(ref,) for ref in weights] + [across]):
         source = (head + (8 - shift)) % 8
         block = []
         for place in (half, 1 - half):
             for ref_x in (own_ref, other_ref):
                 block.append(ref_x[place, source])
-        part = mm(jnp.concatenate(block, axis=0), ref[...])
+        block = jnp.concatenate(block, axis=0)
+        part = jnp.concatenate([mm(block, ref[...]) for ref in refs], axis=1)
         total = part if shift == 0 else total + part
     total = total.astype(BF16)
     for k, ref in enumerate(outs):
@@ -302,56 +309,51 @@
         return lax.optimization_barrier((values, gate))[0]
 
     quarter = out_weight.shape[1] // 4
-    mine = pl.pallas_call(
-        take_kernel,
-        name="take",
-        in_specs=[pl.BlockSpec(memory_space=pl.ANY)],
-        out_specs=vmem(),
-        out_shape=jax.ShapeDtypeStruct((n, quarter), BF16),
-        scratch_shapes=[pltpu.SemaphoreType.DMA],
-        compiler_params=LARGE,
-    )(out_weight)
-    up = [along_z(mine, 1)]
-    down = [along_z(mine, -1)]
+    block = lax.axis_index("core") * 2 + lax.axis_index("xl")
+    mine = lax.dynamic_slice_in_dim(out_weight, block * quarter, quarter, 1)
+    up_one, down_one = along_z(mine, 1), along_z(mine, -1)
 
     pair_shape = jax.ShapeDtypeStruct((n, 2 * n), BF16)
+    half_shape = jax.ShapeDtypeStruct((n // 2, 2 * n), BF16)
     other = moved(carry, flip(1))
-    pair = pl.pallas_call(
+    pair, half = pl.pallas_call(
         pair_kernel,
         name="pair",
         in_specs=[vmem()] * 2,
-        out_specs=vmem(),
-        out_shape=pair_shape,
+        out_specs=[vmem()] * 2,
+        out_shape=[pair_shape, half_shape],
         compiler_params=SMALL,
     )(carry, other)
-    near = [moved(pair, along_x(s)) for s in (1, 2, 3)]
-    ahead, behind = later((up[-1], down[-1]), other)
-    up.append(along_z(ahead, 1))
-    down.append(along_z(behind, -1))
-    total, prefix = pl.pallas_call(
+    near = [moved(half, along_x(s)) for s in (1, 2, 3)]
+    swapped = [moved(value, flip(1)) for value in near]
+    ahead, behind = later((up_one, down_one), near)
+    up_two, down_two = along_z(ahead, 1), along_z(behind, -1)
+    half, prefix = pl.pallas_call(
         row_kernel,
         name="row",
-        in_specs=[vmem()] * 4,
+        in_specs=[vmem()] * 7,
         out_specs=[vmem()] * 2,
-        out_shape=[pair_shape] * 2,
-        scratch_shapes=[pltpu.VMEM((4, n, 2 * n), BF16)],
+        out_shape=[half_shape, pair_shape],
+        scratch_shapes=[pltpu.VMEM((4, n, 2 * n), BF16), pltpu.VMEM((n, 2 * n), BF16)],
         compiler_params=SMALL,
-    )(pair, *near)
-    far = [moved(total, along_y(s)) for s in (1, 2, 3)]
-    ahead, behind = later((up[-1], down[-1]), total)
-    up.append(along_z(ahead, 1))
-    down.append(along_z(behind, -1))
+    )(pair, *near, *swapped)
+    near = [moved(half, along_y(s)) for s in (1, 2, 3)]
+    swapped = [moved(value, flip(1)) for value in near]
+    ahead, behind = later((up_two, down_two), near)
+    up_three, down_three = along_z(ahead, 1), along_z(behind, -1)
     flat = pl.pallas_call(
         read_kernel,
         name="read",
-        in_specs=[vmem()] * 8,
+        in_specs=[vmem()] * 11,
         out_specs=vmem(),
         out_shape=jax.ShapeDtypeStruct((2, rows, n), BF16),
         scratch_shapes=[pltpu.VMEM((4, n, 2 * n), BF16), pltpu.VMEM((n, n), F32)],
         compiler_params=SMALL,
-    )(*far, prefix, other, query, local, out_gain.reshape(1, n))
-    ahead = later(up[-1], far[-1])
-    up.append(along_z(ahead, 1))
+    )(*near, *swapped, prefix, other, query, local, out_gain.reshape(1, n))
+    across = [
+        along_z(up_three[:, : quarter // 2], 1),
+        along_z(down_three[:, quarter // 2 :], -1),
+    ]
     part = rows // 8
     reads = lax.all_to_all(
         flat.reshape(16, part, n), ("xl", "head"), 0, 0, tiled=True
@@ -361,11 +363,11 @@
     kept, to_core, to_half, to_far = pl.pallas_call(
         mix_kernel,
         name="mix",
-        in_specs=[vmem()] * 10,
+        in_specs=[vmem()] * 11,
         out_specs=[vmem()] * 4,
         out_shape=[piece] * 4,
         compiler_params=MIDDLE,
-    )(reads, beside, mine, *up, *down[::-1])
+    )(reads, beside, mine, up_one, up_two, up_three, down_three, down_two, down_one, *across)
     return pl.pallas_call(
         lay_kernel,
         name="lay",

time: 105 us -> 98.8 us (0.941)
  waiting for transfers between devices: 48 us -> 27.5 us
  blocking collectives: 0 us -> 13.9 us
  Pallas kernels: 21.1 us -> 17.2 us
  starting transfers between devices: 31 us -> 33.9 us
  local copies, waits for them, and re-layouts: 2.86 us -> 4.51 us
    ppermute x11 -> x17, waiting for transfers between devices: 34.6 us -> 19.9 us  [moved(): return lax.ppermute(value, SEQ, [(i, place_of(i)) for i in range(count)])]
    all_to_all x0 -> x1, blocking collectives: none -> 13.9 us  [per_device(): lax.all_to_all(flat.reshape(16, part, n), ('xl', 'head'), 0, 0, tiled=True)]
    all_to_all x1 -> x0, waiting for transfers between devices: 6.42 us -> none  [per_device(): lax.all_to_all(flat.reshape(16, part, n), ('xl', 'head'), 0, 0, tiled=True)]
    all_to_all x1 -> x0, starting transfers between devices: 4.3 us -> none  [per_device(): lax.all_to_all(flat.reshape(16, part, n), ('xl', 'head'), 0, 0, tiled=True)]
    pallas_call x4 -> x3, Pallas kernels: 5.93 us -> 1.98 us  [the longest x1 0.71 us: per_device(): pl.pallas_call(mix_kernel, name='mix', in_specs=[vmem()] * 11, out_specs=...]
    ppermute x7 -> x8, starting transfers between devices: 12.2 us -> 16.1 us  [along_z(): return lax.ppermute(value, 'head', [(i, (i + shift) % 8) for i in range(8)])]
    ppermute x11 -> x17, starting transfers between devices: 14.5 us -> 17.9 us  [moved(): return lax.ppermute(value, SEQ, [(i, place_of(i)) for i in range(count)])]
    unnamed x10, local copies, waits for them, and re-layouts: 2.86 us -> 4.44 us
  transfers between devices with their start and end apart: 19 -> 25, of which waited for: 12 -> 13; matrix products, arithmetic and copies ran while one was open for 0% -> 0% of each run, Pallas kernels for 16% -> 16%
where the time goes in v3:
time: 98.8 us; the launch traced here: 98.5 us
  starting transfers between devices  33.9 us (34%)
  waiting for transfers between devices  27.5 us (28%)
  Pallas kernels  17.2 us (17%)
  blocking collectives  13.9 us (14%)
  local copies, waits for them, and re-layouts  4.51 us (5%)
  between operations  1.42 us (1%)
    ppermute x17, waiting for transfers between devices, moved(): return lax.ppermute(value, SEQ, [(i, place_of(i)) for i in range(count)])  19.9 us
    ppermute x17, starting transfers between devices, moved(): return lax.ppermute(value, SEQ, [(i, place_of(i)) for i in range(count)])  17.9 us
    ppermute x8, starting transfers between devices, along_z(): return lax.ppermute(value, 'head', [(i, (i + shift) % 8) for i in range(8)])  16.1 us
    pallas_call x1, Pallas kernels, per_device(): pl.pallas_call(chunk_kernel, name='chunk', grid=(width // KB,), in_specs=...  14.2 us
    all_to_all x1, blocking collectives, per_device(): lax.all_to_all(flat.reshape(16, part, n), ('xl', 'head'), 0, 0, tiled=True)  13.9 us
    ppermute x8, waiting for transfers between devices, along_z(): return lax.ppermute(value, 'head', [(i, (i + shift) % 8) for i in range(8)])  7.61 us
    unnamed x10, local copies, waits for them, and re-layouts  4.44 us
  transfers between devices with their start and end apart: 25, of which 13 were waited for; matrix products, arithmetic and copies ran while one was open for 0% of the time, Pallas kernels for 16%

profile of v3, /device:TPU:1, one launch (start us, length us, event | category | flops | bytes accessed | tf_op | source)
XLA Modules:
  0.0 98.5 jit_solution(13561064212994590137)
XLA Ops:
  0.0 0.0 copy-start
  0.0 1.6 %copy-done = bf16[256,4096]{1,0:T(8,128)(2,1)S(1)} copy-done((bf16[256,4096]{1,0:T(8,128)(2,1)S(1)}, bf16[256,4096]{1,0:T(8,128)(2,1)}, u32[]{:S(2)}) %copy-start) | copy-done | bytes 2097176
  1.6 6.5 %collective-permute-start.15 = (bf16[256,1024]{1,0:T(8,128)(2,1)S(1)}, bf16[256,1024]{1,0:T(8,128)(2,1)S(1)}, u32[]{:S(2)}, u32[]{:S(2)}) collective-permute-start(bf16[256,1024]{1,0:T(8,128)(2,1)S(1)} %constant_dynamic-slice_fusion.refs_0_), channel_id=1, source_target_pairs={{0,7},{1,0},{2,1},{3,2},{4,3},{5,4},{6,5},{7,6},{8,15},{9,8},{10,9... | collective-permute-start | bytes 1572872 | tf_op jit(solution)/shard_map/ppermute | solution.py:306
  8.1 0.0 collective-permute-start.14
  9.4 0.0 copy-start.4
  9.4 14.2 %chunk.1 = (bf16[256,512]{1,0:T(8,128)(2,1)}, f32[256,256]{1,0:T(8,128)}, f32[256,256]{1,0:T(8,128)}) custom-call(f32[1,1]{1,0:T(1,128)} %bitcast.11.scale_ref, f32[1,1]{1,0:T(1,128)} %bitcast.12.rate_ref, bf16[256,4096]{1,0:T(8,128)(2,1)} %x_ref.1, f32[1,4096]{1,0:T(1,128)} %bitcast.18, bf16[3,4096,256]{2,1,0:T(8,128)(2,1)} %bitcast.17, ...), custom_call_target="tpu_custom_call" | custom-call | tf_op jit(solution)/shard_map/chunk/pallas_call | solution.py:264
  23.7 0.9 collective-permute-start
  24.6 1.4 %collective-permute-done.other_ref.refs_7_ = bf16[256,512]{1,0:T(8,128)(2,1)S(1)} collective-permute-done((bf16[256,512]{1,0:T(8,128)(2,1)}, bf16[256,512]{1,0:T(8,128)(2,1)S(1)}, u32[]{:S(2)}, u32[]{:S(2)}) %collective-permute-start) | collective-permute-done | bytes 262176 | tf_op jit(solution)/shard_map/ppermute | solution.py:294
  26.0 0.9 copy-done.1
  26.9 0.3 pair.1
  27.2 2.6 %collective-permute-start.3 = (bf16[128,512]{1,0:T(8,128)(2,1)S(1)}, bf16[128,512]{1,0:T(8,128)(2,1)S(1)}, u32[]{:S(2)}, u32[]{:S(2)}) collective-permute-start(bf16[128,512]{1,0:T(8,128)(2,1)S(1)} %get-tuple-element.22), channel_id=1, source_target_pairs={{0,48},{8,56},{16,0},{24,8},{32,16},{40,24},{48,32},{56,40},{64,11... | collective-permute-start | bytes 393224 | tf_op jit(solution)/shard_map/ppermute | solution.py:294
  29.8 0.5 collective-permute-start.2
  30.3 0.6 collective-permute-start.1
  30.9 4.0 %collective-permute-done.3.refs_2_ = bf16[128,512]{1,0:T(8,128)(2,1)S(1)} collective-permute-done((bf16[128,512]{1,0:T(8,128)(2,1)S(1)}, bf16[128,512]{1,0:T(8,128)(2,1)S(1)}, u32[]{:S(2)}, u32[]{:S(2)}) %collective-permute-start.3) | collective-permute-done | bytes 131104 | tf_op jit(solution)/shard_map/ppermute | solution.py:294
  35.0 0.7 collective-permute-done.2.refs_1_
  35.7 3.8 %collective-permute-done.1.refs_0_ = bf16[128,512]{1,0:T(8,128)(2,1)S(1)} collective-permute-done((bf16[128,512]{1,0:T(8,128)(2,1)S(1)}, bf16[128,512]{1,0:T(8,128)(2,1)S(1)}, u32[]{:S(2)}, u32[]{:S(2)}) %collective-permute-start.1) | collective-permute-done | bytes 131104 | tf_op jit(solution)/shard_map/ppermute | solution.py:294
  39.5 0.0 collective-permute-done.15.refs_6_
  39.5 0.0 collective-permute-done.14.refs_1_
  39.5 0.0 collective-permute-start.16
  39.5 3.0 %collective-permute-start.17 = (bf16[256,1024]{1,0:T(8,128)(2,1)S(1)}, bf16[256,1024]{1,0:T(8,128)(2,1)S(1)}, u32[]{:S(2)}, u32[]{:S(2)}) collective-permute-start(bf16[256,1024]{1,0:T(8,128)(2,1)S(1)} %collective-permute-done.15.refs_6_), channel_id=1, source_target_pairs={{0,7},{1,0},{2,1},{3,2},{4,3},{5,4},{6,5},{7,6},{8,15},{9,8},{10,9... | collective-permute-start | bytes 1572872 | tf_op jit(solution)/shard_map/ppermute | solution.py:306
  42.6 0.8 collective-permute-start.6
  43.3 0.0 collective-permute-start.5
  43.3 0.5 collective-permute-start.4
  43.8 0.5 collective-permute-done.6.refs_5_
  44.3 0.4 collective-permute-done.5.refs_4_
  44.7 0.2 collective-permute-done.4.refs_3_
  44.9 0.6 row.1
  45.4 2.8 %collective-permute-start.9 = (bf16[128,512]{1,0:T(8,128)(2,1)S(1)}, bf16[128,512]{1,0:T(8,128)(2,1)S(1)}, u32[]{:S(2)}, u32[]{:S(2)}) collective-permute-start(bf16[128,512]{1,0:T(8,128)(2,1)S(1)} %get-tuple-element.23), channel_id=1, source_target_pairs={{0,192},{8,200},{16,208},{24,216},{32,224},{40,232},{48,240},{56,2... | collective-permute-start | bytes 393224 | tf_op jit(solution)/shard_map/ppermute | solution.py:294
  48.3 0.3 collective-permute-start.8
  48.6 0.7 collective-permute-start.7
  49.3 4.2 %collective-permute-done.9.refs_2_ = bf16[128,512]{1,0:T(8,128)(2,1)S(1)} collective-permute-done((bf16[128,512]{1,0:T(8,128)(2,1)S(1)}, bf16[128,512]{1,0:T(8,128)(2,1)S(1)}, u32[]{:S(2)}, u32[]{:S(2)}) %collective-permute-start.9) | collective-permute-done | bytes 131104 | tf_op jit(solution)/shard_map/ppermute | solution.py:294
  53.5 1.3 %collective-permute-start.12 = (bf16[128,512]{1,0:T(8,128)(2,1)S(1)}, bf16[128,512]{1,0:T(8,128)(2,1)S(1)}, u32[]{:S(2)}, u32[]{:S(2)}) collective-permute-start(bf16[128,512]{1,0:T(8,128)(2,1)S(1)} %collective-permute-done.9.refs_2_), channel_id=1, source_target_pairs={{0,8},{8,0},{16,24},{24,16},{32,40},{40,32},{48,56},{56,48},{64,72... | collective-permute-start | bytes 393224 | tf_op jit(solution)/shard_map/ppermute | solution.py:294
  54.8 0.0 collective-permute-done.8.refs_1_
  54.8 2.0 %collective-permute-start.11 = (bf16[128,512]{1,0:T(8,128)(2,1)S(1)}, bf16[128,512]{1,0:T(8,128)(2,1)S(1)}, u32[]{:S(2)}, u32[]{:S(2)}) collective-permute-start(bf16[128,512]{1,0:T(8,128)(2,1)S(1)} %collective-permute-done.8.refs_1_), channel_id=1, source_target_pairs={{0,8},{8,0},{16,24},{24,16},{32,40},{40,32},{48,56},{56,48},{64,72... | collective-permute-start | bytes 393224 | tf_op jit(solution)/shard_map/ppermute | solution.py:294
  56.8 1.2 %collective-permute-done.7.refs_0_ = bf16[128,512]{1,0:T(8,128)(2,1)S(1)} collective-permute-done((bf16[128,512]{1,0:T(8,128)(2,1)S(1)}, bf16[128,512]{1,0:T(8,128)(2,1)S(1)}, u32[]{:S(2)}, u32[]{:S(2)}) %collective-permute-start.7) | collective-permute-done | bytes 131104 | tf_op jit(solution)/shard_map/ppermute | solution.py:294
  58.0 0.5 collective-permute-start.10
  58.5 0.0 collective-permute-done.16.refs_2_
  58.5 0.0 collective-permute-done.17.refs_5_
  58.5 0.0 collective-permute-start.18
  58.5 2.7 %collective-permute-start.19 = (bf16[256,1024]{1,0:T(8,128)(2,1)S(1)}, bf16[256,1024]{1,0:T(8,128)(2,1)S(1)}, u32[]{:S(2)}, u32[]{:S(2)}) collective-permute-start(bf16[256,1024]{1,0:T(8,128)(2,1)S(1)} %collective-permute-done.17.refs_5_), channel_id=1, source_target_pairs={{0,7},{1,0},{2,1},{3,2},{4,3},{5,4},{6,5},{7,6},{8,15},{9,8},{10,9... | collective-permute-start | bytes 1572872 | tf_op jit(solution)/shard_map/ppermute | solution.py:306
  61.2 0.0 collective-permute-done.12.refs_5_
  61.2 0.0 collective-permute-done.11.refs_4_
  61.2 0.0 collective-permute-done.10.refs_3_
  61.2 0.0 copy-done.4
  61.2 0.9 copy-done.2
  62.2 0.9 copy-done.3
  63.1 0.7 read.1
  63.8 13.9 %all_to_all.5 = bf16[16,32,256]{2,1,0:T(8,128)(2,1)S(1)} all-to-all(bf16[16,32,256]{2,1,0:T(8,128)(2,1)S(1)} %bitcast.15), channel_id=1, replica_groups=mesh['y'=4,'xh'=2,'xl'=2,'core'=2,'head'=8] {'xl','head'}, dimensions={0} | all-to-all | bytes 524288 | tf_op jit(solution)/shard_map/all_to_all | solution.py:358
  77.7 1.4 %collective-permute-start.13 = (bf16[2,8,32,256]{3,2,1,0:T(8,128)(2,1)S(1)}, bf16[2,8,32,256]{3,2,1,0:T(8,128)(2,1)S(1)}, u32[]{:S(2)}, u32[]{:S(2)}) collective-permute-start(bf16[2,8,32,256]{3,2,1,0:T(8,128)(2,1)S(1)} %bitcast.13), channel_id=1, source_target_pairs={{0,8},{8,0},{16,24},{24,16},{32,40},{40,32},{48,56},{56,48},{64,72... | collective-permute-start | bytes 786440 | tf_op jit(solution)/shard_map/ppermute | solution.py:294
  79.1 0.0 collective-permute-done.18.refs_3_
  79.1 3.8 %collective-permute-start.20 = (bf16[256,512]{1,0:T(8,128)(2,1)S(1)}, bf16[256,512]{1,0:T(8,128)(2,1)S(1)}, u32[]{:S(2)}, u32[]{:S(2)}) collective-permute-start(bf16[256,512]{1,0:T(8,128)(2,1)S(1)} %slice.8), channel_id=1, source_target_pairs={{0,1},{1,2},{2,3},{3,4},{4,5},{5,6},{6,7},{7,0},{8,9},{9,10},{10,1... | collective-permute-start | bytes 786440 | tf_op jit(solution)/shard_map/ppermute | solution.py:306
  82.9 0.0 collective-permute-done.19.refs_4_
  82.9 0.1 collective-permute-start.21
  83.0 0.0 collective-permute-done.13.other_ref
  83.0 5.7 %collective-permute-done.20.refs_7_ = bf16[256,512]{1,0:T(8,128)(2,1)S(1)} collective-permute-done((bf16[256,512]{1,0:T(8,128)(2,1)S(1)}, bf16[256,512]{1,0:T(8,128)(2,1)S(1)}, u32[]{:S(2)}, u32[]{:S(2)}) %collective-permute-start.20) | collective-permute-done | bytes 262176 | tf_op jit(solution)/shard_map/ppermute | solution.py:306
  88.7 1.9 %collective-permute-done.21.refs_8_ = bf16[256,512]{1,0:T(8,128)(2,1)S(1)} collective-permute-done((bf16[256,512]{1,0:T(8,128)(2,1)S(1)}, bf16[256,512]{1,0:T(8,128)(2,1)S(1)}, u32[]{:S(2)}, u32[]{:S(2)}) %collective-permute-start.21) | collective-permute-done | bytes 262176 | tf_op jit(solution)/shard_map/ppermute | solution.py:306
  90.6 0.7 mix.1
  91.3 1.2 %collective-permute-start.22 = (bf16[32,1024]{1,0:T(8,128)(2,1)S(1)}, bf16[32,1024]{1,0:T(8,128)(2,1)S(1)}, u32[]{:S(2)}, u32[]{:S(2)}) collective-permute-start(bf16[32,1024]{1,0:T(8,128)(2,1)S(1)} %get-tuple-element.32), channel_id=1, source_target_pairs={{0,8},{8,0},{16,24},{24,16},{32,40},{40,32},{48,56},{56,48},{64,72... | collective-permute-start | bytes 196616 | tf_op jit(solution)/shard_map/ppermute | solution.py:294
  92.5 0.8 collective-permute-start.23
  93.4 0.9 collective-permute-start.24
  94.2 0.0 collective-permute-done.22.core_ref
  94.3 1.9 %collective-permute-done.23.half_ref = bf16[32,1024]{1,0:T(8,128)(2,1)S(1)} collective-permute-done((bf16[32,1024]{1,0:T(8,128)(2,1)S(1)}, bf16[32,1024]{1,0:T(8,128)(2,1)S(1)}, u32[]{:S(2)}, u32[]{:S(2)}) %collective-permute-start.23) | collective-permute-done | bytes 65568 | tf_op jit(solution)/shard_map/ppermute | solution.py:294
  96.2 1.6 %collective-permute-done.24.far_ref = bf16[32,1024]{1,0:T(8,128)(2,1)S(1)} collective-permute-done((bf16[32,1024]{1,0:T(8,128)(2,1)S(1)}, bf16[32,1024]{1,0:T(8,128)(2,1)S(1)}, u32[]{:S(2)}, u32[]{:S(2)}) %collective-permute-start.24) | collective-permute-done | bytes 65568 | tf_op jit(solution)/shard_map/ppermute | solution.py:294
  97.8 0.7 lay.1
  (6 shorter events, 0.1 us)
Async XLA Ops:
  0.0 1.6 %copy-start = (bf16[256,4096]{1,0:T(8,128)(2,1)S(1)}, bf16[256,4096]{1,0:T(8,128)(2,1)}, u32[]{:S(2)}) copy-start(bf16[256,4096]{1,0:T(8,128)(2,1)} %param.17) | copy-start | bytes 6291460
  1.6 37.9 %collective-permute-start.15 = (bf16[256,1024]{1,0:T(8,128)(2,1)S(1)}, bf16[256,1024]{1,0:T(8,128)(2,1)S(1)}, u32[]{:S(2)}, u32[]{:S(2)}) collective-permute-start(bf16[256,1024]{1,0:T(8,128)(2,1)S(1)} %constant_dynamic-slice_fusion.refs_0_), channel_id=1, source_target_pairs={{0,7},{1,0},{2,1},{3,2},{4,3},{5,4},{6,5},{7,6},{8,15},{9,8},{10,9... | collective-permute-start | bytes 1572872 | tf_op jit(solution)/shard_map/ppermute | solution.py:306
  8.1 31.4 %collective-permute-start.14 = (bf16[256,1024]{1,0:T(8,128)(2,1)S(1)}, bf16[256,1024]{1,0:T(8,128)(2,1)S(1)}, u32[]{:S(2)}, u32[]{:S(2)}) collective-permute-start(bf16[256,1024]{1,0:T(8,128)(2,1)S(1)} %constant_dynamic-slice_fusion.refs_0_), channel_id=1, source_target_pairs={{0,1},{1,2},{2,3},{3,4},{4,5},{5,6},{6,7},{7,0},{8,9},{9,10},{10,1... | collective-permute-start | bytes 1572872 | tf_op jit(solution)/shard_map/ppermute | solution.py:306
  9.4 51.8 %copy-start.4 = (f32[256]{0:T(256)S(1)}, f32[256]{0:T(256)}, u32[]{:S(2)}) copy-start(f32[256]{0:T(256)} %param.16) | copy-start | bytes 3076
  23.7 2.3 %collective-permute-start = (bf16[256,512]{1,0:T(8,128)(2,1)}, bf16[256,512]{1,0:T(8,128)(2,1)S(1)}, u32[]{:S(2)}, u32[]{:S(2)}) collective-permute-start(bf16[256,512]{1,0:T(8,128)(2,1)} %get-tuple-element.20.own_ref), channel_id=1, source_target_pairs={{0,8},{8,0},{16,24},{24,16},{32,40},{40,32},{48,56},{56,48},{64,72... | collective-permute-start | bytes 786440 | tf_op jit(solution)/shard_map/ppermute | solution.py:294
  26.0 0.9 copy-start.1
  27.2 7.7 %collective-permute-start.3 = (bf16[128,512]{1,0:T(8,128)(2,1)S(1)}, bf16[128,512]{1,0:T(8,128)(2,1)S(1)}, u32[]{:S(2)}, u32[]{:S(2)}) collective-permute-start(bf16[128,512]{1,0:T(8,128)(2,1)S(1)} %get-tuple-element.22), channel_id=1, source_target_pairs={{0,48},{8,56},{16,0},{24,8},{32,16},{40,24},{48,32},{56,40},{64,11... | collective-permute-start | bytes 393224 | tf_op jit(solution)/shard_map/ppermute | solution.py:294
  29.8 5.9 %collective-permute-start.2 = (bf16[128,512]{1,0:T(8,128)(2,1)S(1)}, bf16[128,512]{1,0:T(8,128)(2,1)S(1)}, u32[]{:S(2)}, u32[]{:S(2)}) collective-permute-start(bf16[128,512]{1,0:T(8,128)(2,1)S(1)} %get-tuple-element.22), channel_id=1, source_target_pairs={{0,32},{8,40},{16,48},{24,56},{32,0},{40,8},{48,16},{56,24},{64,96... | collective-permute-start | bytes 393224 | tf_op jit(solution)/shard_map/ppermute | solution.py:294
  30.3 9.2 %collective-permute-start.1 = (bf16[128,512]{1,0:T(8,128)(2,1)S(1)}, bf16[128,512]{1,0:T(8,128)(2,1)S(1)}, u32[]{:S(2)}, u32[]{:S(2)}) collective-permute-start(bf16[128,512]{1,0:T(8,128)(2,1)S(1)} %get-tuple-element.22), channel_id=1, source_target_pairs={{0,16},{8,24},{16,32},{24,40},{32,48},{40,56},{48,0},{56,8},{64,80... | collective-permute-start | bytes 393224 | tf_op jit(solution)/shard_map/ppermute | solution.py:294
  39.5 19.0 %collective-permute-start.16 = (bf16[256,1024]{1,0:T(8,128)(2,1)S(1)}, bf16[256,1024]{1,0:T(8,128)(2,1)S(1)}, u32[]{:S(2)}, u32[]{:S(2)}) collective-permute-start(bf16[256,1024]{1,0:T(8,128)(2,1)S(1)} %collective-permute-done.14.refs_1_), channel_id=1, source_target_pairs={{0,1},{1,2},{2,3},{3,4},{4,5},{5,6},{6,7},{7,0},{8,9},{9,10},{10,1... | collective-permute-start | bytes 1572872 | tf_op jit(solution)/shard_map/ppermute | solution.py:306
  39.5 19.0 %collective-permute-start.17 = (bf16[256,1024]{1,0:T(8,128)(2,1)S(1)}, bf16[256,1024]{1,0:T(8,128)(2,1)S(1)}, u32[]{:S(2)}, u32[]{:S(2)}) collective-permute-start(bf16[256,1024]{1,0:T(8,128)(2,1)S(1)} %collective-permute-done.15.refs_6_), channel_id=1, source_target_pairs={{0,7},{1,0},{2,1},{3,2},{4,3},{5,4},{6,5},{7,6},{8,15},{9,8},{10,9... | collective-permute-start | bytes 1572872 | tf_op jit(solution)/shard_map/ppermute | solution.py:306
  42.6 1.8 %collective-permute-start.6 = (bf16[128,512]{1,0:T(8,128)(2,1)S(1)}, bf16[128,512]{1,0:T(8,128)(2,1)S(1)}, u32[]{:S(2)}, u32[]{:S(2)}) collective-permute-start(bf16[128,512]{1,0:T(8,128)(2,1)S(1)} %collective-permute-done.3.refs_2_), channel_id=1, source_target_pairs={{0,8},{8,0},{16,24},{24,16},{32,40},{40,32},{48,56},{56,48},{64,72... | collective-permute-start | bytes 393224 | tf_op jit(solution)/shard_map/ppermute | solution.py:294
  43.3 1.3 %collective-permute-start.5 = (bf16[128,512]{1,0:T(8,128)(2,1)S(1)}, bf16[128,512]{1,0:T(8,128)(2,1)S(1)}, u32[]{:S(2)}, u32[]{:S(2)}) collective-permute-start(bf16[128,512]{1,0:T(8,128)(2,1)S(1)} %collective-permute-done.2.refs_1_), channel_id=1, source_target_pairs={{0,8},{8,0},{16,24},{24,16},{32,40},{40,32},{48,56},{56,48},{64,72... | collective-permute-start | bytes 393224 | tf_op jit(solution)/shard_map/ppermute | solution.py:294
  43.3 1.5 %collective-permute-start.4 = (bf16[128,512]{1,0:T(8,128)(2,1)S(1)}, bf16[128,512]{1,0:T(8,128)(2,1)S(1)}, u32[]{:S(2)}, u32[]{:S(2)}) collective-permute-start(bf16[128,512]{1,0:T(8,128)(2,1)S(1)} %collective-permute-done.1.refs_0_), channel_id=1, source_target_pairs={{0,8},{8,0},{16,24},{24,16},{32,40},{40,32},{48,56},{56,48},{64,72... | collective-permute-start | bytes 393224 | tf_op jit(solution)/shard_map/ppermute | solution.py:294
  45.4 8.0 %collective-permute-start.9 = (bf16[128,512]{1,0:T(8,128)(2,1)S(1)}, bf16[128,512]{1,0:T(8,128)(2,1)S(1)}, u32[]{:S(2)}, u32[]{:S(2)}) collective-permute-start(bf16[128,512]{1,0:T(8,128)(2,1)S(1)} %get-tuple-element.23), channel_id=1, source_target_pairs={{0,192},{8,200},{16,208},{24,216},{32,224},{40,232},{48,240},{56,2... | collective-permute-start | bytes 393224 | tf_op jit(solution)/shard_map/ppermute | solution.py:294
  48.3 6.5 %collective-permute-start.8 = (bf16[128,512]{1,0:T(8,128)(2,1)S(1)}, bf16[128,512]{1,0:T(8,128)(2,1)S(1)}, u32[]{:S(2)}, u32[]{:S(2)}) collective-permute-start(bf16[128,512]{1,0:T(8,128)(2,1)S(1)} %get-tuple-element.23), channel_id=1, source_target_pairs={{0,128},{8,136},{16,144},{24,152},{32,160},{40,168},{48,176},{56,1... | collective-permute-start | bytes 393224 | tf_op jit(solution)/shard_map/ppermute | solution.py:294
  48.6 9.4 %collective-permute-start.7 = (bf16[128,512]{1,0:T(8,128)(2,1)S(1)}, bf16[128,512]{1,0:T(8,128)(2,1)S(1)}, u32[]{:S(2)}, u32[]{:S(2)}) collective-permute-start(bf16[128,512]{1,0:T(8,128)(2,1)S(1)} %get-tuple-element.23), channel_id=1, source_target_pairs={{0,64},{8,72},{16,80},{24,88},{32,96},{40,104},{48,112},{56,120},{... | collective-permute-start | bytes 393224 | tf_op jit(solution)/shard_map/ppermute | solution.py:294
  53.5 7.7 %collective-permute-start.12 = (bf16[128,512]{1,0:T(8,128)(2,1)S(1)}, bf16[128,512]{1,0:T(8,128)(2,1)S(1)}, u32[]{:S(2)}, u32[]{:S(2)}) collective-permute-start(bf16[128,512]{1,0:T(8,128)(2,1)S(1)} %collective-permute-done.9.refs_2_), channel_id=1, source_target_pairs={{0,8},{8,0},{16,24},{24,16},{32,40},{40,32},{48,56},{56,48},{64,72... | collective-permute-start | bytes 393224 | tf_op jit(solution)/shard_map/ppermute | solution.py:294
  54.8 6.4 %collective-permute-start.11 = (bf16[128,512]{1,0:T(8,128)(2,1)S(1)}, bf16[128,512]{1,0:T(8,128)(2,1)S(1)}, u32[]{:S(2)}, u32[]{:S(2)}) collective-permute-start(bf16[128,512]{1,0:T(8,128)(2,1)S(1)} %collective-permute-done.8.refs_1_), channel_id=1, source_target_pairs={{0,8},{8,0},{16,24},{24,16},{32,40},{40,32},{48,56},{56,48},{64,72... | collective-permute-start | bytes 393224 | tf_op jit(solution)/shard_map/ppermute | solution.py:294
  58.0 3.2 %collective-permute-start.10 = (bf16[128,512]{1,0:T(8,128)(2,1)S(1)}, bf16[128,512]{1,0:T(8,128)(2,1)S(1)}, u32[]{:S(2)}, u32[]{:S(2)}) collective-permute-start(bf16[128,512]{1,0:T(8,128)(2,1)S(1)} %collective-permute-done.7.refs_0_), channel_id=1, source_target_pairs={{0,8},{8,0},{16,24},{24,16},{32,40},{40,32},{48,56},{56,48},{64,72... | collective-permute-start | bytes 393224 | tf_op jit(solution)/shard_map/ppermute | solution.py:294
  58.5 20.6 %collective-permute-start.18 = (bf16[256,1024]{1,0:T(8,128)(2,1)S(1)}, bf16[256,1024]{1,0:T(8,128)(2,1)S(1)}, u32[]{:S(2)}, u32[]{:S(2)}) collective-permute-start(bf16[256,1024]{1,0:T(8,128)(2,1)S(1)} %collective-permute-done.16.refs_2_), channel_id=1, source_target_pairs={{0,1},{1,2},{2,3},{3,4},{4,5},{5,6},{6,7},{7,0},{8,9},{9,10},{10,1... | collective-permute-start | bytes 1572872 | tf_op jit(solution)/shard_map/ppermute | solution.py:306
  58.5 24.4 %collective-permute-start.19 = (bf16[256,1024]{1,0:T(8,128)(2,1)S(1)}, bf16[256,1024]{1,0:T(8,128)(2,1)S(1)}, u32[]{:S(2)}, u32[]{:S(2)}) collective-permute-start(bf16[256,1024]{1,0:T(8,128)(2,1)S(1)} %collective-permute-done.17.refs_5_), channel_id=1, source_target_pairs={{0,7},{1,0},{2,1},{3,2},{4,3},{5,4},{6,5},{7,6},{8,15},{9,8},{10,9... | collective-permute-start | bytes 1572872 | tf_op jit(solution)/shard_map/ppermute | solution.py:306
  61.2 1.0 copy-start.2
  62.2 0.9 copy-start.3
  77.7 5.3 %collective-permute-start.13 = (bf16[2,8,32,256]{3,2,1,0:T(8,128)(2,1)S(1)}, bf16[2,8,32,256]{3,2,1,0:T(8,128)(2,1)S(1)}, u32[]{:S(2)}, u32[]{:S(2)}) collective-permute-start(bf16[2,8,32,256]{3,2,1,0:T(8,128)(2,1)S(1)} %bitcast.13), channel_id=1, source_target_pairs={{0,8},{8,0},{16,24},{24,16},{32,40},{40,32},{48,56},{56,48},{64,72... | collective-permute-start | bytes 786440 | tf_op jit(solution)/shard_map/ppermute | solution.py:294
  79.1 9.6 %collective-permute-start.20 = (bf16[256,512]{1,0:T(8,128)(2,1)S(1)}, bf16[256,512]{1,0:T(8,128)(2,1)S(1)}, u32[]{:S(2)}, u32[]{:S(2)}) collective-permute-start(bf16[256,512]{1,0:T(8,128)(2,1)S(1)} %slice.8), channel_id=1, source_target_pairs={{0,1},{1,2},{2,3},{3,4},{4,5},{5,6},{6,7},{7,0},{8,9},{9,10},{10,1... | collective-permute-start | bytes 786440 | tf_op jit(solution)/shard_map/ppermute | solution.py:306
  82.9 7.7 %collective-permute-start.21 = (bf16[256,512]{1,0:T(8,128)(2,1)S(1)}, bf16[256,512]{1,0:T(8,128)(2,1)S(1)}, u32[]{:S(2)}, u32[]{:S(2)}) collective-permute-start(bf16[256,512]{1,0:T(8,128)(2,1)S(1)} %slice.9), channel_id=1, source_target_pairs={{0,7},{1,0},{2,1},{3,2},{4,3},{5,4},{6,5},{7,6},{8,15},{9,8},{10,9... | collective-permute-start | bytes 786440 | tf_op jit(solution)/shard_map/ppermute | solution.py:306
  91.3 2.9 %collective-permute-start.22 = (bf16[32,1024]{1,0:T(8,128)(2,1)S(1)}, bf16[32,1024]{1,0:T(8,128)(2,1)S(1)}, u32[]{:S(2)}, u32[]{:S(2)}) collective-permute-start(bf16[32,1024]{1,0:T(8,128)(2,1)S(1)} %get-tuple-element.32), channel_id=1, source_target_pairs={{0,8},{8,0},{16,24},{24,16},{32,40},{40,32},{48,56},{56,48},{64,72... | collective-permute-start | bytes 196616 | tf_op jit(solution)/shard_map/ppermute | solution.py:294
  92.5 3.7 %collective-permute-start.23 = (bf16[32,1024]{1,0:T(8,128)(2,1)S(1)}, bf16[32,1024]{1,0:T(8,128)(2,1)S(1)}, u32[]{:S(2)}, u32[]{:S(2)}) collective-permute-start(bf16[32,1024]{1,0:T(8,128)(2,1)S(1)} %get-tuple-element.33), channel_id=1, source_target_pairs={{0,16},{8,24},{16,0},{24,8},{32,48},{40,56},{48,32},{56,40},{64,80... | collective-permute-start | bytes 196616 | tf_op jit(solution)/shard_map/ppermute | solution.py:294
  93.4 4.4 %collective-permute-start.24 = (bf16[32,1024]{1,0:T(8,128)(2,1)S(1)}, bf16[32,1024]{1,0:T(8,128)(2,1)S(1)}, u32[]{:S(2)}, u32[]{:S(2)}) collective-permute-start(bf16[32,1024]{1,0:T(8,128)(2,1)S(1)} %get-tuple-element.34), channel_id=1, source_target_pairs={{0,24},{8,16},{16,8},{24,0},{32,56},{40,48},{48,40},{56,32},{64,88... | collective-permute-start | bytes 196616 | tf_op jit(solution)/shard_map/ppermute | solution.py:294

commit v4 on v3

--- a/solution.py
+++ b/solution.py
@@ -72,8 +72,8 @@
         key = unit_rows(acc_ref[1])
         value = acc_ref[2]
         gating = gating_ref[...]
-        beta_row = scale_ref[...] * jax.nn.sigmoid(gating[0:1])
-        logf_row = -rate_ref[...] * jax.nn.softplus(gating[1:2])
+        beta_row = scale_ref[0] * jax.nn.sigmoid(gating[0:1])
+        logf_row = -rate_ref[0] * jax.nn.softplus(gating[1:2])
         reset_row = resets_ref[...].astype(F32)
         t = lax.broadcasted_iota(jnp.int32, (n, n), 0)
         s = lax.broadcasted_iota(jnp.int32, (n, n), 1)
@@ -223,19 +223,13 @@
     out_ref[1] = flat
 
 
-def mix_kernel(own_ref, other_ref, *refs):
-    weights, across, outs = refs[:7], refs[7:9], refs[9:]
-    core, half, head = lax.axis_index("core"), lax.axis_index("xl"), lax.axis_index("head")
+def mix_kernel(own_ref, other_ref, weight_ref, *outs):
+    half = lax.axis_index("xl")
     rows = own_ref.shape[2]
-    for shift, refs in zip((0, 1, 2, 3, 5, 6, 7, 4), [(ref,) for ref in weights] + [across]):
-        source = (head + (8 - shift)) % 8
-        block = []
-        for place in (half, 1 - half):
-            for ref_x in (own_ref, other_ref):
-                block.append(ref_x[place, source])
-        block = jnp.concatenate(block, axis=0)
-        part = jnp.concatenate([mm(block, ref[...]) for ref in refs], axis=1)
-        total = part if shift == 0 else total + part
+    for head in range(weight_ref.shape[0]):
+        block = [ref[place, head] for place in (half, 1 - half) for ref in (own_ref, other_ref)]
+        part = mm(jnp.concatenate(block, axis=0), weight_ref[head])
+        total = part if head == 0 else total + part
     total = total.astype(BF16)
     for k, ref in enumerate(outs):
         ref[...] = total[k * rows : (k + 1) * rows]
@@ -266,8 +260,8 @@
         name="chunk",
         grid=(width // KB,),
         in_specs=[
-            whole((1, 1)),
-            whole((1, 1)),
+            pl.BlockSpec(memory_space=pltpu.SMEM),
+            pl.BlockSpec(memory_space=pltpu.SMEM),
             whole((rows, width)),
             whole((1, width)),
             pl.BlockSpec((3, KB, n), lambda i: (0, i, 0)),
@@ -286,7 +280,7 @@
             pltpu.VMEM((2, rows), F32),
         ],
         compiler_params=LARGE,
-    )(beta_scale.reshape(1, 1), decay_rate.reshape(1, 1), frames, norm_gain.reshape(1, width), weight, gate, resets.reshape(1, rows))
+    )(beta_scale, decay_rate, frames, norm_gain.reshape(1, width), weight, gate, resets.reshape(1, rows))
 
     count = 32
 
@@ -301,17 +295,11 @@
 
     def flip(bits):
         return lambda i: i ^ bits
-
-    def along_z(value, shift):
-        return lax.ppermute(value, "head", [(i, (i + shift) % 8) for i in range(8)])
-
-    def later(values, gate):
-        return lax.optimization_barrier((values, gate))[0]
 
     quarter = out_weight.shape[1] // 4
     block = lax.axis_index("core") * 2 + lax.axis_index("xl")
     mine = lax.dynamic_slice_in_dim(out_weight, block * quarter, quarter, 1)
-    up_one, down_one = along_z(mine, 1), along_z(mine, -1)
+    columns = lax.all_gather(mine, "head", tiled=False)
 
     pair_shape = jax.ShapeDtypeStruct((n, 2 * n), BF16)
     half_shape = jax.ShapeDtypeStruct((n // 2, 2 * n), BF16)
@@ -326,8 +314,6 @@
     )(carry, other)
     near = [moved(half, along_x(s)) for s in (1, 2, 3)]
     swapped = [moved(value, flip(1)) for value in near]
-    ahead, behind = later((up_one, down_one), near)
-    up_two, down_two = along_z(ahead, 1), along_z(behind, -1)
     half, prefix = pl.pallas_call(
         row_kernel,
         name="row",
@@ -339,8 +325,6 @@
     )(pair, *near, *swapped)
     near = [moved(half, along_y(s)) for s in (1, 2, 3)]
     swapped = [moved(value, flip(1)) for value in near]
-    ahead, behind = later((up_two, down_two), near)
-    up_three, down_three = along_z(ahead, 1), along_z(behind, -1)
     flat = pl.pallas_call(
         read_kernel,
         name="read",
@@ -350,10 +334,6 @@
         scratch_shapes=[pltpu.VMEM((4, n, 2 * n), BF16), pltpu.VMEM((n, n), F32)],
         compiler_params=SMALL,
     )(*near, *swapped, prefix, other, query, local, out_gain.reshape(1, n))
-    across = [
-        along_z(up_three[:, : quarter // 2], 1),
-        along_z(down_three[:, quarter // 2 :], -1),
-    ]
     part = rows // 8
     reads = lax.all_to_all(
         flat.reshape(16, part, n), ("xl", "head"), 0, 0, tiled=True
@@ -363,11 +343,11 @@
     kept, to_core, to_half, to_far = pl.pallas_call(
         mix_kernel,
         name="mix",
-        in_specs=[vmem()] * 11,
+        in_specs=[vmem()] * 3,
         out_specs=[vmem()] * 4,
         out_shape=[piece] * 4,
         compiler_params=MIDDLE,
-    )(reads, beside, mine, up_one, up_two, up_three, down_three, down_two, down_one, *across)
+    )(reads, beside, columns)
     return pl.pallas_call(
         lay_kernel,
         name="lay",

time: 98.8 us -> 94.3 us (0.954)
  starting transfers between devices: 33.9 us -> 20.6 us
  between operations: 1.42 us -> 14.7 us
  waiting for transfers between devices: 27.5 us -> 15.6 us
  blocking collectives: 13.9 us -> 18.2 us
  local copies, waits for them, and re-layouts: 4.51 us -> 7.5 us
    ppermute x8 -> x0, starting transfers between devices: 16.1 us -> none  [along_z(): return lax.ppermute(value, 'head', [(i, (i + shift) % 8) for i in range(8)])]
    ppermute x8 -> x0, waiting for transfers between devices: 7.61 us -> none  [along_z(): return lax.ppermute(value, 'head', [(i, (i + shift) % 8) for i in range(8)])]
    ppermute x17, waiting for transfers between devices: 19.9 us -> 15.6 us  [moved(): return lax.ppermute(value, SEQ, [(i, place_of(i)) for i in range(count)])]
    all_to_all x1, blocking collectives: 13.9 us -> 18.2 us  [per_device(): lax.all_to_all(flat.reshape(16, part, n), ('xl', 'head'), 0, 0, tiled=True)]
    ppermute x17, starting transfers between devices: 17.9 us -> 20.6 us  [moved(): return lax.ppermute(value, SEQ, [(i, place_of(i)) for i in range(count)])]
    unnamed x10 -> x12, local copies, waits for them, and re-layouts: 4.44 us -> 6.64 us
  transfers between devices with their start and end apart: 25 -> 18, of which waited for: 13 -> 12; matrix products, arithmetic and copies ran while one was open for 0% -> 0% of each run, Pallas kernels for 16% -> 17%
where the time goes in v4:
time: 94.3 us; the launch traced here: 93.9 us
  starting transfers between devices  20.6 us (22%)
  blocking collectives  18.2 us (19%)
  Pallas kernels  17.3 us (18%)
  waiting for transfers between devices  15.6 us (17%)
  between operations  14.7 us (16%)
  local copies, waits for them, and re-layouts  7.5 us (8%)
    ppermute x17, starting transfers between devices, moved(): return lax.ppermute(value, SEQ, [(i, place_of(i)) for i in range(count)])  20.6 us
    all_to_all x1, blocking collectives, per_device(): lax.all_to_all(flat.reshape(16, part, n), ('xl', 'head'), 0, 0, tiled=True)  18.2 us
    ppermute x17, waiting for transfers between devices, moved(): return lax.ppermute(value, SEQ, [(i, place_of(i)) for i in range(count)])  15.6 us
    pallas_call x1, Pallas kernels, per_device(): pl.pallas_call(chunk_kernel, name='chunk', grid=(width // KB,), in_specs=...  14.3 us
    unnamed x12, local copies, waits for them, and re-layouts  6.64 us
  transfers between devices with their start and end apart: 18, of which 12 were waited for; matrix products, arithmetic and copies ran while one was open for 0% of the time, Pallas kernels for 17%

profile of v4, /device:TPU:1, one launch (start us, length us, event | category | flops | bytes accessed | tf_op | source)
XLA Modules:
  0.0 93.9 jit_solution(2193809197647748335)
XLA Ops:
  6.5 0.0 copy-start
  6.5 0.0 all-gather.3.cloned.1.call-start
  6.5 1.6 %copy-done = bf16[256,4096]{1,0:T(8,128)(2,1)S(1)} copy-done((bf16[256,4096]{1,0:T(8,128)(2,1)S(1)}, bf16[256,4096]{1,0:T(8,128)(2,1)}, u32[]{:S(2)}) %copy-start) | copy-done | bytes 2097176
  8.1 0.9 constant_dynamic-slice_fusion
  9.0 0.0 all-gather.3.cloned.1.call-update
  10.3 0.0 copy-start.5
  10.3 14.3 %chunk.1 = (bf16[256,512]{1,0:T(8,128)(2,1)}, f32[256,256]{1,0:T(8,128)}, f32[256,256]{1,0:T(8,128)}) custom-call(f32[1]{0:T(128)S(6)} %copy.10.scale_ref, f32[1]{0:T(128)S(6)} %copy.11.rate_ref, bf16[256,4096]{1,0:T(8,128)(2,1)} %x_ref.1, f32[1,4096]{1,0:T(1,128)} %bitcast.16, bf16[3,4096,256]{2,1,0:T(8,128)(2,1)} %bitcast.15, bf16[2,4096]{1,0:T(2,128)(2,1)} %bitcast.17, ...), custom_call_target="tpu_custom_call" | custom-call | tf_op jit(solution)/shard_map/chunk/pallas_call | solution.py:258
  24.6 3.2 %collective-permute-start = (bf16[256,512]{1,0:T(8,128)(2,1)}, bf16[256,512]{1,0:T(8,128)(2,1)S(1)}, u32[]{:S(2)}, u32[]{:S(2)}) collective-permute-start(bf16[256,512]{1,0:T(8,128)(2,1)} %get-tuple-element.16.own_ref), channel_id=1, source_target_pairs={{0,8},{8,0},{16,24},{24,16},{32,40},{40,32},{48,56},{56,48},{64,72... | collective-permute-start | bytes 786440 | tf_op jit(solution)/shard_map/ppermute | solution.py:288
  27.8 1.4 %collective-permute-done.other_ref.refs_7_ = bf16[256,512]{1,0:T(8,128)(2,1)S(1)} collective-permute-done((bf16[256,512]{1,0:T(8,128)(2,1)}, bf16[256,512]{1,0:T(8,128)(2,1)S(1)}, u32[]{:S(2)}, u32[]{:S(2)}) %collective-permute-start) | collective-permute-done | bytes 262176 | tf_op jit(solution)/shard_map/ppermute | solution.py:288
  29.2 0.0 copy-start.2
  29.2 0.9 %copy-done.2 = bf16[256,512]{1,0:T(8,128)(2,1)S(1)} copy-done((bf16[256,512]{1,0:T(8,128)(2,1)S(1)}, bf16[256,512]{1,0:T(8,128)(2,1)}, u32[]{:S(2)}) %copy-start.2) | copy-done | bytes 262168
  30.1 0.3 pair.1
  30.4 0.1 collective-permute-start.1
  30.5 1.9 %collective-permute-start.2 = (bf16[128,512]{1,0:T(8,128)(2,1)S(1)}, bf16[128,512]{1,0:T(8,128)(2,1)S(1)}, u32[]{:S(2)}, u32[]{:S(2)}) collective-permute-start(bf16[128,512]{1,0:T(8,128)(2,1)S(1)} %get-tuple-element.18), channel_id=1, source_target_pairs={{0,32},{8,40},{16,48},{24,56},{32,0},{40,8},{48,16},{56,24},{64,96... | collective-permute-start | bytes 393224 | tf_op jit(solution)/shard_map/ppermute | solution.py:288
  32.4 1.1 %collective-permute-start.3 = (bf16[128,512]{1,0:T(8,128)(2,1)S(1)}, bf16[128,512]{1,0:T(8,128)(2,1)S(1)}, u32[]{:S(2)}, u32[]{:S(2)}) collective-permute-start(bf16[128,512]{1,0:T(8,128)(2,1)S(1)} %get-tuple-element.18), channel_id=1, source_target_pairs={{0,48},{8,56},{16,0},{24,8},{32,16},{40,24},{48,32},{56,40},{64,11... | collective-permute-start | bytes 393224 | tf_op jit(solution)/shard_map/ppermute | solution.py:288
  33.6 3.7 %collective-permute-done.1.refs_0_ = bf16[128,512]{1,0:T(8,128)(2,1)S(1)} collective-permute-done((bf16[128,512]{1,0:T(8,128)(2,1)S(1)}, bf16[128,512]{1,0:T(8,128)(2,1)S(1)}, u32[]{:S(2)}, u32[]{:S(2)}) %collective-permute-start.1) | collective-permute-done | bytes 131104 | tf_op jit(solution)/shard_map/ppermute | solution.py:288
  37.3 3.2 %collective-permute-start.4 = (bf16[128,512]{1,0:T(8,128)(2,1)S(1)}, bf16[128,512]{1,0:T(8,128)(2,1)S(1)}, u32[]{:S(2)}, u32[]{:S(2)}) collective-permute-start(bf16[128,512]{1,0:T(8,128)(2,1)S(1)} %collective-permute-done.1.refs_0_), channel_id=1, source_target_pairs={{0,8},{8,0},{16,24},{24,16},{32,40},{40,32},{48,56},{56,48},{64,72... | collective-permute-start | bytes 393224 | tf_op jit(solution)/shard_map/ppermute | solution.py:288
  40.4 0.0 collective-permute-done.2.refs_1_
  40.4 0.0 collective-permute-start.5
  40.4 0.0 collective-permute-done.3.refs_2_
  40.5 0.6 collective-permute-start.6
  41.0 0.4 collective-permute-done.4.refs_3_
  41.4 0.4 collective-permute-done.5.refs_4_
  41.8 0.2 collective-permute-done.6.refs_5_
  42.0 0.6 row.1
  42.6 0.4 collective-permute-start.7
  43.0 2.6 %collective-permute-start.8 = (bf16[128,512]{1,0:T(8,128)(2,1)S(1)}, bf16[128,512]{1,0:T(8,128)(2,1)S(1)}, u32[]{:S(2)}, u32[]{:S(2)}) collective-permute-start(bf16[128,512]{1,0:T(8,128)(2,1)S(1)} %get-tuple-element.19), channel_id=1, source_target_pairs={{0,128},{8,136},{16,144},{24,152},{32,160},{40,168},{48,176},{56,1... | collective-permute-start | bytes 393224 | tf_op jit(solution)/shard_map/ppermute | solution.py:288
  45.6 1.1 %collective-permute-start.9 = (bf16[128,512]{1,0:T(8,128)(2,1)S(1)}, bf16[128,512]{1,0:T(8,128)(2,1)S(1)}, u32[]{:S(2)}, u32[]{:S(2)}) collective-permute-start(bf16[128,512]{1,0:T(8,128)(2,1)S(1)} %get-tuple-element.19), channel_id=1, source_target_pairs={{0,192},{8,200},{16,208},{24,216},{32,224},{40,232},{48,240},{56,2... | collective-permute-start | bytes 393224 | tf_op jit(solution)/shard_map/ppermute | solution.py:288
  46.7 2.0 %collective-permute-done.7.refs_0_ = bf16[128,512]{1,0:T(8,128)(2,1)S(1)} collective-permute-done((bf16[128,512]{1,0:T(8,128)(2,1)S(1)}, bf16[128,512]{1,0:T(8,128)(2,1)S(1)}, u32[]{:S(2)}, u32[]{:S(2)}) %collective-permute-start.7) | collective-permute-done | bytes 131104 | tf_op jit(solution)/shard_map/ppermute | solution.py:288
  48.7 1.4 %collective-permute-start.10 = (bf16[128,512]{1,0:T(8,128)(2,1)S(1)}, bf16[128,512]{1,0:T(8,128)(2,1)S(1)}, u32[]{:S(2)}, u32[]{:S(2)}) collective-permute-start(bf16[128,512]{1,0:T(8,128)(2,1)S(1)} %collective-permute-done.7.refs_0_), channel_id=1, source_target_pairs={{0,8},{8,0},{16,24},{24,16},{32,40},{40,32},{48,56},{56,48},{64,72... | collective-permute-start | bytes 393224 | tf_op jit(solution)/shard_map/ppermute | solution.py:288
  50.1 1.8 %collective-permute-done.8.refs_1_ = bf16[128,512]{1,0:T(8,128)(2,1)S(1)} collective-permute-done((bf16[128,512]{1,0:T(8,128)(2,1)S(1)}, bf16[128,512]{1,0:T(8,128)(2,1)S(1)}, u32[]{:S(2)}, u32[]{:S(2)}) %collective-permute-start.8) | collective-permute-done | bytes 131104 | tf_op jit(solution)/shard_map/ppermute | solution.py:288
  51.9 1.0 %collective-permute-start.11 = (bf16[128,512]{1,0:T(8,128)(2,1)S(1)}, bf16[128,512]{1,0:T(8,128)(2,1)S(1)}, u32[]{:S(2)}, u32[]{:S(2)}) collective-permute-start(bf16[128,512]{1,0:T(8,128)(2,1)S(1)} %collective-permute-done.8.refs_1_), channel_id=1, source_target_pairs={{0,8},{8,0},{16,24},{24,16},{32,40},{40,32},{48,56},{56,48},{64,72... | collective-permute-start | bytes 393224 | tf_op jit(solution)/shard_map/ppermute | solution.py:288
  52.9 0.0 collective-permute-done.9.refs_2_
  52.9 0.3 collective-permute-start.12
  53.2 0.0 collective-permute-done.10.refs_3_
  53.2 0.7 collective-permute-done.11.refs_4_
  53.9 0.4 collective-permute-done.12.refs_5_
  54.2 0.0 copy-done.5
  54.2 0.0 copy-start.3
  54.2 1.0 %copy-done.3 = f32[256,256]{1,0:T(8,128)S(1)} copy-done((f32[256,256]{1,0:T(8,128)S(1)}, f32[256,256]{1,0:T(8,128)}, u32[]{:S(2)}) %copy-start.3) | copy-done | bytes 262168
  55.2 0.0 copy-start.4
  55.2 1.0 %copy-done.4 = f32[256,256]{1,0:T(8,128)S(1)} copy-done((f32[256,256]{1,0:T(8,128)S(1)}, f32[256,256]{1,0:T(8,128)}, u32[]{:S(2)}) %copy-start.4) | copy-done | bytes 262168
  56.1 0.7 read.1
  56.9 18.2 %all_to_all.5 = bf16[16,32,256]{2,1,0:T(8,128)(2,1)S(1)} all-to-all(bf16[16,32,256]{2,1,0:T(8,128)(2,1)S(1)} %bitcast.13), channel_id=1, replica_groups=mesh['y'=4,'xh'=2,'xl'=2,'core'=2,'head'=8] {'xl','head'}, dimensions={0} | all-to-all | bytes 524288 | tf_op jit(solution)/shard_map/all_to_all | solution.py:338
  75.1 1.5 %collective-permute-start.13 = (bf16[2,8,32,256]{3,2,1,0:T(8,128)(2,1)S(1)}, bf16[2,8,32,256]{3,2,1,0:T(8,128)(2,1)S(1)}, u32[]{:S(2)}, u32[]{:S(2)}) collective-permute-start(bf16[2,8,32,256]{3,2,1,0:T(8,128)(2,1)S(1)} %bitcast.11), channel_id=1, source_target_pairs={{0,8},{8,0},{16,24},{24,16},{32,40},{40,32},{48,56},{56,48},{64,72... | collective-permute-start | bytes 786440 | tf_op jit(solution)/shard_map/ppermute | solution.py:288
  76.6 1.2 %collective-permute-done.13.other_ref = bf16[2,8,32,256]{3,2,1,0:T(8,128)(2,1)S(1)} collective-permute-done((bf16[2,8,32,256]{3,2,1,0:T(8,128)(2,1)S(1)}, bf16[2,8,32,256]{3,2,1,0:T(8,128)(2,1)S(1)}, u32[]{:S(2)}, u32[]{:S(2)}) %collective-permute-start.13) | collective-permute-done | bytes 262176 | tf_op jit(solution)/shard_map/ppermute | solution.py:288
  77.7 0.0 all-gather.3.cloned.1.call-done
  77.7 0.0 copy-start.1
  77.7 2.2 %copy-done.1 = bf16[2048,1024]{1,0:T(8,128)(2,1)S(1)} copy-done((bf16[2048,1024]{1,0:T(8,128)(2,1)S(1)}, bf16[2048,1024]{1,0:T(8,128)(2,1)}, u32[]{:S(2)}) %copy-start.1) | copy-done | bytes 4194328
  79.9 0.7 mix.1
  80.6 0.5 collective-permute-start.14
  81.1 0.9 collective-permute-start.15
  82.0 0.9 collective-permute-start.16
  82.9 0.0 collective-permute-done.14.core_ref
  82.9 1.8 %collective-permute-done.15.half_ref = bf16[32,1024]{1,0:T(8,128)(2,1)S(1)} collective-permute-done((bf16[32,1024]{1,0:T(8,128)(2,1)S(1)}, bf16[32,1024]{1,0:T(8,128)(2,1)S(1)}, u32[]{:S(2)}, u32[]{:S(2)}) %collective-permute-start.15) | collective-permute-done | bytes 65568 | tf_op jit(solution)/shard_map/ppermute | solution.py:288
  84.6 1.7 %collective-permute-done.16.far_ref = bf16[32,1024]{1,0:T(8,128)(2,1)S(1)} collective-permute-done((bf16[32,1024]{1,0:T(8,128)(2,1)S(1)}, bf16[32,1024]{1,0:T(8,128)(2,1)S(1)}, u32[]{:S(2)}, u32[]{:S(2)}) %collective-permute-start.16) | collective-permute-done | bytes 65568 | tf_op jit(solution)/shard_map/ppermute | solution.py:288
  86.4 0.7 lay.1
Async XLA Ops:
  6.5 1.6 %copy-start = (bf16[256,4096]{1,0:T(8,128)(2,1)S(1)}, bf16[256,4096]{1,0:T(8,128)(2,1)}, u32[]{:S(2)}) copy-start(bf16[256,4096]{1,0:T(8,128)(2,1)} %param.17) | copy-start | bytes 6291460
  6.5 71.2 %all-gather.3.cloned.1.call-start = ((), (), s32[]{:S(2)}) async-start(), calls=%async_computation.1 | async-start | bytes 4718592 | tf_op jit(solution)/shard_map/all_gather | solution.py:302
  10.3 43.9 %copy-start.5 = (f32[256]{0:T(256)S(1)}, f32[256]{0:T(256)}, u32[]{:S(2)}) copy-start(f32[256]{0:T(256)} %param.16) | copy-start | bytes 3076
  24.6 4.6 %collective-permute-start = (bf16[256,512]{1,0:T(8,128)(2,1)}, bf16[256,512]{1,0:T(8,128)(2,1)S(1)}, u32[]{:S(2)}, u32[]{:S(2)}) collective-permute-start(bf16[256,512]{1,0:T(8,128)(2,1)} %get-tuple-element.16.own_ref), channel_id=1, source_target_pairs={{0,8},{8,0},{16,24},{24,16},{32,40},{40,32},{48,56},{56,48},{64,72... | collective-permute-start | bytes 786440 | tf_op jit(solution)/shard_map/ppermute | solution.py:288
  29.2 0.9 %copy-start.2 = (bf16[256,512]{1,0:T(8,128)(2,1)S(1)}, bf16[256,512]{1,0:T(8,128)(2,1)}, u32[]{:S(2)}) copy-start(bf16[256,512]{1,0:T(8,128)(2,1)} %get-tuple-element.16.own_ref) | copy-start | bytes 786436
  30.4 6.8 %collective-permute-start.1 = (bf16[128,512]{1,0:T(8,128)(2,1)S(1)}, bf16[128,512]{1,0:T(8,128)(2,1)S(1)}, u32[]{:S(2)}, u32[]{:S(2)}) collective-permute-start(bf16[128,512]{1,0:T(8,128)(2,1)S(1)} %get-tuple-element.18), channel_id=1, source_target_pairs={{0,16},{8,24},{16,32},{24,40},{32,48},{40,56},{48,0},{56,8},{64,80... | collective-permute-start | bytes 393224 | tf_op jit(solution)/shard_map/ppermute | solution.py:288
  30.5 9.9 %collective-permute-start.2 = (bf16[128,512]{1,0:T(8,128)(2,1)S(1)}, bf16[128,512]{1,0:T(8,128)(2,1)S(1)}, u32[]{:S(2)}, u32[]{:S(2)}) collective-permute-start(bf16[128,512]{1,0:T(8,128)(2,1)S(1)} %get-tuple-element.18), channel_id=1, source_target_pairs={{0,32},{8,40},{16,48},{24,56},{32,0},{40,8},{48,16},{56,24},{64,96... | collective-permute-start | bytes 393224 | tf_op jit(solution)/shard_map/ppermute | solution.py:288
  32.4 8.0 %collective-permute-start.3 = (bf16[128,512]{1,0:T(8,128)(2,1)S(1)}, bf16[128,512]{1,0:T(8,128)(2,1)S(1)}, u32[]{:S(2)}, u32[]{:S(2)}) collective-permute-start(bf16[128,512]{1,0:T(8,128)(2,1)S(1)} %get-tuple-element.18), channel_id=1, source_target_pairs={{0,48},{8,56},{16,0},{24,8},{32,16},{40,24},{48,32},{56,40},{64,11... | collective-permute-start | bytes 393224 | tf_op jit(solution)/shard_map/ppermute | solution.py:288
  37.3 4.2 %collective-permute-start.4 = (bf16[128,512]{1,0:T(8,128)(2,1)S(1)}, bf16[128,512]{1,0:T(8,128)(2,1)S(1)}, u32[]{:S(2)}, u32[]{:S(2)}) collective-permute-start(bf16[128,512]{1,0:T(8,128)(2,1)S(1)} %collective-permute-done.1.refs_0_), channel_id=1, source_target_pairs={{0,8},{8,0},{16,24},{24,16},{32,40},{40,32},{48,56},{56,48},{64,72... | collective-permute-start | bytes 393224 | tf_op jit(solution)/shard_map/ppermute | solution.py:288
  40.4 1.3 %collective-permute-start.5 = (bf16[128,512]{1,0:T(8,128)(2,1)S(1)}, bf16[128,512]{1,0:T(8,128)(2,1)S(1)}, u32[]{:S(2)}, u32[]{:S(2)}) collective-permute-start(bf16[128,512]{1,0:T(8,128)(2,1)S(1)} %collective-permute-done.2.refs_1_), channel_id=1, source_target_pairs={{0,8},{8,0},{16,24},{24,16},{32,40},{40,32},{48,56},{56,48},{64,72... | collective-permute-start | bytes 393224 | tf_op jit(solution)/shard_map/ppermute | solution.py:288
  40.5 1.6 %collective-permute-start.6 = (bf16[128,512]{1,0:T(8,128)(2,1)S(1)}, bf16[128,512]{1,0:T(8,128)(2,1)S(1)}, u32[]{:S(2)}, u32[]{:S(2)}) collective-permute-start(bf16[128,512]{1,0:T(8,128)(2,1)S(1)} %collective-permute-done.3.refs_2_), channel_id=1, source_target_pairs={{0,8},{8,0},{16,24},{24,16},{32,40},{40,32},{48,56},{56,48},{64,72... | collective-permute-start | bytes 393224 | tf_op jit(solution)/shard_map/ppermute | solution.py:288
  42.6 6.1 %collective-permute-start.7 = (bf16[128,512]{1,0:T(8,128)(2,1)S(1)}, bf16[128,512]{1,0:T(8,128)(2,1)S(1)}, u32[]{:S(2)}, u32[]{:S(2)}) collective-permute-start(bf16[128,512]{1,0:T(8,128)(2,1)S(1)} %get-tuple-element.19), channel_id=1, source_target_pairs={{0,64},{8,72},{16,80},{24,88},{32,96},{40,104},{48,112},{56,120},{... | collective-permute-start | bytes 393224 | tf_op jit(solution)/shard_map/ppermute | solution.py:288
  43.0 8.9 %collective-permute-start.8 = (bf16[128,512]{1,0:T(8,128)(2,1)S(1)}, bf16[128,512]{1,0:T(8,128)(2,1)S(1)}, u32[]{:S(2)}, u32[]{:S(2)}) collective-permute-start(bf16[128,512]{1,0:T(8,128)(2,1)S(1)} %get-tuple-element.19), channel_id=1, source_target_pairs={{0,128},{8,136},{16,144},{24,152},{32,160},{40,168},{48,176},{56,1... | collective-permute-start | bytes 393224 | tf_op jit(solution)/shard_map/ppermute | solution.py:288
  45.6 7.3 %collective-permute-start.9 = (bf16[128,512]{1,0:T(8,128)(2,1)S(1)}, bf16[128,512]{1,0:T(8,128)(2,1)S(1)}, u32[]{:S(2)}, u32[]{:S(2)}) collective-permute-start(bf16[128,512]{1,0:T(8,128)(2,1)S(1)} %get-tuple-element.19), channel_id=1, source_target_pairs={{0,192},{8,200},{16,208},{24,216},{32,224},{40,232},{48,240},{56,2... | collective-permute-start | bytes 393224 | tf_op jit(solution)/shard_map/ppermute | solution.py:288
  48.7 4.5 %collective-permute-start.10 = (bf16[128,512]{1,0:T(8,128)(2,1)S(1)}, bf16[128,512]{1,0:T(8,128)(2,1)S(1)}, u32[]{:S(2)}, u32[]{:S(2)}) collective-permute-start(bf16[128,512]{1,0:T(8,128)(2,1)S(1)} %collective-permute-done.7.refs_0_), channel_id=1, source_target_pairs={{0,8},{8,0},{16,24},{24,16},{32,40},{40,32},{48,56},{56,48},{64,72... | collective-permute-start | bytes 393224 | tf_op jit(solution)/shard_map/ppermute | solution.py:288
  51.9 2.0 %collective-permute-start.11 = (bf16[128,512]{1,0:T(8,128)(2,1)S(1)}, bf16[128,512]{1,0:T(8,128)(2,1)S(1)}, u32[]{:S(2)}, u32[]{:S(2)}) collective-permute-start(bf16[128,512]{1,0:T(8,128)(2,1)S(1)} %collective-permute-done.8.refs_1_), channel_id=1, source_target_pairs={{0,8},{8,0},{16,24},{24,16},{32,40},{40,32},{48,56},{56,48},{64,72... | collective-permute-start | bytes 393224 | tf_op jit(solution)/shard_map/ppermute | solution.py:288
  52.9 1.3 %collective-permute-start.12 = (bf16[128,512]{1,0:T(8,128)(2,1)S(1)}, bf16[128,512]{1,0:T(8,128)(2,1)S(1)}, u32[]{:S(2)}, u32[]{:S(2)}) collective-permute-start(bf16[128,512]{1,0:T(8,128)(2,1)S(1)} %collective-permute-done.9.refs_2_), channel_id=1, source_target_pairs={{0,8},{8,0},{16,24},{24,16},{32,40},{40,32},{48,56},{56,48},{64,72... | collective-permute-start | bytes 393224 | tf_op jit(solution)/shard_map/ppermute | solution.py:288
  54.2 1.0 %copy-start.3 = (f32[256,256]{1,0:T(8,128)S(1)}, f32[256,256]{1,0:T(8,128)}, u32[]{:S(2)}) copy-start(f32[256,256]{1,0:T(8,128)} %get-tuple-element.22.refs_9_) | copy-start | bytes 786436
  55.2 1.0 %copy-start.4 = (f32[256,256]{1,0:T(8,128)S(1)}, f32[256,256]{1,0:T(8,128)}, u32[]{:S(2)}) copy-start(f32[256,256]{1,0:T(8,128)} %get-tuple-element.21.refs_8_) | copy-start | bytes 786436
  75.1 2.7 %collective-permute-start.13 = (bf16[2,8,32,256]{3,2,1,0:T(8,128)(2,1)S(1)}, bf16[2,8,32,256]{3,2,1,0:T(8,128)(2,1)S(1)}, u32[]{:S(2)}, u32[]{:S(2)}) collective-permute-start(bf16[2,8,32,256]{3,2,1,0:T(8,128)(2,1)S(1)} %bitcast.11), channel_id=1, source_target_pairs={{0,8},{8,0},{16,24},{24,16},{32,40},{40,32},{48,56},{56,48},{64,72... | collective-permute-start | bytes 786440 | tf_op jit(solution)/shard_map/ppermute | solution.py:288
  77.7 2.2 %copy-start.1 = (bf16[2048,1024]{1,0:T(8,128)(2,1)S(1)}, bf16[2048,1024]{1,0:T(8,128)(2,1)}, u32[]{:S(2)}) copy-start(bf16[2048,1024]{1,0:T(8,128)(2,1)} %all-gather.3.cloned.1.call-done) | copy-start | bytes 12582916
  80.6 2.2 %collective-permute-start.14 = (bf16[32,1024]{1,0:T(8,128)(2,1)S(1)}, bf16[32,1024]{1,0:T(8,128)(2,1)S(1)}, u32[]{:S(2)}, u32[]{:S(2)}) collective-permute-start(bf16[32,1024]{1,0:T(8,128)(2,1)S(1)} %get-tuple-element.24), channel_id=1, source_target_pairs={{0,8},{8,0},{16,24},{24,16},{32,40},{40,32},{48,56},{56,48},{64,72... | collective-permute-start | bytes 196616 | tf_op jit(solution)/shard_map/ppermute | solution.py:288
  81.1 3.6 %collective-permute-start.15 = (bf16[32,1024]{1,0:T(8,128)(2,1)S(1)}, bf16[32,1024]{1,0:T(8,128)(2,1)S(1)}, u32[]{:S(2)}, u32[]{:S(2)}) collective-permute-start(bf16[32,1024]{1,0:T(8,128)(2,1)S(1)} %get-tuple-element.25), channel_id=1, source_target_pairs={{0,16},{8,24},{16,0},{24,8},{32,48},{40,56},{48,32},{56,40},{64,80... | collective-permute-start | bytes 196616 | tf_op jit(solution)/shard_map/ppermute | solution.py:288
  82.0 4.4 %collective-permute-start.16 = (bf16[32,1024]{1,0:T(8,128)(2,1)S(1)}, bf16[32,1024]{1,0:T(8,128)(2,1)S(1)}, u32[]{:S(2)}, u32[]{:S(2)}) collective-permute-start(bf16[32,1024]{1,0:T(8,128)(2,1)S(1)} %get-tuple-element.26), channel_id=1, source_target_pairs={{0,24},{8,16},{16,8},{24,0},{32,56},{40,48},{48,40},{56,32},{64,88... | collective-permute-start | bytes 196616 | tf_op jit(solution)/shard_map/ppermute | solution.py:288
Sparse Core Ops, SparseCore 0:
  9.1 58.6 all-gather.2

commit v5 on v4

--- a/solution.py
+++ b/solution.py
@@ -6,7 +6,6 @@
 from jax.sharding import Mesh
 from jax.sharding import PartitionSpec as P
 
-KB = 1024
 F32 = jnp.float32
 BF16 = jnp.bfloat16
 NN = (((1,), (0,)), ((), ()))
@@ -15,7 +14,7 @@
 SEQ = ("y", "xh", "xl", "core")
 SMALL = pltpu.CompilerParams(vmem_limit_bytes=8 << 20)
 MIDDLE = pltpu.CompilerParams(vmem_limit_bytes=16 << 20)
-LARGE = pltpu.CompilerParams(vmem_limit_bytes=57 << 20)
+LARGE = pltpu.CompilerParams(vmem_limit_bytes=60 << 20)
 
 
 def mm(a, b, dims=NN):
@@ -36,86 +35,114 @@
     return vectors * lax.rsqrt(jnp.sum(vectors * vectors, axis=-1, keepdims=True) + 1e-06)
 
 
-def chunk_kernel(
-    scale_ref, rate_ref, x_ref, gain_ref, w_ref, gate_ref, resets_ref,
-    carry_ref, local_ref, query_ref,
-    xn_ref, acc_ref, gating_ref,
+def norm_rows(x_ref, gain):
+    x = x_ref[...].astype(F32)
+    rs = lax.rsqrt(jnp.mean(x * x, axis=-1, keepdims=True) + 1e-06)
+    return (x * rs * gain).astype(BF16)
+
+
+def copies(x_hbm, w_hbm, slots, x_buf, w_buf, sems):
+    halves = x_buf.shape[0] // 2
+    depth = w_buf.shape[1] // 2
+    rows = [pl.ds(i * halves, halves) for i in range(2)]
+    parts = [pl.ds(i * depth, depth) for i in range(2)]
+    found = [(x_hbm.at[part], x_buf.at[part]) for part in rows]
+    for slot, j in enumerate(slots):
+        found += [(w_hbm.at[j, part], w_buf.at[slot, part]) for part in parts]
+    found = [pltpu.make_async_copy(a, b, sems.at[i]) for i, (a, b) in enumerate(found)]
+    for copy in found:
+        copy.start()
+    return found
+
+
+def normalise(found, x_buf, xn_buf, gain):
+    half = x_buf.shape[0] // 2
+    for i in range(2):
+        found[i].wait()
+        part = slice(i * half, (i + 1) * half)
+        xn_buf[part] = norm_rows(x_buf.at[part], gain)
+
+
+def project(found, xn_buf, w_buf, slot):
+    depth = w_buf.shape[1] // 2
+    total = None
+    for i in range(2):
+        found[2 + 2 * slot + i].wait()
+        part = slice(i * depth, (i + 1) * depth)
+        product = mm(xn_buf[:, part], w_buf[slot, part])
+        total = product if total is None else total + product
+    return total
+
+
+def fold_kernel(
+    scale_ref, rate_ref, x_hbm, gain_ref, w_hbm, gate_ref, resets_ref,
+    carry_ref, key_ref, solved_ref, decay_ref, gamma_ref,
+    x_buf, xn_buf, w_buf, sems,
 ):
-    step = pl.program_id(0)
-    n = x_ref.shape[0]
-
-    @pl.when(step == 0)
-    def _():
-        x = x_ref[...].astype(F32)
-        rs = lax.rsqrt(jnp.mean(x * x, axis=-1, keepdims=True) + 1e-06)
-        xn_ref[...] = (x * rs * gain_ref[...]).astype(BF16)
-
-    xb = xn_ref[:, pl.ds(pl.multiple_of(step * KB, KB), KB)]
-    parts = [mm(xb, w_ref[j]) for j in range(3)]
-    gating = mm(gate_ref[...], xb, NT)
-
-    @pl.when(step == 0)
-    def _():
-        for j in range(3):
-            acc_ref[j] = parts[j]
-        gating_ref[...] = gating
-
-    @pl.when(step > 0)
-    def _():
-        for j in range(3):
-            acc_ref[j] = acc_ref[j] + parts[j]
-        gating_ref[...] = gating_ref[...] + gating
-
-    @pl.when(step == pl.num_programs(0) - 1)
-    def _():
-        query = unit_rows(acc_ref[0])
-        key = unit_rows(acc_ref[1])
-        value = acc_ref[2]
-        gating = gating_ref[...]
-        beta_row = scale_ref[0] * jax.nn.sigmoid(gating[0:1])
-        logf_row = -rate_ref[0] * jax.nn.softplus(gating[1:2])
-        reset_row = resets_ref[...].astype(F32)
-        t = lax.broadcasted_iota(jnp.int32, (n, n), 0)
-        s = lax.broadcasted_iota(jnp.int32, (n, n), 1)
-        causal = t >= s
-        eye = t == s
-
-        def to_col(row):
-            return jnp.sum(jnp.where(eye, row, 0.0), axis=1, keepdims=True)
-
-        def to_row(col):
-            return jnp.sum(jnp.where(eye, col, 0.0), axis=0, keepdims=True)
-
-        beta = to_col(beta_row)
-        cum = jnp.sum(jnp.where(causal, logf_row, 0.0), axis=1, keepdims=True)
-        seg = jnp.sum(jnp.where(causal, reset_row, 0.0), axis=1, keepdims=True)
-        cum_row = to_row(cum)
-        seg_row = to_row(seg)
-        same = (seg == seg_row) & causal
-        decay = jnp.where(same, jnp.exp(jnp.where(same, cum - cum_row, 0.0)), 0.0)
-        gamma = jnp.where(seg == 0.0, jnp.exp(cum), 0.0)
-        cum_last, seg_last = cum[n - 1 : n], seg[n - 1 : n]
-        tail = jnp.where(seg == seg_last, jnp.exp(cum_last - cum), 0.0)
-        gamma_last = gamma[n - 1 : n]
-
-        ks = split(key)
-        gram = mm3(ks, ks, NT)
-        low = jnp.where(t > s, beta * decay * gram, 0.0)
-        apart = t ^ s
-        inv = jnp.where(eye, 1.0, jnp.where(apart == 1, -low, 0.0))
-        for level in range(1, n.bit_length() - 1):
-            part = jnp.where((apart >> level) == 1, low, 0.0)
-            vs = split(inv)
-            inv = inv - mm3(vs, split(mm3(split(part), vs)))
-        rhs = jnp.concatenate([(beta * gamma) * key, beta * value], axis=1)
-        solved = split(mm3(split(inv), split(rhs)))
-        folded = mm3(split(key * tail), solved, TN)
-        carry_ref[:, :n] = (jnp.where(eye, gamma_last, 0.0) - folded[:, :n]).astype(BF16)
-        carry_ref[:, n:] = folded[:, n:].astype(BF16)
-        scores = mm3(split(query), ks, NT) * decay
-        seen = mm3(split(scores), solved)
-        query_ref[...] = gamma * query - seen[:, :n]
-        local_ref[...] = seen[:, n:]
+    found = copies(x_hbm, w_hbm, (1, 2), x_buf, w_buf, sems)
+    normalise(found, x_buf, xn_buf, gain_ref[...])
+    n = x_buf.shape[0]
+    gating = mm(xn_buf[...], gate_ref[...], NT)
+    key = unit_rows(project(found, xn_buf, w_buf, 0))
+    beta = scale_ref[0] * jax.nn.sigmoid(gating[:, 0:1])
+    logf = -rate_ref[0] * jax.nn.softplus(gating[:, 1:2])
+    reset_row = resets_ref[...].astype(F32)
+    t = lax.broadcasted_iota(jnp.int32, (n, n), 0)
+    s = lax.broadcasted_iota(jnp.int32, (n, n), 1)
+    causal = t >= s
+    eye = t == s
+
+    def to_row(col):
+        return jnp.sum(jnp.where(eye, col, 0.0), axis=0, keepdims=True)
+
+    cum = jnp.sum(jnp.where(causal, to_row(logf), 0.0), axis=1, keepdims=True)
+    seg = jnp.sum(jnp.where(causal, reset_row, 0.0), axis=1, keepdims=True)
+    cum_row = to_row(cum)
+    seg_row = to_row(seg)
+    same = (seg == seg_row) & causal
+    decay = jnp.where(same, jnp.exp(jnp.where(same, cum - cum_row, 0.0)), 0.0)
+    gamma = jnp.where(seg == 0.0, jnp.exp(cum), 0.0)
+    cum_last, seg_last = cum[n - 1 : n], seg[n - 1 : n]
+    tail = jnp.where(seg == seg_last, jnp.exp(cum_last - cum), 0.0)
+    gamma_last = gamma[n - 1 : n]
+    decay_ref[...] = decay
+    gamma_ref[...] = gamma
+    key_ref[...] = key
+
+    ks = split(key)
+    low = jnp.where(t > s, beta * decay * mm3(ks, ks, NT), 0.0)
+    apart = t ^ s
+    inv = jnp.where(eye, 1.0, jnp.where(apart == 1, -low, 0.0))
+    for level in range(1, n.bit_length() - 1):
+        part = jnp.where((apart >> level) == 1, low, 0.0).astype(BF16)
+        rough = inv.astype(BF16)
+        inv = inv - mm(rough, mm(part, rough).astype(BF16))
+    vs = split(inv)
+    left = jnp.where(eye, 1.0, 0.0) - inv - mm3(split(low), vs)
+    inv = inv + mm(vs[0], left.astype(BF16))
+
+    value = project(found, xn_buf, w_buf, 1)
+    rhs = jnp.concatenate([(beta * gamma) * key, beta * value], axis=1)
+    solved = mm3(split(inv), split(rhs))
+    solved_ref[...] = solved
+    folded = mm3(split(key * tail), split(solved), TN)
+    carry_ref[:, :n] = (jnp.where(eye, gamma_last, 0.0) - folded[:, :n]).astype(BF16)
+    carry_ref[:, n:] = folded[:, n:].astype(BF16)
+
+
+def look_kernel(
+    x_hbm, gain_ref, w_hbm, key_ref, solved_ref, decay_ref, gamma_ref,
+    query_ref, local_ref,
+    x_buf, xn_buf, w_buf, sems,
+):
+    found = copies(x_hbm, w_hbm, (0,), x_buf, w_buf, sems)
+    normalise(found, x_buf, xn_buf, gain_ref[...])
+    n = x_buf.shape[0]
+    query = unit_rows(project(found, xn_buf, w_buf, 0))
+    scores = mm3(split(query), split(key_ref[...]), NT) * decay_ref[...]
+    seen = mm3(split(scores), split(solved_ref[...]))
+    query_ref[...] = gamma_ref[...] * query - seen[:, :n]
+    local_ref[...] = seen[:, n:]
 
 
 def after(later, earlier, n):
@@ -243,6 +270,10 @@
         out_ref[:, pl.ds(place, width)] = ref[...]
 
 
+def hbm():
+    return pl.BlockSpec(memory_space=pltpu.HBM)
+
+
 def vmem():
     return pl.BlockSpec(memory_space=pltpu.VMEM)
 
@@ -254,33 +285,47 @@
     n = qkv_weight.shape[2]
     weight = qkv_weight.transpose(1, 0, 2)
     gate = gate_weight.transpose(2, 1, 0).reshape(2, width)
-    whole = lambda shape: pl.BlockSpec(shape, lambda i: (0,) * len(shape), pipeline_mode=pl.Buffered(1))
-    carry, local, query = pl.pallas_call(
-        chunk_kernel,
-        name="chunk",
-        grid=(width // KB,),
-        in_specs=[
-            pl.BlockSpec(memory_space=pltpu.SMEM),
-            pl.BlockSpec(memory_space=pltpu.SMEM),
-            whole((rows, width)),
-            whole((1, width)),
-            pl.BlockSpec((3, KB, n), lambda i: (0, i, 0)),
-            pl.BlockSpec((2, KB), lambda i: (0, i)),
-            whole((1, rows)),
-        ],
-        out_specs=[whole((n, 2 * n)), whole((rows, n)), whole((rows, n))],
+    square = jax.ShapeDtypeStruct((rows, n), F32)
+    gain = norm_gain.reshape(1, width)
+
+    def buffers(matrices):
+        return [
+            pltpu.VMEM((rows, width), BF16),
+            pltpu.VMEM((rows, width), BF16),
+            pltpu.VMEM((matrices, width, n), BF16),
+            pltpu.SemaphoreType.DMA((2 + 2 * matrices,)),
+        ]
+
+    scalar = pl.BlockSpec(memory_space=pltpu.SMEM)
+    carry, key, solved, decay, gamma = pl.pallas_call(
+        fold_kernel,
+        name="fold",
+        in_specs=[scalar, scalar, hbm(), vmem(), hbm(), vmem(), vmem()],
+        out_specs=[vmem()] * 5,
         out_shape=[
             jax.ShapeDtypeStruct((n, 2 * n), BF16),
-            jax.ShapeDtypeStruct((rows, n), F32),
-            jax.ShapeDtypeStruct((rows, n), F32),
+            square,
+            jax.ShapeDtypeStruct((rows, 2 * n), F32),
+            square,
+            jax.ShapeDtypeStruct((rows, 1), F32),
         ],
-        scratch_shapes=[
-            pltpu.VMEM((rows, width), BF16),
-            pltpu.VMEM((3, rows, n), F32),
-            pltpu.VMEM((2, rows), F32),
-        ],
+        scratch_shapes=buffers(2),
         compiler_params=LARGE,
-    )(beta_scale, decay_rate, frames, norm_gain.reshape(1, width), weight, gate, resets.reshape(1, rows))
+    )(beta_scale, decay_rate, frames, gain, weight, gate, resets.reshape(1, rows))
+
+    def look():
+        return pl.pallas_call(
+            look_kernel,
+            name="look",
+            in_specs=[hbm(), vmem(), hbm()] + [vmem()] * 4,
+            out_specs=[vmem()] * 2,
+            out_shape=[square] * 2,
+            scratch_shapes=buffers(1),
+            compiler_params=MIDDLE,
+            cost_estimate=pl.CostEstimate(
+                flops=4 * rows * width * n, bytes_accessed=16 << 20, transcendentals=0
+            ),
+        )(frames, gain, weight, key, solved, decay, gamma)
 
     count = 32
 
@@ -313,6 +358,7 @@
         compiler_params=SMALL,
     )(carry, other)
     near = [moved(half, along_x(s)) for s in (1, 2, 3)]
+    query, local = look()
     swapped = [moved(value, flip(1)) for value in near]
     half, prefix = pl.pallas_call(
         row_kernel,

time: 94.3 us -> 100 us (1.060)
  local copies, waits for them, and re-layouts: 7.5 us -> 13.9 us
  waiting for transfers between devices: 15.6 us -> 14.5 us
    unnamed x12 -> x22, local copies, waits for them, and re-layouts: 6.64 us -> 13.1 us
    ppermute x17, waiting for transfers between devices: 15.6 us -> 14.5 us  [moved(): return lax.ppermute(value, SEQ, [(i, place_of(i)) for i in range(count)])]
    pallas_call x1 -> x2, Pallas kernels: 14.3 us -> 14.9 us  [the longest x1 11.7 us: per_device(): pl.pallas_call(fold_kernel, name='fold', in_specs=[scalar, scalar, hbm(),...]
  transfers between devices with their start and end apart: 18 -> 18, of which waited for: 12 -> 10; matrix products, arithmetic and copies ran while one was open for 0% -> 0% of each run, Pallas kernels for 17% -> 16%
where the time goes in v5:
time: 100 us; the launch traced here: 99.9 us
  starting transfers between devices  21.4 us (21%)
  Pallas kernels  17.9 us (18%)
  blocking collectives  17.4 us (17%)
  between operations  14.8 us (15%)
  waiting for transfers between devices  14.5 us (14%)
  local copies, waits for them, and re-layouts  13.9 us (14%)
    ppermute x17, starting transfers between devices, moved(): return lax.ppermute(value, SEQ, [(i, place_of(i)) for i in range(count)])  21.4 us
    all_to_all x1, blocking collectives, per_device(): lax.all_to_all(flat.reshape(16, part, n), ('xl', 'head'), 0, 0, tiled=True)  17.4 us
    ppermute x17, waiting for transfers between devices, moved(): return lax.ppermute(value, SEQ, [(i, place_of(i)) for i in range(count)])  14.5 us
    unnamed x22, local copies, waits for them, and re-layouts  13.1 us
    pallas_call x1, Pallas kernels, per_device(): pl.pallas_call(fold_kernel, name='fold', in_specs=[scalar, scalar, hbm(),...  11.7 us
    pallas_call x1, Pallas kernels, look(): pl.pallas_call(look_kernel, name='look', in_specs=[hbm(), vmem(), hbm()]...  3.21 us
  transfers between devices with their start and end apart: 18, of which 10 were waited for; matrix products, arithmetic and copies ran while one was open for 0% of the time, Pallas kernels for 16%

profile of v5, /device:TPU:1, one launch (start us, length us, event | category | flops | bytes accessed | tf_op | source)
XLA Modules:
  0.0 99.9 jit_solution(16865317560257407247)
XLA Ops:
  6.5 0.0 copy-start
  6.5 0.0 all-gather.3.cloned.1.call-start
  6.5 1.6 %copy-done = bf16[256,4096]{1,0:T(8,128)(2,1)S(1)} copy-done((bf16[256,4096]{1,0:T(8,128)(2,1)S(1)}, bf16[256,4096]{1,0:T(8,128)(2,1)}, u32[]{:S(2)}) %copy-start) | copy-done | bytes 2097176
  8.1 0.9 constant_dynamic-slice_fusion
  9.0 0.0 all-gather.3.cloned.1.call-update
  10.3 0.0 copy-start.9
  10.3 11.7 %fold.1 = (bf16[256,512]{1,0:T(8,128)(2,1)}, f32[256,256]{1,0:T(8,128)}, f32[256,512]{1,0:T(8,128)}, f32[256,256]{1,0:T(8,128)}, f32[256,1]{1,0:T(8,128)}) custom-call(f32[1]{0:T(128)S(6)} %copy.10.scale_ref, f32[1]{0:T(128)S(6)} %copy.11.rate_ref, bf16[256,4096]{1,0:T(8,128)(2,1)} %x_hbm.3, f32[1,4096]{1,0:T(1,128)} %bitcast.16, ...), custom_call_target="tpu_custom_call" | custom-call | tf_op jit(solution)/shard_map/fold/pallas_call | solution.py:300
  22.0 3.3 %collective-permute-start = (bf16[256,512]{1,0:T(8,128)(2,1)}, bf16[256,512]{1,0:T(8,128)(2,1)S(1)}, u32[]{:S(2)}, u32[]{:S(2)}) collective-permute-start(bf16[256,512]{1,0:T(8,128)(2,1)} %get-tuple-element.20.own_ref), channel_id=1, source_target_pairs={{0,8},{8,0},{16,24},{24,16},{32,40},{40,32},{48,56},{56,48},{64,72... | collective-permute-start | bytes 786440 | tf_op jit(solution)/shard_map/ppermute | solution.py:333
  25.3 1.4 %collective-permute-done.other_ref.refs_7_ = bf16[256,512]{1,0:T(8,128)(2,1)S(1)} collective-permute-done((bf16[256,512]{1,0:T(8,128)(2,1)}, bf16[256,512]{1,0:T(8,128)(2,1)S(1)}, u32[]{:S(2)}, u32[]{:S(2)}) %collective-permute-start) | collective-permute-done | bytes 262176 | tf_op jit(solution)/shard_map/ppermute | solution.py:333
  26.7 0.0 copy-start.7
  26.7 0.9 copy-done.7
  27.6 0.3 pair.1
  27.9 0.1 collective-permute-start.1
  28.0 1.9 %collective-permute-start.2 = (bf16[128,512]{1,0:T(8,128)(2,1)S(1)}, bf16[128,512]{1,0:T(8,128)(2,1)S(1)}, u32[]{:S(2)}, u32[]{:S(2)}) collective-permute-start(bf16[128,512]{1,0:T(8,128)(2,1)S(1)} %get-tuple-element.22), channel_id=1, source_target_pairs={{0,32},{8,40},{16,48},{24,56},{32,0},{40,8},{48,16},{56,24},{64,96... | collective-permute-start | bytes 393224 | tf_op jit(solution)/shard_map/ppermute | solution.py:333
  29.9 1.2 %collective-permute-start.3 = (bf16[128,512]{1,0:T(8,128)(2,1)S(1)}, bf16[128,512]{1,0:T(8,128)(2,1)S(1)}, u32[]{:S(2)}, u32[]{:S(2)}) collective-permute-start(bf16[128,512]{1,0:T(8,128)(2,1)S(1)} %get-tuple-element.22), channel_id=1, source_target_pairs={{0,48},{8,56},{16,0},{24,8},{32,16},{40,24},{48,32},{56,40},{64,11... | collective-permute-start | bytes 393224 | tf_op jit(solution)/shard_map/ppermute | solution.py:333
  31.1 3.7 %collective-permute-done.1.refs_0_ = bf16[128,512]{1,0:T(8,128)(2,1)S(1)} collective-permute-done((bf16[128,512]{1,0:T(8,128)(2,1)S(1)}, bf16[128,512]{1,0:T(8,128)(2,1)S(1)}, u32[]{:S(2)}, u32[]{:S(2)}) %collective-permute-start.1) | collective-permute-done | bytes 131104 | tf_op jit(solution)/shard_map/ppermute | solution.py:333
  34.8 3.2 %collective-permute-start.4 = (bf16[128,512]{1,0:T(8,128)(2,1)S(1)}, bf16[128,512]{1,0:T(8,128)(2,1)S(1)}, u32[]{:S(2)}, u32[]{:S(2)}) collective-permute-start(bf16[128,512]{1,0:T(8,128)(2,1)S(1)} %collective-permute-done.1.refs_0_), channel_id=1, source_target_pairs={{0,8},{8,0},{16,24},{24,16},{32,40},{40,32},{48,56},{56,48},{64,72... | collective-permute-start | bytes 393224 | tf_op jit(solution)/shard_map/ppermute | solution.py:333
  37.9 0.0 collective-permute-done.2.refs_1_
  37.9 0.0 collective-permute-start.5
  37.9 0.0 collective-permute-done.3.refs_2_
  37.9 0.6 collective-permute-start.6
  38.5 0.4 collective-permute-done.4.refs_3_
  38.9 0.4 collective-permute-done.5.refs_4_
  39.3 0.2 collective-permute-done.6.refs_5_
  39.5 0.6 row.1
  40.1 0.4 collective-permute-start.7
  40.5 2.6 %collective-permute-start.8 = (bf16[128,512]{1,0:T(8,128)(2,1)S(1)}, bf16[128,512]{1,0:T(8,128)(2,1)S(1)}, u32[]{:S(2)}, u32[]{:S(2)}) collective-permute-start(bf16[128,512]{1,0:T(8,128)(2,1)S(1)} %get-tuple-element.23), channel_id=1, source_target_pairs={{0,128},{8,136},{16,144},{24,152},{32,160},{40,168},{48,176},{56,1... | collective-permute-start | bytes 393224 | tf_op jit(solution)/shard_map/ppermute | solution.py:333
  43.1 1.1 %collective-permute-start.9 = (bf16[128,512]{1,0:T(8,128)(2,1)S(1)}, bf16[128,512]{1,0:T(8,128)(2,1)S(1)}, u32[]{:S(2)}, u32[]{:S(2)}) collective-permute-start(bf16[128,512]{1,0:T(8,128)(2,1)S(1)} %get-tuple-element.23), channel_id=1, source_target_pairs={{0,192},{8,200},{16,208},{24,216},{32,224},{40,232},{48,240},{56,2... | collective-permute-start | bytes 393224 | tf_op jit(solution)/shard_map/ppermute | solution.py:333
  44.2 2.0 %collective-permute-done.7.refs_0_ = bf16[128,512]{1,0:T(8,128)(2,1)S(1)} collective-permute-done((bf16[128,512]{1,0:T(8,128)(2,1)S(1)}, bf16[128,512]{1,0:T(8,128)(2,1)S(1)}, u32[]{:S(2)}, u32[]{:S(2)}) %collective-permute-start.7) | collective-permute-done | bytes 131104 | tf_op jit(solution)/shard_map/ppermute | solution.py:333
  46.2 1.4 %collective-permute-start.10 = (bf16[128,512]{1,0:T(8,128)(2,1)S(1)}, bf16[128,512]{1,0:T(8,128)(2,1)S(1)}, u32[]{:S(2)}, u32[]{:S(2)}) collective-permute-start(bf16[128,512]{1,0:T(8,128)(2,1)S(1)} %collective-permute-done.7.refs_0_), channel_id=1, source_target_pairs={{0,8},{8,0},{16,24},{24,16},{32,40},{40,32},{48,56},{56,48},{64,72... | collective-permute-start | bytes 393224 | tf_op jit(solution)/shard_map/ppermute | solution.py:333
  47.6 1.8 %collective-permute-done.8.refs_1_ = bf16[128,512]{1,0:T(8,128)(2,1)S(1)} collective-permute-done((bf16[128,512]{1,0:T(8,128)(2,1)S(1)}, bf16[128,512]{1,0:T(8,128)(2,1)S(1)}, u32[]{:S(2)}, u32[]{:S(2)}) %collective-permute-start.8) | collective-permute-done | bytes 131104 | tf_op jit(solution)/shard_map/ppermute | solution.py:333
  49.4 1.0 collective-permute-start.11
  50.4 0.0 collective-permute-done.9.refs_2_
  50.4 0.3 collective-permute-start.12
  50.7 0.0 copy-done.9
  50.7 0.0 copy-start.1
  50.7 2.9 %copy-done.1 = bf16[4096,3,256]{2,0,1:T(8,128)(2,1)S(1)} copy-done((bf16[4096,3,256]{2,0,1:T(8,128)(2,1)S(1)}, bf16[4096,3,256]{2,0,1:T(8,128)(2,1)}, u32[]{:S(2)}) %copy-start.1) | copy-done | bytes 6291480
  53.5 0.0 copy-start.2
  53.5 1.6 %copy-done.2 = bf16[256,4096]{1,0:T(8,128)(2,1)S(1)} copy-done((bf16[256,4096]{1,0:T(8,128)(2,1)S(1)}, bf16[256,4096]{1,0:T(8,128)(2,1)}, u32[]{:S(2)}) %copy-start.2) | copy-done | bytes 2097176
  55.2 0.0 copy-start.4
  55.2 1.1 %copy-done.4 = f32[256,512]{1,0:T(8,128)S(1)} copy-done((f32[256,512]{1,0:T(8,128)S(1)}, f32[256,512]{1,0:T(8,128)}, u32[]{:S(2)}) %copy-start.4) | copy-done | bytes 524312
  56.2 0.0 copy-start.5
  56.2 0.9 copy-done.5
  57.2 0.9 copy-done.6
  58.1 0.0 copy-start.8
  58.1 0.9 copy-done.8
  59.0 3.2 %look.1 = (f32[256,256]{1,0:T(8,128)S(1)}, f32[256,256]{1,0:T(8,128)S(1)}) custom-call(bf16[256,4096]{1,0:T(8,128)(2,1)S(1)} %copy-done.2, f32[1,4096]{1,0:T(1,128)S(1)} %bitcast.17, bf16[3,4096,256]{2,1,0:T(8,128)(2,1)S(1)} %bitcast.11, f32[256,256]{1,0:T(8,128)S(1)} %copy-done.5, f32[256,512]{1,0:T(8,128)S(1)} %copy-done.4, f32[256,256]{1,0:T(8,128)S(1)} %copy-done.6, ...), custom_call_target="tpu_custom_call" | custom-call | flops 1073741824 | bytes 16777216 | tf_op jit(solution)/shard_map/look/pallas_call | solution.py:317
  62.2 0.0 collective-permute-done.10.refs_3_
  62.2 0.0 collective-permute-done.11.refs_4_
  62.3 0.0 collective-permute-done.12.refs_5_
  62.3 0.0 copy-done.10
  62.3 0.7 read.1
  63.0 17.4 %all_to_all.5 = bf16[16,32,256]{2,1,0:T(8,128)(2,1)S(1)} all-to-all(bf16[16,32,256]{2,1,0:T(8,128)(2,1)S(1)} %bitcast.15), channel_id=1, replica_groups=mesh['y'=4,'xh'=2,'xl'=2,'core'=2,'head'=8] {'xl','head'}, dimensions={0} | all-to-all | bytes 524288 | tf_op jit(solution)/shard_map/all_to_all | solution.py:384
  80.4 2.1 %collective-permute-start.13 = (bf16[2,8,32,256]{3,2,1,0:T(8,128)(2,1)S(1)}, bf16[2,8,32,256]{3,2,1,0:T(8,128)(2,1)S(1)}, u32[]{:S(2)}, u32[]{:S(2)}) collective-permute-start(bf16[2,8,32,256]{3,2,1,0:T(8,128)(2,1)S(1)} %bitcast.13), channel_id=1, source_target_pairs={{0,8},{8,0},{16,24},{24,16},{32,40},{40,32},{48,56},{56,48},{64,72... | collective-permute-start | bytes 786440 | tf_op jit(solution)/shard_map/ppermute | solution.py:333
  82.5 1.2 %collective-permute-done.13.other_ref = bf16[2,8,32,256]{3,2,1,0:T(8,128)(2,1)S(1)} collective-permute-done((bf16[2,8,32,256]{3,2,1,0:T(8,128)(2,1)S(1)}, bf16[2,8,32,256]{3,2,1,0:T(8,128)(2,1)S(1)}, u32[]{:S(2)}, u32[]{:S(2)}) %collective-permute-start.13) | collective-permute-done | bytes 262176 | tf_op jit(solution)/shard_map/ppermute | solution.py:333
  83.7 2.2 %copy-done.3 = bf16[2048,1024]{1,0:T(8,128)(2,1)S(1)} copy-done((bf16[2048,1024]{1,0:T(8,128)(2,1)S(1)}, bf16[2048,1024]{1,0:T(8,128)(2,1)}, u32[]{:S(2)}) %copy-start.3) | copy-done | bytes 4194328
  85.9 0.7 mix.1
  86.6 0.5 collective-permute-start.14
  87.1 0.9 collective-permute-start.15
  87.9 0.9 collective-permute-start.16
  88.9 0.0 collective-permute-done.14.core_ref
  88.9 1.8 %collective-permute-done.15.half_ref = bf16[32,1024]{1,0:T(8,128)(2,1)S(1)} collective-permute-done((bf16[32,1024]{1,0:T(8,128)(2,1)S(1)}, bf16[32,1024]{1,0:T(8,128)(2,1)S(1)}, u32[]{:S(2)}, u32[]{:S(2)}) %collective-permute-start.15) | collective-permute-done | bytes 65568 | tf_op jit(solution)/shard_map/ppermute | solution.py:333
  90.6 1.7 %collective-permute-done.16.far_ref = bf16[32,1024]{1,0:T(8,128)(2,1)S(1)} collective-permute-done((bf16[32,1024]{1,0:T(8,128)(2,1)S(1)}, bf16[32,1024]{1,0:T(8,128)(2,1)S(1)}, u32[]{:S(2)}, u32[]{:S(2)}) %collective-permute-start.16) | collective-permute-done | bytes 65568 | tf_op jit(solution)/shard_map/ppermute | solution.py:333
  92.3 0.7 lay.1
  (4 shorter events, 0.0 us)
Async XLA Ops:
  6.5 1.6 %copy-start = (bf16[256,4096]{1,0:T(8,128)(2,1)S(1)}, bf16[256,4096]{1,0:T(8,128)(2,1)}, u32[]{:S(2)}) copy-start(bf16[256,4096]{1,0:T(8,128)(2,1)} %param.17) | copy-start | bytes 6291460
  6.5 77.2 %all-gather.3.cloned.1.call-start = ((), (), s32[]{:S(2)}) async-start(), calls=%async_computation.1 | async-start | bytes 4718592 | tf_op jit(solution)/shard_map/all_gather | solution.py:347
  10.3 40.4 %copy-start.9 = (f32[4096]{0:T(1024)S(1)}, f32[4096]{0:T(1024)}, u32[]{:S(2)}) copy-start(f32[4096]{0:T(1024)} %param.10) | copy-start | bytes 49156
  22.0 4.7 %collective-permute-start = (bf16[256,512]{1,0:T(8,128)(2,1)}, bf16[256,512]{1,0:T(8,128)(2,1)S(1)}, u32[]{:S(2)}, u32[]{:S(2)}) collective-permute-start(bf16[256,512]{1,0:T(8,128)(2,1)} %get-tuple-element.20.own_ref), channel_id=1, source_target_pairs={{0,8},{8,0},{16,24},{24,16},{32,40},{40,32},{48,56},{56,48},{64,72... | collective-permute-start | bytes 786440 | tf_op jit(solution)/shard_map/ppermute | solution.py:333
  26.7 0.9 copy-start.7
  27.9 6.8 %collective-permute-start.1 = (bf16[128,512]{1,0:T(8,128)(2,1)S(1)}, bf16[128,512]{1,0:T(8,128)(2,1)S(1)}, u32[]{:S(2)}, u32[]{:S(2)}) collective-permute-start(bf16[128,512]{1,0:T(8,128)(2,1)S(1)} %get-tuple-element.22), channel_id=1, source_target_pairs={{0,16},{8,24},{16,32},{24,40},{32,48},{40,56},{48,0},{56,8},{64,80... | collective-permute-start | bytes 393224 | tf_op jit(solution)/shard_map/ppermute | solution.py:333
  28.0 9.9 %collective-permute-start.2 = (bf16[128,512]{1,0:T(8,128)(2,1)S(1)}, bf16[128,512]{1,0:T(8,128)(2,1)S(1)}, u32[]{:S(2)}, u32[]{:S(2)}) collective-permute-start(bf16[128,512]{1,0:T(8,128)(2,1)S(1)} %get-tuple-element.22), channel_id=1, source_target_pairs={{0,32},{8,40},{16,48},{24,56},{32,0},{40,8},{48,16},{56,24},{64,96... | collective-permute-start | bytes 393224 | tf_op jit(solution)/shard_map/ppermute | solution.py:333
  29.9 8.0 %collective-permute-start.3 = (bf16[128,512]{1,0:T(8,128)(2,1)S(1)}, bf16[128,512]{1,0:T(8,128)(2,1)S(1)}, u32[]{:S(2)}, u32[]{:S(2)}) collective-permute-start(bf16[128,512]{1,0:T(8,128)(2,1)S(1)} %get-tuple-element.22), channel_id=1, source_target_pairs={{0,48},{8,56},{16,0},{24,8},{32,16},{40,24},{48,32},{56,40},{64,11... | collective-permute-start | bytes 393224 | tf_op jit(solution)/shard_map/ppermute | solution.py:333
  34.8 4.2 %collective-permute-start.4 = (bf16[128,512]{1,0:T(8,128)(2,1)S(1)}, bf16[128,512]{1,0:T(8,128)(2,1)S(1)}, u32[]{:S(2)}, u32[]{:S(2)}) collective-permute-start(bf16[128,512]{1,0:T(8,128)(2,1)S(1)} %collective-permute-done.1.refs_0_), channel_id=1, source_target_pairs={{0,8},{8,0},{16,24},{24,16},{32,40},{40,32},{48,56},{56,48},{64,72... | collective-permute-start | bytes 393224 | tf_op jit(solution)/shard_map/ppermute | solution.py:333
  37.9 1.3 %collective-permute-start.5 = (bf16[128,512]{1,0:T(8,128)(2,1)S(1)}, bf16[128,512]{1,0:T(8,128)(2,1)S(1)}, u32[]{:S(2)}, u32[]{:S(2)}) collective-permute-start(bf16[128,512]{1,0:T(8,128)(2,1)S(1)} %collective-permute-done.2.refs_1_), channel_id=1, source_target_pairs={{0,8},{8,0},{16,24},{24,16},{32,40},{40,32},{48,56},{56,48},{64,72... | collective-permute-start | bytes 393224 | tf_op jit(solution)/shard_map/ppermute | solution.py:333
  37.9 1.6 %collective-permute-start.6 = (bf16[128,512]{1,0:T(8,128)(2,1)S(1)}, bf16[128,512]{1,0:T(8,128)(2,1)S(1)}, u32[]{:S(2)}, u32[]{:S(2)}) collective-permute-start(bf16[128,512]{1,0:T(8,128)(2,1)S(1)} %collective-permute-done.3.refs_2_), channel_id=1, source_target_pairs={{0,8},{8,0},{16,24},{24,16},{32,40},{40,32},{48,56},{56,48},{64,72... | collective-permute-start | bytes 393224 | tf_op jit(solution)/shard_map/ppermute | solution.py:333
  40.1 6.1 %collective-permute-start.7 = (bf16[128,512]{1,0:T(8,128)(2,1)S(1)}, bf16[128,512]{1,0:T(8,128)(2,1)S(1)}, u32[]{:S(2)}, u32[]{:S(2)}) collective-permute-start(bf16[128,512]{1,0:T(8,128)(2,1)S(1)} %get-tuple-element.23), channel_id=1, source_target_pairs={{0,64},{8,72},{16,80},{24,88},{32,96},{40,104},{48,112},{56,120},{... | collective-permute-start | bytes 393224 | tf_op jit(solution)/shard_map/ppermute | solution.py:333
  40.5 8.9 %collective-permute-start.8 = (bf16[128,512]{1,0:T(8,128)(2,1)S(1)}, bf16[128,512]{1,0:T(8,128)(2,1)S(1)}, u32[]{:S(2)}, u32[]{:S(2)}) collective-permute-start(bf16[128,512]{1,0:T(8,128)(2,1)S(1)} %get-tuple-element.23), channel_id=1, source_target_pairs={{0,128},{8,136},{16,144},{24,152},{32,160},{40,168},{48,176},{56,1... | collective-permute-start | bytes 393224 | tf_op jit(solution)/shard_map/ppermute | solution.py:333
  43.1 7.3 %collective-permute-start.9 = (bf16[128,512]{1,0:T(8,128)(2,1)S(1)}, bf16[128,512]{1,0:T(8,128)(2,1)S(1)}, u32[]{:S(2)}, u32[]{:S(2)}) collective-permute-start(bf16[128,512]{1,0:T(8,128)(2,1)S(1)} %get-tuple-element.23), channel_id=1, source_target_pairs={{0,192},{8,200},{16,208},{24,216},{32,224},{40,232},{48,240},{56,2... | collective-permute-start | bytes 393224 | tf_op jit(solution)/shard_map/ppermute | solution.py:333
  46.2 16.0 %collective-permute-start.10 = (bf16[128,512]{1,0:T(8,128)(2,1)S(1)}, bf16[128,512]{1,0:T(8,128)(2,1)S(1)}, u32[]{:S(2)}, u32[]{:S(2)}) collective-permute-start(bf16[128,512]{1,0:T(8,128)(2,1)S(1)} %collective-permute-done.7.refs_0_), channel_id=1, source_target_pairs={{0,8},{8,0},{16,24},{24,16},{32,40},{40,32},{48,56},{56,48},{64,72... | collective-permute-start | bytes 393224 | tf_op jit(solution)/shard_map/ppermute | solution.py:333
  49.4 12.9 %collective-permute-start.11 = (bf16[128,512]{1,0:T(8,128)(2,1)S(1)}, bf16[128,512]{1,0:T(8,128)(2,1)S(1)}, u32[]{:S(2)}, u32[]{:S(2)}) collective-permute-start(bf16[128,512]{1,0:T(8,128)(2,1)S(1)} %collective-permute-done.8.refs_1_), channel_id=1, source_target_pairs={{0,8},{8,0},{16,24},{24,16},{32,40},{40,32},{48,56},{56,48},{64,72... | collective-permute-start | bytes 393224 | tf_op jit(solution)/shard_map/ppermute | solution.py:333
  50.4 11.9 %collective-permute-start.12 = (bf16[128,512]{1,0:T(8,128)(2,1)S(1)}, bf16[128,512]{1,0:T(8,128)(2,1)S(1)}, u32[]{:S(2)}, u32[]{:S(2)}) collective-permute-start(bf16[128,512]{1,0:T(8,128)(2,1)S(1)} %collective-permute-done.9.refs_2_), channel_id=1, source_target_pairs={{0,8},{8,0},{16,24},{24,16},{32,40},{40,32},{48,56},{56,48},{64,72... | collective-permute-start | bytes 393224 | tf_op jit(solution)/shard_map/ppermute | solution.py:333
  50.7 2.9 %copy-start.1 = (bf16[4096,3,256]{2,0,1:T(8,128)(2,1)S(1)}, bf16[4096,3,256]{2,0,1:T(8,128)(2,1)}, u32[]{:S(2)}) copy-start(bf16[4096,3,256]{2,0,1:T(8,128)(2,1)} %param.11) | copy-start | bytes 18874372
  53.5 1.6 %copy-start.2 = (bf16[256,4096]{1,0:T(8,128)(2,1)S(1)}, bf16[256,4096]{1,0:T(8,128)(2,1)}, u32[]{:S(2)}) copy-start(bf16[256,4096]{1,0:T(8,128)(2,1)} %x_hbm.3) | copy-start | bytes 6291460
  55.2 1.1 %copy-start.4 = (f32[256,512]{1,0:T(8,128)S(1)}, f32[256,512]{1,0:T(8,128)}, u32[]{:S(2)}) copy-start(f32[256,512]{1,0:T(8,128)} %get-tuple-element.26.solved_ref) | copy-start | bytes 1572868
  56.2 0.9 copy-start.5
  57.2 0.9 copy-start.6
  58.1 0.9 copy-start.8
  59.0 3.3 %copy-start.10 = (f32[256]{0:T(256)S(1)}, f32[256]{0:T(256)}, u32[]{:S(2)}) copy-start(f32[256]{0:T(256)} %param.16) | copy-start | bytes 3076
  80.4 3.3 %collective-permute-start.13 = (bf16[2,8,32,256]{3,2,1,0:T(8,128)(2,1)S(1)}, bf16[2,8,32,256]{3,2,1,0:T(8,128)(2,1)S(1)}, u32[]{:S(2)}, u32[]{:S(2)}) collective-permute-start(bf16[2,8,32,256]{3,2,1,0:T(8,128)(2,1)S(1)} %bitcast.13), channel_id=1, source_target_pairs={{0,8},{8,0},{16,24},{24,16},{32,40},{40,32},{48,56},{56,48},{64,72... | collective-permute-start | bytes 786440 | tf_op jit(solution)/shard_map/ppermute | solution.py:333
  83.7 2.2 %copy-start.3 = (bf16[2048,1024]{1,0:T(8,128)(2,1)S(1)}, bf16[2048,1024]{1,0:T(8,128)(2,1)}, u32[]{:S(2)}) copy-start(bf16[2048,1024]{1,0:T(8,128)(2,1)} %all-gather.3.cloned.1.call-done) | copy-start | bytes 12582916
  86.6 2.3 %collective-permute-start.14 = (bf16[32,1024]{1,0:T(8,128)(2,1)S(1)}, bf16[32,1024]{1,0:T(8,128)(2,1)S(1)}, u32[]{:S(2)}, u32[]{:S(2)}) collective-permute-start(bf16[32,1024]{1,0:T(8,128)(2,1)S(1)} %get-tuple-element.32), channel_id=1, source_target_pairs={{0,8},{8,0},{16,24},{24,16},{32,40},{40,32},{48,56},{56,48},{64,72... | collective-permute-start | bytes 196616 | tf_op jit(solution)/shard_map/ppermute | solution.py:333
  87.1 3.6 %collective-permute-start.15 = (bf16[32,1024]{1,0:T(8,128)(2,1)S(1)}, bf16[32,1024]{1,0:T(8,128)(2,1)S(1)}, u32[]{:S(2)}, u32[]{:S(2)}) collective-permute-start(bf16[32,1024]{1,0:T(8,128)(2,1)S(1)} %get-tuple-element.33), channel_id=1, source_target_pairs={{0,16},{8,24},{16,0},{24,8},{32,48},{40,56},{48,32},{56,40},{64,80... | collective-permute-start | bytes 196616 | tf_op jit(solution)/shard_map/ppermute | solution.py:333
  87.9 4.4 %collective-permute-start.16 = (bf16[32,1024]{1,0:T(8,128)(2,1)S(1)}, bf16[32,1024]{1,0:T(8,128)(2,1)S(1)}, u32[]{:S(2)}, u32[]{:S(2)}) collective-permute-start(bf16[32,1024]{1,0:T(8,128)(2,1)S(1)} %get-tuple-element.34), channel_id=1, source_target_pairs={{0,24},{8,16},{16,8},{24,0},{32,56},{40,48},{48,40},{56,32},{64,88... | collective-permute-start | bytes 196616 | tf_op jit(solution)/shard_map/ppermute | solution.py:333
Sparse Core Ops, SparseCore 0:
  9.1 58.6 all-gather.2

commit v6 on v5

--- a/solution.py
+++ b/solution.py
@@ -75,15 +75,23 @@
 
 
 def fold_kernel(
-    scale_ref, rate_ref, x_hbm, gain_ref, w_hbm, gate_ref, resets_ref,
+    scale_hbm, rate_hbm, x_hbm, gain_ref, w_hbm, gate_ref, resets_ref,
     carry_ref, key_ref, solved_ref, decay_ref, gamma_ref,
-    x_buf, xn_buf, w_buf, sems,
+    x_buf, xn_buf, w_buf, sems, scale_ref, rate_ref, scalar_sems,
 ):
+    scalars = [
+        pltpu.make_async_copy(a, b, scalar_sems.at[i])
+        for i, (a, b) in enumerate(((scale_hbm, scale_ref), (rate_hbm, rate_ref)))
+    ]
+    for copy in scalars:
+        copy.start()
     found = copies(x_hbm, w_hbm, (1, 2), x_buf, w_buf, sems)
     normalise(found, x_buf, xn_buf, gain_ref[...])
     n = x_buf.shape[0]
     gating = mm(xn_buf[...], gate_ref[...], NT)
     key = unit_rows(project(found, xn_buf, w_buf, 0))
+    for copy in scalars:
+        copy.wait()
     beta = scale_ref[0] * jax.nn.sigmoid(gating[:, 0:1])
     logf = -rate_ref[0] * jax.nn.softplus(gating[:, 1:2])
     reset_row = resets_ref[...].astype(F32)
@@ -250,24 +258,46 @@
     out_ref[1] = flat
 
 
-def mix_kernel(own_ref, other_ref, weight_ref, *outs):
+def take_kernel(whole_ref, out_ref):
+    out_ref[...] = whole_ref[...]
+
+
+def mix_kernel(
+    own_ref, other_ref, mine_ref, one_ref, two_ref, three_ref, four_ref, keep_ref, send_ref, total
+):
+    core, half, head = lax.axis_index("core"), lax.axis_index("xl"), lax.axis_index("head")
+    kept = keep_ref.shape[0]
+    width = four_ref.shape[1]
+
+    def rows(steps):
+        source = (head + (2 * core - 1) * steps + 8) % 8
+        block = [ref[place, source] for ref in (own_ref, other_ref) for place in (half, 1 - half)]
+        return jnp.concatenate(block, axis=0)
+
+    total[...] = mm(rows(1), one_ref[...]) + mm(rows(2), two_ref[...]) + mm(rows(3), three_ref[...])
+
+    @pl.when(core == 0)
+    def _():
+        total[...] = total[...] + mm(rows(0), mine_ref[...])
+
+    part = pl.ds(pl.multiple_of(core * width, width), width)
+    total[:, part] = total[:, part] + mm(rows(4), four_ref[...])
+    keep_ref[...] = total[:kept]
+    send_ref[...] = total[kept:].astype(BF16)
+
+
+def add_kernel(keep_ref, come_ref, mine_ref, send_ref):
+    total = (keep_ref[...] + come_ref[...].astype(F32)).astype(BF16)
+    rows = mine_ref.shape[0]
+    mine_ref[...] = total[:rows]
+    send_ref[...] = total[rows:]
+
+
+def lay_kernel(mine_ref, come_ref, out_ref):
+    width = mine_ref.shape[1]
     half = lax.axis_index("xl")
-    rows = own_ref.shape[2]
-    for head in range(weight_ref.shape[0]):
-        block = [ref[place, head] for place in (half, 1 - half) for ref in (own_ref, other_ref)]
-        part = mm(jnp.concatenate(block, axis=0), weight_ref[head])
-        total = part if head == 0 else total + part
-    total = total.astype(BF16)
-    for k, ref in enumerate(outs):
-        ref[...] = total[k * rows : (k + 1) * rows]
-
-
-def lay_kernel(mine_ref, core_ref, half_ref, far_ref, out_ref):
-    width = mine_ref.shape[1]
-    block = lax.axis_index("core") * 2 + lax.axis_index("xl")
-    for flip, ref in ((0, mine_ref), (2, core_ref), (1, half_ref), (3, far_ref)):
-        place = pl.multiple_of((block ^ flip) * width, width)
-        out_ref[:, pl.ds(place, width)] = ref[...]
+    out_ref[:, pl.ds(pl.multiple_of(half * width, width), width)] = mine_ref[...]
+    out_ref[:, pl.ds(pl.multiple_of((1 - half) * width, width), width)] = come_ref[...]
 
 
 def hbm():
@@ -296,11 +326,10 @@
             pltpu.SemaphoreType.DMA((2 + 2 * matrices,)),
         ]
 
-    scalar = pl.BlockSpec(memory_space=pltpu.SMEM)
     carry, key, solved, decay, gamma = pl.pallas_call(
         fold_kernel,
         name="fold",
-        in_specs=[scalar, scalar, hbm(), vmem(), hbm(), vmem(), vmem()],
+        in_specs=[hbm(), hbm(), hbm(), vmem(), hbm(), vmem(), vmem()],
         out_specs=[vmem()] * 5,
         out_shape=[
             jax.ShapeDtypeStruct((n, 2 * n), BF16),
@@ -309,7 +338,8 @@
             square,
             jax.ShapeDtypeStruct((rows, 1), F32),
         ],
-        scratch_shapes=buffers(2),
+        scratch_shapes=buffers(2)
+        + [pltpu.SMEM((1,), F32), pltpu.SMEM((1,), F32), pltpu.SemaphoreType.DMA((2,))],
         compiler_params=LARGE,
     )(beta_scale, decay_rate, frames, gain, weight, gate, resets.reshape(1, rows))
 
@@ -321,7 +351,7 @@
             out_specs=[vmem()] * 2,
             out_shape=[square] * 2,
             scratch_shapes=buffers(1),
-            compiler_params=MIDDLE,
+            compiler_params=LARGE,
             cost_estimate=pl.CostEstimate(
                 flops=4 * rows * width * n, bytes_accessed=16 << 20, transcendentals=0
             ),
@@ -341,10 +371,25 @@
     def flip(bits):
         return lambda i: i ^ bits
 
-    quarter = out_weight.shape[1] // 4
-    block = lax.axis_index("core") * 2 + lax.axis_index("xl")
-    mine = lax.dynamic_slice_in_dim(out_weight, block * quarter, quarter, 1)
-    columns = lax.all_gather(mine, "head", tiled=False)
+    def around(value):
+        up = [(z, (z + 1) % 8) for z in range(8)]
+        down = [(8 + z, 8 + (z + 7) % 8) for z in range(8)]
+        return lax.ppermute(value, ("core", "head"), up + down)
+
+    def later(value, gate):
+        return lax.optimization_barrier((value, gate))[0]
+
+    wide = out_weight.shape[1] // 2
+    mine = pl.pallas_call(
+        take_kernel,
+        name="take",
+        grid=(4,),
+        in_specs=[pl.BlockSpec((n // 4, wide), lambda i: (i, lax.axis_index("xl")))],
+        out_specs=pl.BlockSpec((n // 4, wide), lambda i: (i, 0)),
+        out_shape=jax.ShapeDtypeStruct((n, wide), BF16),
+        compiler_params=LARGE,
+    )(out_weight)
+    one = around(mine)
 
     pair_shape = jax.ShapeDtypeStruct((n, 2 * n), BF16)
     half_shape = jax.ShapeDtypeStruct((n // 2, 2 * n), BF16)
@@ -357,8 +402,9 @@
         out_shape=[pair_shape, half_shape],
         compiler_params=SMALL,
     )(carry, other)
+    two = around(later(one, half))
     near = [moved(half, along_x(s)) for s in (1, 2, 3)]
-    query, local = look()
+    near, (query, local) = lax.optimization_barrier((near, look()))
     swapped = [moved(value, flip(1)) for value in near]
     half, prefix = pl.pallas_call(
         row_kernel,
@@ -369,6 +415,7 @@
         scratch_shapes=[pltpu.VMEM((4, n, 2 * n), BF16), pltpu.VMEM((n, 2 * n), BF16)],
         compiler_params=SMALL,
     )(pair, *near, *swapped)
+    three = around(later(two, half))
     near = [moved(half, along_y(s)) for s in (1, 2, 3)]
     swapped = [moved(value, flip(1)) for value in near]
     flat = pl.pallas_call(
@@ -381,27 +428,43 @@
         compiler_params=SMALL,
     )(*near, *swapped, prefix, other, query, local, out_gain.reshape(1, n))
     part = rows // 8
+    flat, three = lax.optimization_barrier((flat, three))
+    four = around(
+        lax.dynamic_slice_in_dim(three, lax.axis_index("core") * (wide // 2), wide // 2, 1)
+    )
     reads = lax.all_to_all(
         flat.reshape(16, part, n), ("xl", "head"), 0, 0, tiled=True
     ).reshape(2, 8, part, n)
     beside = moved(reads, flip(1))
-    piece = jax.ShapeDtypeStruct((part, quarter), BF16)
-    kept, to_core, to_half, to_far = pl.pallas_call(
+    keep, send = pl.pallas_call(
         mix_kernel,
         name="mix",
-        in_specs=[vmem()] * 3,
-        out_specs=[vmem()] * 4,
-        out_shape=[piece] * 4,
+        in_specs=[vmem()] * 7,
+        out_specs=[vmem()] * 2,
+        out_shape=[
+            jax.ShapeDtypeStruct((2 * part, wide), F32),
+            jax.ShapeDtypeStruct((2 * part, wide), BF16),
+        ],
+        scratch_shapes=[pltpu.VMEM((4 * part, wide), F32)],
         compiler_params=MIDDLE,
-    )(reads, beside, columns)
+    )(reads, beside, mine, one, two, three, four)
+    piece = jax.ShapeDtypeStruct((part, wide), BF16)
+    kept, send = pl.pallas_call(
+        add_kernel,
+        name="add",
+        in_specs=[vmem()] * 2,
+        out_specs=[vmem()] * 2,
+        out_shape=[piece] * 2,
+        compiler_params=SMALL,
+    )(keep, moved(send, flip(1)))
     return pl.pallas_call(
         lay_kernel,
         name="lay",
-        in_specs=[vmem()] * 4,
+        in_specs=[vmem()] * 2,
         out_specs=vmem(),
-        out_shape=jax.ShapeDtypeStruct((part, 4 * quarter), BF16),
+        out_shape=jax.ShapeDtypeStruct((part, 2 * wide), BF16),
         compiler_params=SMALL,
-    )(kept, moved(to_core, flip(1)), moved(to_half, flip(2)), moved(to_far, flip(3)))
+    )(kept, moved(send, flip(2)))
 
 
 def solution(mesh):

time: 100 us -> 92.8 us (0.928)
  blocking collectives: 17.4 us -> 0 us
  between operations: 14.8 us -> 1.44 us
  waiting for transfers between devices: 14.5 us -> 26.1 us
  starting transfers between devices: 21.4 us -> 32.7 us
  Pallas kernels: 17.9 us -> 25.5 us
  local copies, waits for them, and re-layouts: 13.9 us -> 6.58 us
    all_to_all x1 -> x0, blocking collectives: 17.4 us -> none  [per_device(): lax.all_to_all(flat.reshape(16, part, n), ('xl', 'head'), 0, 0, tiled=True)]
    ppermute x0 -> x4, starting transfers between devices: none -> 11.1 us  [around(): return lax.ppermute(value, ('core', 'head'), up + down)]
    unnamed x22 -> x16, local copies, waits for them, and re-layouts: 13.1 us -> 5.74 us
    all_to_all x0 -> x1, waiting for transfers between devices: none -> 5.73 us  [per_device(): lax.all_to_all(flat.reshape(16, part, n), ('xl', 'head'), 0, 0, tiled=True)]
    all_to_all x0 -> x1, starting transfers between devices: none -> 5.11 us  [per_device(): lax.all_to_all(flat.reshape(16, part, n), ('xl', 'head'), 0, 0, tiled=True)]
    ppermute x17 -> x16, starting transfers between devices: 21.4 us -> 16.5 us  [moved(): return lax.ppermute(value, SEQ, [(i, place_of(i)) for i in range(count)])]
    pallas_call x3 -> x5, Pallas kernels: 13.1 us -> 17.8 us  [the longest x1 11.7 us: per_device(): pl.pallas_call(fold_kernel, name='fold', in_specs=[hbm(), hbm(), hbm(), v...]
    ppermute x0 -> x4, waiting for transfers between devices: none -> 3.11 us  [around(): return lax.ppermute(value, ('core', 'head'), up + down)]
  transfers between devices with their start and end apart: 18 -> 21, of which waited for: 10 -> 12; matrix products, arithmetic and copies ran while one was open for 0% -> 1% of each run, Pallas kernels for 16% -> 21%
where the time goes in v6:
time: 92.8 us; the launch traced here: 92.3 us
  starting transfers between devices  32.7 us (35%)
  waiting for transfers between devices  26.1 us (28%)
  Pallas kernels  25.5 us (27%)
  local copies, waits for them, and re-layouts  6.58 us (7%)
  between operations  1.44 us (2%)
    ppermute x16, waiting for transfers between devices, moved(): return lax.ppermute(value, SEQ, [(i, place_of(i)) for i in range(count)])  17.3 us
    ppermute x16, starting transfers between devices, moved(): return lax.ppermute(value, SEQ, [(i, place_of(i)) for i in range(count)])  16.5 us
    pallas_call x1, Pallas kernels, per_device(): pl.pallas_call(fold_kernel, name='fold', in_specs=[hbm(), hbm(), hbm(), v...  11.7 us
    ppermute x4, starting transfers between devices, around(): return lax.ppermute(value, ('core', 'head'), up + down)  11.1 us
    pallas_call x1, Pallas kernels, look(): pl.pallas_call(look_kernel, name='look', in_specs=[hbm(), vmem(), hbm()]...  6.1 us
    unnamed x16, local copies, waits for them, and re-layouts  5.74 us
    all_to_all x1, waiting for transfers between devices, per_device(): lax.all_to_all(flat.reshape(16, part, n), ('xl', 'head'), 0, 0, tiled=True)  5.73 us
    all_to_all x1, starting transfers between devices, per_device(): lax.all_to_all(flat.reshape(16, part, n), ('xl', 'head'), 0, 0, tiled=True)  5.11 us
  transfers between devices with their start and end apart: 21, of which 12 were waited for; matrix products, arithmetic and copies ran while one was open for 1% of the time, Pallas kernels for 21%

profile of v6, /device:TPU:1, one launch (start us, length us, event | category | flops | bytes accessed | tf_op | source)
XLA Modules:
  0.0 92.3 jit_solution(7214464806410143492)
XLA Ops:
  0.0 3.4 %take.1.mine_ref = bf16[256,2048]{1,0:T(8,128)(2,1)} custom-call(bf16[256,4096]{1,0:T(8,128)(2,1)} %whole_ref.1), custom_call_target="tpu_custom_call" | custom-call | tf_op jit(solution)/shard_map/take/pallas_call | solution.py:383
  3.4 6.4 %collective-permute-start.13 = (bf16[256,2048]{1,0:T(8,128)(2,1)}, bf16[256,2048]{1,0:T(8,128)(2,1)S(1)}, u32[]{:S(2)}, u32[]{:S(2)}) collective-permute-start(bf16[256,2048]{1,0:T(8,128)(2,1)} %take.1.mine_ref), channel_id=1, source_target_pairs={{0,1},{1,2},{2,3},{3,4},{4,5},{5,6},{6,7},{7,0},{8,15},{9,8},{10,9... | collective-permute-start | bytes 3145736 | tf_op jit(solution)/shard_map/ppermute | solution.py:377
  11.1 11.7 %fold.1 = (bf16[256,512]{1,0:T(8,128)(2,1)}, f32[256,256]{1,0:T(8,128)}, f32[256,512]{1,0:T(8,128)}, f32[256,256]{1,0:T(8,128)}, f32[256,1]{1,0:T(8,128)}) custom-call(f32[1]{0:T(128)S(6)} %copy.10.scale_hbm, f32[1]{0:T(128)S(6)} %copy.11.rate_hbm, bf16[256,4096]{1,0:T(8,128)(2,1)} %x_hbm.3, f32[1,4096]{1,0:T(1,128)} %bitcast.15, ...), custom_call_target="tpu_custom_call" | custom-call | tf_op jit(solution)/shard_map/fold/pallas_call | solution.py:329
  22.8 0.1 collective-permute-start
  22.9 1.7 %collective-permute-done.other_ref.refs_7_ = bf16[256,512]{1,0:T(8,128)(2,1)S(1)} collective-permute-done((bf16[256,512]{1,0:T(8,128)(2,1)}, bf16[256,512]{1,0:T(8,128)(2,1)S(1)}, u32[]{:S(2)}, u32[]{:S(2)}) %collective-permute-start) | collective-permute-done | bytes 262176 | tf_op jit(solution)/shard_map/ppermute | solution.py:363
  24.6 0.0 copy-start.4
  24.6 0.9 %copy-done.4 = bf16[256,512]{1,0:T(8,128)(2,1)S(1)} copy-done((bf16[256,512]{1,0:T(8,128)(2,1)S(1)}, bf16[256,512]{1,0:T(8,128)(2,1)}, u32[]{:S(2)}) %copy-start.4) | copy-done | bytes 262168
  25.6 0.3 pair.1
  25.9 0.0 collective-permute-done.13.one_ref
  25.9 0.8 collective-permute-start.14
  26.7 2.5 %collective-permute-start.3 = (bf16[128,512]{1,0:T(8,128)(2,1)S(1)}, bf16[128,512]{1,0:T(8,128)(2,1)S(1)}, u32[]{:S(2)}, u32[]{:S(2)}) collective-permute-start(bf16[128,512]{1,0:T(8,128)(2,1)S(1)} %get-tuple-element.31), channel_id=1, source_target_pairs={{0,48},{8,56},{16,0},{24,8},{32,16},{40,24},{48,32},{56,40},{64,11... | collective-permute-start | bytes 393224 | tf_op jit(solution)/shard_map/ppermute | solution.py:363
  29.2 0.5 collective-permute-start.2
  29.7 0.6 collective-permute-start.1
  30.3 0.0 copy-start.7
  30.3 6.1 %look.1 = (f32[256,256]{1,0:T(8,128)}, f32[256,256]{1,0:T(8,128)}) custom-call(bf16[256,4096]{1,0:T(8,128)(2,1)} %x_hbm.3, f32[1,4096]{1,0:T(1,128)} %bitcast.16, bf16[3,4096,256]{2,1,0:T(8,128)(2,1)} %bitcast.14, f32[256,256]{1,0:T(8,128)} %get-tuple-element.32.key_ref, f32[256,512]{1,0:T(8,128)} %get-tuple-element.33.solved_ref, ...), custom_call_target="tpu_custom_call" | custom-call | flops 1073741824 | bytes 16777216 | tf_op jit(solution)/shard_map/look/pallas_call | solution.py:347
  36.4 0.0 collective-permute-done.3.refs_2_
  36.4 0.0 collective-permute-done.2.refs_1_
  36.4 2.5 %collective-permute-done.1.refs_0_ = bf16[128,512]{1,0:T(8,128)(2,1)S(1)} collective-permute-done((bf16[128,512]{1,0:T(8,128)(2,1)S(1)}, bf16[128,512]{1,0:T(8,128)(2,1)S(1)}, u32[]{:S(2)}, u32[]{:S(2)}) %collective-permute-start.1) | collective-permute-done | bytes 131104 | tf_op jit(solution)/shard_map/ppermute | solution.py:363
  38.9 0.4 collective-permute-start.4
  39.4 0.1 collective-permute-start.5
  39.5 0.4 collective-permute-start.6
  39.9 0.5 collective-permute-done.4.refs_3_
  40.4 0.4 collective-permute-done.5.refs_4_
  40.7 0.2 collective-permute-done.6.refs_5_
  40.9 0.6 row.1
  41.5 0.0 copy-start
  41.5 0.0 collective-permute-done.14.two_ref
  41.5 0.0 copy-start.1
  41.5 1.0 %copy-done.1 = bf16[256,2048]{1,0:T(8,128)(2,1)} copy-done((bf16[256,2048]{1,0:T(8,128)(2,1)}, bf16[256,2048]{1,0:T(8,128)(2,1)S(1)}, u32[]{:S(2)}) %copy-start.1) | copy-done | bytes 1048600
  42.5 1.3 %collective-permute-start.15 = (bf16[256,2048]{1,0:T(8,128)(2,1)}, bf16[256,2048]{1,0:T(8,128)(2,1)S(1)}, u32[]{:S(2)}, u32[]{:S(2)}) collective-permute-start(bf16[256,2048]{1,0:T(8,128)(2,1)} %copy-done.1), channel_id=1, source_target_pairs={{0,1},{1,2},{2,3},{3,4},{4,5},{5,6},{6,7},{7,0},{8,15},{9,8},{10,9... | collective-permute-start | bytes 3145736 | tf_op jit(solution)/shard_map/ppermute | solution.py:377
  43.8 2.7 %collective-permute-start.9 = (bf16[128,512]{1,0:T(8,128)(2,1)S(1)}, bf16[128,512]{1,0:T(8,128)(2,1)S(1)}, u32[]{:S(2)}, u32[]{:S(2)}) collective-permute-start(bf16[128,512]{1,0:T(8,128)(2,1)S(1)} %get-tuple-element.41), channel_id=1, source_target_pairs={{0,192},{8,200},{16,208},{24,216},{32,224},{40,232},{48,240},{56,2... | collective-permute-start | bytes 393224 | tf_op jit(solution)/shard_map/ppermute | solution.py:363
  46.5 0.3 collective-permute-start.8
  46.9 0.7 collective-permute-start.7
  47.6 4.6 %collective-permute-done.9.refs_2_ = bf16[128,512]{1,0:T(8,128)(2,1)S(1)} collective-permute-done((bf16[128,512]{1,0:T(8,128)(2,1)S(1)}, bf16[128,512]{1,0:T(8,128)(2,1)S(1)}, u32[]{:S(2)}, u32[]{:S(2)}) %collective-permute-start.9) | collective-permute-done | bytes 131104 | tf_op jit(solution)/shard_map/ppermute | solution.py:363
  52.2 0.9 collective-permute-start.12
  53.1 0.0 collective-permute-done.8.refs_1_
  53.1 1.5 %collective-permute-start.11 = (bf16[128,512]{1,0:T(8,128)(2,1)S(1)}, bf16[128,512]{1,0:T(8,128)(2,1)S(1)}, u32[]{:S(2)}, u32[]{:S(2)}) collective-permute-start(bf16[128,512]{1,0:T(8,128)(2,1)S(1)} %collective-permute-done.8.refs_1_), channel_id=1, source_target_pairs={{0,8},{8,0},{16,24},{24,16},{32,40},{40,32},{48,56},{56,48},{64,72... | collective-permute-start | bytes 393224 | tf_op jit(solution)/shard_map/ppermute | solution.py:363
  54.6 1.7 %collective-permute-done.7.refs_0_ = bf16[128,512]{1,0:T(8,128)(2,1)S(1)} collective-permute-done((bf16[128,512]{1,0:T(8,128)(2,1)S(1)}, bf16[128,512]{1,0:T(8,128)(2,1)S(1)}, u32[]{:S(2)}, u32[]{:S(2)}) %collective-permute-start.7) | collective-permute-done | bytes 131104 | tf_op jit(solution)/shard_map/ppermute | solution.py:363
  56.3 0.5 collective-permute-start.10
  56.8 0.0 collective-permute-done.12.refs_5_
  56.8 0.0 collective-permute-done.11.refs_4_
  56.8 1.0 %collective-permute-done.10.refs_3_ = bf16[128,512]{1,0:T(8,128)(2,1)S(1)} collective-permute-done((bf16[128,512]{1,0:T(8,128)(2,1)S(1)}, bf16[128,512]{1,0:T(8,128)(2,1)S(1)}, u32[]{:S(2)}, u32[]{:S(2)}) %collective-permute-start.10) | collective-permute-done | bytes 131104 | tf_op jit(solution)/shard_map/ppermute | solution.py:363
  57.8 0.0 copy-done.7
  57.8 0.9 %copy-done.5 = f32[256,256]{1,0:T(8,128)S(1)} copy-done((f32[256,256]{1,0:T(8,128)S(1)}, f32[256,256]{1,0:T(8,128)}, u32[]{:S(2)}) %copy-start.5) | copy-done | bytes 262168
  58.7 0.9 %copy-done.6 = f32[256,256]{1,0:T(8,128)S(1)} copy-done((f32[256,256]{1,0:T(8,128)S(1)}, f32[256,256]{1,0:T(8,128)}, u32[]{:S(2)}) %copy-start.6) | copy-done | bytes 262168
  59.7 0.7 read.1
  60.4 0.0 copy-start.3
  60.4 0.7 copy-done.3
  61.1 0.0 collective-permute-done.15.three_ref
  61.1 5.1 %all-to-all-start = ((bf16[16,32,256]{2,1,0:T(8,128)(2,1)}), bf16[16,32,256]{2,1,0:T(8,128)(2,1)S(1)}, u32[]{:S(2)}, u32[]{:S(2)}) async-start(bf16[16,32,256]{2,1,0:T(8,128)(2,1)} %bitcast.11), calls=%async_computation | async-start | bytes 524288 | tf_op jit(solution)/shard_map/all_to_all | solution.py:435
  66.2 0.8 constant_dynamic-slice_fusion
  67.0 2.6 %collective-permute-start.17 = (bf16[256,1024]{1,0:T(8,128)(2,1)}, bf16[256,1024]{1,0:T(8,128)(2,1)}, u32[]{:S(2)}, u32[]{:S(2)}) collective-permute-start(bf16[256,1024]{1,0:T(8,128)(2,1)} %constant_dynamic-slice_fusion), channel_id=1, source_target_pairs={{0,1},{1,2},{2,3},{3,4},{4,5},{5,6},{6,7},{7,0},{8,15},{9,8},{10,9... | collective-permute-start | bytes 1572872 | tf_op jit(solution)/shard_map/ppermute | solution.py:377
  69.6 5.7 %all-to-all-done = bf16[16,32,256]{2,1,0:T(8,128)(2,1)S(1)} async-done(((bf16[16,32,256]{2,1,0:T(8,128)(2,1)}), bf16[16,32,256]{2,1,0:T(8,128)(2,1)S(1)}, u32[]{:S(2)}, u32[]{:S(2)}) %all-to-all-start) | async-done | bytes 262176 | tf_op jit(solution)/shard_map/all_to_all | solution.py:435
  75.3 1.9 %collective-permute-start.16 = (bf16[2,8,32,256]{3,2,1,0:T(8,128)(2,1)S(1)}, bf16[2,8,32,256]{3,2,1,0:T(8,128)(2,1)S(1)}, u32[]{:S(2)}, u32[]{:S(2)}) collective-permute-start(bf16[2,8,32,256]{3,2,1,0:T(8,128)(2,1)S(1)} %bitcast.9), channel_id=1, source_target_pairs={{0,8},{8,0},{16,24},{24,16},{32,40},{40,32},{48,56},{56,48},{64,72... | collective-permute-start | bytes 786440 | tf_op jit(solution)/shard_map/ppermute | solution.py:363
  77.2 3.1 %collective-permute-done.17.four_ref = bf16[256,1024]{1,0:T(8,128)(2,1)} collective-permute-done((bf16[256,1024]{1,0:T(8,128)(2,1)}, bf16[256,1024]{1,0:T(8,128)(2,1)}, u32[]{:S(2)}, u32[]{:S(2)}) %collective-permute-start.17) | collective-permute-done | bytes 524320 | tf_op jit(solution)/shard_map/ppermute | solution.py:377
  80.3 0.0 collective-permute-done.16.other_ref
  80.4 0.0 copy-done
  80.4 1.2 %copy-done.2 = bf16[256,2048]{1,0:T(8,128)(2,1)S(1)} copy-done((bf16[256,2048]{1,0:T(8,128)(2,1)S(1)}, bf16[256,2048]{1,0:T(8,128)(2,1)}, u32[]{:S(2)}) %copy-start.2) | copy-done | bytes 1048600
  81.6 2.0 %mix.1 = (f32[64,2048]{1,0:T(8,128)S(1)}, bf16[64,2048]{1,0:T(8,128)(2,1)S(1)}) custom-call(bf16[2,8,32,256]{3,2,1,0:T(8,128)(2,1)S(1)} %bitcast.10, bf16[2,8,32,256]{3,2,1,0:T(8,128)(2,1)S(1)} %collective-permute-done.16.other_ref, bf16[256,2048]{1,0:T(8,128)(2,1)S(1)} %copy-done, bf16[256,2048]{1,0:T(8,128)(2,1)S(1)} %collective-permute-done.13.one_ref, ...), custom_call_target="tpu_custom_call" | custom-call | tf_op jit(solution)/shard_map/mix/pallas_call | solution.py:439
  83.6 2.0 %collective-permute-start.18 = (bf16[64,2048]{1,0:T(8,128)(2,1)S(1)}, bf16[64,2048]{1,0:T(8,128)(2,1)S(1)}, u32[]{:S(2)}, u32[]{:S(2)}) collective-permute-start(bf16[64,2048]{1,0:T(8,128)(2,1)S(1)} %get-tuple-element.50), channel_id=1, source_target_pairs={{0,8},{8,0},{16,24},{24,16},{32,40},{40,32},{48,56},{56,48},{64,72... | collective-permute-start | bytes 786440 | tf_op jit(solution)/shard_map/ppermute | solution.py:363
  85.6 1.2 %collective-permute-done.18.come_ref = bf16[64,2048]{1,0:T(8,128)(2,1)S(1)} collective-permute-done((bf16[64,2048]{1,0:T(8,128)(2,1)S(1)}, bf16[64,2048]{1,0:T(8,128)(2,1)S(1)}, u32[]{:S(2)}, u32[]{:S(2)}) %collective-permute-start.18) | collective-permute-done | bytes 262176 | tf_op jit(solution)/shard_map/ppermute | solution.py:363
  86.8 1.3 %collective-permute-start.19 = (bf16[32,2048]{1,0:T(8,128)(2,1)S(1)}, bf16[32,2048]{1,0:T(8,128)(2,1)S(1)}, u32[]{:S(2)}, u32[]{:S(2)}) collective-permute-start(bf16[32,2048]{1,0:T(8,128)(2,1)S(1)} %get-tuple-element.52), channel_id=1, source_target_pairs={{0,16},{8,24},{16,0},{24,8},{32,48},{40,56},{48,32},{56,40},{64,80... | collective-permute-start | bytes 393224 | tf_op jit(solution)/shard_map/ppermute | solution.py:363
  88.0 3.5 %collective-permute-done.19.come_ref = bf16[32,2048]{1,0:T(8,128)(2,1)S(1)} collective-permute-done((bf16[32,2048]{1,0:T(8,128)(2,1)S(1)}, bf16[32,2048]{1,0:T(8,128)(2,1)S(1)}, u32[]{:S(2)}, u32[]{:S(2)}) %collective-permute-start.19) | collective-permute-done | bytes 131104 | tf_op jit(solution)/shard_map/ppermute | solution.py:363
  91.6 0.7 lay.1
  (4 shorter events, 0.1 us)
Async XLA Ops:
  3.4 22.5 %collective-permute-start.13 = (bf16[256,2048]{1,0:T(8,128)(2,1)}, bf16[256,2048]{1,0:T(8,128)(2,1)S(1)}, u32[]{:S(2)}, u32[]{:S(2)}) collective-permute-start(bf16[256,2048]{1,0:T(8,128)(2,1)} %take.1.mine_ref), channel_id=1, source_target_pairs={{0,1},{1,2},{2,3},{3,4},{4,5},{5,6},{6,7},{7,0},{8,15},{9,8},{10,9... | collective-permute-start | bytes 3145736 | tf_op jit(solution)/shard_map/ppermute | solution.py:377
  22.8 1.8 %collective-permute-start = (bf16[256,512]{1,0:T(8,128)(2,1)}, bf16[256,512]{1,0:T(8,128)(2,1)S(1)}, u32[]{:S(2)}, u32[]{:S(2)}) collective-permute-start(bf16[256,512]{1,0:T(8,128)(2,1)} %get-tuple-element.29.own_ref), channel_id=1, source_target_pairs={{0,8},{8,0},{16,24},{24,16},{32,40},{40,32},{48,56},{56,48},{64,72... | collective-permute-start | bytes 786440 | tf_op jit(solution)/shard_map/ppermute | solution.py:363
  24.6 1.0 %copy-start.4 = (bf16[256,512]{1,0:T(8,128)(2,1)S(1)}, bf16[256,512]{1,0:T(8,128)(2,1)}, u32[]{:S(2)}) copy-start(bf16[256,512]{1,0:T(8,128)(2,1)} %get-tuple-element.29.own_ref) | copy-start | bytes 786436
  25.9 15.6 %collective-permute-start.14 = (bf16[256,2048]{1,0:T(8,128)(2,1)S(1)}, bf16[256,2048]{1,0:T(8,128)(2,1)S(1)}, u32[]{:S(2)}, u32[]{:S(2)}) collective-permute-start(bf16[256,2048]{1,0:T(8,128)(2,1)S(1)} %collective-permute-done.13.one_ref), channel_id=1, source_target_pairs={{0,1},{1,2},{2,3},{3,4},{4,5},{5,6},{6,7},{7,0},{8,15},{9,8},{10,9... | collective-permute-start | bytes 3145736 | tf_op jit(solution)/shard_map/ppermute | solution.py:377
  26.7 9.7 %collective-permute-start.3 = (bf16[128,512]{1,0:T(8,128)(2,1)S(1)}, bf16[128,512]{1,0:T(8,128)(2,1)S(1)}, u32[]{:S(2)}, u32[]{:S(2)}) collective-permute-start(bf16[128,512]{1,0:T(8,128)(2,1)S(1)} %get-tuple-element.31), channel_id=1, source_target_pairs={{0,48},{8,56},{16,0},{24,8},{32,16},{40,24},{48,32},{56,40},{64,11... | collective-permute-start | bytes 393224 | tf_op jit(solution)/shard_map/ppermute | solution.py:363
  29.2 7.3 %collective-permute-start.2 = (bf16[128,512]{1,0:T(8,128)(2,1)S(1)}, bf16[128,512]{1,0:T(8,128)(2,1)S(1)}, u32[]{:S(2)}, u32[]{:S(2)}) collective-permute-start(bf16[128,512]{1,0:T(8,128)(2,1)S(1)} %get-tuple-element.31), channel_id=1, source_target_pairs={{0,32},{8,40},{16,48},{24,56},{32,0},{40,8},{48,16},{56,24},{64,96... | collective-permute-start | bytes 393224 | tf_op jit(solution)/shard_map/ppermute | solution.py:363
  29.7 9.3 %collective-permute-start.1 = (bf16[128,512]{1,0:T(8,128)(2,1)S(1)}, bf16[128,512]{1,0:T(8,128)(2,1)S(1)}, u32[]{:S(2)}, u32[]{:S(2)}) collective-permute-start(bf16[128,512]{1,0:T(8,128)(2,1)S(1)} %get-tuple-element.31), channel_id=1, source_target_pairs={{0,16},{8,24},{16,32},{24,40},{32,48},{40,56},{48,0},{56,8},{64,80... | collective-permute-start | bytes 393224 | tf_op jit(solution)/shard_map/ppermute | solution.py:363
  30.3 27.5 %copy-start.7 = (f32[256]{0:T(256)S(1)}, f32[256]{0:T(256)}, u32[]{:S(2)}) copy-start(f32[256]{0:T(256)} %param.16) | copy-start | bytes 3076
  38.9 1.4 %collective-permute-start.4 = (bf16[128,512]{1,0:T(8,128)(2,1)S(1)}, bf16[128,512]{1,0:T(8,128)(2,1)S(1)}, u32[]{:S(2)}, u32[]{:S(2)}) collective-permute-start(bf16[128,512]{1,0:T(8,128)(2,1)S(1)} %collective-permute-done.1.refs_0_), channel_id=1, source_target_pairs={{0,8},{8,0},{16,24},{24,16},{32,40},{40,32},{48,56},{56,48},{64,72... | collective-permute-start | bytes 393224 | tf_op jit(solution)/shard_map/ppermute | solution.py:363
  39.4 1.3 %collective-permute-start.5 = (bf16[128,512]{1,0:T(8,128)(2,1)S(1)}, bf16[128,512]{1,0:T(8,128)(2,1)S(1)}, u32[]{:S(2)}, u32[]{:S(2)}) collective-permute-start(bf16[128,512]{1,0:T(8,128)(2,1)S(1)} %collective-permute-done.2.refs_1_), channel_id=1, source_target_pairs={{0,8},{8,0},{16,24},{24,16},{32,40},{40,32},{48,56},{56,48},{64,72... | collective-permute-start | bytes 393224 | tf_op jit(solution)/shard_map/ppermute | solution.py:363
  39.5 1.5 %collective-permute-start.6 = (bf16[128,512]{1,0:T(8,128)(2,1)S(1)}, bf16[128,512]{1,0:T(8,128)(2,1)S(1)}, u32[]{:S(2)}, u32[]{:S(2)}) collective-permute-start(bf16[128,512]{1,0:T(8,128)(2,1)S(1)} %collective-permute-done.3.refs_2_), channel_id=1, source_target_pairs={{0,8},{8,0},{16,24},{24,16},{32,40},{40,32},{48,56},{56,48},{64,72... | collective-permute-start | bytes 393224 | tf_op jit(solution)/shard_map/ppermute | solution.py:363
  41.5 38.8 %copy-start = (bf16[256,2048]{1,0:T(8,128)(2,1)S(1)}, bf16[256,2048]{1,0:T(8,128)(2,1)}, u32[]{:S(2)}) copy-start(bf16[256,2048]{1,0:T(8,128)(2,1)} %take.1.mine_ref) | copy-start | bytes 3145732
  41.5 1.0 %copy-start.1 = (bf16[256,2048]{1,0:T(8,128)(2,1)}, bf16[256,2048]{1,0:T(8,128)(2,1)S(1)}, u32[]{:S(2)}) copy-start(bf16[256,2048]{1,0:T(8,128)(2,1)S(1)} %collective-permute-done.14.two_ref) | copy-start | bytes 3145732
  42.5 18.6 %collective-permute-start.15 = (bf16[256,2048]{1,0:T(8,128)(2,1)}, bf16[256,2048]{1,0:T(8,128)(2,1)S(1)}, u32[]{:S(2)}, u32[]{:S(2)}) collective-permute-start(bf16[256,2048]{1,0:T(8,128)(2,1)} %copy-done.1), channel_id=1, source_target_pairs={{0,1},{1,2},{2,3},{3,4},{4,5},{5,6},{6,7},{7,0},{8,15},{9,8},{10,9... | collective-permute-start | bytes 3145736 | tf_op jit(solution)/shard_map/ppermute | solution.py:377
  43.8 8.4 %collective-permute-start.9 = (bf16[128,512]{1,0:T(8,128)(2,1)S(1)}, bf16[128,512]{1,0:T(8,128)(2,1)S(1)}, u32[]{:S(2)}, u32[]{:S(2)}) collective-permute-start(bf16[128,512]{1,0:T(8,128)(2,1)S(1)} %get-tuple-element.41), channel_id=1, source_target_pairs={{0,192},{8,200},{16,208},{24,216},{32,224},{40,232},{48,240},{56,2... | collective-permute-start | bytes 393224 | tf_op jit(solution)/shard_map/ppermute | solution.py:363
  46.5 6.5 %collective-permute-start.8 = (bf16[128,512]{1,0:T(8,128)(2,1)S(1)}, bf16[128,512]{1,0:T(8,128)(2,1)S(1)}, u32[]{:S(2)}, u32[]{:S(2)}) collective-permute-start(bf16[128,512]{1,0:T(8,128)(2,1)S(1)} %get-tuple-element.41), channel_id=1, source_target_pairs={{0,128},{8,136},{16,144},{24,152},{32,160},{40,168},{48,176},{56,1... | collective-permute-start | bytes 393224 | tf_op jit(solution)/shard_map/ppermute | solution.py:363
  46.9 9.4 %collective-permute-start.7 = (bf16[128,512]{1,0:T(8,128)(2,1)S(1)}, bf16[128,512]{1,0:T(8,128)(2,1)S(1)}, u32[]{:S(2)}, u32[]{:S(2)}) collective-permute-start(bf16[128,512]{1,0:T(8,128)(2,1)S(1)} %get-tuple-element.41), channel_id=1, source_target_pairs={{0,64},{8,72},{16,80},{24,88},{32,96},{40,104},{48,112},{56,120},{... | collective-permute-start | bytes 393224 | tf_op jit(solution)/shard_map/ppermute | solution.py:363
  52.2 4.6 %collective-permute-start.12 = (bf16[128,512]{1,0:T(8,128)(2,1)S(1)}, bf16[128,512]{1,0:T(8,128)(2,1)S(1)}, u32[]{:S(2)}, u32[]{:S(2)}) collective-permute-start(bf16[128,512]{1,0:T(8,128)(2,1)S(1)} %collective-permute-done.9.refs_2_), channel_id=1, source_target_pairs={{0,8},{8,0},{16,24},{24,16},{32,40},{40,32},{48,56},{56,48},{64,72... | collective-permute-start | bytes 393224 | tf_op jit(solution)/shard_map/ppermute | solution.py:363
  53.1 3.7 %collective-permute-start.11 = (bf16[128,512]{1,0:T(8,128)(2,1)S(1)}, bf16[128,512]{1,0:T(8,128)(2,1)S(1)}, u32[]{:S(2)}, u32[]{:S(2)}) collective-permute-start(bf16[128,512]{1,0:T(8,128)(2,1)S(1)} %collective-permute-done.8.refs_1_), channel_id=1, source_target_pairs={{0,8},{8,0},{16,24},{24,16},{32,40},{40,32},{48,56},{56,48},{64,72... | collective-permute-start | bytes 393224 | tf_op jit(solution)/shard_map/ppermute | solution.py:363
  56.3 1.5 %collective-permute-start.10 = (bf16[128,512]{1,0:T(8,128)(2,1)S(1)}, bf16[128,512]{1,0:T(8,128)(2,1)S(1)}, u32[]{:S(2)}, u32[]{:S(2)}) collective-permute-start(bf16[128,512]{1,0:T(8,128)(2,1)S(1)} %collective-permute-done.7.refs_0_), channel_id=1, source_target_pairs={{0,8},{8,0},{16,24},{24,16},{32,40},{40,32},{48,56},{56,48},{64,72... | collective-permute-start | bytes 393224 | tf_op jit(solution)/shard_map/ppermute | solution.py:363
  57.8 1.0 %copy-start.5 = (f32[256,256]{1,0:T(8,128)S(1)}, f32[256,256]{1,0:T(8,128)}, u32[]{:S(2)}) copy-start(f32[256,256]{1,0:T(8,128)} %get-tuple-element.43.refs_8_) | copy-start | bytes 786436
  58.7 0.9 %copy-start.6 = (f32[256,256]{1,0:T(8,128)S(1)}, f32[256,256]{1,0:T(8,128)}, u32[]{:S(2)}) copy-start(f32[256,256]{1,0:T(8,128)} %get-tuple-element.44.refs_9_) | copy-start | bytes 786436
  60.4 0.7 copy-start.3
  61.1 14.3 %all-to-all-start = ((bf16[16,32,256]{2,1,0:T(8,128)(2,1)}), bf16[16,32,256]{2,1,0:T(8,128)(2,1)S(1)}, u32[]{:S(2)}, u32[]{:S(2)}) async-start(bf16[16,32,256]{2,1,0:T(8,128)(2,1)} %bitcast.11), calls=%async_computation | async-start | bytes 524288 | tf_op jit(solution)/shard_map/all_to_all | solution.py:435
  67.0 13.3 %collective-permute-start.17 = (bf16[256,1024]{1,0:T(8,128)(2,1)}, bf16[256,1024]{1,0:T(8,128)(2,1)}, u32[]{:S(2)}, u32[]{:S(2)}) collective-permute-start(bf16[256,1024]{1,0:T(8,128)(2,1)} %constant_dynamic-slice_fusion), channel_id=1, source_target_pairs={{0,1},{1,2},{2,3},{3,4},{4,5},{5,6},{6,7},{7,0},{8,15},{9,8},{10,9... | collective-permute-start | bytes 1572872 | tf_op jit(solution)/shard_map/ppermute | solution.py:377
  75.3 5.0 %collective-permute-start.16 = (bf16[2,8,32,256]{3,2,1,0:T(8,128)(2,1)S(1)}, bf16[2,8,32,256]{3,2,1,0:T(8,128)(2,1)S(1)}, u32[]{:S(2)}, u32[]{:S(2)}) collective-permute-start(bf16[2,8,32,256]{3,2,1,0:T(8,128)(2,1)S(1)} %bitcast.9), channel_id=1, source_target_pairs={{0,8},{8,0},{16,24},{24,16},{32,40},{40,32},{48,56},{56,48},{64,72... | collective-permute-start | bytes 786440 | tf_op jit(solution)/shard_map/ppermute | solution.py:363
  80.4 1.2 %copy-start.2 = (bf16[256,2048]{1,0:T(8,128)(2,1)S(1)}, bf16[256,2048]{1,0:T(8,128)(2,1)}, u32[]{:S(2)}) copy-start(bf16[256,2048]{1,0:T(8,128)(2,1)} %copy-done.1) | copy-start | bytes 3145732
  83.6 3.2 %collective-permute-start.18 = (bf16[64,2048]{1,0:T(8,128)(2,1)S(1)}, bf16[64,2048]{1,0:T(8,128)(2,1)S(1)}, u32[]{:S(2)}, u32[]{:S(2)}) collective-permute-start(bf16[64,2048]{1,0:T(8,128)(2,1)S(1)} %get-tuple-element.50), channel_id=1, source_target_pairs={{0,8},{8,0},{16,24},{24,16},{32,40},{40,32},{48,56},{56,48},{64,72... | collective-permute-start | bytes 786440 | tf_op jit(solution)/shard_map/ppermute | solution.py:363
  86.8 4.8 %collective-permute-start.19 = (bf16[32,2048]{1,0:T(8,128)(2,1)S(1)}, bf16[32,2048]{1,0:T(8,128)(2,1)S(1)}, u32[]{:S(2)}, u32[]{:S(2)}) collective-permute-start(bf16[32,2048]{1,0:T(8,128)(2,1)S(1)} %get-tuple-element.52), channel_id=1, source_target_pairs={{0,16},{8,24},{16,0},{24,8},{32,48},{40,56},{48,32},{56,40},{64,80... | collective-permute-start | bytes 393224 | tf_op jit(solution)/shard_map/ppermute | solution.py:363

commit v7 on v6

--- a/solution.py
+++ b/solution.py
@@ -14,7 +14,7 @@
 SEQ = ("y", "xh", "xl", "core")
 SMALL = pltpu.CompilerParams(vmem_limit_bytes=8 << 20)
 MIDDLE = pltpu.CompilerParams(vmem_limit_bytes=16 << 20)
-LARGE = pltpu.CompilerParams(vmem_limit_bytes=60 << 20)
+LARGE = pltpu.CompilerParams(vmem_limit_bytes=58 << 20)
 
 
 def mm(a, b, dims=NN):
@@ -140,7 +140,7 @@
 
 def look_kernel(
     x_hbm, gain_ref, w_hbm, key_ref, solved_ref, decay_ref, gamma_ref,
-    query_ref, local_ref,
+    out_ref,
     x_buf, xn_buf, w_buf, sems,
 ):
     found = copies(x_hbm, w_hbm, (0,), x_buf, w_buf, sems)
@@ -149,8 +149,8 @@
     query = unit_rows(project(found, xn_buf, w_buf, 0))
     scores = mm3(split(query), split(key_ref[...]), NT) * decay_ref[...]
     seen = mm3(split(scores), split(solved_ref[...]))
-    query_ref[...] = gamma_ref[...] * query - seen[:, :n]
-    local_ref[...] = seen[:, n:]
+    out_ref[:, :n] = gamma_ref[...] * query - seen[:, :n]
+    out_ref[:, n:] = seen[:, n:]
 
 
 def after(later, earlier, n):
@@ -220,8 +220,8 @@
 
 def read_kernel(*refs):
     near, swapped = refs[:3], refs[3:6]
-    prefix_ref, other_ref, query_ref, local_ref, gain_ref, out_ref, held, state = refs[6:]
-    n = query_ref.shape[0]
+    prefix_ref, other_ref, look_ref, gain_ref, out_ref, held, state = refs[6:]
+    n = look_ref.shape[0]
     place = lax.axis_index("y")
     for shift, ref, swap in zip((1, 2, 3), near, swapped):
         hold(held, (place + (4 - shift)) % 4, ref, swap)
@@ -251,15 +251,19 @@
     def _():
         state[...] = push(other_ref[...], state[...])
 
-    read = local_ref[...] + mm3(split(query_ref[...]), split(state[...]))
+    read = look_ref[:, n:] + mm3(split(look_ref[:, :n]), split(state[...]))
     read = read * lax.rsqrt(jnp.mean(read * read, axis=-1, keepdims=True) + 1e-06)
     flat = (read * gain_ref[...]).astype(BF16)
     out_ref[0] = flat
     out_ref[1] = flat
 
 
-def take_kernel(whole_ref, out_ref):
-    out_ref[...] = whole_ref[...]
+def take_kernel(whole_ref, out_ref, sem):
+    width = out_ref.shape[1]
+    columns = pl.ds(pl.multiple_of(lax.axis_index("xl") * width, width), width)
+    copy = pltpu.make_async_copy(whole_ref.at[:, columns], out_ref, sem)
+    copy.start()
+    copy.wait()
 
 
 def mix_kernel(
@@ -348,8 +352,8 @@
             look_kernel,
             name="look",
             in_specs=[hbm(), vmem(), hbm()] + [vmem()] * 4,
-            out_specs=[vmem()] * 2,
-            out_shape=[square] * 2,
+            out_specs=vmem(),
+            out_shape=jax.ShapeDtypeStruct((rows, 2 * n), F32),
             scratch_shapes=buffers(1),
             compiler_params=LARGE,
             cost_estimate=pl.CostEstimate(
@@ -383,10 +387,10 @@
     mine = pl.pallas_call(
         take_kernel,
         name="take",
-        grid=(4,),
-        in_specs=[pl.BlockSpec((n // 4, wide), lambda i: (i, lax.axis_index("xl")))],
-        out_specs=pl.BlockSpec((n // 4, wide), lambda i: (i, 0)),
+        in_specs=[hbm()],
+        out_specs=vmem(),
         out_shape=jax.ShapeDtypeStruct((n, wide), BF16),
+        scratch_shapes=[pltpu.SemaphoreType.DMA],
         compiler_params=LARGE,
     )(out_weight)
     one = around(mine)
@@ -394,6 +398,7 @@
     pair_shape = jax.ShapeDtypeStruct((n, 2 * n), BF16)
     half_shape = jax.ShapeDtypeStruct((n // 2, 2 * n), BF16)
     other = moved(carry, flip(1))
+    two = around(later(one, other))
     pair, half = pl.pallas_call(
         pair_kernel,
         name="pair",
@@ -402,9 +407,9 @@
         out_shape=[pair_shape, half_shape],
         compiler_params=SMALL,
     )(carry, other)
-    two = around(later(one, half))
     near = [moved(half, along_x(s)) for s in (1, 2, 3)]
-    near, (query, local) = lax.optimization_barrier((near, look()))
+    near, looked = lax.optimization_barrier((near, look()))
+    three = around(later(two, near))
     swapped = [moved(value, flip(1)) for value in near]
     half, prefix = pl.pallas_call(
         row_kernel,
@@ -415,23 +420,24 @@
         scratch_shapes=[pltpu.VMEM((4, n, 2 * n), BF16), pltpu.VMEM((n, 2 * n), BF16)],
         compiler_params=SMALL,
     )(pair, *near, *swapped)
-    three = around(later(two, half))
     near = [moved(half, along_y(s)) for s in (1, 2, 3)]
+    four = around(
+        later(
+            lax.dynamic_slice_in_dim(three, lax.axis_index("core") * (wide // 2), wide // 2, 1), near
+        )
+    )
     swapped = [moved(value, flip(1)) for value in near]
     flat = pl.pallas_call(
         read_kernel,
         name="read",
-        in_specs=[vmem()] * 11,
+        in_specs=[vmem()] * 10,
         out_specs=vmem(),
         out_shape=jax.ShapeDtypeStruct((2, rows, n), BF16),
         scratch_shapes=[pltpu.VMEM((4, n, 2 * n), BF16), pltpu.VMEM((n, n), F32)],
         compiler_params=SMALL,
-    )(*near, *swapped, prefix, other, query, local, out_gain.reshape(1, n))
+    )(*near, *swapped, prefix, other, looked, out_gain.reshape(1, n))
     part = rows // 8
-    flat, three = lax.optimization_barrier((flat, three))
-    four = around(
-        lax.dynamic_slice_in_dim(three, lax.axis_index("core") * (wide // 2), wide // 2, 1)
-    )
+    flat, four = lax.optimization_barrier((flat, four))
     reads = lax.all_to_all(
         flat.reshape(16, part, n), ("xl", "head"), 0, 0, tiled=True
     ).reshape(2, 8, part, n)

time: 92.8 us -> 92.9 us (level)
  blocking collectives: 0 us -> 13.8 us
  starting transfers between devices: 32.7 us -> 25.8 us
  local copies, waits for them, and re-layouts: 6.58 us -> 1.01 us
    all_to_all x0 -> x1, blocking collectives: none -> 13.8 us  [per_device(): lax.all_to_all(flat.reshape(16, part, n), ('xl', 'head'), 0, 0, tiled=True)]
    ppermute x4, waiting for transfers between devices: 3.11 us -> 9.31 us  [around(): return lax.ppermute(value, ('core', 'head'), up + down)]
    all_to_all x1 -> x0, waiting for transfers between devices: 5.73 us -> none  [per_device(): lax.all_to_all(flat.reshape(16, part, n), ('xl', 'head'), 0, 0, tiled=True)]
    all_to_all x1 -> x0, starting transfers between devices: 5.11 us -> none  [per_device(): lax.all_to_all(flat.reshape(16, part, n), ('xl', 'head'), 0, 0, tiled=True)]
    unnamed x16 -> x12, local copies, waits for them, and re-layouts: 5.74 us -> 0.97 us
    ppermute x16, starting transfers between devices: 16.5 us -> 14.3 us  [moved(): return lax.ppermute(value, SEQ, [(i, place_of(i)) for i in range(count)])]
    ppermute x16, waiting for transfers between devices: 17.3 us -> 16 us  [moved(): return lax.ppermute(value, SEQ, [(i, place_of(i)) for i in range(count)])]
    pallas_call x2, Pallas kernels: 4.07 us -> 2.92 us  [the longest x1 2.22 us: per_device(): pl.pallas_call(take_kernel, name='take', in_specs=[hbm()], out_specs=vmem...]
  transfers between devices with their start and end apart: 21 -> 20, of which waited for: 12 -> 14; matrix products, arithmetic and copies ran while one was open for 1% -> 0% of each run, Pallas kernels for 21% -> 22%
where the time goes in v7:
time: 92.9 us; the launch traced here: 92.6 us
  starting transfers between devices  25.8 us (28%)
  Pallas kernels  25.3 us (27%)
  waiting for transfers between devices  25.3 us (27%)
  blocking collectives  13.8 us (15%)
  between operations  1.44 us (2%)
  local copies, waits for them, and re-layouts  1.01 us (1%)
    ppermute x16, waiting for transfers between devices, moved(): return lax.ppermute(value, SEQ, [(i, place_of(i)) for i in range(count)])  16 us
    ppermute x16, starting transfers between devices, moved(): return lax.ppermute(value, SEQ, [(i, place_of(i)) for i in range(count)])  14.3 us
    all_to_all x1, blocking collectives, per_device(): lax.all_to_all(flat.reshape(16, part, n), ('xl', 'head'), 0, 0, tiled=True)  13.8 us
    pallas_call x1, Pallas kernels, per_device(): pl.pallas_call(fold_kernel, name='fold', in_specs=[hbm(), hbm(), hbm(), v...  11.7 us
    ppermute x4, starting transfers between devices, around(): return lax.ppermute(value, ('core', 'head'), up + down)  11.5 us
    ppermute x4, waiting for transfers between devices, around(): return lax.ppermute(value, ('core', 'head'), up + down)  9.31 us
    pallas_call x1, Pallas kernels, look(): pl.pallas_call(look_kernel, name='look', in_specs=[hbm(), vmem(), hbm()]...  6.18 us
    pallas_call x1, Pallas kernels, per_device(): pl.pallas_call(take_kernel, name='take', in_specs=[hbm()], out_specs=vmem...  2.22 us
  transfers between devices with their start and end apart: 20, of which 14 were waited for; matrix products, arithmetic and copies ran while one was open for 0% of the time, Pallas kernels for 22%

profile of v7, /device:TPU:1, one launch (start us, length us, event | category | flops | bytes accessed | tf_op | source)
XLA Modules:
  0.0 92.6 jit_solution(17494056987004969637)
XLA Ops:
  0.0 2.2 %take.1.mine_ref = bf16[256,2048]{1,0:T(8,128)(2,1)} custom-call(bf16[256,4096]{1,0:T(8,128)(2,1)} %whole_ref.1), custom_call_target="tpu_custom_call" | custom-call | tf_op jit(solution)/shard_map/take/pallas_call | solution.py:387
  2.2 6.5 %collective-permute-start.13 = (bf16[256,2048]{1,0:T(8,128)(2,1)}, bf16[256,2048]{1,0:T(8,128)(2,1)S(1)}, u32[]{:S(2)}, u32[]{:S(2)}) collective-permute-start(bf16[256,2048]{1,0:T(8,128)(2,1)} %take.1.mine_ref), channel_id=1, source_target_pairs={{0,1},{1,2},{2,3},{3,4},{4,5},{5,6},{6,7},{7,0},{8,15},{9,8},{10,9... | collective-permute-start | bytes 3145736 | tf_op jit(solution)/shard_map/ppermute | solution.py:381
  10.0 11.7 %fold.1 = (bf16[256,512]{1,0:T(8,128)(2,1)}, f32[256,256]{1,0:T(8,128)}, f32[256,512]{1,0:T(8,128)}, f32[256,256]{1,0:T(8,128)}, f32[256,1]{1,0:T(8,128)}) custom-call(f32[1]{0:T(128)S(6)} %copy.10.scale_hbm, f32[1]{0:T(128)S(6)} %copy.11.rate_hbm, bf16[256,4096]{1,0:T(8,128)(2,1)} %x_hbm.3, f32[1,4096]{1,0:T(1,128)} %bitcast.15, ...), custom_call_target="tpu_custom_call" | custom-call | tf_op jit(solution)/shard_map/fold/pallas_call | solution.py:333
  21.8 0.1 collective-permute-start
  21.9 1.7 %collective-permute-done.other_ref.refs_7_ = bf16[256,512]{1,0:T(8,128)(2,1)S(1)} collective-permute-done((bf16[256,512]{1,0:T(8,128)(2,1)}, bf16[256,512]{1,0:T(8,128)(2,1)S(1)}, u32[]{:S(2)}, u32[]{:S(2)}) %collective-permute-start) | collective-permute-done | bytes 262176 | tf_op jit(solution)/shard_map/ppermute | solution.py:367
  23.6 0.0 collective-permute-done.13.one_ref
  23.6 0.0 copy-start.2
  23.6 0.7 collective-permute-start.14
  24.3 0.0 copy-start.4
  24.3 0.9 %copy-done.4 = bf16[256,512]{1,0:T(8,128)(2,1)S(1)} copy-done((bf16[256,512]{1,0:T(8,128)(2,1)S(1)}, bf16[256,512]{1,0:T(8,128)(2,1)}, u32[]{:S(2)}) %copy-start.4) | copy-done | bytes 262168
  25.3 0.3 pair.1
  25.5 2.6 %collective-permute-start.3 = (bf16[128,512]{1,0:T(8,128)(2,1)S(1)}, bf16[128,512]{1,0:T(8,128)(2,1)S(1)}, u32[]{:S(2)}, u32[]{:S(2)}) collective-permute-start(bf16[128,512]{1,0:T(8,128)(2,1)S(1)} %get-tuple-element.29), channel_id=1, source_target_pairs={{0,48},{8,56},{16,0},{24,8},{32,16},{40,24},{48,32},{56,40},{64,11... | collective-permute-start | bytes 393224 | tf_op jit(solution)/shard_map/ppermute | solution.py:367
  28.1 0.5 collective-permute-start.2
  28.6 0.6 collective-permute-start.1
  29.2 6.2 %look.1.refs_8_ = f32[256,512]{1,0:T(8,128)} custom-call(bf16[256,4096]{1,0:T(8,128)(2,1)} %x_hbm.3, f32[1,4096]{1,0:T(1,128)} %bitcast.16, bf16[3,4096,256]{2,1,0:T(8,128)(2,1)} %bitcast.14, f32[256,256]{1,0:T(8,128)} %get-tuple-element.30.key_ref, f32[256,512]{1,0:T(8,128)} %get-tuple-element.31.solved_ref, f32[256,256]{1,0:T(8,128)} %get-tuple-element.32.decay_ref, ...), custom_call_target="tpu_custom_call" | custom-call | flops 1073741824 | bytes 16777216 | tf_op jit(solution)/shard_map/look/pallas_call | solution.py:351
  35.4 0.0 copy-done.2
  35.4 0.0 copy-start.1
  35.4 0.0 copy-start.5
  35.4 0.0 collective-permute-done.3.refs_2_
  35.5 0.0 collective-permute-done.2.refs_1_
  35.5 2.5 %collective-permute-done.1.refs_0_ = bf16[128,512]{1,0:T(8,128)(2,1)S(1)} collective-permute-done((bf16[128,512]{1,0:T(8,128)(2,1)S(1)}, bf16[128,512]{1,0:T(8,128)(2,1)S(1)}, u32[]{:S(2)}, u32[]{:S(2)}) %collective-permute-start.1) | collective-permute-done | bytes 131104 | tf_op jit(solution)/shard_map/ppermute | solution.py:367
  38.0 0.0 collective-permute-done.14.two_ref
  38.0 1.3 %collective-permute-start.15 = (bf16[256,2048]{1,0:T(8,128)(2,1)}, bf16[256,2048]{1,0:T(8,128)(2,1)S(1)}, u32[]{:S(2)}, u32[]{:S(2)}) collective-permute-start(bf16[256,2048]{1,0:T(8,128)(2,1)} %collective-permute-done.14.two_ref), channel_id=1, source_target_pairs={{0,1},{1,2},{2,3},{3,4},{4,5},{5,6},{6,7},{7,0},{8,15},{9,8},{10,9... | collective-permute-start | bytes 3145736 | tf_op jit(solution)/shard_map/ppermute | solution.py:381
  39.3 0.6 collective-permute-start.4
  39.8 0.0 collective-permute-start.5
  39.9 0.5 collective-permute-start.6
  40.4 0.5 collective-permute-done.4.refs_3_
  40.8 0.4 collective-permute-done.5.refs_4_
  41.2 0.2 collective-permute-done.6.refs_5_
  41.4 1.2 %row.1 = (bf16[128,512]{1,0:T(8,128)(2,1)}, bf16[256,512]{1,0:T(8,128)(2,1)S(1)}) custom-call(bf16[256,512]{1,0:T(8,128)(2,1)S(1)} %get-tuple-element.28.own_ref, bf16[128,512]{1,0:T(8,128)(2,1)S(1)} %collective-permute-done.1.refs_0_, bf16[128,512]{1,0:T(8,128)(2,1)S(1)} %collective-permute-done.2.refs_1_, ...), custom_call_target="tpu_custom_call" | custom-call | tf_op jit(solution)/shard_map/row/pallas_call | solution.py:414
  42.6 0.0 copy-start
  42.6 2.7 %collective-permute-start.9 = (bf16[128,512]{1,0:T(8,128)(2,1)}, bf16[128,512]{1,0:T(8,128)(2,1)S(1)}, u32[]{:S(2)}, u32[]{:S(2)}) collective-permute-start(bf16[128,512]{1,0:T(8,128)(2,1)} %get-tuple-element.37), channel_id=1, source_target_pairs={{0,192},{8,200},{16,208},{24,216},{32,224},{40,232},{48,240},{56,2... | collective-permute-start | bytes 393224 | tf_op jit(solution)/shard_map/ppermute | solution.py:367
  45.3 0.3 collective-permute-start.8
  45.7 0.7 collective-permute-start.7
  46.4 0.0 copy-start.3
  46.4 5.8 %collective-permute-done.15.three_ref = bf16[256,2048]{1,0:T(8,128)(2,1)S(1)} collective-permute-done((bf16[256,2048]{1,0:T(8,128)(2,1)}, bf16[256,2048]{1,0:T(8,128)(2,1)S(1)}, u32[]{:S(2)}, u32[]{:S(2)}) %collective-permute-start.15) | collective-permute-done | bytes 1048608 | tf_op jit(solution)/shard_map/ppermute | solution.py:381
  52.2 0.0 collective-permute-done.9.refs_2_
  52.2 0.0 collective-permute-done.8.refs_1_
  52.2 3.1 %collective-permute-done.7.refs_0_ = bf16[128,512]{1,0:T(8,128)(2,1)S(1)} collective-permute-done((bf16[128,512]{1,0:T(8,128)(2,1)}, bf16[128,512]{1,0:T(8,128)(2,1)S(1)}, u32[]{:S(2)}, u32[]{:S(2)}) %collective-permute-start.7) | collective-permute-done | bytes 131104 | tf_op jit(solution)/shard_map/ppermute | solution.py:367
  55.3 3.0 %collective-permute-start.16 = (bf16[256,1024]{1,0:T(8,128)(2,1)S(1)}, bf16[256,1024]{1,0:T(8,128)(2,1)S(1)}, u32[]{:S(2)}, u32[]{:S(2)}) collective-permute-start(bf16[256,1024]{1,0:T(8,128)(2,1)S(1)} %constant_dynamic-slice_fusion), channel_id=1, source_target_pairs={{0,1},{1,2},{2,3},{3,4},{4,5},{5,6},{6,7},{7,0},{8,15},{9,8},{10,9... | collective-permute-start | bytes 1572872 | tf_op jit(solution)/shard_map/ppermute | solution.py:381
  58.2 0.0 collective-permute-start.12
  58.2 0.5 collective-permute-start.11
  58.8 0.0 collective-permute-start.10
  58.8 0.8 collective-permute-done.12.refs_5_
  59.6 0.2 collective-permute-done.11.refs_4_
  59.8 0.3 collective-permute-done.10.refs_3_
  60.1 0.0 copy-done.1
  60.1 0.0 copy-done.5
  60.1 0.7 read.1
  60.8 3.6 %collective-permute-done.16.four_ref = bf16[256,1024]{1,0:T(8,128)(2,1)S(1)} collective-permute-done((bf16[256,1024]{1,0:T(8,128)(2,1)S(1)}, bf16[256,1024]{1,0:T(8,128)(2,1)S(1)}, u32[]{:S(2)}, u32[]{:S(2)}) %collective-permute-start.16) | collective-permute-done | bytes 524320 | tf_op jit(solution)/shard_map/ppermute | solution.py:381
  64.4 13.8 %all_to_all.5 = bf16[16,32,256]{2,1,0:T(8,128)(2,1)S(1)} all-to-all(bf16[16,32,256]{2,1,0:T(8,128)(2,1)S(1)} %bitcast.11), channel_id=1, replica_groups=mesh['y'=4,'xh'=2,'xl'=2,'core'=2,'head'=8] {'xl','head'}, dimensions={0} | all-to-all | bytes 524288 | tf_op jit(solution)/shard_map/all_to_all | solution.py:441
  78.2 3.6 %collective-permute-start.17 = (bf16[2,8,32,256]{3,2,1,0:T(8,128)(2,1)S(1)}, bf16[2,8,32,256]{3,2,1,0:T(8,128)(2,1)S(1)}, u32[]{:S(2)}, u32[]{:S(2)}) collective-permute-start(bf16[2,8,32,256]{3,2,1,0:T(8,128)(2,1)S(1)} %bitcast.9), channel_id=1, source_target_pairs={{0,8},{8,0},{16,24},{24,16},{32,40},{40,32},{48,56},{56,48},{64,72... | collective-permute-start | bytes 786440 | tf_op jit(solution)/shard_map/ppermute | solution.py:367
  81.8 1.2 %collective-permute-done.17.other_ref = bf16[2,8,32,256]{3,2,1,0:T(8,128)(2,1)S(1)} collective-permute-done((bf16[2,8,32,256]{3,2,1,0:T(8,128)(2,1)S(1)}, bf16[2,8,32,256]{3,2,1,0:T(8,128)(2,1)S(1)}, u32[]{:S(2)}, u32[]{:S(2)}) %collective-permute-start.17) | collective-permute-done | bytes 262176 | tf_op jit(solution)/shard_map/ppermute | solution.py:367
  82.9 0.0 copy-done
  82.9 0.0 copy-done.3
  82.9 2.2 %mix.1 = (f32[64,2048]{1,0:T(8,128)S(1)}, bf16[64,2048]{1,0:T(8,128)(2,1)S(1)}) custom-call(bf16[2,8,32,256]{3,2,1,0:T(8,128)(2,1)S(1)} %bitcast.10, bf16[2,8,32,256]{3,2,1,0:T(8,128)(2,1)S(1)} %collective-permute-done.17.other_ref, bf16[256,2048]{1,0:T(8,128)(2,1)S(1)} %copy-done, bf16[256,2048]{1,0:T(8,128)(2,1)S(1)} %copy-done.3, ...), custom_call_target="tpu_custom_call" | custom-call | tf_op jit(solution)/shard_map/mix/pallas_call | solution.py:445
  85.1 0.8 collective-permute-start.18
  85.9 1.2 %collective-permute-done.18.come_ref = bf16[64,2048]{1,0:T(8,128)(2,1)S(1)} collective-permute-done((bf16[64,2048]{1,0:T(8,128)(2,1)S(1)}, bf16[64,2048]{1,0:T(8,128)(2,1)S(1)}, u32[]{:S(2)}, u32[]{:S(2)}) %collective-permute-start.18) | collective-permute-done | bytes 262176 | tf_op jit(solution)/shard_map/ppermute | solution.py:367
  87.1 0.8 collective-permute-start.19
  87.9 4.0 %collective-permute-done.19.come_ref = bf16[32,2048]{1,0:T(8,128)(2,1)S(1)} collective-permute-done((bf16[32,2048]{1,0:T(8,128)(2,1)S(1)}, bf16[32,2048]{1,0:T(8,128)(2,1)S(1)}, u32[]{:S(2)}, u32[]{:S(2)}) %collective-permute-start.19) | collective-permute-done | bytes 131104 | tf_op jit(solution)/shard_map/ppermute | solution.py:367
  91.9 0.7 lay.1
  (2 shorter events, 0.1 us)
Async XLA Ops:
  2.2 21.4 %collective-permute-start.13 = (bf16[256,2048]{1,0:T(8,128)(2,1)}, bf16[256,2048]{1,0:T(8,128)(2,1)S(1)}, u32[]{:S(2)}, u32[]{:S(2)}) collective-permute-start(bf16[256,2048]{1,0:T(8,128)(2,1)} %take.1.mine_ref), channel_id=1, source_target_pairs={{0,1},{1,2},{2,3},{3,4},{4,5},{5,6},{6,7},{7,0},{8,15},{9,8},{10,9... | collective-permute-start | bytes 3145736 | tf_op jit(solution)/shard_map/ppermute | solution.py:381
  21.8 1.8 %collective-permute-start = (bf16[256,512]{1,0:T(8,128)(2,1)}, bf16[256,512]{1,0:T(8,128)(2,1)S(1)}, u32[]{:S(2)}, u32[]{:S(2)}) collective-permute-start(bf16[256,512]{1,0:T(8,128)(2,1)} %get-tuple-element.27.own_ref), channel_id=1, source_target_pairs={{0,8},{8,0},{16,24},{24,16},{32,40},{40,32},{48,56},{56,48},{64,72... | collective-permute-start | bytes 786440 | tf_op jit(solution)/shard_map/ppermute | solution.py:367
  23.6 11.8 %copy-start.2 = (bf16[256,2048]{1,0:T(8,128)(2,1)}, bf16[256,2048]{1,0:T(8,128)(2,1)S(1)}, u32[]{:S(2)}) copy-start(bf16[256,2048]{1,0:T(8,128)(2,1)S(1)} %collective-permute-done.13.one_ref) | copy-start | bytes 3145732
  23.6 14.4 %collective-permute-start.14 = (bf16[256,2048]{1,0:T(8,128)(2,1)S(1)}, bf16[256,2048]{1,0:T(8,128)(2,1)}, u32[]{:S(2)}, u32[]{:S(2)}) collective-permute-start(bf16[256,2048]{1,0:T(8,128)(2,1)S(1)} %collective-permute-done.13.one_ref), channel_id=1, source_target_pairs={{0,1},{1,2},{2,3},{3,4},{4,5},{5,6},{6,7},{7,0},{8,15},{9,8},{10,9... | collective-permute-start | bytes 3145736 | tf_op jit(solution)/shard_map/ppermute | solution.py:381
  24.3 0.9 %copy-start.4 = (bf16[256,512]{1,0:T(8,128)(2,1)S(1)}, bf16[256,512]{1,0:T(8,128)(2,1)}, u32[]{:S(2)}) copy-start(bf16[256,512]{1,0:T(8,128)(2,1)} %get-tuple-element.27.own_ref) | copy-start | bytes 786436
  25.5 9.9 %collective-permute-start.3 = (bf16[128,512]{1,0:T(8,128)(2,1)S(1)}, bf16[128,512]{1,0:T(8,128)(2,1)S(1)}, u32[]{:S(2)}, u32[]{:S(2)}) collective-permute-start(bf16[128,512]{1,0:T(8,128)(2,1)S(1)} %get-tuple-element.29), channel_id=1, source_target_pairs={{0,48},{8,56},{16,0},{24,8},{32,16},{40,24},{48,32},{56,40},{64,11... | collective-permute-start | bytes 393224 | tf_op jit(solution)/shard_map/ppermute | solution.py:367
  28.1 7.4 %collective-permute-start.2 = (bf16[128,512]{1,0:T(8,128)(2,1)S(1)}, bf16[128,512]{1,0:T(8,128)(2,1)S(1)}, u32[]{:S(2)}, u32[]{:S(2)}) collective-permute-start(bf16[128,512]{1,0:T(8,128)(2,1)S(1)} %get-tuple-element.29), channel_id=1, source_target_pairs={{0,32},{8,40},{16,48},{24,56},{32,0},{40,8},{48,16},{56,24},{64,96... | collective-permute-start | bytes 393224 | tf_op jit(solution)/shard_map/ppermute | solution.py:367
  28.6 9.4 %collective-permute-start.1 = (bf16[128,512]{1,0:T(8,128)(2,1)S(1)}, bf16[128,512]{1,0:T(8,128)(2,1)S(1)}, u32[]{:S(2)}, u32[]{:S(2)}) collective-permute-start(bf16[128,512]{1,0:T(8,128)(2,1)S(1)} %get-tuple-element.29), channel_id=1, source_target_pairs={{0,16},{8,24},{16,32},{24,40},{32,48},{40,56},{48,0},{56,8},{64,80... | collective-permute-start | bytes 393224 | tf_op jit(solution)/shard_map/ppermute | solution.py:367
  35.4 24.7 %copy-start.1 = (f32[256,512]{1,0:T(8,128)S(1)}, f32[256,512]{1,0:T(8,128)}, u32[]{:S(2)}) copy-start(f32[256,512]{1,0:T(8,128)} %look.1.refs_8_) | copy-start | bytes 1572868
  35.4 24.7 %copy-start.5 = (f32[256]{0:T(256)S(1)}, f32[256]{0:T(256)}, u32[]{:S(2)}) copy-start(f32[256]{0:T(256)} %param.16) | copy-start | bytes 3076
  38.0 14.2 %collective-permute-start.15 = (bf16[256,2048]{1,0:T(8,128)(2,1)}, bf16[256,2048]{1,0:T(8,128)(2,1)S(1)}, u32[]{:S(2)}, u32[]{:S(2)}) collective-permute-start(bf16[256,2048]{1,0:T(8,128)(2,1)} %collective-permute-done.14.two_ref), channel_id=1, source_target_pairs={{0,1},{1,2},{2,3},{3,4},{4,5},{5,6},{6,7},{7,0},{8,15},{9,8},{10,9... | collective-permute-start | bytes 3145736 | tf_op jit(solution)/shard_map/ppermute | solution.py:381
  39.3 1.5 %collective-permute-start.4 = (bf16[128,512]{1,0:T(8,128)(2,1)S(1)}, bf16[128,512]{1,0:T(8,128)(2,1)S(1)}, u32[]{:S(2)}, u32[]{:S(2)}) collective-permute-start(bf16[128,512]{1,0:T(8,128)(2,1)S(1)} %collective-permute-done.1.refs_0_), channel_id=1, source_target_pairs={{0,8},{8,0},{16,24},{24,16},{32,40},{40,32},{48,56},{56,48},{64,72... | collective-permute-start | bytes 393224 | tf_op jit(solution)/shard_map/ppermute | solution.py:367
  39.8 1.3 %collective-permute-start.5 = (bf16[128,512]{1,0:T(8,128)(2,1)S(1)}, bf16[128,512]{1,0:T(8,128)(2,1)S(1)}, u32[]{:S(2)}, u32[]{:S(2)}) collective-permute-start(bf16[128,512]{1,0:T(8,128)(2,1)S(1)} %collective-permute-done.2.refs_1_), channel_id=1, source_target_pairs={{0,8},{8,0},{16,24},{24,16},{32,40},{40,32},{48,56},{56,48},{64,72... | collective-permute-start | bytes 393224 | tf_op jit(solution)/shard_map/ppermute | solution.py:367
  39.9 1.5 %collective-permute-start.6 = (bf16[128,512]{1,0:T(8,128)(2,1)S(1)}, bf16[128,512]{1,0:T(8,128)(2,1)S(1)}, u32[]{:S(2)}, u32[]{:S(2)}) collective-permute-start(bf16[128,512]{1,0:T(8,128)(2,1)S(1)} %collective-permute-done.3.refs_2_), channel_id=1, source_target_pairs={{0,8},{8,0},{16,24},{24,16},{32,40},{40,32},{48,56},{56,48},{64,72... | collective-permute-start | bytes 393224 | tf_op jit(solution)/shard_map/ppermute | solution.py:367
  42.6 40.3 %copy-start = (bf16[256,2048]{1,0:T(8,128)(2,1)S(1)}, bf16[256,2048]{1,0:T(8,128)(2,1)}, u32[]{:S(2)}) copy-start(bf16[256,2048]{1,0:T(8,128)(2,1)} %take.1.mine_ref) | copy-start | bytes 3145732
  42.6 9.6 %collective-permute-start.9 = (bf16[128,512]{1,0:T(8,128)(2,1)}, bf16[128,512]{1,0:T(8,128)(2,1)S(1)}, u32[]{:S(2)}, u32[]{:S(2)}) collective-permute-start(bf16[128,512]{1,0:T(8,128)(2,1)} %get-tuple-element.37), channel_id=1, source_target_pairs={{0,192},{8,200},{16,208},{24,216},{32,224},{40,232},{48,240},{56,2... | collective-permute-start | bytes 393224 | tf_op jit(solution)/shard_map/ppermute | solution.py:367
  45.3 6.9 %collective-permute-start.8 = (bf16[128,512]{1,0:T(8,128)(2,1)}, bf16[128,512]{1,0:T(8,128)(2,1)S(1)}, u32[]{:S(2)}, u32[]{:S(2)}) collective-permute-start(bf16[128,512]{1,0:T(8,128)(2,1)} %get-tuple-element.37), channel_id=1, source_target_pairs={{0,128},{8,136},{16,144},{24,152},{32,160},{40,168},{48,176},{56,1... | collective-permute-start | bytes 393224 | tf_op jit(solution)/shard_map/ppermute | solution.py:367
  45.7 9.6 %collective-permute-start.7 = (bf16[128,512]{1,0:T(8,128)(2,1)}, bf16[128,512]{1,0:T(8,128)(2,1)S(1)}, u32[]{:S(2)}, u32[]{:S(2)}) collective-permute-start(bf16[128,512]{1,0:T(8,128)(2,1)} %get-tuple-element.37), channel_id=1, source_target_pairs={{0,64},{8,72},{16,80},{24,88},{32,96},{40,104},{48,112},{56,120},{... | collective-permute-start | bytes 393224 | tf_op jit(solution)/shard_map/ppermute | solution.py:367
  46.4 36.5 %copy-start.3 = (bf16[256,2048]{1,0:T(8,128)(2,1)S(1)}, bf16[256,2048]{1,0:T(8,128)(2,1)}, u32[]{:S(2)}) copy-start(bf16[256,2048]{1,0:T(8,128)(2,1)} %copy-done.2) | copy-start | bytes 3145732
  55.3 9.1 %collective-permute-start.16 = (bf16[256,1024]{1,0:T(8,128)(2,1)S(1)}, bf16[256,1024]{1,0:T(8,128)(2,1)S(1)}, u32[]{:S(2)}, u32[]{:S(2)}) collective-permute-start(bf16[256,1024]{1,0:T(8,128)(2,1)S(1)} %constant_dynamic-slice_fusion), channel_id=1, source_target_pairs={{0,1},{1,2},{2,3},{3,4},{4,5},{5,6},{6,7},{7,0},{8,15},{9,8},{10,9... | collective-permute-start | bytes 1572872 | tf_op jit(solution)/shard_map/ppermute | solution.py:381
  58.2 1.3 %collective-permute-start.12 = (bf16[128,512]{1,0:T(8,128)(2,1)S(1)}, bf16[128,512]{1,0:T(8,128)(2,1)S(1)}, u32[]{:S(2)}, u32[]{:S(2)}) collective-permute-start(bf16[128,512]{1,0:T(8,128)(2,1)S(1)} %collective-permute-done.9.refs_2_), channel_id=1, source_target_pairs={{0,8},{8,0},{16,24},{24,16},{32,40},{40,32},{48,56},{56,48},{64,72... | collective-permute-start | bytes 393224 | tf_op jit(solution)/shard_map/ppermute | solution.py:367
  58.2 1.5 %collective-permute-start.11 = (bf16[128,512]{1,0:T(8,128)(2,1)S(1)}, bf16[128,512]{1,0:T(8,128)(2,1)S(1)}, u32[]{:S(2)}, u32[]{:S(2)}) collective-permute-start(bf16[128,512]{1,0:T(8,128)(2,1)S(1)} %collective-permute-done.8.refs_1_), channel_id=1, source_target_pairs={{0,8},{8,0},{16,24},{24,16},{32,40},{40,32},{48,56},{56,48},{64,72... | collective-permute-start | bytes 393224 | tf_op jit(solution)/shard_map/ppermute | solution.py:367
  58.8 1.3 %collective-permute-start.10 = (bf16[128,512]{1,0:T(8,128)(2,1)S(1)}, bf16[128,512]{1,0:T(8,128)(2,1)S(1)}, u32[]{:S(2)}, u32[]{:S(2)}) collective-permute-start(bf16[128,512]{1,0:T(8,128)(2,1)S(1)} %collective-permute-done.7.refs_0_), channel_id=1, source_target_pairs={{0,8},{8,0},{16,24},{24,16},{32,40},{40,32},{48,56},{56,48},{64,72... | collective-permute-start | bytes 393224 | tf_op jit(solution)/shard_map/ppermute | solution.py:367
  78.2 4.8 %collective-permute-start.17 = (bf16[2,8,32,256]{3,2,1,0:T(8,128)(2,1)S(1)}, bf16[2,8,32,256]{3,2,1,0:T(8,128)(2,1)S(1)}, u32[]{:S(2)}, u32[]{:S(2)}) collective-permute-start(bf16[2,8,32,256]{3,2,1,0:T(8,128)(2,1)S(1)} %bitcast.9), channel_id=1, source_target_pairs={{0,8},{8,0},{16,24},{24,16},{32,40},{40,32},{48,56},{56,48},{64,72... | collective-permute-start | bytes 786440 | tf_op jit(solution)/shard_map/ppermute | solution.py:367
  85.1 1.9 %collective-permute-start.18 = (bf16[64,2048]{1,0:T(8,128)(2,1)S(1)}, bf16[64,2048]{1,0:T(8,128)(2,1)S(1)}, u32[]{:S(2)}, u32[]{:S(2)}) collective-permute-start(bf16[64,2048]{1,0:T(8,128)(2,1)S(1)} %get-tuple-element.46), channel_id=1, source_target_pairs={{0,8},{8,0},{16,24},{24,16},{32,40},{40,32},{48,56},{56,48},{64,72... | collective-permute-start | bytes 786440 | tf_op jit(solution)/shard_map/ppermute | solution.py:367
  87.1 4.8 %collective-permute-start.19 = (bf16[32,2048]{1,0:T(8,128)(2,1)S(1)}, bf16[32,2048]{1,0:T(8,128)(2,1)S(1)}, u32[]{:S(2)}, u32[]{:S(2)}) collective-permute-start(bf16[32,2048]{1,0:T(8,128)(2,1)S(1)} %get-tuple-element.48), channel_id=1, source_target_pairs={{0,16},{8,24},{16,0},{24,8},{32,48},{40,56},{48,32},{56,40},{64,80... | collective-permute-start | bytes 393224 | tf_op jit(solution)/shard_map/ppermute | solution.py:367

commit v8 on v7

--- a/solution.py
+++ b/solution.py
@@ -75,23 +75,40 @@
 
 
 def fold_kernel(
-    scale_hbm, rate_hbm, x_hbm, gain_ref, w_hbm, gate_ref, resets_ref,
-    carry_ref, key_ref, solved_ref, decay_ref, gamma_ref,
-    x_buf, xn_buf, w_buf, sems, scale_ref, rate_ref, scalar_sems,
+    scale_hbm, rate_hbm, x_hbm, gain_hbm, w_hbm, gate_hbm, resets_hbm,
+    carry_ref, key_hbm, solved_hbm, decay_hbm, gamma_hbm,
+    x_buf, xn_buf, w_buf, sems, scale_ref, rate_ref, gain_ref, gate_ref, resets_ref, small_sems,
+    key_ref, solved_ref, decay_ref, gamma_ref, out_sems,
 ):
-    scalars = [
-        pltpu.make_async_copy(a, b, scalar_sems.at[i])
-        for i, (a, b) in enumerate(((scale_hbm, scale_ref), (rate_hbm, rate_ref)))
+    small = [
+        pltpu.make_async_copy(a, b, small_sems.at[i])
+        for i, (a, b) in enumerate(
+            (
+                (gain_hbm, gain_ref),
+                (gate_hbm, gate_ref),
+                (resets_hbm, resets_ref),
+                (scale_hbm, scale_ref),
+                (rate_hbm, rate_ref),
+            )
+        )
     ]
-    for copy in scalars:
+    for copy in small:
         copy.start()
     found = copies(x_hbm, w_hbm, (1, 2), x_buf, w_buf, sems)
+    small[0].wait()
     normalise(found, x_buf, xn_buf, gain_ref[...])
     n = x_buf.shape[0]
+    for copy in small[1:] + found[2:]:
+        copy.wait()
+    kept = []
+
+    def keep(value, ref, target):
+        ref[...] = value
+        kept.append(pltpu.make_async_copy(ref, target, out_sems.at[len(kept)]))
+        kept[-1].start()
+
     gating = mm(xn_buf[...], gate_ref[...], NT)
-    key = unit_rows(project(found, xn_buf, w_buf, 0))
-    for copy in scalars:
-        copy.wait()
+    key = unit_rows(mm(xn_buf[...], w_buf[0]))
     beta = scale_ref[0] * jax.nn.sigmoid(gating[:, 0:1])
     logf = -rate_ref[0] * jax.nn.softplus(gating[:, 1:2])
     reset_row = resets_ref[...].astype(F32)
@@ -113,29 +130,36 @@
     cum_last, seg_last = cum[n - 1 : n], seg[n - 1 : n]
     tail = jnp.where(seg == seg_last, jnp.exp(cum_last - cum), 0.0)
     gamma_last = gamma[n - 1 : n]
-    decay_ref[...] = decay
-    gamma_ref[...] = gamma
-    key_ref[...] = key
+    keep(key, key_ref, key_hbm)
+    keep(decay, decay_ref, decay_hbm)
+    keep(gamma, gamma_ref, gamma_hbm)
 
     ks = split(key)
     low = jnp.where(t > s, beta * decay * mm3(ks, ks, NT), 0.0)
     apart = t ^ s
     inv = jnp.where(eye, 1.0, jnp.where(apart == 1, -low, 0.0))
-    for level in range(1, n.bit_length() - 1):
+    levels = range(1, n.bit_length() - 1)
+    depth = xn_buf.shape[1] // (len(levels) + 1)
+    value = mm(xn_buf[:, :depth], w_buf[1, :depth])
+    for level in levels:
         part = jnp.where((apart >> level) == 1, low, 0.0).astype(BF16)
         rough = inv.astype(BF16)
-        inv = inv - mm(rough, mm(part, rough).astype(BF16))
+        inner = mm(part, rough).astype(BF16)
+        chunk = slice(level * depth, (level + 1) * depth)
+        value = value + mm(xn_buf[:, chunk], w_buf[1, chunk])
+        inv = inv - mm(rough, inner)
     vs = split(inv)
     left = jnp.where(eye, 1.0, 0.0) - inv - mm3(split(low), vs)
     inv = inv + mm(vs[0], left.astype(BF16))
 
-    value = project(found, xn_buf, w_buf, 1)
     rhs = jnp.concatenate([(beta * gamma) * key, beta * value], axis=1)
     solved = mm3(split(inv), split(rhs))
-    solved_ref[...] = solved
+    keep(solved, solved_ref, solved_hbm)
     folded = mm3(split(key * tail), split(solved), TN)
     carry_ref[:, :n] = (jnp.where(eye, gamma_last, 0.0) - folded[:, :n]).astype(BF16)
     carry_ref[:, n:] = folded[:, n:].astype(BF16)
+    for copy in kept:
+        copy.wait()
 
 
 def look_kernel(
@@ -333,8 +357,8 @@
     carry, key, solved, decay, gamma = pl.pallas_call(
         fold_kernel,
         name="fold",
-        in_specs=[hbm(), hbm(), hbm(), vmem(), hbm(), vmem(), vmem()],
-        out_specs=[vmem()] * 5,
+        in_specs=[hbm()] * 7,
+        out_specs=[vmem()] + [hbm()] * 4,
         out_shape=[
             jax.ShapeDtypeStruct((n, 2 * n), BF16),
             square,
@@ -343,7 +367,19 @@
             jax.ShapeDtypeStruct((rows, 1), F32),
         ],
         scratch_shapes=buffers(2)
-        + [pltpu.SMEM((1,), F32), pltpu.SMEM((1,), F32), pltpu.SemaphoreType.DMA((2,))],
+        + [
+            pltpu.SMEM((1,), F32),
+            pltpu.SMEM((1,), F32),
+            pltpu.VMEM((1, width), F32),
+            pltpu.VMEM((2, width), BF16),
+            pltpu.VMEM((1, rows), jnp.int32),
+            pltpu.SemaphoreType.DMA((5,)),
+            pltpu.VMEM((rows, n), F32),
+            pltpu.VMEM((rows, 2 * n), F32),
+            pltpu.VMEM((rows, n), F32),
+            pltpu.VMEM((rows, 1), F32),
+            pltpu.SemaphoreType.DMA((4,)),
+        ],
         compiler_params=LARGE,
     )(beta_scale, decay_rate, frames, gain, weight, gate, resets.reshape(1, rows))
 
@@ -409,7 +445,6 @@
     )(carry, other)
     near = [moved(half, along_x(s)) for s in (1, 2, 3)]
     near, looked = lax.optimization_barrier((near, look()))
-    three = around(later(two, near))
     swapped = [moved(value, flip(1)) for value in near]
     half, prefix = pl.pallas_call(
         row_kernel,
@@ -420,12 +455,8 @@
         scratch_shapes=[pltpu.VMEM((4, n, 2 * n), BF16), pltpu.VMEM((n, 2 * n), BF16)],
         compiler_params=SMALL,
     )(pair, *near, *swapped)
+    three = around(later(two, half))
     near = [moved(half, along_y(s)) for s in (1, 2, 3)]
-    four = around(
-        later(
-            lax.dynamic_slice_in_dim(three, lax.axis_index("core") * (wide // 2), wide // 2, 1), near
-        )
-    )
     swapped = [moved(value, flip(1)) for value in near]
     flat = pl.pallas_call(
         read_kernel,
@@ -437,7 +468,11 @@
         compiler_params=SMALL,
     )(*near, *swapped, prefix, other, looked, out_gain.reshape(1, n))
     part = rows // 8
-    flat, four = lax.optimization_barrier((flat, four))
+    part_three = lax.dynamic_slice_in_dim(
+        three, lax.axis_index("core") * (wide // 2), wide // 2, 1
+    )
+    flat, part_three = lax.optimization_barrier((flat, part_three))
+    four = around(part_three)
     reads = lax.all_to_all(
         flat.reshape(16, part, n), ("xl", "head"), 0, 0, tiled=True
     ).reshape(2, 8, part, n)

time: 92.9 us -> 92.1 us (level)
  blocking collectives: 13.8 us -> 0 us
  starting transfers between devices: 25.8 us -> 34.3 us
  local copies, waits for them, and re-layouts: 1.01 us -> 5.18 us
  waiting for transfers between devices: 25.3 us -> 27 us
  Pallas kernels: 25.3 us -> 23.8 us
    all_to_all x1 -> x0, blocking collectives: 13.8 us -> none  [per_device(): lax.all_to_all(flat.reshape(16, part, n), ('xl', 'head'), 0, 0, tiled=True)]
    all_to_all x0 -> x1, waiting for transfers between devices: none -> 6.57 us  [per_device(): lax.all_to_all(flat.reshape(16, part, n), ('xl', 'head'), 0, 0, tiled=True)]
    ppermute x4, waiting for transfers between devices: 9.31 us -> 3.11 us  [around(): return lax.ppermute(value, ('core', 'head'), up + down)]
    all_to_all x0 -> x1, starting transfers between devices: none -> 6 us  [per_device(): lax.all_to_all(flat.reshape(16, part, n), ('xl', 'head'), 0, 0, tiled=True)]
    unnamed x12 -> x14, local copies, waits for them, and re-layouts: 0.97 us -> 4.34 us
    ppermute x16, starting transfers between devices: 14.3 us -> 16.5 us  [moved(): return lax.ppermute(value, SEQ, [(i, place_of(i)) for i in range(count)])]
    pallas_call x1, Pallas kernels: 11.7 us -> 9.65 us  [per_device(): pl.pallas_call(fold_kernel, name='fold', in_specs=[hbm()] * 7, out_specs=...]
    ppermute x16, waiting for transfers between devices: 16 us -> 17.3 us  [moved(): return lax.ppermute(value, SEQ, [(i, place_of(i)) for i in range(count)])]
  transfers between devices with their start and end apart: 20 -> 21, of which waited for: 14 -> 12; matrix products, arithmetic and copies ran while one was open for 0% -> 0% of each run, Pallas kernels for 22% -> 20%
where the time goes in v8:
time: 92.1 us; the launch traced here: 91.7 us
  starting transfers between devices  34.3 us (37%)
  waiting for transfers between devices  27 us (29%)
  Pallas kernels  23.8 us (26%)
  local copies, waits for them, and re-layouts  5.18 us (6%)
  between operations  1.42 us (2%)
    ppermute x16, waiting for transfers between devices, moved(): return lax.ppermute(value, SEQ, [(i, place_of(i)) for i in range(count)])  17.3 us
    ppermute x16, starting transfers between devices, moved(): return lax.ppermute(value, SEQ, [(i, place_of(i)) for i in range(count)])  16.5 us
    ppermute x4, starting transfers between devices, around(): return lax.ppermute(value, ('core', 'head'), up + down)  11.8 us
    pallas_call x1, Pallas kernels, per_device(): pl.pallas_call(fold_kernel, name='fold', in_specs=[hbm()] * 7, out_specs=...  9.65 us
    all_to_all x1, waiting for transfers between devices, per_device(): lax.all_to_all(flat.reshape(16, part, n), ('xl', 'head'), 0, 0, tiled=True)  6.57 us
    pallas_call x1, Pallas kernels, look(): pl.pallas_call(look_kernel, name='look', in_specs=[hbm(), vmem(), hbm()]...  6.19 us
    all_to_all x1, starting transfers between devices, per_device(): lax.all_to_all(flat.reshape(16, part, n), ('xl', 'head'), 0, 0, tiled=True)  6 us
    unnamed x14, local copies, waits for them, and re-layouts  4.34 us
  transfers between devices with their start and end apart: 21, of which 12 were waited for; matrix products, arithmetic and copies ran while one was open for 0% of the time, Pallas kernels for 20%

profile of v8, /device:TPU:1, one launch (start us, length us, event | category | flops | bytes accessed | tf_op | source)
XLA Modules:
  0.0 91.7 jit_solution(12309006189819539682)
XLA Ops:
  0.0 2.2 %take.1.mine_ref = bf16[256,2048]{1,0:T(8,128)(2,1)} custom-call(bf16[256,4096]{1,0:T(8,128)(2,1)} %whole_ref.1), custom_call_target="tpu_custom_call" | custom-call | tf_op jit(solution)/shard_map/take/pallas_call | solution.py:423
  2.2 6.5 %collective-permute-start.13 = (bf16[256,2048]{1,0:T(8,128)(2,1)}, bf16[256,2048]{1,0:T(8,128)(2,1)S(1)}, u32[]{:S(2)}, u32[]{:S(2)}) collective-permute-start(bf16[256,2048]{1,0:T(8,128)(2,1)} %take.1.mine_ref), channel_id=1, source_target_pairs={{0,1},{1,2},{2,3},{3,4},{4,5},{5,6},{6,7},{7,0},{8,15},{9,8},{10,9... | collective-permute-start | bytes 3145736 | tf_op jit(solution)/shard_map/ppermute | solution.py:417
  10.0 9.7 %fold.1 = (bf16[256,512]{1,0:T(8,128)(2,1)}, f32[256,256]{1,0:T(8,128)}, f32[256,512]{1,0:T(8,128)}, f32[256,256]{1,0:T(8,128)}, f32[256,1]{1,0:T(8,128)}) custom-call(f32[1]{0:T(128)S(6)} %copy.10.scale_hbm, f32[1]{0:T(128)S(6)} %copy.11.rate_hbm, bf16[256,4096]{1,0:T(8,128)(2,1)} %x_hbm.3, f32[1,4096]{1,0:T(1,128)} %bitcast.15, ...), custom_call_target="tpu_custom_call" | custom-call | tf_op jit(solution)/shard_map/fold/pallas_call | solution.py:357
  19.7 0.1 collective-permute-start
  19.8 1.7 %collective-permute-done.other_ref.refs_7_ = bf16[256,512]{1,0:T(8,128)(2,1)S(1)} collective-permute-done((bf16[256,512]{1,0:T(8,128)(2,1)}, bf16[256,512]{1,0:T(8,128)(2,1)S(1)}, u32[]{:S(2)}, u32[]{:S(2)}) %collective-permute-start) | collective-permute-done | bytes 262176 | tf_op jit(solution)/shard_map/ppermute | solution.py:403
  21.5 0.0 collective-permute-done.13.one_ref
  21.5 2.3 %collective-permute-start.14 = (bf16[256,2048]{1,0:T(8,128)(2,1)S(1)}, bf16[256,2048]{1,0:T(8,128)(2,1)}, u32[]{:S(2)}, u32[]{:S(2)}) collective-permute-start(bf16[256,2048]{1,0:T(8,128)(2,1)S(1)} %collective-permute-done.13.one_ref), channel_id=1, source_target_pairs={{0,1},{1,2},{2,3},{3,4},{4,5},{5,6},{6,7},{7,0},{8,15},{9,8},{10,9... | collective-permute-start | bytes 3145736 | tf_op jit(solution)/shard_map/ppermute | solution.py:417
  23.8 0.0 copy-start.3
  23.8 0.9 %copy-done.3 = bf16[256,512]{1,0:T(8,128)(2,1)S(1)} copy-done((bf16[256,512]{1,0:T(8,128)(2,1)S(1)}, bf16[256,512]{1,0:T(8,128)(2,1)}, u32[]{:S(2)}) %copy-start.3) | copy-done | bytes 262168
  24.7 0.3 pair.1
  25.0 2.6 %collective-permute-start.3 = (bf16[128,512]{1,0:T(8,128)(2,1)S(1)}, bf16[128,512]{1,0:T(8,128)(2,1)S(1)}, u32[]{:S(2)}, u32[]{:S(2)}) collective-permute-start(bf16[128,512]{1,0:T(8,128)(2,1)S(1)} %get-tuple-element.28), channel_id=1, source_target_pairs={{0,48},{8,56},{16,0},{24,8},{32,16},{40,24},{48,32},{56,40},{64,11... | collective-permute-start | bytes 393224 | tf_op jit(solution)/shard_map/ppermute | solution.py:403
  27.5 0.5 collective-permute-start.2
  28.1 0.6 collective-permute-start.1
  28.7 0.0 copy-start.6
  28.7 6.2 %look.1.refs_8_ = f32[256,512]{1,0:T(8,128)} custom-call(bf16[256,4096]{1,0:T(8,128)(2,1)} %x_hbm.3, f32[1,4096]{1,0:T(1,128)} %bitcast.16, bf16[3,4096,256]{2,1,0:T(8,128)(2,1)} %bitcast.14, f32[256,256]{1,0:T(8,128)} %get-tuple-element.29.key_ref, f32[256,512]{1,0:T(8,128)} %get-tuple-element.30.solved_ref, f32[256,256]{1,0:T(8,128)} %get-tuple-element.31.decay_ref, ...), custom_call_target="tpu_custom_call" | custom-call | flops 1073741824 | bytes 16777216 | tf_op jit(solution)/shard_map/look/pallas_call | solution.py:387
  34.9 0.0 collective-permute-done.3.refs_2_
  34.9 0.0 collective-permute-done.2.refs_1_
  34.9 2.2 %collective-permute-done.1.refs_0_ = bf16[128,512]{1,0:T(8,128)(2,1)S(1)} collective-permute-done((bf16[128,512]{1,0:T(8,128)(2,1)S(1)}, bf16[128,512]{1,0:T(8,128)(2,1)S(1)}, u32[]{:S(2)}, u32[]{:S(2)}) %collective-permute-start.1) | collective-permute-done | bytes 131104 | tf_op jit(solution)/shard_map/ppermute | solution.py:403
  37.1 0.3 collective-permute-start.4
  37.4 0.2 collective-permute-start.5
  37.6 0.3 collective-permute-start.6
  37.9 0.6 collective-permute-done.4.refs_3_
  38.5 0.3 collective-permute-done.5.refs_4_
  38.7 0.2 collective-permute-done.6.refs_5_
  39.0 0.6 row.1
  39.5 0.0 copy-start.4
  39.6 0.7 copy-done.4
  40.2 0.0 copy-start
  40.2 0.0 collective-permute-done.14.two_ref
  40.3 0.4 collective-permute-start.15
  40.7 2.7 %collective-permute-start.9 = (bf16[128,512]{1,0:T(8,128)(2,1)S(1)}, bf16[128,512]{1,0:T(8,128)(2,1)S(1)}, u32[]{:S(2)}, u32[]{:S(2)}) collective-permute-start(bf16[128,512]{1,0:T(8,128)(2,1)S(1)} %get-tuple-element.36), channel_id=1, source_target_pairs={{0,192},{8,200},{16,208},{24,216},{32,224},{40,232},{48,240},{56,2... | collective-permute-start | bytes 393224 | tf_op jit(solution)/shard_map/ppermute | solution.py:403
  43.4 0.3 collective-permute-start.8
  43.8 0.7 collective-permute-start.7
  44.4 4.6 %collective-permute-done.9.refs_2_ = bf16[128,512]{1,0:T(8,128)(2,1)S(1)} collective-permute-done((bf16[128,512]{1,0:T(8,128)(2,1)S(1)}, bf16[128,512]{1,0:T(8,128)(2,1)S(1)}, u32[]{:S(2)}, u32[]{:S(2)}) %collective-permute-start.9) | collective-permute-done | bytes 131104 | tf_op jit(solution)/shard_map/ppermute | solution.py:403
  49.1 0.9 collective-permute-start.12
  49.9 0.0 collective-permute-done.8.refs_1_
  49.9 1.7 %collective-permute-start.11 = (bf16[128,512]{1,0:T(8,128)(2,1)}, bf16[128,512]{1,0:T(8,128)(2,1)}, u32[]{:S(2)}, u32[]{:S(2)}) collective-permute-start(bf16[128,512]{1,0:T(8,128)(2,1)} %collective-permute-done.8.refs_1_), channel_id=1, source_target_pairs={{0,8},{8,0},{16,24},{24,16},{32,40},{40,32},{48,56},{56,48},{64,72... | collective-permute-start | bytes 393224 | tf_op jit(solution)/shard_map/ppermute | solution.py:403
  51.6 1.6 %collective-permute-done.7.refs_0_ = bf16[128,512]{1,0:T(8,128)(2,1)} collective-permute-done((bf16[128,512]{1,0:T(8,128)(2,1)S(1)}, bf16[128,512]{1,0:T(8,128)(2,1)}, u32[]{:S(2)}, u32[]{:S(2)}) %collective-permute-start.7) | collective-permute-done | bytes 131104 | tf_op jit(solution)/shard_map/ppermute | solution.py:403
  53.2 0.5 collective-permute-start.10
  53.7 0.0 collective-permute-done.12.refs_5_
  53.7 0.0 collective-permute-done.11.refs_4_
  53.7 1.3 %collective-permute-done.10.refs_3_ = bf16[128,512]{1,0:T(8,128)(2,1)} collective-permute-done((bf16[128,512]{1,0:T(8,128)(2,1)}, bf16[128,512]{1,0:T(8,128)(2,1)}, u32[]{:S(2)}, u32[]{:S(2)}) %collective-permute-start.10) | collective-permute-done | bytes 131104 | tf_op jit(solution)/shard_map/ppermute | solution.py:403
  55.1 0.0 copy-done.6
  55.1 0.0 copy-start.1
  55.1 1.0 %copy-done.1 = f32[256,512]{1,0:T(8,128)S(1)} copy-done((f32[256,512]{1,0:T(8,128)S(1)}, f32[256,512]{1,0:T(8,128)}, u32[]{:S(2)}) %copy-start.1) | copy-done | bytes 524312
  56.1 0.9 %copy-done.5 = bf16[256,512]{1,0:T(8,128)(2,1)S(1)} copy-done((bf16[256,512]{1,0:T(8,128)(2,1)S(1)}, bf16[256,512]{1,0:T(8,128)(2,1)}, u32[]{:S(2)}) %copy-start.5) | copy-done | bytes 262168
  57.1 1.9 %read.1 = bf16[2,256,256]{2,1,0:T(8,128)(2,1)S(1)} custom-call(bf16[128,512]{1,0:T(8,128)(2,1)} %collective-permute-done.7.refs_0_, bf16[128,512]{1,0:T(8,128)(2,1)} %collective-permute-done.8.refs_1_, bf16[128,512]{1,0:T(8,128)(2,1)S(1)} %collective-permute-done.9.refs_2_, bf16[128,512]{1,0:T(8,128)(2,1)} %collective-permute-done.10.refs_3_, ...), custom_call_target="tpu_custom_call" | custom-call | tf_op jit(solution)/shard_map/read/pallas_call | solution.py:461
  58.9 0.0 copy-start.2
  58.9 0.7 copy-done.2
  59.6 0.0 collective-permute-done.15.three_ref
  59.6 0.8 constant_dynamic-slice_fusion
  60.5 6.0 %all-to-all-start = ((bf16[16,32,256]{2,1,0:T(8,128)(2,1)}), bf16[16,32,256]{2,1,0:T(8,128)(2,1)S(1)}, u32[]{:S(2)}, u32[]{:S(2)}) async-start(bf16[16,32,256]{2,1,0:T(8,128)(2,1)} %bitcast.11), calls=%async_computation | async-start | bytes 524288 | tf_op jit(solution)/shard_map/all_to_all | solution.py:476
  66.5 2.6 %collective-permute-start.17 = (bf16[256,1024]{1,0:T(8,128)(2,1)}, bf16[256,1024]{1,0:T(8,128)(2,1)}, u32[]{:S(2)}, u32[]{:S(2)}) collective-permute-start(bf16[256,1024]{1,0:T(8,128)(2,1)} %constant_dynamic-slice_fusion), channel_id=1, source_target_pairs={{0,1},{1,2},{2,3},{3,4},{4,5},{5,6},{6,7},{7,0},{8,15},{9,8},{10,9... | collective-permute-start | bytes 1572872 | tf_op jit(solution)/shard_map/ppermute | solution.py:417
  69.1 6.6 %all-to-all-done = bf16[16,32,256]{2,1,0:T(8,128)(2,1)S(1)} async-done(((bf16[16,32,256]{2,1,0:T(8,128)(2,1)}), bf16[16,32,256]{2,1,0:T(8,128)(2,1)S(1)}, u32[]{:S(2)}, u32[]{:S(2)}) %all-to-all-start) | async-done | bytes 262176 | tf_op jit(solution)/shard_map/all_to_all | solution.py:476
  75.6 1.9 %collective-permute-start.16 = (bf16[2,8,32,256]{3,2,1,0:T(8,128)(2,1)S(1)}, bf16[2,8,32,256]{3,2,1,0:T(8,128)(2,1)S(1)}, u32[]{:S(2)}, u32[]{:S(2)}) collective-permute-start(bf16[2,8,32,256]{3,2,1,0:T(8,128)(2,1)S(1)} %bitcast.9), channel_id=1, source_target_pairs={{0,8},{8,0},{16,24},{24,16},{32,40},{40,32},{48,56},{56,48},{64,72... | collective-permute-start | bytes 786440 | tf_op jit(solution)/shard_map/ppermute | solution.py:403
  77.5 3.1 %collective-permute-done.17.four_ref = bf16[256,1024]{1,0:T(8,128)(2,1)} collective-permute-done((bf16[256,1024]{1,0:T(8,128)(2,1)}, bf16[256,1024]{1,0:T(8,128)(2,1)}, u32[]{:S(2)}, u32[]{:S(2)}) %collective-permute-start.17) | collective-permute-done | bytes 524320 | tf_op jit(solution)/shard_map/ppermute | solution.py:417
  80.6 0.0 collective-permute-done.16.other_ref
  80.6 0.0 copy-done
  80.6 2.3 %mix.1 = (f32[64,2048]{1,0:T(8,128)S(1)}, bf16[64,2048]{1,0:T(8,128)(2,1)S(1)}) custom-call(bf16[2,8,32,256]{3,2,1,0:T(8,128)(2,1)S(1)} %bitcast.10, bf16[2,8,32,256]{3,2,1,0:T(8,128)(2,1)S(1)} %collective-permute-done.16.other_ref, bf16[256,2048]{1,0:T(8,128)(2,1)S(1)} %copy-done, bf16[256,2048]{1,0:T(8,128)(2,1)S(1)} %collective-permute-done.13.one_ref, ...), custom_call_target="tpu_custom_call" | custom-call | tf_op jit(solution)/shard_map/mix/pallas_call | solution.py:480
  83.0 2.0 %collective-permute-start.18 = (bf16[64,2048]{1,0:T(8,128)(2,1)S(1)}, bf16[64,2048]{1,0:T(8,128)(2,1)S(1)}, u32[]{:S(2)}, u32[]{:S(2)}) collective-permute-start(bf16[64,2048]{1,0:T(8,128)(2,1)S(1)} %get-tuple-element.44), channel_id=1, source_target_pairs={{0,8},{8,0},{16,24},{24,16},{32,40},{40,32},{48,56},{56,48},{64,72... | collective-permute-start | bytes 786440 | tf_op jit(solution)/shard_map/ppermute | solution.py:403
  84.9 1.2 %collective-permute-done.18.come_ref = bf16[64,2048]{1,0:T(8,128)(2,1)S(1)} collective-permute-done((bf16[64,2048]{1,0:T(8,128)(2,1)S(1)}, bf16[64,2048]{1,0:T(8,128)(2,1)S(1)}, u32[]{:S(2)}, u32[]{:S(2)}) %collective-permute-start.18) | collective-permute-done | bytes 262176 | tf_op jit(solution)/shard_map/ppermute | solution.py:403
  86.2 1.3 %collective-permute-start.19 = (bf16[32,2048]{1,0:T(8,128)(2,1)S(1)}, bf16[32,2048]{1,0:T(8,128)(2,1)S(1)}, u32[]{:S(2)}, u32[]{:S(2)}) collective-permute-start(bf16[32,2048]{1,0:T(8,128)(2,1)S(1)} %get-tuple-element.46), channel_id=1, source_target_pairs={{0,16},{8,24},{16,0},{24,8},{32,48},{40,56},{48,32},{56,40},{64,80... | collective-permute-start | bytes 393224 | tf_op jit(solution)/shard_map/ppermute | solution.py:403
  87.4 3.5 %collective-permute-done.19.come_ref = bf16[32,2048]{1,0:T(8,128)(2,1)S(1)} collective-permute-done((bf16[32,2048]{1,0:T(8,128)(2,1)S(1)}, bf16[32,2048]{1,0:T(8,128)(2,1)S(1)}, u32[]{:S(2)}, u32[]{:S(2)}) %collective-permute-start.19) | collective-permute-done | bytes 131104 | tf_op jit(solution)/shard_map/ppermute | solution.py:403
  91.0 0.7 lay.1
  (2 shorter events, 0.0 us)
Async XLA Ops:
  2.2 19.3 %collective-permute-start.13 = (bf16[256,2048]{1,0:T(8,128)(2,1)}, bf16[256,2048]{1,0:T(8,128)(2,1)S(1)}, u32[]{:S(2)}, u32[]{:S(2)}) collective-permute-start(bf16[256,2048]{1,0:T(8,128)(2,1)} %take.1.mine_ref), channel_id=1, source_target_pairs={{0,1},{1,2},{2,3},{3,4},{4,5},{5,6},{6,7},{7,0},{8,15},{9,8},{10,9... | collective-permute-start | bytes 3145736 | tf_op jit(solution)/shard_map/ppermute | solution.py:417
  19.7 1.8 %collective-permute-start = (bf16[256,512]{1,0:T(8,128)(2,1)}, bf16[256,512]{1,0:T(8,128)(2,1)S(1)}, u32[]{:S(2)}, u32[]{:S(2)}) collective-permute-start(bf16[256,512]{1,0:T(8,128)(2,1)} %get-tuple-element.26.own_ref), channel_id=1, source_target_pairs={{0,8},{8,0},{16,24},{24,16},{32,40},{40,32},{48,56},{56,48},{64,72... | collective-permute-start | bytes 786440 | tf_op jit(solution)/shard_map/ppermute | solution.py:403
  21.5 18.8 %collective-permute-start.14 = (bf16[256,2048]{1,0:T(8,128)(2,1)S(1)}, bf16[256,2048]{1,0:T(8,128)(2,1)}, u32[]{:S(2)}, u32[]{:S(2)}) collective-permute-start(bf16[256,2048]{1,0:T(8,128)(2,1)S(1)} %collective-permute-done.13.one_ref), channel_id=1, source_target_pairs={{0,1},{1,2},{2,3},{3,4},{4,5},{5,6},{6,7},{7,0},{8,15},{9,8},{10,9... | collective-permute-start | bytes 3145736 | tf_op jit(solution)/shard_map/ppermute | solution.py:417
  23.8 0.9 %copy-start.3 = (bf16[256,512]{1,0:T(8,128)(2,1)S(1)}, bf16[256,512]{1,0:T(8,128)(2,1)}, u32[]{:S(2)}) copy-start(bf16[256,512]{1,0:T(8,128)(2,1)} %get-tuple-element.26.own_ref) | copy-start | bytes 786436
  25.0 9.9 %collective-permute-start.3 = (bf16[128,512]{1,0:T(8,128)(2,1)S(1)}, bf16[128,512]{1,0:T(8,128)(2,1)S(1)}, u32[]{:S(2)}, u32[]{:S(2)}) collective-permute-start(bf16[128,512]{1,0:T(8,128)(2,1)S(1)} %get-tuple-element.28), channel_id=1, source_target_pairs={{0,48},{8,56},{16,0},{24,8},{32,16},{40,24},{48,32},{56,40},{64,11... | collective-permute-start | bytes 393224 | tf_op jit(solution)/shard_map/ppermute | solution.py:403
  27.5 7.3 %collective-permute-start.2 = (bf16[128,512]{1,0:T(8,128)(2,1)S(1)}, bf16[128,512]{1,0:T(8,128)(2,1)S(1)}, u32[]{:S(2)}, u32[]{:S(2)}) collective-permute-start(bf16[128,512]{1,0:T(8,128)(2,1)S(1)} %get-tuple-element.28), channel_id=1, source_target_pairs={{0,32},{8,40},{16,48},{24,56},{32,0},{40,8},{48,16},{56,24},{64,96... | collective-permute-start | bytes 393224 | tf_op jit(solution)/shard_map/ppermute | solution.py:403
  28.1 9.0 %collective-permute-start.1 = (bf16[128,512]{1,0:T(8,128)(2,1)S(1)}, bf16[128,512]{1,0:T(8,128)(2,1)S(1)}, u32[]{:S(2)}, u32[]{:S(2)}) collective-permute-start(bf16[128,512]{1,0:T(8,128)(2,1)S(1)} %get-tuple-element.28), channel_id=1, source_target_pairs={{0,16},{8,24},{16,32},{24,40},{32,48},{40,56},{48,0},{56,8},{64,80... | collective-permute-start | bytes 393224 | tf_op jit(solution)/shard_map/ppermute | solution.py:403
  28.7 26.4 %copy-start.6 = (f32[256]{0:T(256)S(1)}, f32[256]{0:T(256)}, u32[]{:S(2)}) copy-start(f32[256]{0:T(256)} %param.16) | copy-start | bytes 3076
  37.1 1.3 %collective-permute-start.4 = (bf16[128,512]{1,0:T(8,128)(2,1)S(1)}, bf16[128,512]{1,0:T(8,128)(2,1)S(1)}, u32[]{:S(2)}, u32[]{:S(2)}) collective-permute-start(bf16[128,512]{1,0:T(8,128)(2,1)S(1)} %collective-permute-done.1.refs_0_), channel_id=1, source_target_pairs={{0,8},{8,0},{16,24},{24,16},{32,40},{40,32},{48,56},{56,48},{64,72... | collective-permute-start | bytes 393224 | tf_op jit(solution)/shard_map/ppermute | solution.py:403
  37.4 1.3 %collective-permute-start.5 = (bf16[128,512]{1,0:T(8,128)(2,1)S(1)}, bf16[128,512]{1,0:T(8,128)(2,1)S(1)}, u32[]{:S(2)}, u32[]{:S(2)}) collective-permute-start(bf16[128,512]{1,0:T(8,128)(2,1)S(1)} %collective-permute-done.2.refs_1_), channel_id=1, source_target_pairs={{0,8},{8,0},{16,24},{24,16},{32,40},{40,32},{48,56},{56,48},{64,72... | collective-permute-start | bytes 393224 | tf_op jit(solution)/shard_map/ppermute | solution.py:403
  37.6 1.3 %collective-permute-start.6 = (bf16[128,512]{1,0:T(8,128)(2,1)S(1)}, bf16[128,512]{1,0:T(8,128)(2,1)S(1)}, u32[]{:S(2)}, u32[]{:S(2)}) collective-permute-start(bf16[128,512]{1,0:T(8,128)(2,1)S(1)} %collective-permute-done.3.refs_2_), channel_id=1, source_target_pairs={{0,8},{8,0},{16,24},{24,16},{32,40},{40,32},{48,56},{56,48},{64,72... | collective-permute-start | bytes 393224 | tf_op jit(solution)/shard_map/ppermute | solution.py:403
  39.5 0.7 copy-start.4
  40.2 40.4 %copy-start = (bf16[256,2048]{1,0:T(8,128)(2,1)S(1)}, bf16[256,2048]{1,0:T(8,128)(2,1)}, u32[]{:S(2)}) copy-start(bf16[256,2048]{1,0:T(8,128)(2,1)} %take.1.mine_ref) | copy-start | bytes 3145732
  40.3 19.4 %collective-permute-start.15 = (bf16[256,2048]{1,0:T(8,128)(2,1)}, bf16[256,2048]{1,0:T(8,128)(2,1)S(1)}, u32[]{:S(2)}, u32[]{:S(2)}) collective-permute-start(bf16[256,2048]{1,0:T(8,128)(2,1)} %collective-permute-done.14.two_ref), channel_id=1, source_target_pairs={{0,1},{1,2},{2,3},{3,4},{4,5},{5,6},{6,7},{7,0},{8,15},{9,8},{10,9... | collective-permute-start | bytes 3145736 | tf_op jit(solution)/shard_map/ppermute | solution.py:417
  40.7 8.4 %collective-permute-start.9 = (bf16[128,512]{1,0:T(8,128)(2,1)S(1)}, bf16[128,512]{1,0:T(8,128)(2,1)S(1)}, u32[]{:S(2)}, u32[]{:S(2)}) collective-permute-start(bf16[128,512]{1,0:T(8,128)(2,1)S(1)} %get-tuple-element.36), channel_id=1, source_target_pairs={{0,192},{8,200},{16,208},{24,216},{32,224},{40,232},{48,240},{56,2... | collective-permute-start | bytes 393224 | tf_op jit(solution)/shard_map/ppermute | solution.py:403
  43.4 6.5 %collective-permute-start.8 = (bf16[128,512]{1,0:T(8,128)(2,1)S(1)}, bf16[128,512]{1,0:T(8,128)(2,1)}, u32[]{:S(2)}, u32[]{:S(2)}) collective-permute-start(bf16[128,512]{1,0:T(8,128)(2,1)S(1)} %get-tuple-element.36), channel_id=1, source_target_pairs={{0,128},{8,136},{16,144},{24,152},{32,160},{40,168},{48,176},{56,1... | collective-permute-start | bytes 393224 | tf_op jit(solution)/shard_map/ppermute | solution.py:403
  43.8 9.5 %collective-permute-start.7 = (bf16[128,512]{1,0:T(8,128)(2,1)S(1)}, bf16[128,512]{1,0:T(8,128)(2,1)}, u32[]{:S(2)}, u32[]{:S(2)}) collective-permute-start(bf16[128,512]{1,0:T(8,128)(2,1)S(1)} %get-tuple-element.36), channel_id=1, source_target_pairs={{0,64},{8,72},{16,80},{24,88},{32,96},{40,104},{48,112},{56,120},{... | collective-permute-start | bytes 393224 | tf_op jit(solution)/shard_map/ppermute | solution.py:403
  49.1 4.7 %collective-permute-start.12 = (bf16[128,512]{1,0:T(8,128)(2,1)S(1)}, bf16[128,512]{1,0:T(8,128)(2,1)}, u32[]{:S(2)}, u32[]{:S(2)}) collective-permute-start(bf16[128,512]{1,0:T(8,128)(2,1)S(1)} %collective-permute-done.9.refs_2_), channel_id=1, source_target_pairs={{0,8},{8,0},{16,24},{24,16},{32,40},{40,32},{48,56},{56,48},{64,72... | collective-permute-start | bytes 393224 | tf_op jit(solution)/shard_map/ppermute | solution.py:403
  49.9 3.8 %collective-permute-start.11 = (bf16[128,512]{1,0:T(8,128)(2,1)}, bf16[128,512]{1,0:T(8,128)(2,1)}, u32[]{:S(2)}, u32[]{:S(2)}) collective-permute-start(bf16[128,512]{1,0:T(8,128)(2,1)} %collective-permute-done.8.refs_1_), channel_id=1, source_target_pairs={{0,8},{8,0},{16,24},{24,16},{32,40},{40,32},{48,56},{56,48},{64,72... | collective-permute-start | bytes 393224 | tf_op jit(solution)/shard_map/ppermute | solution.py:403
  53.2 1.8 %collective-permute-start.10 = (bf16[128,512]{1,0:T(8,128)(2,1)}, bf16[128,512]{1,0:T(8,128)(2,1)}, u32[]{:S(2)}, u32[]{:S(2)}) collective-permute-start(bf16[128,512]{1,0:T(8,128)(2,1)} %collective-permute-done.7.refs_0_), channel_id=1, source_target_pairs={{0,8},{8,0},{16,24},{24,16},{32,40},{40,32},{48,56},{56,48},{64,72... | collective-permute-start | bytes 393224 | tf_op jit(solution)/shard_map/ppermute | solution.py:403
  55.1 1.0 %copy-start.1 = (f32[256,512]{1,0:T(8,128)S(1)}, f32[256,512]{1,0:T(8,128)}, u32[]{:S(2)}) copy-start(f32[256,512]{1,0:T(8,128)} %look.1.refs_8_) | copy-start | bytes 1572868
  56.1 0.9 %copy-start.5 = (bf16[256,512]{1,0:T(8,128)(2,1)S(1)}, bf16[256,512]{1,0:T(8,128)(2,1)}, u32[]{:S(2)}) copy-start(bf16[256,512]{1,0:T(8,128)(2,1)} %copy-done.4) | copy-start | bytes 786436
  58.9 0.7 copy-start.2
  60.5 15.2 %all-to-all-start = ((bf16[16,32,256]{2,1,0:T(8,128)(2,1)}), bf16[16,32,256]{2,1,0:T(8,128)(2,1)S(1)}, u32[]{:S(2)}, u32[]{:S(2)}) async-start(bf16[16,32,256]{2,1,0:T(8,128)(2,1)} %bitcast.11), calls=%async_computation | async-start | bytes 524288 | tf_op jit(solution)/shard_map/all_to_all | solution.py:476
  66.5 14.2 %collective-permute-start.17 = (bf16[256,1024]{1,0:T(8,128)(2,1)}, bf16[256,1024]{1,0:T(8,128)(2,1)}, u32[]{:S(2)}, u32[]{:S(2)}) collective-permute-start(bf16[256,1024]{1,0:T(8,128)(2,1)} %constant_dynamic-slice_fusion), channel_id=1, source_target_pairs={{0,1},{1,2},{2,3},{3,4},{4,5},{5,6},{6,7},{7,0},{8,15},{9,8},{10,9... | collective-permute-start | bytes 1572872 | tf_op jit(solution)/shard_map/ppermute | solution.py:417
  75.6 5.0 %collective-permute-start.16 = (bf16[2,8,32,256]{3,2,1,0:T(8,128)(2,1)S(1)}, bf16[2,8,32,256]{3,2,1,0:T(8,128)(2,1)S(1)}, u32[]{:S(2)}, u32[]{:S(2)}) collective-permute-start(bf16[2,8,32,256]{3,2,1,0:T(8,128)(2,1)S(1)} %bitcast.9), channel_id=1, source_target_pairs={{0,8},{8,0},{16,24},{24,16},{32,40},{40,32},{48,56},{56,48},{64,72... | collective-permute-start | bytes 786440 | tf_op jit(solution)/shard_map/ppermute | solution.py:403
  83.0 3.2 %collective-permute-start.18 = (bf16[64,2048]{1,0:T(8,128)(2,1)S(1)}, bf16[64,2048]{1,0:T(8,128)(2,1)S(1)}, u32[]{:S(2)}, u32[]{:S(2)}) collective-permute-start(bf16[64,2048]{1,0:T(8,128)(2,1)S(1)} %get-tuple-element.44), channel_id=1, source_target_pairs={{0,8},{8,0},{16,24},{24,16},{32,40},{40,32},{48,56},{56,48},{64,72... | collective-permute-start | bytes 786440 | tf_op jit(solution)/shard_map/ppermute | solution.py:403
  86.2 4.8 %collective-permute-start.19 = (bf16[32,2048]{1,0:T(8,128)(2,1)S(1)}, bf16[32,2048]{1,0:T(8,128)(2,1)S(1)}, u32[]{:S(2)}, u32[]{:S(2)}) collective-permute-start(bf16[32,2048]{1,0:T(8,128)(2,1)S(1)} %get-tuple-element.46), channel_id=1, source_target_pairs={{0,16},{8,24},{16,0},{24,8},{32,48},{40,56},{48,32},{56,40},{64,80... | collective-permute-start | bytes 393224 | tf_op jit(solution)/shard_map/ppermute | solution.py:403

commit v9 on v8

--- a/solution.py
+++ b/solution.py
@@ -13,7 +13,7 @@
 TN = (((0,), (0,)), ((), ()))
 SEQ = ("y", "xh", "xl", "core")
 SMALL = pltpu.CompilerParams(vmem_limit_bytes=8 << 20)
-MIDDLE = pltpu.CompilerParams(vmem_limit_bytes=16 << 20)
+WHOLE = pltpu.CompilerParams(vmem_limit_bytes=52 << 20)
 LARGE = pltpu.CompilerParams(vmem_limit_bytes=58 << 20)
 
 
@@ -284,48 +284,39 @@
 
 def take_kernel(whole_ref, out_ref, sem):
     width = out_ref.shape[1]
-    columns = pl.ds(pl.multiple_of(lax.axis_index("xl") * width, width), width)
+    block = lax.axis_index("core") * 2 + lax.axis_index("xl")
+    columns = pl.ds(pl.multiple_of(block * width, width), width)
     copy = pltpu.make_async_copy(whole_ref.at[:, columns], out_ref, sem)
     copy.start()
     copy.wait()
 
 
-def mix_kernel(
-    own_ref, other_ref, mine_ref, one_ref, two_ref, three_ref, four_ref, keep_ref, send_ref, total
-):
-    core, half, head = lax.axis_index("core"), lax.axis_index("xl"), lax.axis_index("head")
-    kept = keep_ref.shape[0]
-    width = four_ref.shape[1]
-
-    def rows(steps):
-        source = (head + (2 * core - 1) * steps + 8) % 8
-        block = [ref[place, source] for ref in (own_ref, other_ref) for place in (half, 1 - half)]
-        return jnp.concatenate(block, axis=0)
-
-    total[...] = mm(rows(1), one_ref[...]) + mm(rows(2), two_ref[...]) + mm(rows(3), three_ref[...])
-
-    @pl.when(core == 0)
-    def _():
-        total[...] = total[...] + mm(rows(0), mine_ref[...])
-
-    part = pl.ds(pl.multiple_of(core * width, width), width)
-    total[:, part] = total[:, part] + mm(rows(4), four_ref[...])
-    keep_ref[...] = total[:kept]
-    send_ref[...] = total[kept:].astype(BF16)
-
-
-def add_kernel(keep_ref, come_ref, mine_ref, send_ref):
-    total = (keep_ref[...] + come_ref[...].astype(F32)).astype(BF16)
-    rows = mine_ref.shape[0]
-    mine_ref[...] = total[:rows]
-    send_ref[...] = total[rows:]
-
-
-def lay_kernel(mine_ref, come_ref, out_ref):
+def mix_kernel(own_ref, other_ref, weight_hbm, *refs):
+    outs, weight_ref, sems = refs[:-2], refs[-2], refs[-1]
+    found = [
+        pltpu.make_async_copy(weight_hbm.at[head], weight_ref.at[head], sems.at[head])
+        for head in range(weight_ref.shape[0])
+    ]
+    for copy in found:
+        copy.start()
+    half = lax.axis_index("xl")
+    rows = own_ref.shape[2]
+    for head, copy in enumerate(found):
+        block = [ref[place, head] for place in (half, 1 - half) for ref in (own_ref, other_ref)]
+        copy.wait()
+        part = mm(jnp.concatenate(block, axis=0), weight_ref[head])
+        total = part if head == 0 else total + part
+    total = total.astype(BF16)
+    for k, ref in enumerate(outs):
+        ref[...] = total[k * rows : (k + 1) * rows]
+
+
+def lay_kernel(mine_ref, core_ref, half_ref, far_ref, out_ref):
     width = mine_ref.shape[1]
-    half = lax.axis_index("xl")
-    out_ref[:, pl.ds(pl.multiple_of(half * width, width), width)] = mine_ref[...]
-    out_ref[:, pl.ds(pl.multiple_of((1 - half) * width, width), width)] = come_ref[...]
+    block = lax.axis_index("core") * 2 + lax.axis_index("xl")
+    for flip, ref in ((0, mine_ref), (2, core_ref), (1, half_ref), (3, far_ref)):
+        place = pl.multiple_of((block ^ flip) * width, width)
+        out_ref[:, pl.ds(place, width)] = ref[...]
 
 
 def hbm():
@@ -411,30 +402,21 @@
     def flip(bits):
         return lambda i: i ^ bits
 
-    def around(value):
-        up = [(z, (z + 1) % 8) for z in range(8)]
-        down = [(8 + z, 8 + (z + 7) % 8) for z in range(8)]
-        return lax.ppermute(value, ("core", "head"), up + down)
-
-    def later(value, gate):
-        return lax.optimization_barrier((value, gate))[0]
-
-    wide = out_weight.shape[1] // 2
+    quarter = out_weight.shape[1] // 4
     mine = pl.pallas_call(
         take_kernel,
         name="take",
         in_specs=[hbm()],
         out_specs=vmem(),
-        out_shape=jax.ShapeDtypeStruct((n, wide), BF16),
+        out_shape=jax.ShapeDtypeStruct((n, quarter), BF16),
         scratch_shapes=[pltpu.SemaphoreType.DMA],
         compiler_params=LARGE,
     )(out_weight)
-    one = around(mine)
+    columns = lax.all_gather(mine, "head", tiled=False)
 
     pair_shape = jax.ShapeDtypeStruct((n, 2 * n), BF16)
     half_shape = jax.ShapeDtypeStruct((n // 2, 2 * n), BF16)
     other = moved(carry, flip(1))
-    two = around(later(one, other))
     pair, half = pl.pallas_call(
         pair_kernel,
         name="pair",
@@ -455,7 +437,6 @@
         scratch_shapes=[pltpu.VMEM((4, n, 2 * n), BF16), pltpu.VMEM((n, 2 * n), BF16)],
         compiler_params=SMALL,
     )(pair, *near, *swapped)
-    three = around(later(two, half))
     near = [moved(half, along_y(s)) for s in (1, 2, 3)]
     swapped = [moved(value, flip(1)) for value in near]
     flat = pl.pallas_call(
@@ -468,44 +449,28 @@
         compiler_params=SMALL,
     )(*near, *swapped, prefix, other, looked, out_gain.reshape(1, n))
     part = rows // 8
-    part_three = lax.dynamic_slice_in_dim(
-        three, lax.axis_index("core") * (wide // 2), wide // 2, 1
-    )
-    flat, part_three = lax.optimization_barrier((flat, part_three))
-    four = around(part_three)
     reads = lax.all_to_all(
         flat.reshape(16, part, n), ("xl", "head"), 0, 0, tiled=True
     ).reshape(2, 8, part, n)
     beside = moved(reads, flip(1))
-    keep, send = pl.pallas_call(
+    piece = jax.ShapeDtypeStruct((part, quarter), BF16)
+    kept, to_core, to_half, to_far = pl.pallas_call(
         mix_kernel,
         name="mix",
-        in_specs=[vmem()] * 7,
-        out_specs=[vmem()] * 2,
-        out_shape=[
-            jax.ShapeDtypeStruct((2 * part, wide), F32),
-            jax.ShapeDtypeStruct((2 * part, wide), BF16),
-        ],
-        scratch_shapes=[pltpu.VMEM((4 * part, wide), F32)],
-        compiler_params=MIDDLE,
-    )(reads, beside, mine, one, two, three, four)
-    piece = jax.ShapeDtypeStruct((part, wide), BF16)
-    kept, send = pl.pallas_call(
-        add_kernel,
-        name="add",
-        in_specs=[vmem()] * 2,
-        out_specs=[vmem()] * 2,
-        out_shape=[piece] * 2,
-        compiler_params=SMALL,
-    )(keep, moved(send, flip(1)))
+        in_specs=[vmem(), vmem(), hbm()],
+        out_specs=[vmem()] * 4,
+        out_shape=[piece] * 4,
+        scratch_shapes=[pltpu.VMEM((8, n, quarter), BF16), pltpu.SemaphoreType.DMA((8,))],
+        compiler_params=WHOLE,
+    )(reads, beside, columns)
     return pl.pallas_call(
         lay_kernel,
         name="lay",
-        in_specs=[vmem()] * 2,
+        in_specs=[vmem()] * 4,
         out_specs=vmem(),
-        out_shape=jax.ShapeDtypeStruct((part, 2 * wide), BF16),
+        out_shape=jax.ShapeDtypeStruct((part, 4 * quarter), BF16),
         compiler_params=SMALL,
-    )(kept, moved(send, flip(2)))
+    )(kept, moved(to_core, flip(1)), moved(to_half, flip(2)), moved(to_far, flip(3)))
 
 
 def solution(mesh):

time: 92.1 us -> 91.8 us (level)
  blocking collectives: 0 us -> 21 us
  starting transfers between devices: 34.3 us -> 18.8 us
  waiting for transfers between devices: 27 us -> 12.4 us
  between operations: 1.42 us -> 14.8 us
  local copies, waits for them, and re-layouts: 5.18 us -> 2.03 us
  Pallas kernels: 23.8 us -> 22.5 us
    all_to_all x0 -> x1, blocking collectives: none -> 21 us  [per_device(): lax.all_to_all(flat.reshape(16, part, n), ('xl', 'head'), 0, 0, tiled=True)]
    ppermute x4 -> x0, starting transfers between devices: 11.8 us -> none  [around(): return lax.ppermute(value, ('core', 'head'), up + down)]
    all_to_all x1 -> x0, waiting for transfers between devices: 6.57 us -> none  [per_device(): lax.all_to_all(flat.reshape(16, part, n), ('xl', 'head'), 0, 0, tiled=True)]
    all_to_all x1 -> x0, starting transfers between devices: 6 us -> none  [per_device(): lax.all_to_all(flat.reshape(16, part, n), ('xl', 'head'), 0, 0, tiled=True)]
    ppermute x16 -> x17, waiting for transfers between devices: 17.3 us -> 12.4 us  [moved(): return lax.ppermute(value, SEQ, [(i, place_of(i)) for i in range(count)])]
    ppermute x4 -> x0, waiting for transfers between devices: 3.11 us -> none  [around(): return lax.ppermute(value, ('core', 'head'), up + down)]
    unnamed x14 -> x6, local copies, waits for them, and re-layouts: 4.34 us -> 2.03 us
    ppermute x16 -> x17, starting transfers between devices: 16.5 us -> 18.8 us  [moved(): return lax.ppermute(value, SEQ, [(i, place_of(i)) for i in range(count)])]
  transfers between devices with their start and end apart: 21 -> 18, of which waited for: 12 -> 11; matrix products, arithmetic and copies ran while one was open for 0% -> 0% of each run, Pallas kernels for 20% -> 19%
where the time goes in v9:
time: 91.8 us; the launch traced here: 91.5 us
  Pallas kernels  22.5 us (25%)
  blocking collectives  21 us (23%)
  starting transfers between devices  18.8 us (20%)
  between operations  14.8 us (16%)
  waiting for transfers between devices  12.4 us (14%)
  local copies, waits for them, and re-layouts  2.03 us (2%)
    all_to_all x1, blocking collectives, per_device(): lax.all_to_all(flat.reshape(16, part, n), ('xl', 'head'), 0, 0, tiled=True)  21 us
    ppermute x17, starting transfers between devices, moved(): return lax.ppermute(value, SEQ, [(i, place_of(i)) for i in range(count)])  18.8 us
    ppermute x17, waiting for transfers between devices, moved(): return lax.ppermute(value, SEQ, [(i, place_of(i)) for i in range(count)])  12.4 us
    pallas_call x1, Pallas kernels, per_device(): pl.pallas_call(fold_kernel, name='fold', in_specs=[hbm()] * 7, out_specs=...  9.67 us
    pallas_call x1, Pallas kernels, look(): pl.pallas_call(look_kernel, name='look', in_specs=[hbm(), vmem(), hbm()]...  6.21 us
    pallas_call x1, Pallas kernels, per_device(): pl.pallas_call(mix_kernel, name='mix', in_specs=[vmem(), vmem(), hbm()],...  2.45 us
    unnamed x6, local copies, waits for them, and re-layouts  2.03 us
    pallas_call x1, Pallas kernels, per_device(): pl.pallas_call(take_kernel, name='take', in_specs=[hbm()], out_specs=vmem...  1.85 us
  transfers between devices with their start and end apart: 18, of which 11 were waited for; matrix products, arithmetic and copies ran while one was open for 0% of the time, Pallas kernels for 19%

profile of v9, /device:TPU:1, one launch (start us, length us, event | category | flops | bytes accessed | tf_op | source)
XLA Modules:
  0.0 91.5 jit_solution(16759354104657949930)
XLA Ops:
  6.5 0.0 all-gather.3.cloned.1.call-start
  6.5 1.9 %take.1 = bf16[256,1024]{1,0:T(8,128)(2,1)} custom-call(bf16[256,4096]{1,0:T(8,128)(2,1)} %whole_ref.1), custom_call_target="tpu_custom_call" | custom-call | tf_op jit(solution)/shard_map/take/pallas_call | solution.py:406
  8.4 0.0 all-gather.3.cloned.1.call-update
  9.7 9.7 %fold.1 = (bf16[256,512]{1,0:T(8,128)(2,1)}, f32[256,256]{1,0:T(8,128)}, f32[256,512]{1,0:T(8,128)}, f32[256,256]{1,0:T(8,128)}, f32[256,1]{1,0:T(8,128)}) custom-call(f32[1]{0:T(128)S(6)} %copy.10.scale_hbm, f32[1]{0:T(128)S(6)} %copy.11.rate_hbm, bf16[256,4096]{1,0:T(8,128)(2,1)} %x_hbm.3, f32[1,4096]{1,0:T(1,128)} %bitcast.17, ...), custom_call_target="tpu_custom_call" | custom-call | tf_op jit(solution)/shard_map/fold/pallas_call | solution.py:348
  19.4 3.3 %collective-permute-start = (bf16[256,512]{1,0:T(8,128)(2,1)}, bf16[256,512]{1,0:T(8,128)(2,1)S(1)}, u32[]{:S(2)}, u32[]{:S(2)}) collective-permute-start(bf16[256,512]{1,0:T(8,128)(2,1)} %get-tuple-element.22.own_ref), channel_id=1, source_target_pairs={{0,8},{8,0},{16,24},{24,16},{32,40},{40,32},{48,56},{56,48},{64,72... | collective-permute-start | bytes 786440 | tf_op jit(solution)/shard_map/ppermute | solution.py:394
  22.7 1.4 %collective-permute-done.other_ref.refs_7_ = bf16[256,512]{1,0:T(8,128)(2,1)S(1)} collective-permute-done((bf16[256,512]{1,0:T(8,128)(2,1)}, bf16[256,512]{1,0:T(8,128)(2,1)S(1)}, u32[]{:S(2)}, u32[]{:S(2)}) %collective-permute-start) | collective-permute-done | bytes 262176 | tf_op jit(solution)/shard_map/ppermute | solution.py:394
  24.1 0.0 copy-start.1
  24.1 1.0 %copy-done.1 = bf16[256,512]{1,0:T(8,128)(2,1)S(1)} copy-done((bf16[256,512]{1,0:T(8,128)(2,1)S(1)}, bf16[256,512]{1,0:T(8,128)(2,1)}, u32[]{:S(2)}) %copy-start.1) | copy-done | bytes 262168
  25.1 0.3 pair.1
  25.3 0.1 collective-permute-start.1
  25.4 1.9 %collective-permute-start.2 = (bf16[128,512]{1,0:T(8,128)(2,1)S(1)}, bf16[128,512]{1,0:T(8,128)(2,1)S(1)}, u32[]{:S(2)}, u32[]{:S(2)}) collective-permute-start(bf16[128,512]{1,0:T(8,128)(2,1)S(1)} %get-tuple-element.24), channel_id=1, source_target_pairs={{0,32},{8,40},{16,48},{24,56},{32,0},{40,8},{48,16},{56,24},{64,96... | collective-permute-start | bytes 393224 | tf_op jit(solution)/shard_map/ppermute | solution.py:394
  27.3 1.2 %collective-permute-start.3 = (bf16[128,512]{1,0:T(8,128)(2,1)S(1)}, bf16[128,512]{1,0:T(8,128)(2,1)S(1)}, u32[]{:S(2)}, u32[]{:S(2)}) collective-permute-start(bf16[128,512]{1,0:T(8,128)(2,1)S(1)} %get-tuple-element.24), channel_id=1, source_target_pairs={{0,48},{8,56},{16,0},{24,8},{32,16},{40,24},{48,32},{56,40},{64,11... | collective-permute-start | bytes 393224 | tf_op jit(solution)/shard_map/ppermute | solution.py:394
  28.5 0.0 copy-start.2
  28.5 6.2 %look.1.refs_8_ = f32[256,512]{1,0:T(8,128)} custom-call(bf16[256,4096]{1,0:T(8,128)(2,1)} %x_hbm.3, f32[1,4096]{1,0:T(1,128)} %bitcast.18, bf16[3,4096,256]{2,1,0:T(8,128)(2,1)} %bitcast.15, f32[256,256]{1,0:T(8,128)} %get-tuple-element.25.key_ref, f32[256,512]{1,0:T(8,128)} %get-tuple-element.26.solved_ref, f32[256,256]{1,0:T(8,128)} %get-tuple-element.27.decay_ref, ...), custom_call_target="tpu_custom_call" | custom-call | flops 1073741824 | bytes 16777216 | tf_op jit(solution)/shard_map/look/pallas_call | solution.py:378
  34.7 0.0 collective-permute-done.1.refs_0_
  34.7 0.0 collective-permute-done.2.refs_1_
  34.7 0.0 collective-permute-done.3.refs_2_
  34.7 1.3 %collective-permute-start.4 = (bf16[128,512]{1,0:T(8,128)(2,1)S(1)}, bf16[128,512]{1,0:T(8,128)(2,1)S(1)}, u32[]{:S(2)}, u32[]{:S(2)}) collective-permute-start(bf16[128,512]{1,0:T(8,128)(2,1)S(1)} %collective-permute-done.1.refs_0_), channel_id=1, source_target_pairs={{0,8},{8,0},{16,24},{24,16},{32,40},{40,32},{48,56},{56,48},{64,72... | collective-permute-start | bytes 393224 | tf_op jit(solution)/shard_map/ppermute | solution.py:394
  36.0 0.1 collective-permute-start.5
  36.1 0.4 collective-permute-start.6
  36.5 0.5 collective-permute-done.4.refs_3_
  37.0 0.4 collective-permute-done.5.refs_4_
  37.4 0.2 collective-permute-done.6.refs_5_
  37.6 0.6 row.1
  38.1 1.4 %collective-permute-start.7 = (bf16[128,512]{1,0:T(8,128)(2,1)S(1)}, bf16[128,512]{1,0:T(8,128)(2,1)S(1)}, u32[]{:S(2)}, u32[]{:S(2)}) collective-permute-start(bf16[128,512]{1,0:T(8,128)(2,1)S(1)} %get-tuple-element.32), channel_id=1, source_target_pairs={{0,64},{8,72},{16,80},{24,88},{32,96},{40,104},{48,112},{56,120},{... | collective-permute-start | bytes 393224 | tf_op jit(solution)/shard_map/ppermute | solution.py:394
  39.5 2.6 %collective-permute-start.8 = (bf16[128,512]{1,0:T(8,128)(2,1)S(1)}, bf16[128,512]{1,0:T(8,128)(2,1)S(1)}, u32[]{:S(2)}, u32[]{:S(2)}) collective-permute-start(bf16[128,512]{1,0:T(8,128)(2,1)S(1)} %get-tuple-element.32), channel_id=1, source_target_pairs={{0,128},{8,136},{16,144},{24,152},{32,160},{40,168},{48,176},{56,1... | collective-permute-start | bytes 393224 | tf_op jit(solution)/shard_map/ppermute | solution.py:394
  42.1 1.1 %collective-permute-start.9 = (bf16[128,512]{1,0:T(8,128)(2,1)S(1)}, bf16[128,512]{1,0:T(8,128)(2,1)S(1)}, u32[]{:S(2)}, u32[]{:S(2)}) collective-permute-start(bf16[128,512]{1,0:T(8,128)(2,1)S(1)} %get-tuple-element.32), channel_id=1, source_target_pairs={{0,192},{8,200},{16,208},{24,216},{32,224},{40,232},{48,240},{56,2... | collective-permute-start | bytes 393224 | tf_op jit(solution)/shard_map/ppermute | solution.py:394
  43.2 1.2 %collective-permute-done.7.refs_0_ = bf16[128,512]{1,0:T(8,128)(2,1)S(1)} collective-permute-done((bf16[128,512]{1,0:T(8,128)(2,1)S(1)}, bf16[128,512]{1,0:T(8,128)(2,1)S(1)}, u32[]{:S(2)}, u32[]{:S(2)}) %collective-permute-start.7) | collective-permute-done | bytes 131104 | tf_op jit(solution)/shard_map/ppermute | solution.py:394
  44.4 1.0 %collective-permute-start.10 = (bf16[128,512]{1,0:T(8,128)(2,1)S(1)}, bf16[128,512]{1,0:T(8,128)(2,1)S(1)}, u32[]{:S(2)}, u32[]{:S(2)}) collective-permute-start(bf16[128,512]{1,0:T(8,128)(2,1)S(1)} %collective-permute-done.7.refs_0_), channel_id=1, source_target_pairs={{0,8},{8,0},{16,24},{24,16},{32,40},{40,32},{48,56},{56,48},{64,72... | collective-permute-start | bytes 393224 | tf_op jit(solution)/shard_map/ppermute | solution.py:394
  45.4 2.8 %collective-permute-done.8.refs_1_ = bf16[128,512]{1,0:T(8,128)(2,1)S(1)} collective-permute-done((bf16[128,512]{1,0:T(8,128)(2,1)S(1)}, bf16[128,512]{1,0:T(8,128)(2,1)S(1)}, u32[]{:S(2)}, u32[]{:S(2)}) %collective-permute-start.8) | collective-permute-done | bytes 131104 | tf_op jit(solution)/shard_map/ppermute | solution.py:394
  48.2 1.1 %collective-permute-start.11 = (bf16[128,512]{1,0:T(8,128)(2,1)S(1)}, bf16[128,512]{1,0:T(8,128)(2,1)S(1)}, u32[]{:S(2)}, u32[]{:S(2)}) collective-permute-start(bf16[128,512]{1,0:T(8,128)(2,1)S(1)} %collective-permute-done.8.refs_1_), channel_id=1, source_target_pairs={{0,8},{8,0},{16,24},{24,16},{32,40},{40,32},{48,56},{56,48},{64,72... | collective-permute-start | bytes 393224 | tf_op jit(solution)/shard_map/ppermute | solution.py:394
  49.4 0.0 collective-permute-done.9.refs_2_
  49.4 0.0 collective-permute-start.12
  49.4 0.0 collective-permute-done.10.refs_3_
  49.4 1.0 %collective-permute-done.11.refs_4_ = bf16[128,512]{1,0:T(8,128)(2,1)S(1)} collective-permute-done((bf16[128,512]{1,0:T(8,128)(2,1)S(1)}, bf16[128,512]{1,0:T(8,128)(2,1)S(1)}, u32[]{:S(2)}, u32[]{:S(2)}) %collective-permute-start.11) | collective-permute-done | bytes 131104 | tf_op jit(solution)/shard_map/ppermute | solution.py:394
  50.4 0.4 collective-permute-done.12.refs_5_
  50.7 0.0 copy-done.2
  50.7 0.0 copy-start
  50.7 1.0 %copy-done = f32[256,512]{1,0:T(8,128)S(1)} copy-done((f32[256,512]{1,0:T(8,128)S(1)}, f32[256,512]{1,0:T(8,128)}, u32[]{:S(2)}) %copy-start) | copy-done | bytes 524312
  51.8 0.7 read.1
  52.5 21.0 %all_to_all.5 = bf16[16,32,256]{2,1,0:T(8,128)(2,1)S(1)} all-to-all(bf16[16,32,256]{2,1,0:T(8,128)(2,1)S(1)} %bitcast.12), channel_id=1, replica_groups=mesh['y'=4,'xh'=2,'xl'=2,'core'=2,'head'=8] {'xl','head'}, dimensions={0} | all-to-all | bytes 524288 | tf_op jit(solution)/shard_map/all_to_all | solution.py:452
  73.5 1.1 %collective-permute-start.13 = (bf16[2,8,32,256]{3,2,1,0:T(8,128)(2,1)S(1)}, bf16[2,8,32,256]{3,2,1,0:T(8,128)(2,1)S(1)}, u32[]{:S(2)}, u32[]{:S(2)}) collective-permute-start(bf16[2,8,32,256]{3,2,1,0:T(8,128)(2,1)S(1)} %bitcast.10), channel_id=1, source_target_pairs={{0,8},{8,0},{16,24},{24,16},{32,40},{40,32},{48,56},{56,48},{64,72... | collective-permute-start | bytes 786440 | tf_op jit(solution)/shard_map/ppermute | solution.py:394
  74.6 1.2 %collective-permute-done.13.other_ref = bf16[2,8,32,256]{3,2,1,0:T(8,128)(2,1)S(1)} collective-permute-done((bf16[2,8,32,256]{3,2,1,0:T(8,128)(2,1)S(1)}, bf16[2,8,32,256]{3,2,1,0:T(8,128)(2,1)S(1)}, u32[]{:S(2)}, u32[]{:S(2)}) %collective-permute-start.13) | collective-permute-done | bytes 262176 | tf_op jit(solution)/shard_map/ppermute | solution.py:394
  75.8 0.0 all-gather.3.cloned.1.call-done
  75.8 2.4 %mix.1 = (bf16[32,1024]{1,0:T(8,128)(2,1)S(1)}, bf16[32,1024]{1,0:T(8,128)(2,1)S(1)}, bf16[32,1024]{1,0:T(8,128)(2,1)S(1)}, bf16[32,1024]{1,0:T(8,128)(2,1)S(1)}) custom-call(bf16[2,8,32,256]{3,2,1,0:T(8,128)(2,1)S(1)} %bitcast.11, bf16[2,8,32,256]{3,2,1,0:T(8,128)(2,1)S(1)} %collective-permute-done.13.other_ref, bf16[8,256,1024]{2,1,0:T(8,128)(2,1)} %bitcast.16), custom_call_target="tpu_custom_call" | custom-call | tf_op jit(solution)/shard_map/mix/pallas_call | solution.py:457
  78.2 0.5 collective-permute-start.14
  78.7 0.4 collective-permute-start.15
  79.1 1.4 %collective-permute-start.16 = (bf16[32,1024]{1,0:T(8,128)(2,1)S(1)}, bf16[32,1024]{1,0:T(8,128)(2,1)S(1)}, u32[]{:S(2)}, u32[]{:S(2)}) collective-permute-start(bf16[32,1024]{1,0:T(8,128)(2,1)S(1)} %get-tuple-element.38), channel_id=1, source_target_pairs={{0,24},{8,16},{16,8},{24,0},{32,56},{40,48},{48,40},{56,32},{64,88... | collective-permute-start | bytes 196616 | tf_op jit(solution)/shard_map/ppermute | solution.py:394
  80.5 0.0 collective-permute-done.14.core_ref
  80.5 1.8 %collective-permute-done.15.half_ref = bf16[32,1024]{1,0:T(8,128)(2,1)S(1)} collective-permute-done((bf16[32,1024]{1,0:T(8,128)(2,1)S(1)}, bf16[32,1024]{1,0:T(8,128)(2,1)S(1)}, u32[]{:S(2)}, u32[]{:S(2)}) %collective-permute-start.15) | collective-permute-done | bytes 65568 | tf_op jit(solution)/shard_map/ppermute | solution.py:394
  82.2 1.7 %collective-permute-done.16.far_ref = bf16[32,1024]{1,0:T(8,128)(2,1)S(1)} collective-permute-done((bf16[32,1024]{1,0:T(8,128)(2,1)S(1)}, bf16[32,1024]{1,0:T(8,128)(2,1)S(1)}, u32[]{:S(2)}, u32[]{:S(2)}) %collective-permute-start.16) | collective-permute-done | bytes 65568 | tf_op jit(solution)/shard_map/ppermute | solution.py:394
  83.9 0.7 lay.1
Async XLA Ops:
  6.5 69.2 %all-gather.3.cloned.1.call-start = ((), (), s32[]{:S(2)}) async-start(), calls=%async_computation.1 | async-start | bytes 4718592 | tf_op jit(solution)/shard_map/all_gather | solution.py:415
  19.4 4.7 %collective-permute-start = (bf16[256,512]{1,0:T(8,128)(2,1)}, bf16[256,512]{1,0:T(8,128)(2,1)S(1)}, u32[]{:S(2)}, u32[]{:S(2)}) collective-permute-start(bf16[256,512]{1,0:T(8,128)(2,1)} %get-tuple-element.22.own_ref), channel_id=1, source_target_pairs={{0,8},{8,0},{16,24},{24,16},{32,40},{40,32},{48,56},{56,48},{64,72... | collective-permute-start | bytes 786440 | tf_op jit(solution)/shard_map/ppermute | solution.py:394
  24.1 1.0 %copy-start.1 = (bf16[256,512]{1,0:T(8,128)(2,1)S(1)}, bf16[256,512]{1,0:T(8,128)(2,1)}, u32[]{:S(2)}) copy-start(bf16[256,512]{1,0:T(8,128)(2,1)} %get-tuple-element.22.own_ref) | copy-start | bytes 786436
  25.3 9.4 %collective-permute-start.1 = (bf16[128,512]{1,0:T(8,128)(2,1)S(1)}, bf16[128,512]{1,0:T(8,128)(2,1)S(1)}, u32[]{:S(2)}, u32[]{:S(2)}) collective-permute-start(bf16[128,512]{1,0:T(8,128)(2,1)S(1)} %get-tuple-element.24), channel_id=1, source_target_pairs={{0,16},{8,24},{16,32},{24,40},{32,48},{40,56},{48,0},{56,8},{64,80... | collective-permute-start | bytes 393224 | tf_op jit(solution)/shard_map/ppermute | solution.py:394
  25.4 9.3 %collective-permute-start.2 = (bf16[128,512]{1,0:T(8,128)(2,1)S(1)}, bf16[128,512]{1,0:T(8,128)(2,1)S(1)}, u32[]{:S(2)}, u32[]{:S(2)}) collective-permute-start(bf16[128,512]{1,0:T(8,128)(2,1)S(1)} %get-tuple-element.24), channel_id=1, source_target_pairs={{0,32},{8,40},{16,48},{24,56},{32,0},{40,8},{48,16},{56,24},{64,96... | collective-permute-start | bytes 393224 | tf_op jit(solution)/shard_map/ppermute | solution.py:394
  27.3 7.4 %collective-permute-start.3 = (bf16[128,512]{1,0:T(8,128)(2,1)S(1)}, bf16[128,512]{1,0:T(8,128)(2,1)S(1)}, u32[]{:S(2)}, u32[]{:S(2)}) collective-permute-start(bf16[128,512]{1,0:T(8,128)(2,1)S(1)} %get-tuple-element.24), channel_id=1, source_target_pairs={{0,48},{8,56},{16,0},{24,8},{32,16},{40,24},{48,32},{56,40},{64,11... | collective-permute-start | bytes 393224 | tf_op jit(solution)/shard_map/ppermute | solution.py:394
  28.5 22.3 %copy-start.2 = (f32[256]{0:T(256)S(1)}, f32[256]{0:T(256)}, u32[]{:S(2)}) copy-start(f32[256]{0:T(256)} %param.16) | copy-start | bytes 3076
  34.7 2.3 %collective-permute-start.4 = (bf16[128,512]{1,0:T(8,128)(2,1)S(1)}, bf16[128,512]{1,0:T(8,128)(2,1)S(1)}, u32[]{:S(2)}, u32[]{:S(2)}) collective-permute-start(bf16[128,512]{1,0:T(8,128)(2,1)S(1)} %collective-permute-done.1.refs_0_), channel_id=1, source_target_pairs={{0,8},{8,0},{16,24},{24,16},{32,40},{40,32},{48,56},{56,48},{64,72... | collective-permute-start | bytes 393224 | tf_op jit(solution)/shard_map/ppermute | solution.py:394
  36.0 1.3 %collective-permute-start.5 = (bf16[128,512]{1,0:T(8,128)(2,1)S(1)}, bf16[128,512]{1,0:T(8,128)(2,1)S(1)}, u32[]{:S(2)}, u32[]{:S(2)}) collective-permute-start(bf16[128,512]{1,0:T(8,128)(2,1)S(1)} %collective-permute-done.2.refs_1_), channel_id=1, source_target_pairs={{0,8},{8,0},{16,24},{24,16},{32,40},{40,32},{48,56},{56,48},{64,72... | collective-permute-start | bytes 393224 | tf_op jit(solution)/shard_map/ppermute | solution.py:394
  36.1 1.4 %collective-permute-start.6 = (bf16[128,512]{1,0:T(8,128)(2,1)S(1)}, bf16[128,512]{1,0:T(8,128)(2,1)S(1)}, u32[]{:S(2)}, u32[]{:S(2)}) collective-permute-start(bf16[128,512]{1,0:T(8,128)(2,1)S(1)} %collective-permute-done.3.refs_2_), channel_id=1, source_target_pairs={{0,8},{8,0},{16,24},{24,16},{32,40},{40,32},{48,56},{56,48},{64,72... | collective-permute-start | bytes 393224 | tf_op jit(solution)/shard_map/ppermute | solution.py:394
  38.1 6.3 %collective-permute-start.7 = (bf16[128,512]{1,0:T(8,128)(2,1)S(1)}, bf16[128,512]{1,0:T(8,128)(2,1)S(1)}, u32[]{:S(2)}, u32[]{:S(2)}) collective-permute-start(bf16[128,512]{1,0:T(8,128)(2,1)S(1)} %get-tuple-element.32), channel_id=1, source_target_pairs={{0,64},{8,72},{16,80},{24,88},{32,96},{40,104},{48,112},{56,120},{... | collective-permute-start | bytes 393224 | tf_op jit(solution)/shard_map/ppermute | solution.py:394
  39.5 8.7 %collective-permute-start.8 = (bf16[128,512]{1,0:T(8,128)(2,1)S(1)}, bf16[128,512]{1,0:T(8,128)(2,1)S(1)}, u32[]{:S(2)}, u32[]{:S(2)}) collective-permute-start(bf16[128,512]{1,0:T(8,128)(2,1)S(1)} %get-tuple-element.32), channel_id=1, source_target_pairs={{0,128},{8,136},{16,144},{24,152},{32,160},{40,168},{48,176},{56,1... | collective-permute-start | bytes 393224 | tf_op jit(solution)/shard_map/ppermute | solution.py:394
  42.1 7.3 %collective-permute-start.9 = (bf16[128,512]{1,0:T(8,128)(2,1)S(1)}, bf16[128,512]{1,0:T(8,128)(2,1)S(1)}, u32[]{:S(2)}, u32[]{:S(2)}) collective-permute-start(bf16[128,512]{1,0:T(8,128)(2,1)S(1)} %get-tuple-element.32), channel_id=1, source_target_pairs={{0,192},{8,200},{16,208},{24,216},{32,224},{40,232},{48,240},{56,2... | collective-permute-start | bytes 393224 | tf_op jit(solution)/shard_map/ppermute | solution.py:394
  44.4 5.0 %collective-permute-start.10 = (bf16[128,512]{1,0:T(8,128)(2,1)S(1)}, bf16[128,512]{1,0:T(8,128)(2,1)S(1)}, u32[]{:S(2)}, u32[]{:S(2)}) collective-permute-start(bf16[128,512]{1,0:T(8,128)(2,1)S(1)} %collective-permute-done.7.refs_0_), channel_id=1, source_target_pairs={{0,8},{8,0},{16,24},{24,16},{32,40},{40,32},{48,56},{56,48},{64,72... | collective-permute-start | bytes 393224 | tf_op jit(solution)/shard_map/ppermute | solution.py:394
  48.2 2.1 %collective-permute-start.11 = (bf16[128,512]{1,0:T(8,128)(2,1)S(1)}, bf16[128,512]{1,0:T(8,128)(2,1)S(1)}, u32[]{:S(2)}, u32[]{:S(2)}) collective-permute-start(bf16[128,512]{1,0:T(8,128)(2,1)S(1)} %collective-permute-done.8.refs_1_), channel_id=1, source_target_pairs={{0,8},{8,0},{16,24},{24,16},{32,40},{40,32},{48,56},{56,48},{64,72... | collective-permute-start | bytes 393224 | tf_op jit(solution)/shard_map/ppermute | solution.py:394
  49.4 1.3 %collective-permute-start.12 = (bf16[128,512]{1,0:T(8,128)(2,1)S(1)}, bf16[128,512]{1,0:T(8,128)(2,1)S(1)}, u32[]{:S(2)}, u32[]{:S(2)}) collective-permute-start(bf16[128,512]{1,0:T(8,128)(2,1)S(1)} %collective-permute-done.9.refs_2_), channel_id=1, source_target_pairs={{0,8},{8,0},{16,24},{24,16},{32,40},{40,32},{48,56},{56,48},{64,72... | collective-permute-start | bytes 393224 | tf_op jit(solution)/shard_map/ppermute | solution.py:394
  50.7 1.1 %copy-start = (f32[256,512]{1,0:T(8,128)S(1)}, f32[256,512]{1,0:T(8,128)}, u32[]{:S(2)}) copy-start(f32[256,512]{1,0:T(8,128)} %look.1.refs_8_) | copy-start | bytes 1572868
  73.5 2.3 %collective-permute-start.13 = (bf16[2,8,32,256]{3,2,1,0:T(8,128)(2,1)S(1)}, bf16[2,8,32,256]{3,2,1,0:T(8,128)(2,1)S(1)}, u32[]{:S(2)}, u32[]{:S(2)}) collective-permute-start(bf16[2,8,32,256]{3,2,1,0:T(8,128)(2,1)S(1)} %bitcast.10), channel_id=1, source_target_pairs={{0,8},{8,0},{16,24},{24,16},{32,40},{40,32},{48,56},{56,48},{64,72... | collective-permute-start | bytes 786440 | tf_op jit(solution)/shard_map/ppermute | solution.py:394
  78.2 2.2 %collective-permute-start.14 = (bf16[32,1024]{1,0:T(8,128)(2,1)S(1)}, bf16[32,1024]{1,0:T(8,128)(2,1)S(1)}, u32[]{:S(2)}, u32[]{:S(2)}) collective-permute-start(bf16[32,1024]{1,0:T(8,128)(2,1)S(1)} %get-tuple-element.36), channel_id=1, source_target_pairs={{0,8},{8,0},{16,24},{24,16},{32,40},{40,32},{48,56},{56,48},{64,72... | collective-permute-start | bytes 196616 | tf_op jit(solution)/shard_map/ppermute | solution.py:394
  78.7 3.6 %collective-permute-start.15 = (bf16[32,1024]{1,0:T(8,128)(2,1)S(1)}, bf16[32,1024]{1,0:T(8,128)(2,1)S(1)}, u32[]{:S(2)}, u32[]{:S(2)}) collective-permute-start(bf16[32,1024]{1,0:T(8,128)(2,1)S(1)} %get-tuple-element.37), channel_id=1, source_target_pairs={{0,16},{8,24},{16,0},{24,8},{32,48},{40,56},{48,32},{56,40},{64,80... | collective-permute-start | bytes 196616 | tf_op jit(solution)/shard_map/ppermute | solution.py:394
  79.1 4.8 %collective-permute-start.16 = (bf16[32,1024]{1,0:T(8,128)(2,1)S(1)}, bf16[32,1024]{1,0:T(8,128)(2,1)S(1)}, u32[]{:S(2)}, u32[]{:S(2)}) collective-permute-start(bf16[32,1024]{1,0:T(8,128)(2,1)S(1)} %get-tuple-element.38), channel_id=1, source_target_pairs={{0,24},{8,16},{16,8},{24,0},{32,56},{40,48},{48,40},{56,32},{64,88... | collective-permute-start | bytes 196616 | tf_op jit(solution)/shard_map/ppermute | solution.py:394
Sparse Core Ops, SparseCore 0:
  9.1 63.3 all-gather.2

commit v10 on v8

--- a/solution.py
+++ b/solution.py
@@ -11,7 +11,7 @@
 NN = (((1,), (0,)), ((), ()))
 NT = (((1,), (1,)), ((), ()))
 TN = (((0,), (0,)), ((), ()))
-SEQ = ("y", "xh", "xl", "core")
+SEQ = ("yh", "yl", "xh", "xl", "core")
 SMALL = pltpu.CompilerParams(vmem_limit_bytes=8 << 20)
 MIDDLE = pltpu.CompilerParams(vmem_limit_bytes=16 << 20)
 LARGE = pltpu.CompilerParams(vmem_limit_bytes=58 << 20)
@@ -246,7 +246,7 @@
     near, swapped = refs[:3], refs[3:6]
     prefix_ref, other_ref, look_ref, gain_ref, out_ref, held, state = refs[6:]
     n = look_ref.shape[0]
-    place = lax.axis_index("y")
+    place = lax.axis_index("yh") * 2 + lax.axis_index("yl")
     for shift, ref, swap in zip((1, 2, 3), near, swapped):
         hold(held, (place + (4 - shift)) % 4, ref, swap)
 
@@ -278,13 +278,17 @@
     read = look_ref[:, n:] + mm3(split(look_ref[:, :n]), split(state[...]))
     read = read * lax.rsqrt(jnp.mean(read * read, axis=-1, keepdims=True) + 1e-06)
     flat = (read * gain_ref[...]).astype(BF16)
-    out_ref[0] = flat
-    out_ref[1] = flat
+    for copy in range(out_ref.shape[0]):
+        out_ref[copy] = flat
+
+
+def column_block():
+    return lax.axis_index("yl") * 2 + lax.axis_index("xl")
 
 
 def take_kernel(whole_ref, out_ref, sem):
     width = out_ref.shape[1]
-    columns = pl.ds(pl.multiple_of(lax.axis_index("xl") * width, width), width)
+    columns = pl.ds(pl.multiple_of(column_block() * width, width), width)
     copy = pltpu.make_async_copy(whole_ref.at[:, columns], out_ref, sem)
     copy.start()
     copy.wait()
@@ -293,13 +297,13 @@
 def mix_kernel(
     own_ref, other_ref, mine_ref, one_ref, two_ref, three_ref, four_ref, keep_ref, send_ref, total
 ):
-    core, half, head = lax.axis_index("core"), lax.axis_index("xl"), lax.axis_index("head")
+    core, here, head = lax.axis_index("core"), column_block(), lax.axis_index("head")
     kept = keep_ref.shape[0]
     width = four_ref.shape[1]
 
     def rows(steps):
         source = (head + (2 * core - 1) * steps + 8) % 8
-        block = [ref[place, source] for ref in (own_ref, other_ref) for place in (half, 1 - half)]
+        block = [ref[here ^ k, source] for ref in (own_ref, other_ref) for k in range(4)]
         return jnp.concatenate(block, axis=0)
 
     total[...] = mm(rows(1), one_ref[...]) + mm(rows(2), two_ref[...]) + mm(rows(3), three_ref[...])
@@ -314,18 +318,19 @@
     send_ref[...] = total[kept:].astype(BF16)
 
 
-def add_kernel(keep_ref, come_ref, mine_ref, send_ref):
+def add_kernel(keep_ref, come_ref, *outs):
     total = (keep_ref[...] + come_ref[...].astype(F32)).astype(BF16)
-    rows = mine_ref.shape[0]
-    mine_ref[...] = total[:rows]
-    send_ref[...] = total[rows:]
-
-
-def lay_kernel(mine_ref, come_ref, out_ref):
-    width = mine_ref.shape[1]
-    half = lax.axis_index("xl")
-    out_ref[:, pl.ds(pl.multiple_of(half * width, width), width)] = mine_ref[...]
-    out_ref[:, pl.ds(pl.multiple_of((1 - half) * width, width), width)] = come_ref[...]
+    rows = outs[0].shape[0]
+    for k, ref in enumerate(outs):
+        ref[...] = total[k * rows : (k + 1) * rows]
+
+
+def lay_kernel(*refs):
+    pieces, out_ref = refs[:-1], refs[-1]
+    width = pieces[0].shape[1]
+    here = column_block()
+    for k, ref in enumerate(pieces):
+        out_ref[:, pl.ds(pl.multiple_of((here ^ k) * width, width), width)] = ref[...]
 
 
 def hbm():
@@ -419,7 +424,7 @@
     def later(value, gate):
         return lax.optimization_barrier((value, gate))[0]
 
-    wide = out_weight.shape[1] // 2
+    wide = out_weight.shape[1] // 4
     mine = pl.pallas_call(
         take_kernel,
         name="take",
@@ -445,6 +450,7 @@
     )(carry, other)
     near = [moved(half, along_x(s)) for s in (1, 2, 3)]
     near, looked = lax.optimization_barrier((near, look()))
+    three = around(later(two, near))
     swapped = [moved(value, flip(1)) for value in near]
     half, prefix = pl.pallas_call(
         row_kernel,
@@ -455,27 +461,26 @@
         scratch_shapes=[pltpu.VMEM((4, n, 2 * n), BF16), pltpu.VMEM((n, 2 * n), BF16)],
         compiler_params=SMALL,
     )(pair, *near, *swapped)
-    three = around(later(two, half))
     near = [moved(half, along_y(s)) for s in (1, 2, 3)]
+    part_three = lax.dynamic_slice_in_dim(
+        three, lax.axis_index("core") * (wide // 2), wide // 2, 1
+    )
+    four = around(later(part_three, near))
     swapped = [moved(value, flip(1)) for value in near]
     flat = pl.pallas_call(
         read_kernel,
         name="read",
         in_specs=[vmem()] * 10,
         out_specs=vmem(),
-        out_shape=jax.ShapeDtypeStruct((2, rows, n), BF16),
+        out_shape=jax.ShapeDtypeStruct((4, rows, n), BF16),
         scratch_shapes=[pltpu.VMEM((4, n, 2 * n), BF16), pltpu.VMEM((n, n), F32)],
         compiler_params=SMALL,
     )(*near, *swapped, prefix, other, looked, out_gain.reshape(1, n))
     part = rows // 8
-    part_three = lax.dynamic_slice_in_dim(
-        three, lax.axis_index("core") * (wide // 2), wide // 2, 1
-    )
-    flat, part_three = lax.optimization_barrier((flat, part_three))
-    four = around(part_three)
+    flat, four = lax.optimization_barrier((flat, four))
     reads = lax.all_to_all(
-        flat.reshape(16, part, n), ("xl", "head"), 0, 0, tiled=True
-    ).reshape(2, 8, part, n)
+        flat.reshape(32, part, n), ("yl", "xl", "head"), 0, 0, tiled=True
+    ).reshape(4, 8, part, n)
     beside = moved(reads, flip(1))
     keep, send = pl.pallas_call(
         mix_kernel,
@@ -483,33 +488,33 @@
         in_specs=[vmem()] * 7,
         out_specs=[vmem()] * 2,
         out_shape=[
-            jax.ShapeDtypeStruct((2 * part, wide), F32),
-            jax.ShapeDtypeStruct((2 * part, wide), BF16),
+            jax.ShapeDtypeStruct((4 * part, wide), F32),
+            jax.ShapeDtypeStruct((4 * part, wide), BF16),
         ],
-        scratch_shapes=[pltpu.VMEM((4 * part, wide), F32)],
+        scratch_shapes=[pltpu.VMEM((8 * part, wide), F32)],
         compiler_params=MIDDLE,
     )(reads, beside, mine, one, two, three, four)
     piece = jax.ShapeDtypeStruct((part, wide), BF16)
-    kept, send = pl.pallas_call(
+    kept, to_x, to_y, to_both = pl.pallas_call(
         add_kernel,
         name="add",
         in_specs=[vmem()] * 2,
-        out_specs=[vmem()] * 2,
-        out_shape=[piece] * 2,
+        out_specs=[vmem()] * 4,
+        out_shape=[piece] * 4,
         compiler_params=SMALL,
     )(keep, moved(send, flip(1)))
     return pl.pallas_call(
         lay_kernel,
         name="lay",
-        in_specs=[vmem()] * 2,
+        in_specs=[vmem()] * 4,
         out_specs=vmem(),
-        out_shape=jax.ShapeDtypeStruct((part, 2 * wide), BF16),
+        out_shape=jax.ShapeDtypeStruct((part, 4 * wide), BF16),
         compiler_params=SMALL,
-    )(kept, moved(send, flip(2)))
+    )(kept, moved(to_x, flip(2)), moved(to_y, flip(8)), moved(to_both, flip(10)))
 
 
 def solution(mesh):
-    fine = Mesh(mesh.devices.reshape(4, 2, 2, 2, 8), SEQ + ("head",))
+    fine = Mesh(mesh.devices.reshape(2, 2, 2, 2, 2, 8), SEQ + ("head",))
     in_specs = (
         P(SEQ, None),
         P(),

time: 92.1 us -> 91.6 us (level)
  blocking collectives: 0 us -> 19.3 us
  starting transfers between devices: 34.3 us -> 27.2 us
  waiting for transfers between devices: 27 us -> 20.1 us
  local copies, waits for them, and re-layouts: 5.18 us -> 2.02 us
  Pallas kernels: 23.8 us -> 21 us
    all_to_all x0 -> x1, blocking collectives: none -> 19.3 us  [per_device(): lax.all_to_all(flat.reshape(32, part, n), ('yl', 'xl', 'head'), 0, 0, til...]
    all_to_all x1 -> x0, waiting for transfers between devices: 6.57 us -> none  [per_device(): lax.all_to_all(flat.reshape(16, part, n), ('xl', 'head'), 0, 0, tiled=True)]
    all_to_all x1 -> x0, starting transfers between devices: 6 us -> none  [per_device(): lax.all_to_all(flat.reshape(16, part, n), ('xl', 'head'), 0, 0, tiled=True)]
    unnamed x14 -> x8, local copies, waits for them, and re-layouts: 4.34 us -> 2 us
    ppermute x4, waiting for transfers between devices: 3.11 us -> 1.06 us  [around(): return lax.ppermute(value, ('core', 'head'), up + down)]
    ppermute x4, starting transfers between devices: 11.8 us -> 9.94 us  [around(): return lax.ppermute(value, ('core', 'head'), up + down)]
    ppermute x16 -> x18, waiting for transfers between devices: 17.3 us -> 19.1 us  [moved(): return lax.ppermute(value, SEQ, [(i, place_of(i)) for i in range(count)])]
    pallas_call x1, Pallas kernels: 2.3 us -> 0.9 us  [per_device(): pl.pallas_call(mix_kernel, name='mix', in_specs=[vmem()] * 7, out_specs=[...]
  transfers between devices with their start and end apart: 21 -> 22, of which waited for: 12 -> 17; matrix products, arithmetic and copies ran while one was open for 0% -> 0% of each run, Pallas kernels for 20% -> 19%
where the time goes in v10:
time: 91.6 us; the launch traced here: 91 us
  starting transfers between devices  27.2 us (30%)
  Pallas kernels  21 us (23%)
  waiting for transfers between devices  20.1 us (22%)
  blocking collectives  19.3 us (21%)
  local copies, waits for them, and re-layouts  2.02 us (2%)
  between operations  1.42 us (2%)
    all_to_all x1, blocking collectives, per_device(): lax.all_to_all(flat.reshape(32, part, n), ('yl', 'xl', 'head'), 0, 0, til...  19.3 us
    ppermute x18, waiting for transfers between devices, moved(): return lax.ppermute(value, SEQ, [(i, place_of(i)) for i in range(count)])  19.1 us
    ppermute x18, starting transfers between devices, moved(): return lax.ppermute(value, SEQ, [(i, place_of(i)) for i in range(count)])  17.3 us
    ppermute x4, starting transfers between devices, around(): return lax.ppermute(value, ('core', 'head'), up + down)  9.94 us
    pallas_call x1, Pallas kernels, per_device(): pl.pallas_call(fold_kernel, name='fold', in_specs=[hbm()] * 7, out_specs=...  9.66 us
    pallas_call x1, Pallas kernels, look(): pl.pallas_call(look_kernel, name='look', in_specs=[hbm(), vmem(), hbm()]...  6.21 us
    unnamed x8, local copies, waits for them, and re-layouts  2 us
    pallas_call x1, Pallas kernels, per_device(): pl.pallas_call(take_kernel, name='take', in_specs=[hbm()], out_specs=vmem...  1.87 us
  transfers between devices with their start and end apart: 22, of which 17 were waited for; matrix products, arithmetic and copies ran while one was open for 0% of the time, Pallas kernels for 19%

profile of v10, /device:TPU:1, one launch (start us, length us, event | category | flops | bytes accessed | tf_op | source)
XLA Modules:
  0.0 91.0 jit_solution(4444736586610818628)
XLA Ops:
  0.0 1.9 %take.1.mine_ref = bf16[256,1024]{1,0:T(8,128)(2,1)} custom-call(bf16[256,4096]{1,0:T(8,128)(2,1)} %whole_ref.1), custom_call_target="tpu_custom_call" | custom-call | tf_op jit(solution)/shard_map/take/pallas_call | solution.py:428
  1.9 6.5 %collective-permute-start.13 = (bf16[256,1024]{1,0:T(8,128)(2,1)}, bf16[256,1024]{1,0:T(8,128)(2,1)S(1)}, u32[]{:S(2)}, u32[]{:S(2)}) collective-permute-start(bf16[256,1024]{1,0:T(8,128)(2,1)} %take.1.mine_ref), channel_id=1, source_target_pairs={{0,1},{1,2},{2,3},{3,4},{4,5},{5,6},{6,7},{7,0},{8,15},{9,8},{10,9... | collective-permute-start | bytes 1572872 | tf_op jit(solution)/shard_map/ppermute | solution.py:422
  9.7 9.7 %fold.1 = (bf16[256,512]{1,0:T(8,128)(2,1)}, f32[256,256]{1,0:T(8,128)}, f32[256,512]{1,0:T(8,128)}, f32[256,256]{1,0:T(8,128)}, f32[256,1]{1,0:T(8,128)}) custom-call(f32[1]{0:T(128)S(6)} %copy.10.scale_hbm, f32[1]{0:T(128)S(6)} %copy.11.rate_hbm, bf16[256,4096]{1,0:T(8,128)(2,1)} %x_hbm.3, f32[1,4096]{1,0:T(1,128)} %bitcast.15, ...), custom_call_target="tpu_custom_call" | custom-call | tf_op jit(solution)/shard_map/fold/pallas_call | solution.py:362
  19.3 0.1 collective-permute-start
  19.4 1.7 %collective-permute-done.other_ref.refs_7_ = bf16[256,512]{1,0:T(8,128)(2,1)S(1)} collective-permute-done((bf16[256,512]{1,0:T(8,128)(2,1)}, bf16[256,512]{1,0:T(8,128)(2,1)S(1)}, u32[]{:S(2)}, u32[]{:S(2)}) %collective-permute-start) | collective-permute-done | bytes 262176 | tf_op jit(solution)/shard_map/ppermute | solution.py:408
  21.2 0.0 collective-permute-done.13.one_ref
  21.2 0.7 collective-permute-start.14
  21.9 0.0 copy-start.2
  21.9 0.9 %copy-done.2 = bf16[256,512]{1,0:T(8,128)(2,1)S(1)} copy-done((bf16[256,512]{1,0:T(8,128)(2,1)S(1)}, bf16[256,512]{1,0:T(8,128)(2,1)}, u32[]{:S(2)}) %copy-start.2) | copy-done | bytes 262168
  22.8 0.3 pair.1
  23.1 2.6 %collective-permute-start.3 = (bf16[128,512]{1,0:T(8,128)(2,1)S(1)}, bf16[128,512]{1,0:T(8,128)(2,1)S(1)}, u32[]{:S(2)}, u32[]{:S(2)}) collective-permute-start(bf16[128,512]{1,0:T(8,128)(2,1)S(1)} %get-tuple-element.31), channel_id=1, source_target_pairs={{0,48},{8,56},{16,0},{24,8},{32,16},{40,24},{48,32},{56,40},{64,11... | collective-permute-start | bytes 393224 | tf_op jit(solution)/shard_map/ppermute | solution.py:408
  25.7 0.5 collective-permute-start.2
  26.2 0.6 collective-permute-start.1
  26.8 0.0 copy-start.3
  26.8 6.2 %look.1.refs_8_ = f32[256,512]{1,0:T(8,128)} custom-call(bf16[256,4096]{1,0:T(8,128)(2,1)} %x_hbm.3, f32[1,4096]{1,0:T(1,128)} %bitcast.16, bf16[3,4096,256]{2,1,0:T(8,128)(2,1)} %bitcast.14, f32[256,256]{1,0:T(8,128)} %get-tuple-element.32.key_ref, f32[256,512]{1,0:T(8,128)} %get-tuple-element.33.solved_ref, f32[256,256]{1,0:T(8,128)} %get-tuple-element.34.decay_ref, ...), custom_call_target="tpu_custom_call" | custom-call | flops 1073741824 | bytes 16777216 | tf_op jit(solution)/shard_map/look/pallas_call | solution.py:392
  33.0 0.0 collective-permute-done.3.refs_2_
  33.0 0.0 collective-permute-done.2.refs_1_
  33.0 2.4 %collective-permute-done.1.refs_0_ = bf16[128,512]{1,0:T(8,128)(2,1)S(1)} collective-permute-done((bf16[128,512]{1,0:T(8,128)(2,1)S(1)}, bf16[128,512]{1,0:T(8,128)(2,1)S(1)}, u32[]{:S(2)}, u32[]{:S(2)}) %collective-permute-start.1) | collective-permute-done | bytes 131104 | tf_op jit(solution)/shard_map/ppermute | solution.py:408
  35.5 0.0 collective-permute-done.14.two_ref
  35.5 0.6 collective-permute-start.15
  36.1 0.7 collective-permute-start.4
  36.8 0.0 collective-permute-start.5
  36.8 0.5 collective-permute-start.6
  37.3 0.5 collective-permute-done.4.refs_3_
  37.8 0.4 collective-permute-done.5.refs_4_
  38.1 0.2 collective-permute-done.6.refs_5_
  38.3 0.6 row.1
  38.9 0.0 copy-start
  38.9 2.8 %collective-permute-start.9 = (bf16[128,512]{1,0:T(8,128)(2,1)S(1)}, bf16[128,512]{1,0:T(8,128)(2,1)S(1)}, u32[]{:S(2)}, u32[]{:S(2)}) collective-permute-start(bf16[128,512]{1,0:T(8,128)(2,1)S(1)} %get-tuple-element.39), channel_id=1, source_target_pairs={{0,192},{8,200},{16,208},{24,216},{32,224},{40,232},{48,240},{56,2... | collective-permute-start | bytes 393224 | tf_op jit(solution)/shard_map/ppermute | solution.py:408
  41.7 0.4 collective-permute-start.8
  42.1 0.7 collective-permute-start.7
  42.7 1.1 %collective-permute-done.15.three_ref = bf16[256,1024]{1,0:T(8,128)(2,1)S(1)} collective-permute-done((bf16[256,1024]{1,0:T(8,128)(2,1)S(1)}, bf16[256,1024]{1,0:T(8,128)(2,1)S(1)}, u32[]{:S(2)}, u32[]{:S(2)}) %collective-permute-start.15) | collective-permute-done | bytes 524320 | tf_op jit(solution)/shard_map/ppermute | solution.py:422
  43.8 3.1 %collective-permute-done.9.refs_2_ = bf16[128,512]{1,0:T(8,128)(2,1)S(1)} collective-permute-done((bf16[128,512]{1,0:T(8,128)(2,1)S(1)}, bf16[128,512]{1,0:T(8,128)(2,1)S(1)}, u32[]{:S(2)}, u32[]{:S(2)}) %collective-permute-start.9) | collective-permute-done | bytes 131104 | tf_op jit(solution)/shard_map/ppermute | solution.py:408
  46.9 0.7 collective-permute-done.8.refs_1_
  47.7 3.8 %collective-permute-done.7.refs_0_ = bf16[128,512]{1,0:T(8,128)(2,1)S(1)} collective-permute-done((bf16[128,512]{1,0:T(8,128)(2,1)S(1)}, bf16[128,512]{1,0:T(8,128)(2,1)S(1)}, u32[]{:S(2)}, u32[]{:S(2)}) %collective-permute-start.7) | collective-permute-done | bytes 131104 | tf_op jit(solution)/shard_map/ppermute | solution.py:408
  51.4 2.1 %collective-permute-start.16 = (bf16[256,512]{1,0:T(8,128)(2,1)S(1)}, bf16[256,512]{1,0:T(8,128)(2,1)S(1)}, u32[]{:S(2)}, u32[]{:S(2)}) collective-permute-start(bf16[256,512]{1,0:T(8,128)(2,1)S(1)} %constant_dynamic-slice_fusion), channel_id=1, source_target_pairs={{0,1},{1,2},{2,3},{3,4},{4,5},{5,6},{6,7},{7,0},{8,15},{9,8},{10,9... | collective-permute-start | bytes 786440 | tf_op jit(solution)/shard_map/ppermute | solution.py:422
  53.5 0.0 collective-permute-start.12
  53.5 0.5 collective-permute-start.11
  54.1 0.0 collective-permute-start.10
  54.1 0.8 collective-permute-done.12.refs_5_
  54.9 0.2 collective-permute-done.11.refs_4_
  55.1 0.3 collective-permute-done.10.refs_3_
  55.4 0.0 copy-done.3
  55.4 0.0 copy-start.1
  55.4 1.0 %copy-done.1 = f32[256,512]{1,0:T(8,128)S(1)} copy-done((f32[256,512]{1,0:T(8,128)S(1)}, f32[256,512]{1,0:T(8,128)}, u32[]{:S(2)}) %copy-start.1) | copy-done | bytes 524312
  56.4 0.7 read.1
  57.2 0.0 collective-permute-done.16.four_ref
  57.2 19.3 %all_to_all.5 = bf16[32,32,256]{2,1,0:T(8,128)(2,1)S(1)} all-to-all(bf16[32,32,256]{2,1,0:T(8,128)(2,1)S(1)} %bitcast.11), channel_id=1, replica_groups=mesh['yh'=2,'yl'=2,'xh'=2,'xl'=2,'core'=2,'head'=8] {'yl','xl','head'}, dimensions={0} | all-to-all | bytes 1048576 | tf_op jit(solution)/shard_map/all_to_all | solution.py:481
  76.4 4.5 %collective-permute-start.17 = (bf16[4,8,32,256]{3,2,1,0:T(8,128)(2,1)S(1)}, bf16[4,8,32,256]{3,2,1,0:T(8,128)(2,1)S(1)}, u32[]{:S(2)}, u32[]{:S(2)}) collective-permute-start(bf16[4,8,32,256]{3,2,1,0:T(8,128)(2,1)S(1)} %bitcast.9), channel_id=1, source_target_pairs={{0,8},{8,0},{16,24},{24,16},{32,40},{40,32},{48,56},{56,48},{64,72... | collective-permute-start | bytes 1572872 | tf_op jit(solution)/shard_map/ppermute | solution.py:408
  80.9 1.5 %collective-permute-done.17.other_ref = bf16[4,8,32,256]{3,2,1,0:T(8,128)(2,1)S(1)} collective-permute-done((bf16[4,8,32,256]{3,2,1,0:T(8,128)(2,1)S(1)}, bf16[4,8,32,256]{3,2,1,0:T(8,128)(2,1)S(1)}, u32[]{:S(2)}, u32[]{:S(2)}) %collective-permute-start.17) | collective-permute-done | bytes 524320 | tf_op jit(solution)/shard_map/ppermute | solution.py:408
  82.4 0.0 copy-done
  82.4 0.9 mix.1
  83.3 0.8 collective-permute-start.18
  84.1 1.2 %collective-permute-done.18.come_ref = bf16[128,1024]{1,0:T(8,128)(2,1)S(1)} collective-permute-done((bf16[128,1024]{1,0:T(8,128)(2,1)S(1)}, bf16[128,1024]{1,0:T(8,128)(2,1)S(1)}, u32[]{:S(2)}, u32[]{:S(2)}) %collective-permute-start.18) | collective-permute-done | bytes 262176 | tf_op jit(solution)/shard_map/ppermute | solution.py:408
  85.3 0.1 collective-permute-start.19
  85.4 0.8 collective-permute-start.20
  86.2 1.9 %collective-permute-start.21 = (bf16[32,1024]{1,0:T(8,128)(2,1)S(1)}, bf16[32,1024]{1,0:T(8,128)(2,1)S(1)}, u32[]{:S(2)}, u32[]{:S(2)}) collective-permute-start(bf16[32,1024]{1,0:T(8,128)(2,1)S(1)} %get-tuple-element.52), channel_id=1, source_target_pairs={{0,80},{8,88},{16,64},{24,72},{32,112},{40,120},{48,96},{56,104},{... | collective-permute-start | bytes 196616 | tf_op jit(solution)/shard_map/ppermute | solution.py:408
  88.0 0.5 collective-permute-done.19.refs_1_
  88.5 0.1 collective-permute-done.20.refs_2_
  88.6 1.6 %collective-permute-done.21.refs_3_ = bf16[32,1024]{1,0:T(8,128)(2,1)S(1)} collective-permute-done((bf16[32,1024]{1,0:T(8,128)(2,1)S(1)}, bf16[32,1024]{1,0:T(8,128)(2,1)S(1)}, u32[]{:S(2)}, u32[]{:S(2)}) %collective-permute-start.21) | collective-permute-done | bytes 65568 | tf_op jit(solution)/shard_map/ppermute | solution.py:408
  90.3 0.7 lay.1
  (2 shorter events, 0.1 us)
Async XLA Ops:
  1.9 19.3 %collective-permute-start.13 = (bf16[256,1024]{1,0:T(8,128)(2,1)}, bf16[256,1024]{1,0:T(8,128)(2,1)S(1)}, u32[]{:S(2)}, u32[]{:S(2)}) collective-permute-start(bf16[256,1024]{1,0:T(8,128)(2,1)} %take.1.mine_ref), channel_id=1, source_target_pairs={{0,1},{1,2},{2,3},{3,4},{4,5},{5,6},{6,7},{7,0},{8,15},{9,8},{10,9... | collective-permute-start | bytes 1572872 | tf_op jit(solution)/shard_map/ppermute | solution.py:422
  19.3 1.8 %collective-permute-start = (bf16[256,512]{1,0:T(8,128)(2,1)}, bf16[256,512]{1,0:T(8,128)(2,1)S(1)}, u32[]{:S(2)}, u32[]{:S(2)}) collective-permute-start(bf16[256,512]{1,0:T(8,128)(2,1)} %get-tuple-element.29.own_ref), channel_id=1, source_target_pairs={{0,8},{8,0},{16,24},{24,16},{32,40},{40,32},{48,56},{56,48},{64,72... | collective-permute-start | bytes 786440 | tf_op jit(solution)/shard_map/ppermute | solution.py:408
  21.2 14.3 %collective-permute-start.14 = (bf16[256,1024]{1,0:T(8,128)(2,1)S(1)}, bf16[256,1024]{1,0:T(8,128)(2,1)S(1)}, u32[]{:S(2)}, u32[]{:S(2)}) collective-permute-start(bf16[256,1024]{1,0:T(8,128)(2,1)S(1)} %collective-permute-done.13.one_ref), channel_id=1, source_target_pairs={{0,1},{1,2},{2,3},{3,4},{4,5},{5,6},{6,7},{7,0},{8,15},{9,8},{10,9... | collective-permute-start | bytes 1572872 | tf_op jit(solution)/shard_map/ppermute | solution.py:422
  21.9 0.9 %copy-start.2 = (bf16[256,512]{1,0:T(8,128)(2,1)S(1)}, bf16[256,512]{1,0:T(8,128)(2,1)}, u32[]{:S(2)}) copy-start(bf16[256,512]{1,0:T(8,128)(2,1)} %get-tuple-element.29.own_ref) | copy-start | bytes 786436
  23.1 9.9 %collective-permute-start.3 = (bf16[128,512]{1,0:T(8,128)(2,1)S(1)}, bf16[128,512]{1,0:T(8,128)(2,1)S(1)}, u32[]{:S(2)}, u32[]{:S(2)}) collective-permute-start(bf16[128,512]{1,0:T(8,128)(2,1)S(1)} %get-tuple-element.31), channel_id=1, source_target_pairs={{0,48},{8,56},{16,0},{24,8},{32,16},{40,24},{48,32},{56,40},{64,11... | collective-permute-start | bytes 393224 | tf_op jit(solution)/shard_map/ppermute | solution.py:408
  25.7 7.4 %collective-permute-start.2 = (bf16[128,512]{1,0:T(8,128)(2,1)S(1)}, bf16[128,512]{1,0:T(8,128)(2,1)S(1)}, u32[]{:S(2)}, u32[]{:S(2)}) collective-permute-start(bf16[128,512]{1,0:T(8,128)(2,1)S(1)} %get-tuple-element.31), channel_id=1, source_target_pairs={{0,32},{8,40},{16,48},{24,56},{32,0},{40,8},{48,16},{56,24},{64,96... | collective-permute-start | bytes 393224 | tf_op jit(solution)/shard_map/ppermute | solution.py:408
  26.2 9.3 %collective-permute-start.1 = (bf16[128,512]{1,0:T(8,128)(2,1)S(1)}, bf16[128,512]{1,0:T(8,128)(2,1)S(1)}, u32[]{:S(2)}, u32[]{:S(2)}) collective-permute-start(bf16[128,512]{1,0:T(8,128)(2,1)S(1)} %get-tuple-element.31), channel_id=1, source_target_pairs={{0,16},{8,24},{16,32},{24,40},{32,48},{40,56},{48,0},{56,8},{64,80... | collective-permute-start | bytes 393224 | tf_op jit(solution)/shard_map/ppermute | solution.py:408
  26.8 28.6 %copy-start.3 = (f32[256]{0:T(256)S(1)}, f32[256]{0:T(256)}, u32[]{:S(2)}) copy-start(f32[256]{0:T(256)} %param.16) | copy-start | bytes 3076
  35.5 8.3 %collective-permute-start.15 = (bf16[256,1024]{1,0:T(8,128)(2,1)S(1)}, bf16[256,1024]{1,0:T(8,128)(2,1)S(1)}, u32[]{:S(2)}, u32[]{:S(2)}) collective-permute-start(bf16[256,1024]{1,0:T(8,128)(2,1)S(1)} %collective-permute-done.14.two_ref), channel_id=1, source_target_pairs={{0,1},{1,2},{2,3},{3,4},{4,5},{5,6},{6,7},{7,0},{8,15},{9,8},{10,9... | collective-permute-start | bytes 1572872 | tf_op jit(solution)/shard_map/ppermute | solution.py:422
  36.1 1.7 %collective-permute-start.4 = (bf16[128,512]{1,0:T(8,128)(2,1)S(1)}, bf16[128,512]{1,0:T(8,128)(2,1)S(1)}, u32[]{:S(2)}, u32[]{:S(2)}) collective-permute-start(bf16[128,512]{1,0:T(8,128)(2,1)S(1)} %collective-permute-done.1.refs_0_), channel_id=1, source_target_pairs={{0,8},{8,0},{16,24},{24,16},{32,40},{40,32},{48,56},{56,48},{64,72... | collective-permute-start | bytes 393224 | tf_op jit(solution)/shard_map/ppermute | solution.py:408
  36.8 1.3 %collective-permute-start.5 = (bf16[128,512]{1,0:T(8,128)(2,1)S(1)}, bf16[128,512]{1,0:T(8,128)(2,1)S(1)}, u32[]{:S(2)}, u32[]{:S(2)}) collective-permute-start(bf16[128,512]{1,0:T(8,128)(2,1)S(1)} %collective-permute-done.2.refs_1_), channel_id=1, source_target_pairs={{0,8},{8,0},{16,24},{24,16},{32,40},{40,32},{48,56},{56,48},{64,72... | collective-permute-start | bytes 393224 | tf_op jit(solution)/shard_map/ppermute | solution.py:408
  36.8 1.5 %collective-permute-start.6 = (bf16[128,512]{1,0:T(8,128)(2,1)S(1)}, bf16[128,512]{1,0:T(8,128)(2,1)S(1)}, u32[]{:S(2)}, u32[]{:S(2)}) collective-permute-start(bf16[128,512]{1,0:T(8,128)(2,1)S(1)} %collective-permute-done.3.refs_2_), channel_id=1, source_target_pairs={{0,8},{8,0},{16,24},{24,16},{32,40},{40,32},{48,56},{56,48},{64,72... | collective-permute-start | bytes 393224 | tf_op jit(solution)/shard_map/ppermute | solution.py:408
  38.9 43.5 %copy-start = (bf16[256,1024]{1,0:T(8,128)(2,1)S(1)}, bf16[256,1024]{1,0:T(8,128)(2,1)}, u32[]{:S(2)}) copy-start(bf16[256,1024]{1,0:T(8,128)(2,1)} %take.1.mine_ref) | copy-start | bytes 1572868
  38.9 8.0 %collective-permute-start.9 = (bf16[128,512]{1,0:T(8,128)(2,1)S(1)}, bf16[128,512]{1,0:T(8,128)(2,1)S(1)}, u32[]{:S(2)}, u32[]{:S(2)}) collective-permute-start(bf16[128,512]{1,0:T(8,128)(2,1)S(1)} %get-tuple-element.39), channel_id=1, source_target_pairs={{0,192},{8,200},{16,208},{24,216},{32,224},{40,232},{48,240},{56,2... | collective-permute-start | bytes 393224 | tf_op jit(solution)/shard_map/ppermute | solution.py:408
  41.7 6.0 %collective-permute-start.8 = (bf16[128,512]{1,0:T(8,128)(2,1)S(1)}, bf16[128,512]{1,0:T(8,128)(2,1)S(1)}, u32[]{:S(2)}, u32[]{:S(2)}) collective-permute-start(bf16[128,512]{1,0:T(8,128)(2,1)S(1)} %get-tuple-element.39), channel_id=1, source_target_pairs={{0,128},{8,136},{16,144},{24,152},{32,160},{40,168},{48,176},{56,1... | collective-permute-start | bytes 393224 | tf_op jit(solution)/shard_map/ppermute | solution.py:408
  42.1 9.4 %collective-permute-start.7 = (bf16[128,512]{1,0:T(8,128)(2,1)S(1)}, bf16[128,512]{1,0:T(8,128)(2,1)S(1)}, u32[]{:S(2)}, u32[]{:S(2)}) collective-permute-start(bf16[128,512]{1,0:T(8,128)(2,1)S(1)} %get-tuple-element.39), channel_id=1, source_target_pairs={{0,64},{8,72},{16,80},{24,88},{32,96},{40,104},{48,112},{56,120},{... | collective-permute-start | bytes 393224 | tf_op jit(solution)/shard_map/ppermute | solution.py:408
  51.4 5.7 %collective-permute-start.16 = (bf16[256,512]{1,0:T(8,128)(2,1)S(1)}, bf16[256,512]{1,0:T(8,128)(2,1)S(1)}, u32[]{:S(2)}, u32[]{:S(2)}) collective-permute-start(bf16[256,512]{1,0:T(8,128)(2,1)S(1)} %constant_dynamic-slice_fusion), channel_id=1, source_target_pairs={{0,1},{1,2},{2,3},{3,4},{4,5},{5,6},{6,7},{7,0},{8,15},{9,8},{10,9... | collective-permute-start | bytes 786440 | tf_op jit(solution)/shard_map/ppermute | solution.py:422
  53.5 1.3 %collective-permute-start.12 = (bf16[128,512]{1,0:T(8,128)(2,1)S(1)}, bf16[128,512]{1,0:T(8,128)(2,1)S(1)}, u32[]{:S(2)}, u32[]{:S(2)}) collective-permute-start(bf16[128,512]{1,0:T(8,128)(2,1)S(1)} %collective-permute-done.9.refs_2_), channel_id=1, source_target_pairs={{0,8},{8,0},{16,24},{24,16},{32,40},{40,32},{48,56},{56,48},{64,72... | collective-permute-start | bytes 393224 | tf_op jit(solution)/shard_map/ppermute | solution.py:408
  53.5 1.5 %collective-permute-start.11 = (bf16[128,512]{1,0:T(8,128)(2,1)S(1)}, bf16[128,512]{1,0:T(8,128)(2,1)S(1)}, u32[]{:S(2)}, u32[]{:S(2)}) collective-permute-start(bf16[128,512]{1,0:T(8,128)(2,1)S(1)} %collective-permute-done.8.refs_1_), channel_id=1, source_target_pairs={{0,8},{8,0},{16,24},{24,16},{32,40},{40,32},{48,56},{56,48},{64,72... | collective-permute-start | bytes 393224 | tf_op jit(solution)/shard_map/ppermute | solution.py:408
  54.1 1.3 %collective-permute-start.10 = (bf16[128,512]{1,0:T(8,128)(2,1)S(1)}, bf16[128,512]{1,0:T(8,128)(2,1)S(1)}, u32[]{:S(2)}, u32[]{:S(2)}) collective-permute-start(bf16[128,512]{1,0:T(8,128)(2,1)S(1)} %collective-permute-done.7.refs_0_), channel_id=1, source_target_pairs={{0,8},{8,0},{16,24},{24,16},{32,40},{40,32},{48,56},{56,48},{64,72... | collective-permute-start | bytes 393224 | tf_op jit(solution)/shard_map/ppermute | solution.py:408
  55.4 1.0 %copy-start.1 = (f32[256,512]{1,0:T(8,128)S(1)}, f32[256,512]{1,0:T(8,128)}, u32[]{:S(2)}) copy-start(f32[256,512]{1,0:T(8,128)} %look.1.refs_8_) | copy-start | bytes 1572868
  76.4 6.0 %collective-permute-start.17 = (bf16[4,8,32,256]{3,2,1,0:T(8,128)(2,1)S(1)}, bf16[4,8,32,256]{3,2,1,0:T(8,128)(2,1)S(1)}, u32[]{:S(2)}, u32[]{:S(2)}) collective-permute-start(bf16[4,8,32,256]{3,2,1,0:T(8,128)(2,1)S(1)} %bitcast.9), channel_id=1, source_target_pairs={{0,8},{8,0},{16,24},{24,16},{32,40},{40,32},{48,56},{56,48},{64,72... | collective-permute-start | bytes 1572872 | tf_op jit(solution)/shard_map/ppermute | solution.py:408
  83.3 1.9 %collective-permute-start.18 = (bf16[128,1024]{1,0:T(8,128)(2,1)S(1)}, bf16[128,1024]{1,0:T(8,128)(2,1)S(1)}, u32[]{:S(2)}, u32[]{:S(2)}) collective-permute-start(bf16[128,1024]{1,0:T(8,128)(2,1)S(1)} %get-tuple-element.48), channel_id=1, source_target_pairs={{0,8},{8,0},{16,24},{24,16},{32,40},{40,32},{48,56},{56,48},{64,72... | collective-permute-start | bytes 786440 | tf_op jit(solution)/shard_map/ppermute | solution.py:408
  85.3 3.2 %collective-permute-start.19 = (bf16[32,1024]{1,0:T(8,128)(2,1)S(1)}, bf16[32,1024]{1,0:T(8,128)(2,1)S(1)}, u32[]{:S(2)}, u32[]{:S(2)}) collective-permute-start(bf16[32,1024]{1,0:T(8,128)(2,1)S(1)} %get-tuple-element.50), channel_id=1, source_target_pairs={{0,16},{8,24},{16,0},{24,8},{32,48},{40,56},{48,32},{56,40},{64,80... | collective-permute-start | bytes 196616 | tf_op jit(solution)/shard_map/ppermute | solution.py:408
  85.4 3.2 %collective-permute-start.20 = (bf16[32,1024]{1,0:T(8,128)(2,1)S(1)}, bf16[32,1024]{1,0:T(8,128)(2,1)S(1)}, u32[]{:S(2)}, u32[]{:S(2)}) collective-permute-start(bf16[32,1024]{1,0:T(8,128)(2,1)S(1)} %get-tuple-element.51), channel_id=1, source_target_pairs={{0,64},{8,72},{16,80},{24,88},{32,96},{40,104},{48,112},{56,120},{... | collective-permute-start | bytes 196616 | tf_op jit(solution)/shard_map/ppermute | solution.py:408
  86.2 4.1 %collective-permute-start.21 = (bf16[32,1024]{1,0:T(8,128)(2,1)S(1)}, bf16[32,1024]{1,0:T(8,128)(2,1)S(1)}, u32[]{:S(2)}, u32[]{:S(2)}) collective-permute-start(bf16[32,1024]{1,0:T(8,128)(2,1)S(1)} %get-tuple-element.52), channel_id=1, source_target_pairs={{0,80},{8,88},{16,64},{24,72},{32,112},{40,120},{48,96},{56,104},{... | collective-permute-start | bytes 196616 | tf_op jit(solution)/shard_map/ppermute | solution.py:408

commit v11 on v10

--- a/solution.py
+++ b/solution.py
@@ -416,9 +416,9 @@
     def flip(bits):
         return lambda i: i ^ bits
 
-    def around(value):
-        up = [(z, (z + 1) % 8) for z in range(8)]
-        down = [(8 + z, 8 + (z + 7) % 8) for z in range(8)]
+    def around(value, steps):
+        up = [(z, (z + steps) % 8) for z in range(8)]
+        down = [(8 + z, 8 + (z + 8 - steps) % 8) for z in range(8)]
         return lax.ppermute(value, ("core", "head"), up + down)
 
     def later(value, gate):
@@ -434,12 +434,12 @@
         scratch_shapes=[pltpu.SemaphoreType.DMA],
         compiler_params=LARGE,
     )(out_weight)
-    one = around(mine)
+    one = around(mine, 1)
+    two = around(mine, 2)
 
     pair_shape = jax.ShapeDtypeStruct((n, 2 * n), BF16)
     half_shape = jax.ShapeDtypeStruct((n // 2, 2 * n), BF16)
     other = moved(carry, flip(1))
-    two = around(later(one, other))
     pair, half = pl.pallas_call(
         pair_kernel,
         name="pair",
@@ -450,7 +450,12 @@
     )(carry, other)
     near = [moved(half, along_x(s)) for s in (1, 2, 3)]
     near, looked = lax.optimization_barrier((near, look()))
-    three = around(later(two, near))
+    ready = later(two, near)
+    three = around(ready, 1)
+    part_two = lax.dynamic_slice_in_dim(
+        ready, lax.axis_index("core") * (wide // 2), wide // 2, 1
+    )
+    four = around(part_two, 2)
     swapped = [moved(value, flip(1)) for value in near]
     half, prefix = pl.pallas_call(
         row_kernel,
@@ -462,10 +467,7 @@
         compiler_params=SMALL,
     )(pair, *near, *swapped)
     near = [moved(half, along_y(s)) for s in (1, 2, 3)]
-    part_three = lax.dynamic_slice_in_dim(
-        three, lax.axis_index("core") * (wide // 2), wide // 2, 1
-    )
-    four = around(later(part_three, near))
+    near, three, four = lax.optimization_barrier((near, three, four))
     swapped = [moved(value, flip(1)) for value in near]
     flat = pl.pallas_call(
         read_kernel,
@@ -477,7 +479,6 @@
         compiler_params=SMALL,
     )(*near, *swapped, prefix, other, looked, out_gain.reshape(1, n))
     part = rows // 8
-    flat, four = lax.optimization_barrier((flat, four))
     reads = lax.all_to_all(
         flat.reshape(32, part, n), ("yl", "xl", "head"), 0, 0, tiled=True
     ).reshape(4, 8, part, n)

time: 91.6 us -> 92.9 us (1.014)
  blocking collectives: 19.3 us -> 0 us
  starting transfers between devices: 27.2 us -> 39.4 us
  waiting for transfers between devices: 20.1 us -> 27.2 us
    all_to_all x1 -> x0, blocking collectives: 19.3 us -> none  [per_device(): lax.all_to_all(flat.reshape(32, part, n), ('yl', 'xl', 'head'), 0, 0, til...]
    all_to_all x0 -> x1, waiting for transfers between devices: none -> 12.1 us  [per_device(): lax.all_to_all(flat.reshape(32, part, n), ('yl', 'xl', 'head'), 0, 0, til...]
    all_to_all x0 -> x1, starting transfers between devices: none -> 7.11 us  [per_device(): lax.all_to_all(flat.reshape(32, part, n), ('yl', 'xl', 'head'), 0, 0, til...]
    ppermute x18, waiting for transfers between devices: 19.1 us -> 12.2 us  [moved(): return lax.ppermute(value, SEQ, [(i, place_of(i)) for i in range(count)])]
    ppermute x18, starting transfers between devices: 17.3 us -> 20.8 us  [moved(): return lax.ppermute(value, SEQ, [(i, place_of(i)) for i in range(count)])]
    ppermute x4, waiting for transfers between devices: 1.06 us -> 2.95 us  [around(): return lax.ppermute(value, ('core', 'head'), up + down)]
    ppermute x4, starting transfers between devices: 9.94 us -> 11.5 us  [around(): return lax.ppermute(value, ('core', 'head'), up + down)]
  transfers between devices with their start and end apart: 22 -> 23, of which waited for: 17 -> 14; matrix products, arithmetic and copies ran while one was open for 0% -> 0% of each run, Pallas kernels for 19% -> 18%
where the time goes in v11:
time: 92.9 us; the launch traced here: 91.8 us
  starting transfers between devices  39.4 us (42%)
  waiting for transfers between devices  27.2 us (29%)
  Pallas kernels  21.8 us (23%)
  local copies, waits for them, and re-layouts  2.02 us (2%)
  between operations  1.44 us (2%)
    ppermute x18, starting transfers between devices, moved(): return lax.ppermute(value, SEQ, [(i, place_of(i)) for i in range(count)])  20.8 us
    ppermute x18, waiting for transfers between devices, moved(): return lax.ppermute(value, SEQ, [(i, place_of(i)) for i in range(count)])  12.2 us
    all_to_all x1, waiting for transfers between devices, per_device(): lax.all_to_all(flat.reshape(32, part, n), ('yl', 'xl', 'head'), 0, 0, til...  12.1 us
    ppermute x4, starting transfers between devices, around(): return lax.ppermute(value, ('core', 'head'), up + down)  11.5 us
    pallas_call x1, Pallas kernels, per_device(): pl.pallas_call(fold_kernel, name='fold', in_specs=[hbm()] * 7, out_specs=...  9.67 us
    all_to_all x1, starting transfers between devices, per_device(): lax.all_to_all(flat.reshape(32, part, n), ('yl', 'xl', 'head'), 0, 0, til...  7.11 us
    pallas_call x1, Pallas kernels, look(): pl.pallas_call(look_kernel, name='look', in_specs=[hbm(), vmem(), hbm()]...  6.2 us
    ppermute x4, waiting for transfers between devices, around(): return lax.ppermute(value, ('core', 'head'), up + down)  2.95 us
  transfers between devices with their start and end apart: 23, of which 14 were waited for; matrix products, arithmetic and copies ran while one was open for 0% of the time, Pallas kernels for 18%

profile of v11, /device:TPU:1, one launch (start us, length us, event | category | flops | bytes accessed | tf_op | source)
XLA Modules:
  0.0 91.8 jit_solution(8936365651945146853)
XLA Ops:
  0.0 1.9 %take.1.mine_ref = bf16[256,1024]{1,0:T(8,128)(2,1)} custom-call(bf16[256,4096]{1,0:T(8,128)(2,1)} %whole_ref.1), custom_call_target="tpu_custom_call" | custom-call | tf_op jit(solution)/shard_map/take/pallas_call | solution.py:428
  1.9 6.9 %collective-permute-start.10 = (bf16[256,1024]{1,0:T(8,128)(2,1)}, bf16[256,1024]{1,0:T(8,128)(2,1)S(1)}, u32[]{:S(2)}, u32[]{:S(2)}) collective-permute-start(bf16[256,1024]{1,0:T(8,128)(2,1)} %take.1.mine_ref), channel_id=1, source_target_pairs={{0,2},{1,3},{2,4},{3,5},{4,6},{5,7},{6,0},{7,1},{8,14},{9,15},{10,... | collective-permute-start | bytes 1572872 | tf_op jit(solution)/shard_map/ppermute | solution.py:422
  10.1 9.7 %fold.1 = (bf16[256,512]{1,0:T(8,128)(2,1)}, f32[256,256]{1,0:T(8,128)}, f32[256,512]{1,0:T(8,128)}, f32[256,256]{1,0:T(8,128)}, f32[256,1]{1,0:T(8,128)}) custom-call(f32[1]{0:T(128)S(6)} %copy.10.scale_hbm, f32[1]{0:T(128)S(6)} %copy.11.rate_hbm, bf16[256,4096]{1,0:T(8,128)(2,1)} %x_hbm.3, f32[1,4096]{1,0:T(1,128)} %bitcast.14, ...), custom_call_target="tpu_custom_call" | custom-call | tf_op jit(solution)/shard_map/fold/pallas_call | solution.py:362
  19.8 0.1 collective-permute-start
  19.9 1.7 %collective-permute-done.other_ref.refs_7_ = bf16[256,512]{1,0:T(8,128)(2,1)S(1)} collective-permute-done((bf16[256,512]{1,0:T(8,128)(2,1)}, bf16[256,512]{1,0:T(8,128)(2,1)S(1)}, u32[]{:S(2)}, u32[]{:S(2)}) %collective-permute-start) | collective-permute-done | bytes 262176 | tf_op jit(solution)/shard_map/ppermute | solution.py:408
  21.6 0.0 copy-start.2
  21.6 0.9 %copy-done.2 = bf16[256,512]{1,0:T(8,128)(2,1)S(1)} copy-done((bf16[256,512]{1,0:T(8,128)(2,1)S(1)}, bf16[256,512]{1,0:T(8,128)(2,1)}, u32[]{:S(2)}) %copy-start.2) | copy-done | bytes 262168
  22.6 0.3 pair.1
  22.8 1.3 %collective-permute-start.1 = (bf16[128,512]{1,0:T(8,128)(2,1)S(1)}, bf16[128,512]{1,0:T(8,128)(2,1)S(1)}, u32[]{:S(2)}, u32[]{:S(2)}) collective-permute-start(bf16[128,512]{1,0:T(8,128)(2,1)S(1)} %get-tuple-element.32), channel_id=1, source_target_pairs={{0,16},{8,24},{16,32},{24,40},{32,48},{40,56},{48,0},{56,8},{64,80... | collective-permute-start | bytes 393224 | tf_op jit(solution)/shard_map/ppermute | solution.py:408
  24.1 2.4 %collective-permute-start.2 = (bf16[128,512]{1,0:T(8,128)(2,1)S(1)}, bf16[128,512]{1,0:T(8,128)(2,1)S(1)}, u32[]{:S(2)}, u32[]{:S(2)}) collective-permute-start(bf16[128,512]{1,0:T(8,128)(2,1)S(1)} %get-tuple-element.32), channel_id=1, source_target_pairs={{0,32},{8,40},{16,48},{24,56},{32,0},{40,8},{48,16},{56,24},{64,96... | collective-permute-start | bytes 393224 | tf_op jit(solution)/shard_map/ppermute | solution.py:408
  26.6 1.2 %collective-permute-start.3 = (bf16[128,512]{1,0:T(8,128)(2,1)S(1)}, bf16[128,512]{1,0:T(8,128)(2,1)S(1)}, u32[]{:S(2)}, u32[]{:S(2)}) collective-permute-start(bf16[128,512]{1,0:T(8,128)(2,1)S(1)} %get-tuple-element.32), channel_id=1, source_target_pairs={{0,48},{8,56},{16,0},{24,8},{32,16},{40,24},{48,32},{56,40},{64,11... | collective-permute-start | bytes 393224 | tf_op jit(solution)/shard_map/ppermute | solution.py:408
  27.7 0.0 copy-start.3
  27.7 6.2 %look.1.refs_8_ = f32[256,512]{1,0:T(8,128)} custom-call(bf16[256,4096]{1,0:T(8,128)(2,1)} %x_hbm.3, f32[1,4096]{1,0:T(1,128)} %bitcast.15, bf16[3,4096,256]{2,1,0:T(8,128)(2,1)} %bitcast.13, f32[256,256]{1,0:T(8,128)} %get-tuple-element.33.key_ref, f32[256,512]{1,0:T(8,128)} %get-tuple-element.34.solved_ref, f32[256,256]{1,0:T(8,128)} %get-tuple-element.35.decay_ref, ...), custom_call_target="tpu_custom_call" | custom-call | flops 1073741824 | bytes 16777216 | tf_op jit(solution)/shard_map/look/pallas_call | solution.py:392
  33.9 0.0 collective-permute-done.1.refs_0_
  34.0 0.0 collective-permute-done.2.refs_1_
  34.0 0.0 collective-permute-done.3.refs_2_
  34.0 0.0 collective-permute-done.10.two_ref
  34.0 0.8 collective-permute-start.11
  34.8 1.3 %collective-permute-start.4 = (bf16[128,512]{1,0:T(8,128)(2,1)S(1)}, bf16[128,512]{1,0:T(8,128)(2,1)S(1)}, u32[]{:S(2)}, u32[]{:S(2)}) collective-permute-start(bf16[128,512]{1,0:T(8,128)(2,1)S(1)} %collective-permute-done.1.refs_0_), channel_id=1, source_target_pairs={{0,8},{8,0},{16,24},{24,16},{32,40},{40,32},{48,56},{56,48},{64,72... | collective-permute-start | bytes 393224 | tf_op jit(solution)/shard_map/ppermute | solution.py:408
  36.1 0.0 collective-permute-start.5
  36.1 0.5 collective-permute-start.6
  36.6 1.2 %collective-permute-start.12 = (bf16[256,512]{1,0:T(8,128)(2,1)S(1)}, bf16[256,512]{1,0:T(8,128)(2,1)S(1)}, u32[]{:S(2)}, u32[]{:S(2)}) collective-permute-start(bf16[256,512]{1,0:T(8,128)(2,1)S(1)} %constant_dynamic-slice_fusion), channel_id=1, source_target_pairs={{0,2},{1,3},{2,4},{3,5},{4,6},{5,7},{6,0},{7,1},{8,14},{9,15},{10,... | collective-permute-start | bytes 786440 | tf_op jit(solution)/shard_map/ppermute | solution.py:422
  37.8 0.0 collective-permute-done.4.refs_3_
  37.8 0.0 collective-permute-done.5.refs_4_
  37.8 0.0 collective-permute-done.6.refs_5_
  37.8 0.0 copy-start
  37.9 0.6 row.1
  38.4 1.4 %collective-permute-start.7 = (bf16[128,512]{1,0:T(8,128)(2,1)S(1)}, bf16[128,512]{1,0:T(8,128)(2,1)S(1)}, u32[]{:S(2)}, u32[]{:S(2)}) collective-permute-start(bf16[128,512]{1,0:T(8,128)(2,1)S(1)} %get-tuple-element.40), channel_id=1, source_target_pairs={{0,64},{8,72},{16,80},{24,88},{32,96},{40,104},{48,112},{56,120},{... | collective-permute-start | bytes 393224 | tf_op jit(solution)/shard_map/ppermute | solution.py:408
  39.8 2.6 %collective-permute-start.8 = (bf16[128,512]{1,0:T(8,128)(2,1)S(1)}, bf16[128,512]{1,0:T(8,128)(2,1)S(1)}, u32[]{:S(2)}, u32[]{:S(2)}) collective-permute-start(bf16[128,512]{1,0:T(8,128)(2,1)S(1)} %get-tuple-element.40), channel_id=1, source_target_pairs={{0,128},{8,136},{16,144},{24,152},{32,160},{40,168},{48,176},{56,1... | collective-permute-start | bytes 393224 | tf_op jit(solution)/shard_map/ppermute | solution.py:408
  42.4 1.1 %collective-permute-start.9 = (bf16[128,512]{1,0:T(8,128)(2,1)S(1)}, bf16[128,512]{1,0:T(8,128)(2,1)S(1)}, u32[]{:S(2)}, u32[]{:S(2)}) collective-permute-start(bf16[128,512]{1,0:T(8,128)(2,1)S(1)} %get-tuple-element.40), channel_id=1, source_target_pairs={{0,192},{8,200},{16,208},{24,216},{32,224},{40,232},{48,240},{56,2... | collective-permute-start | bytes 393224 | tf_op jit(solution)/shard_map/ppermute | solution.py:408
  43.5 0.4 collective-permute-done.7.refs_0_
  43.9 3.8 %collective-permute-done.8.refs_1_ = bf16[128,512]{1,0:T(8,128)(2,1)S(1)} collective-permute-done((bf16[128,512]{1,0:T(8,128)(2,1)S(1)}, bf16[128,512]{1,0:T(8,128)(2,1)S(1)}, u32[]{:S(2)}, u32[]{:S(2)}) %collective-permute-start.8) | collective-permute-done | bytes 131104 | tf_op jit(solution)/shard_map/ppermute | solution.py:408
  47.7 0.3 collective-permute-done.9.refs_2_
  48.0 0.5 collective-permute-done.12.four_ref
  48.5 0.0 collective-permute-done.11.three_ref
  48.5 1.3 %collective-permute-start.13 = (bf16[128,512]{1,0:T(8,128)(2,1)S(1)}, bf16[128,512]{1,0:T(8,128)(2,1)S(1)}, u32[]{:S(2)}, u32[]{:S(2)}) collective-permute-start(bf16[128,512]{1,0:T(8,128)(2,1)S(1)} %collective-permute-done.7.refs_0_), channel_id=1, source_target_pairs={{0,8},{8,0},{16,24},{24,16},{32,40},{40,32},{48,56},{56,48},{64,72... | collective-permute-start | bytes 393224 | tf_op jit(solution)/shard_map/ppermute | solution.py:408
  49.8 0.1 collective-permute-start.14
  49.9 0.4 collective-permute-start.15
  50.3 0.5 collective-permute-done.13.refs_3_
  50.8 0.4 collective-permute-done.14.refs_4_
  51.1 0.2 collective-permute-done.15.refs_5_
  51.3 0.0 copy-done.3
  51.3 0.0 copy-start.1
  51.3 1.0 %copy-done.1 = f32[256,512]{1,0:T(8,128)S(1)} copy-done((f32[256,512]{1,0:T(8,128)S(1)}, f32[256,512]{1,0:T(8,128)}, u32[]{:S(2)}) %copy-start.1) | copy-done | bytes 524312
  52.4 1.5 %read.1 = bf16[4,256,256]{2,1,0:T(8,128)(2,1)} custom-call(bf16[128,512]{1,0:T(8,128)(2,1)S(1)} %collective-permute-done.7.refs_0_, bf16[128,512]{1,0:T(8,128)(2,1)S(1)} %collective-permute-done.8.refs_1_, bf16[128,512]{1,0:T(8,128)(2,1)S(1)} %collective-permute-done.9.refs_2_, bf16[128,512]{1,0:T(8,128)(2,1)S(1)} %collective-permute-done.13.refs_3_, ...), custom_call_target="tpu_custom_call" | custom-call | tf_op jit(solution)/shard_map/read/pallas_call | solution.py:472
  53.9 7.1 %all-to-all-start = ((bf16[32,32,256]{2,1,0:T(8,128)(2,1)}), bf16[32,32,256]{2,1,0:T(8,128)(2,1)S(1)}, u32[]{:S(2)}, u32[]{:S(2)}) async-start(bf16[32,32,256]{2,1,0:T(8,128)(2,1)} %bitcast.6), calls=%async_computation | async-start | bytes 1048576 | tf_op jit(solution)/shard_map/all_to_all | solution.py:482
  61.0 0.0 copy-done
  61.0 2.5 %collective-permute-start.17 = (bf16[256,1024]{1,0:T(8,128)(2,1)S(1)}, bf16[256,1024]{1,0:T(8,128)(2,1)S(1)}, u32[]{:S(2)}, u32[]{:S(2)}) collective-permute-start(bf16[256,1024]{1,0:T(8,128)(2,1)S(1)} %copy-done), channel_id=1, source_target_pairs={{0,1},{1,2},{2,3},{3,4},{4,5},{5,6},{6,7},{7,0},{8,15},{9,8},{10,9... | collective-permute-start | bytes 1572872 | tf_op jit(solution)/shard_map/ppermute | solution.py:422
  63.5 12.1 %all-to-all-done = bf16[32,32,256]{2,1,0:T(8,128)(2,1)S(1)} async-done(((bf16[32,32,256]{2,1,0:T(8,128)(2,1)}), bf16[32,32,256]{2,1,0:T(8,128)(2,1)S(1)}, u32[]{:S(2)}, u32[]{:S(2)}) %all-to-all-start) | async-done | bytes 524320 | tf_op jit(solution)/shard_map/all_to_all | solution.py:482
  75.6 2.5 %collective-permute-start.16 = (bf16[4,8,32,256]{3,2,1,0:T(8,128)(2,1)S(1)}, bf16[4,8,32,256]{3,2,1,0:T(8,128)(2,1)S(1)}, u32[]{:S(2)}, u32[]{:S(2)}) collective-permute-start(bf16[4,8,32,256]{3,2,1,0:T(8,128)(2,1)S(1)} %bitcast.9), channel_id=1, source_target_pairs={{0,8},{8,0},{16,24},{24,16},{32,40},{40,32},{48,56},{56,48},{64,72... | collective-permute-start | bytes 1572872 | tf_op jit(solution)/shard_map/ppermute | solution.py:408
  78.1 2.4 %collective-permute-done.17.one_ref = bf16[256,1024]{1,0:T(8,128)(2,1)S(1)} collective-permute-done((bf16[256,1024]{1,0:T(8,128)(2,1)S(1)}, bf16[256,1024]{1,0:T(8,128)(2,1)S(1)}, u32[]{:S(2)}, u32[]{:S(2)}) %collective-permute-start.17) | collective-permute-done | bytes 524320 | tf_op jit(solution)/shard_map/ppermute | solution.py:422
  80.5 0.0 collective-permute-done.16.other_ref
  80.5 0.9 mix.1
  81.4 1.9 %collective-permute-start.18 = (bf16[128,1024]{1,0:T(8,128)(2,1)S(1)}, bf16[128,1024]{1,0:T(8,128)(2,1)S(1)}, u32[]{:S(2)}, u32[]{:S(2)}) collective-permute-start(bf16[128,1024]{1,0:T(8,128)(2,1)S(1)} %get-tuple-element.50), channel_id=1, source_target_pairs={{0,8},{8,0},{16,24},{24,16},{32,40},{40,32},{48,56},{56,48},{64,72... | collective-permute-start | bytes 786440 | tf_op jit(solution)/shard_map/ppermute | solution.py:408
  83.3 1.2 %collective-permute-done.18.come_ref = bf16[128,1024]{1,0:T(8,128)(2,1)S(1)} collective-permute-done((bf16[128,1024]{1,0:T(8,128)(2,1)S(1)}, bf16[128,1024]{1,0:T(8,128)(2,1)S(1)}, u32[]{:S(2)}, u32[]{:S(2)}) %collective-permute-start.18) | collective-permute-done | bytes 262176 | tf_op jit(solution)/shard_map/ppermute | solution.py:408
  84.5 1.3 %collective-permute-start.19 = (bf16[32,1024]{1,0:T(8,128)(2,1)S(1)}, bf16[32,1024]{1,0:T(8,128)(2,1)S(1)}, u32[]{:S(2)}, u32[]{:S(2)}) collective-permute-start(bf16[32,1024]{1,0:T(8,128)(2,1)S(1)} %get-tuple-element.52), channel_id=1, source_target_pairs={{0,16},{8,24},{16,0},{24,8},{32,48},{40,56},{48,32},{56,40},{64,80... | collective-permute-start | bytes 196616 | tf_op jit(solution)/shard_map/ppermute | solution.py:408
  85.8 1.3 %collective-permute-start.20 = (bf16[32,1024]{1,0:T(8,128)(2,1)S(1)}, bf16[32,1024]{1,0:T(8,128)(2,1)S(1)}, u32[]{:S(2)}, u32[]{:S(2)}) collective-permute-start(bf16[32,1024]{1,0:T(8,128)(2,1)S(1)} %get-tuple-element.53), channel_id=1, source_target_pairs={{0,64},{8,72},{16,80},{24,88},{32,96},{40,104},{48,112},{56,120},{... | collective-permute-start | bytes 196616 | tf_op jit(solution)/shard_map/ppermute | solution.py:408
  87.1 0.2 collective-permute-start.21
  87.3 0.5 collective-permute-done.19.refs_1_
  87.8 1.2 %collective-permute-done.20.refs_2_ = bf16[32,1024]{1,0:T(8,128)(2,1)S(1)} collective-permute-done((bf16[32,1024]{1,0:T(8,128)(2,1)S(1)}, bf16[32,1024]{1,0:T(8,128)(2,1)S(1)}, u32[]{:S(2)}, u32[]{:S(2)}) %collective-permute-start.20) | collective-permute-done | bytes 65568 | tf_op jit(solution)/shard_map/ppermute | solution.py:408
  88.9 2.2 %collective-permute-done.21.refs_3_ = bf16[32,1024]{1,0:T(8,128)(2,1)S(1)} collective-permute-done((bf16[32,1024]{1,0:T(8,128)(2,1)S(1)}, bf16[32,1024]{1,0:T(8,128)(2,1)S(1)}, u32[]{:S(2)}, u32[]{:S(2)}) %collective-permute-start.21) | collective-permute-done | bytes 65568 | tf_op jit(solution)/shard_map/ppermute | solution.py:408
  91.1 0.7 lay.1
  (2 shorter events, 0.1 us)
Async XLA Ops:
  1.9 32.1 %collective-permute-start.10 = (bf16[256,1024]{1,0:T(8,128)(2,1)}, bf16[256,1024]{1,0:T(8,128)(2,1)S(1)}, u32[]{:S(2)}, u32[]{:S(2)}) collective-permute-start(bf16[256,1024]{1,0:T(8,128)(2,1)} %take.1.mine_ref), channel_id=1, source_target_pairs={{0,2},{1,3},{2,4},{3,5},{4,6},{5,7},{6,0},{7,1},{8,14},{9,15},{10,... | collective-permute-start | bytes 1572872 | tf_op jit(solution)/shard_map/ppermute | solution.py:422
  19.8 1.8 %collective-permute-start = (bf16[256,512]{1,0:T(8,128)(2,1)}, bf16[256,512]{1,0:T(8,128)(2,1)S(1)}, u32[]{:S(2)}, u32[]{:S(2)}) collective-permute-start(bf16[256,512]{1,0:T(8,128)(2,1)} %get-tuple-element.30.own_ref), channel_id=1, source_target_pairs={{0,8},{8,0},{16,24},{24,16},{32,40},{40,32},{48,56},{56,48},{64,72... | collective-permute-start | bytes 786440 | tf_op jit(solution)/shard_map/ppermute | solution.py:408
  21.6 1.0 %copy-start.2 = (bf16[256,512]{1,0:T(8,128)(2,1)S(1)}, bf16[256,512]{1,0:T(8,128)(2,1)}, u32[]{:S(2)}) copy-start(bf16[256,512]{1,0:T(8,128)(2,1)} %get-tuple-element.30.own_ref) | copy-start | bytes 786436
  22.8 11.1 %collective-permute-start.1 = (bf16[128,512]{1,0:T(8,128)(2,1)S(1)}, bf16[128,512]{1,0:T(8,128)(2,1)S(1)}, u32[]{:S(2)}, u32[]{:S(2)}) collective-permute-start(bf16[128,512]{1,0:T(8,128)(2,1)S(1)} %get-tuple-element.32), channel_id=1, source_target_pairs={{0,16},{8,24},{16,32},{24,40},{32,48},{40,56},{48,0},{56,8},{64,80... | collective-permute-start | bytes 393224 | tf_op jit(solution)/shard_map/ppermute | solution.py:408
  24.1 9.8 %collective-permute-start.2 = (bf16[128,512]{1,0:T(8,128)(2,1)S(1)}, bf16[128,512]{1,0:T(8,128)(2,1)S(1)}, u32[]{:S(2)}, u32[]{:S(2)}) collective-permute-start(bf16[128,512]{1,0:T(8,128)(2,1)S(1)} %get-tuple-element.32), channel_id=1, source_target_pairs={{0,32},{8,40},{16,48},{24,56},{32,0},{40,8},{48,16},{56,24},{64,96... | collective-permute-start | bytes 393224 | tf_op jit(solution)/shard_map/ppermute | solution.py:408
  26.6 7.4 %collective-permute-start.3 = (bf16[128,512]{1,0:T(8,128)(2,1)S(1)}, bf16[128,512]{1,0:T(8,128)(2,1)S(1)}, u32[]{:S(2)}, u32[]{:S(2)}) collective-permute-start(bf16[128,512]{1,0:T(8,128)(2,1)S(1)} %get-tuple-element.32), channel_id=1, source_target_pairs={{0,48},{8,56},{16,0},{24,8},{32,16},{40,24},{48,32},{56,40},{64,11... | collective-permute-start | bytes 393224 | tf_op jit(solution)/shard_map/ppermute | solution.py:408
  27.7 23.6 %copy-start.3 = (f32[256]{0:T(256)S(1)}, f32[256]{0:T(256)}, u32[]{:S(2)}) copy-start(f32[256]{0:T(256)} %param.16) | copy-start | bytes 3076
  34.0 14.5 %collective-permute-start.11 = (bf16[256,1024]{1,0:T(8,128)(2,1)S(1)}, bf16[256,1024]{1,0:T(8,128)(2,1)S(1)}, u32[]{:S(2)}, u32[]{:S(2)}) collective-permute-start(bf16[256,1024]{1,0:T(8,128)(2,1)S(1)} %collective-permute-done.10.two_ref), channel_id=1, source_target_pairs={{0,1},{1,2},{2,3},{3,4},{4,5},{5,6},{6,7},{7,0},{8,15},{9,8},{10,9... | collective-permute-start | bytes 1572872 | tf_op jit(solution)/shard_map/ppermute | solution.py:422
  34.8 3.1 %collective-permute-start.4 = (bf16[128,512]{1,0:T(8,128)(2,1)S(1)}, bf16[128,512]{1,0:T(8,128)(2,1)S(1)}, u32[]{:S(2)}, u32[]{:S(2)}) collective-permute-start(bf16[128,512]{1,0:T(8,128)(2,1)S(1)} %collective-permute-done.1.refs_0_), channel_id=1, source_target_pairs={{0,8},{8,0},{16,24},{24,16},{32,40},{40,32},{48,56},{56,48},{64,72... | collective-permute-start | bytes 393224 | tf_op jit(solution)/shard_map/ppermute | solution.py:408
  36.1 1.8 %collective-permute-start.5 = (bf16[128,512]{1,0:T(8,128)(2,1)S(1)}, bf16[128,512]{1,0:T(8,128)(2,1)S(1)}, u32[]{:S(2)}, u32[]{:S(2)}) collective-permute-start(bf16[128,512]{1,0:T(8,128)(2,1)S(1)} %collective-permute-done.2.refs_1_), channel_id=1, source_target_pairs={{0,8},{8,0},{16,24},{24,16},{32,40},{40,32},{48,56},{56,48},{64,72... | collective-permute-start | bytes 393224 | tf_op jit(solution)/shard_map/ppermute | solution.py:408
  36.1 1.8 %collective-permute-start.6 = (bf16[128,512]{1,0:T(8,128)(2,1)S(1)}, bf16[128,512]{1,0:T(8,128)(2,1)S(1)}, u32[]{:S(2)}, u32[]{:S(2)}) collective-permute-start(bf16[128,512]{1,0:T(8,128)(2,1)S(1)} %collective-permute-done.3.refs_2_), channel_id=1, source_target_pairs={{0,8},{8,0},{16,24},{24,16},{32,40},{40,32},{48,56},{56,48},{64,72... | collective-permute-start | bytes 393224 | tf_op jit(solution)/shard_map/ppermute | solution.py:408
  36.6 11.9 %collective-permute-start.12 = (bf16[256,512]{1,0:T(8,128)(2,1)S(1)}, bf16[256,512]{1,0:T(8,128)(2,1)S(1)}, u32[]{:S(2)}, u32[]{:S(2)}) collective-permute-start(bf16[256,512]{1,0:T(8,128)(2,1)S(1)} %constant_dynamic-slice_fusion), channel_id=1, source_target_pairs={{0,2},{1,3},{2,4},{3,5},{4,6},{5,7},{6,0},{7,1},{8,14},{9,15},{10,... | collective-permute-start | bytes 786440 | tf_op jit(solution)/shard_map/ppermute | solution.py:422
  37.8 23.2 %copy-start = (bf16[256,1024]{1,0:T(8,128)(2,1)S(1)}, bf16[256,1024]{1,0:T(8,128)(2,1)}, u32[]{:S(2)}) copy-start(bf16[256,1024]{1,0:T(8,128)(2,1)} %take.1.mine_ref) | copy-start | bytes 1572868
  38.4 5.5 %collective-permute-start.7 = (bf16[128,512]{1,0:T(8,128)(2,1)S(1)}, bf16[128,512]{1,0:T(8,128)(2,1)S(1)}, u32[]{:S(2)}, u32[]{:S(2)}) collective-permute-start(bf16[128,512]{1,0:T(8,128)(2,1)S(1)} %get-tuple-element.40), channel_id=1, source_target_pairs={{0,64},{8,72},{16,80},{24,88},{32,96},{40,104},{48,112},{56,120},{... | collective-permute-start | bytes 393224 | tf_op jit(solution)/shard_map/ppermute | solution.py:408
  39.8 7.9 %collective-permute-start.8 = (bf16[128,512]{1,0:T(8,128)(2,1)S(1)}, bf16[128,512]{1,0:T(8,128)(2,1)S(1)}, u32[]{:S(2)}, u32[]{:S(2)}) collective-permute-start(bf16[128,512]{1,0:T(8,128)(2,1)S(1)} %get-tuple-element.40), channel_id=1, source_target_pairs={{0,128},{8,136},{16,144},{24,152},{32,160},{40,168},{48,176},{56,1... | collective-permute-start | bytes 393224 | tf_op jit(solution)/shard_map/ppermute | solution.py:408
  42.4 5.5 %collective-permute-start.9 = (bf16[128,512]{1,0:T(8,128)(2,1)S(1)}, bf16[128,512]{1,0:T(8,128)(2,1)S(1)}, u32[]{:S(2)}, u32[]{:S(2)}) collective-permute-start(bf16[128,512]{1,0:T(8,128)(2,1)S(1)} %get-tuple-element.40), channel_id=1, source_target_pairs={{0,192},{8,200},{16,208},{24,216},{32,224},{40,232},{48,240},{56,2... | collective-permute-start | bytes 393224 | tf_op jit(solution)/shard_map/ppermute | solution.py:408
  48.5 2.3 %collective-permute-start.13 = (bf16[128,512]{1,0:T(8,128)(2,1)S(1)}, bf16[128,512]{1,0:T(8,128)(2,1)S(1)}, u32[]{:S(2)}, u32[]{:S(2)}) collective-permute-start(bf16[128,512]{1,0:T(8,128)(2,1)S(1)} %collective-permute-done.7.refs_0_), channel_id=1, source_target_pairs={{0,8},{8,0},{16,24},{24,16},{32,40},{40,32},{48,56},{56,48},{64,72... | collective-permute-start | bytes 393224 | tf_op jit(solution)/shard_map/ppermute | solution.py:408
  49.8 1.3 %collective-permute-start.14 = (bf16[128,512]{1,0:T(8,128)(2,1)S(1)}, bf16[128,512]{1,0:T(8,128)(2,1)S(1)}, u32[]{:S(2)}, u32[]{:S(2)}) collective-permute-start(bf16[128,512]{1,0:T(8,128)(2,1)S(1)} %collective-permute-done.8.refs_1_), channel_id=1, source_target_pairs={{0,8},{8,0},{16,24},{24,16},{32,40},{40,32},{48,56},{56,48},{64,72... | collective-permute-start | bytes 393224 | tf_op jit(solution)/shard_map/ppermute | solution.py:408
  49.9 1.4 %collective-permute-start.15 = (bf16[128,512]{1,0:T(8,128)(2,1)S(1)}, bf16[128,512]{1,0:T(8,128)(2,1)S(1)}, u32[]{:S(2)}, u32[]{:S(2)}) collective-permute-start(bf16[128,512]{1,0:T(8,128)(2,1)S(1)} %collective-permute-done.9.refs_2_), channel_id=1, source_target_pairs={{0,8},{8,0},{16,24},{24,16},{32,40},{40,32},{48,56},{56,48},{64,72... | collective-permute-start | bytes 393224 | tf_op jit(solution)/shard_map/ppermute | solution.py:408
  51.3 1.0 %copy-start.1 = (f32[256,512]{1,0:T(8,128)S(1)}, f32[256,512]{1,0:T(8,128)}, u32[]{:S(2)}) copy-start(f32[256,512]{1,0:T(8,128)} %look.1.refs_8_) | copy-start | bytes 1572868
  53.9 21.7 %all-to-all-start = ((bf16[32,32,256]{2,1,0:T(8,128)(2,1)}), bf16[32,32,256]{2,1,0:T(8,128)(2,1)S(1)}, u32[]{:S(2)}, u32[]{:S(2)}) async-start(bf16[32,32,256]{2,1,0:T(8,128)(2,1)} %bitcast.6), calls=%async_computation | async-start | bytes 1048576 | tf_op jit(solution)/shard_map/all_to_all | solution.py:482
  61.0 19.5 %collective-permute-start.17 = (bf16[256,1024]{1,0:T(8,128)(2,1)S(1)}, bf16[256,1024]{1,0:T(8,128)(2,1)S(1)}, u32[]{:S(2)}, u32[]{:S(2)}) collective-permute-start(bf16[256,1024]{1,0:T(8,128)(2,1)S(1)} %copy-done), channel_id=1, source_target_pairs={{0,1},{1,2},{2,3},{3,4},{4,5},{5,6},{6,7},{7,0},{8,15},{9,8},{10,9... | collective-permute-start | bytes 1572872 | tf_op jit(solution)/shard_map/ppermute | solution.py:422
  75.6 4.9 %collective-permute-start.16 = (bf16[4,8,32,256]{3,2,1,0:T(8,128)(2,1)S(1)}, bf16[4,8,32,256]{3,2,1,0:T(8,128)(2,1)S(1)}, u32[]{:S(2)}, u32[]{:S(2)}) collective-permute-start(bf16[4,8,32,256]{3,2,1,0:T(8,128)(2,1)S(1)} %bitcast.9), channel_id=1, source_target_pairs={{0,8},{8,0},{16,24},{24,16},{32,40},{40,32},{48,56},{56,48},{64,72... | collective-permute-start | bytes 1572872 | tf_op jit(solution)/shard_map/ppermute | solution.py:408
  81.4 3.1 %collective-permute-start.18 = (bf16[128,1024]{1,0:T(8,128)(2,1)S(1)}, bf16[128,1024]{1,0:T(8,128)(2,1)S(1)}, u32[]{:S(2)}, u32[]{:S(2)}) collective-permute-start(bf16[128,1024]{1,0:T(8,128)(2,1)S(1)} %get-tuple-element.50), channel_id=1, source_target_pairs={{0,8},{8,0},{16,24},{24,16},{32,40},{40,32},{48,56},{56,48},{64,72... | collective-permute-start | bytes 786440 | tf_op jit(solution)/shard_map/ppermute | solution.py:408
  84.5 3.2 %collective-permute-start.19 = (bf16[32,1024]{1,0:T(8,128)(2,1)S(1)}, bf16[32,1024]{1,0:T(8,128)(2,1)S(1)}, u32[]{:S(2)}, u32[]{:S(2)}) collective-permute-start(bf16[32,1024]{1,0:T(8,128)(2,1)S(1)} %get-tuple-element.52), channel_id=1, source_target_pairs={{0,16},{8,24},{16,0},{24,8},{32,48},{40,56},{48,32},{56,40},{64,80... | collective-permute-start | bytes 196616 | tf_op jit(solution)/shard_map/ppermute | solution.py:408
  85.8 3.1 %collective-permute-start.20 = (bf16[32,1024]{1,0:T(8,128)(2,1)S(1)}, bf16[32,1024]{1,0:T(8,128)(2,1)S(1)}, u32[]{:S(2)}, u32[]{:S(2)}) collective-permute-start(bf16[32,1024]{1,0:T(8,128)(2,1)S(1)} %get-tuple-element.53), channel_id=1, source_target_pairs={{0,64},{8,72},{16,80},{24,88},{32,96},{40,104},{48,112},{56,120},{... | collective-permute-start | bytes 196616 | tf_op jit(solution)/shard_map/ppermute | solution.py:408
  87.1 4.0 %collective-permute-start.21 = (bf16[32,1024]{1,0:T(8,128)(2,1)S(1)}, bf16[32,1024]{1,0:T(8,128)(2,1)S(1)}, u32[]{:S(2)}, u32[]{:S(2)}) collective-permute-start(bf16[32,1024]{1,0:T(8,128)(2,1)S(1)} %get-tuple-element.54), channel_id=1, source_target_pairs={{0,80},{8,88},{16,64},{24,72},{32,112},{40,120},{48,96},{56,104},{... | collective-permute-start | bytes 196616 | tf_op jit(solution)/shard_map/ppermute | solution.py:408

commit v12 on v10

--- a/solution.py
+++ b/solution.py
@@ -14,7 +14,7 @@
 SEQ = ("yh", "yl", "xh", "xl", "core")
 SMALL = pltpu.CompilerParams(vmem_limit_bytes=8 << 20)
 MIDDLE = pltpu.CompilerParams(vmem_limit_bytes=16 << 20)
-LARGE = pltpu.CompilerParams(vmem_limit_bytes=58 << 20)
+LARGE = pltpu.CompilerParams(vmem_limit_bytes=52 << 20)
 
 
 def mm(a, b, dims=NN):

time: 91.6 us -> 89.7 us (0.979)
  waiting for transfers between devices: 20.1 us -> 23 us
  Pallas kernels: 21 us -> 18.2 us
  local copies, waits for them, and re-layouts: 2.02 us -> 0.03 us
    ppermute x18, waiting for transfers between devices: 19.1 us -> 21.7 us  [moved(): return lax.ppermute(value, SEQ, [(i, place_of(i)) for i in range(count)])]
    pallas_call x1, Pallas kernels: 6.21 us -> 4.17 us  [look(): pl.pallas_call(look_kernel, name='look', in_specs=[hbm(), vmem(), hbm()]...]
    unnamed x8, local copies, waits for them, and re-layouts: 2 us -> 0.01 us
  transfers between devices with their start and end apart: 22 -> 22, of which waited for: 17 -> 20; matrix products, arithmetic and copies ran while one was open for 0% -> 0% of each run, Pallas kernels for 19% -> 17%
where the time goes in v12:
time: 89.7 us; the launch traced here: 89.3 us
  starting transfers between devices  27.1 us (30%)
  waiting for transfers between devices  23 us (26%)
  blocking collectives  19.5 us (22%)
  Pallas kernels  18.2 us (20%)
  between operations  1.41 us (2%)
    ppermute x18, waiting for transfers between devices, moved(): return lax.ppermute(value, SEQ, [(i, place_of(i)) for i in range(count)])  21.7 us
    all_to_all x1, blocking collectives, per_device(): lax.all_to_all(flat.reshape(32, part, n), ('yl', 'xl', 'head'), 0, 0, til...  19.5 us
    ppermute x18, starting transfers between devices, moved(): return lax.ppermute(value, SEQ, [(i, place_of(i)) for i in range(count)])  17.2 us
    ppermute x4, starting transfers between devices, around(): return lax.ppermute(value, ('core', 'head'), up + down)  9.94 us
    pallas_call x1, Pallas kernels, per_device(): pl.pallas_call(fold_kernel, name='fold', in_specs=[hbm()] * 7, out_specs=...  9.06 us
    pallas_call x1, Pallas kernels, look(): pl.pallas_call(look_kernel, name='look', in_specs=[hbm(), vmem(), hbm()]...  4.17 us
  transfers between devices with their start and end apart: 22, of which 20 were waited for; matrix products, arithmetic and copies ran while one was open for 0% of the time, Pallas kernels for 17%

profile of v12, /device:TPU:1, one launch (start us, length us, event | category | flops | bytes accessed | tf_op | source)
XLA Modules:
  0.0 89.3 jit_solution(10972800096435321023)
XLA Ops:
  0.0 0.0 copy-start.2
  0.0 0.0 copy-start.1
  0.0 0.0 copy-start
  0.0 1.1 %take.1.mine_ref = bf16[256,1024]{1,0:T(8,128)(2,1)S(1)} custom-call(bf16[256,4096]{1,0:T(8,128)(2,1)} %whole_ref.1), custom_call_target="tpu_custom_call" | custom-call | tf_op jit(solution)/shard_map/take/pallas_call | solution.py:428
  1.1 6.5 %collective-permute-start.13 = (bf16[256,1024]{1,0:T(8,128)(2,1)S(1)}, bf16[256,1024]{1,0:T(8,128)(2,1)S(1)}, u32[]{:S(2)}, u32[]{:S(2)}) collective-permute-start(bf16[256,1024]{1,0:T(8,128)(2,1)S(1)} %take.1.mine_ref), channel_id=1, source_target_pairs={{0,1},{1,2},{2,3},{3,4},{4,5},{5,6},{6,7},{7,0},{8,15},{9,8},{10,9... | collective-permute-start | bytes 1572872 | tf_op jit(solution)/shard_map/ppermute | solution.py:422
  8.9 0.0 copy-done.2
  8.9 0.0 copy-done.1
  8.9 0.0 copy-done
  8.9 9.1 %fold.1 = (bf16[256,512]{1,0:T(8,128)(2,1)S(1)}, f32[256,256]{1,0:T(8,128)S(1)}, f32[256,512]{1,0:T(8,128)S(1)}, f32[256,256]{1,0:T(8,128)S(1)}, f32[256,1]{1,0:T(8,128)S(1)}) custom-call(f32[1]{0:T(128)S(6)} %copy.10.scale_hbm, f32[1]{0:T(128)S(6)} %copy.11.rate_hbm, bf16[256,4096]{1,0:T(8,128)(2,1)} %x_hbm.3, f32[1,4096]{1,0:T(1,128)S(1)} %bitcast.12, ...), custom_call_target="tpu_custom_call" | custom-call | tf_op jit(solution)/shard_map/fold/pallas_call | solution.py:362
  18.0 0.1 collective-permute-start
  18.1 1.5 %collective-permute-done.other_ref.refs_7_ = bf16[256,512]{1,0:T(8,128)(2,1)S(1)} collective-permute-done((bf16[256,512]{1,0:T(8,128)(2,1)S(1)}, bf16[256,512]{1,0:T(8,128)(2,1)S(1)}, u32[]{:S(2)}, u32[]{:S(2)}) %collective-permute-start) | collective-permute-done | bytes 262176 | tf_op jit(solution)/shard_map/ppermute | solution.py:408
  19.6 0.0 collective-permute-done.13.one_ref
  19.6 0.7 collective-permute-start.14
  20.3 0.3 pair.1
  20.6 2.6 %collective-permute-start.3 = (bf16[128,512]{1,0:T(8,128)(2,1)S(1)}, bf16[128,512]{1,0:T(8,128)(2,1)S(1)}, u32[]{:S(2)}, u32[]{:S(2)}) collective-permute-start(bf16[128,512]{1,0:T(8,128)(2,1)S(1)} %get-tuple-element.31), channel_id=1, source_target_pairs={{0,48},{8,56},{16,0},{24,8},{32,16},{40,24},{48,32},{56,40},{64,11... | collective-permute-start | bytes 393224 | tf_op jit(solution)/shard_map/ppermute | solution.py:408
  23.2 0.5 collective-permute-start.2
  23.7 0.6 collective-permute-start.1
  24.3 0.0 copy-start.3
  24.3 4.2 %look.1.refs_8_ = f32[256,512]{1,0:T(8,128)S(1)} custom-call(bf16[256,4096]{1,0:T(8,128)(2,1)} %x_hbm.3, f32[1,4096]{1,0:T(1,128)S(1)} %bitcast.13, bf16[3,4096,256]{2,1,0:T(8,128)(2,1)} %bitcast.18, f32[256,256]{1,0:T(8,128)S(1)} %get-tuple-element.32.key_ref, f32[256,512]{1,0:T(8,128)S(1)} %get-tuple-element.33.solved_ref, ...), custom_call_target="tpu_custom_call" | custom-call | flops 1073741824 | bytes 16777216 | tf_op jit(solution)/shard_map/look/pallas_call | solution.py:392
  28.5 0.7 collective-permute-done.3.refs_2_
  29.2 0.9 collective-permute-done.2.refs_1_
  30.1 2.9 %collective-permute-done.1.refs_0_ = bf16[128,512]{1,0:T(8,128)(2,1)S(1)} collective-permute-done((bf16[128,512]{1,0:T(8,128)(2,1)S(1)}, bf16[128,512]{1,0:T(8,128)(2,1)S(1)}, u32[]{:S(2)}, u32[]{:S(2)}) %collective-permute-start.1) | collective-permute-done | bytes 131104 | tf_op jit(solution)/shard_map/ppermute | solution.py:408
  33.0 0.0 collective-permute-done.14.two_ref
  33.0 0.6 collective-permute-start.15
  33.6 0.7 collective-permute-start.4
  34.3 0.0 collective-permute-start.5
  34.3 0.5 collective-permute-start.6
  34.8 0.5 collective-permute-done.4.refs_3_
  35.3 0.4 collective-permute-done.5.refs_4_
  35.6 0.2 collective-permute-done.6.refs_5_
  35.8 1.2 %row.1 = (bf16[128,512]{1,0:T(8,128)(2,1)}, bf16[256,512]{1,0:T(8,128)(2,1)S(1)}) custom-call(bf16[256,512]{1,0:T(8,128)(2,1)S(1)} %get-tuple-element.30.own_ref, bf16[128,512]{1,0:T(8,128)(2,1)S(1)} %collective-permute-done.1.refs_0_, bf16[128,512]{1,0:T(8,128)(2,1)S(1)} %collective-permute-done.2.refs_1_, ...), custom_call_target="tpu_custom_call" | custom-call | tf_op jit(solution)/shard_map/row/pallas_call | solution.py:455
  37.0 2.7 %collective-permute-start.9 = (bf16[128,512]{1,0:T(8,128)(2,1)}, bf16[128,512]{1,0:T(8,128)(2,1)S(1)}, u32[]{:S(2)}, u32[]{:S(2)}) collective-permute-start(bf16[128,512]{1,0:T(8,128)(2,1)} %get-tuple-element.39), channel_id=1, source_target_pairs={{0,192},{8,200},{16,208},{24,216},{32,224},{40,232},{48,240},{56,2... | collective-permute-start | bytes 393224 | tf_op jit(solution)/shard_map/ppermute | solution.py:408
  39.8 0.3 collective-permute-start.8
  40.1 0.7 collective-permute-start.7
  40.8 0.5 collective-permute-done.15.three_ref
  41.3 4.0 %collective-permute-done.9.refs_2_ = bf16[128,512]{1,0:T(8,128)(2,1)S(1)} collective-permute-done((bf16[128,512]{1,0:T(8,128)(2,1)}, bf16[128,512]{1,0:T(8,128)(2,1)S(1)}, u32[]{:S(2)}, u32[]{:S(2)}) %collective-permute-start.9) | collective-permute-done | bytes 131104 | tf_op jit(solution)/shard_map/ppermute | solution.py:408
  45.3 0.6 collective-permute-done.8.refs_1_
  46.0 3.8 %collective-permute-done.7.refs_0_ = bf16[128,512]{1,0:T(8,128)(2,1)S(1)} collective-permute-done((bf16[128,512]{1,0:T(8,128)(2,1)}, bf16[128,512]{1,0:T(8,128)(2,1)S(1)}, u32[]{:S(2)}, u32[]{:S(2)}) %collective-permute-start.7) | collective-permute-done | bytes 131104 | tf_op jit(solution)/shard_map/ppermute | solution.py:408
  49.7 2.1 %collective-permute-start.16 = (bf16[256,512]{1,0:T(8,128)(2,1)S(1)}, bf16[256,512]{1,0:T(8,128)(2,1)S(1)}, u32[]{:S(2)}, u32[]{:S(2)}) collective-permute-start(bf16[256,512]{1,0:T(8,128)(2,1)S(1)} %constant_dynamic-slice_fusion), channel_id=1, source_target_pairs={{0,1},{1,2},{2,3},{3,4},{4,5},{5,6},{6,7},{7,0},{8,15},{9,8},{10,9... | collective-permute-start | bytes 786440 | tf_op jit(solution)/shard_map/ppermute | solution.py:422
  51.8 0.0 collective-permute-start.12
  51.8 0.5 collective-permute-start.11
  52.3 0.0 collective-permute-start.10
  52.3 0.8 collective-permute-done.12.refs_5_
  53.2 0.2 collective-permute-done.11.refs_4_
  53.4 0.3 collective-permute-done.10.refs_3_
  53.7 0.0 copy-done.3
  53.7 0.7 read.1
  54.4 0.8 collective-permute-done.16.four_ref
  55.2 19.5 %all_to_all.5 = bf16[32,32,256]{2,1,0:T(8,128)(2,1)S(1)} all-to-all(bf16[32,32,256]{2,1,0:T(8,128)(2,1)S(1)} %bitcast.11), channel_id=1, replica_groups=mesh['yh'=2,'yl'=2,'xh'=2,'xl'=2,'core'=2,'head'=8] {'yl','xl','head'}, dimensions={0} | all-to-all | bytes 1048576 | tf_op jit(solution)/shard_map/all_to_all | solution.py:481
  74.7 4.5 %collective-permute-start.17 = (bf16[4,8,32,256]{3,2,1,0:T(8,128)(2,1)S(1)}, bf16[4,8,32,256]{3,2,1,0:T(8,128)(2,1)S(1)}, u32[]{:S(2)}, u32[]{:S(2)}) collective-permute-start(bf16[4,8,32,256]{3,2,1,0:T(8,128)(2,1)S(1)} %bitcast.9), channel_id=1, source_target_pairs={{0,8},{8,0},{16,24},{24,16},{32,40},{40,32},{48,56},{56,48},{64,72... | collective-permute-start | bytes 1572872 | tf_op jit(solution)/shard_map/ppermute | solution.py:408
  79.2 1.5 %collective-permute-done.17.other_ref = bf16[4,8,32,256]{3,2,1,0:T(8,128)(2,1)S(1)} collective-permute-done((bf16[4,8,32,256]{3,2,1,0:T(8,128)(2,1)S(1)}, bf16[4,8,32,256]{3,2,1,0:T(8,128)(2,1)S(1)}, u32[]{:S(2)}, u32[]{:S(2)}) %collective-permute-start.17) | collective-permute-done | bytes 524320 | tf_op jit(solution)/shard_map/ppermute | solution.py:408
  80.7 0.9 %mix.1 = (f32[128,1024]{1,0:T(8,128)S(1)}, bf16[128,1024]{1,0:T(8,128)(2,1)S(1)}) custom-call(bf16[4,8,32,256]{3,2,1,0:T(8,128)(2,1)S(1)} %bitcast.10, bf16[4,8,32,256]{3,2,1,0:T(8,128)(2,1)S(1)} %collective-permute-done.17.other_ref, bf16[256,1024]{1,0:T(8,128)(2,1)S(1)} %take.1.mine_ref, bf16[256,1024]{1,0:T(8,128)(2,1)S(1)} %collective-permute-done.13.one_ref, ...), custom_call_target="tpu_custom_call" | custom-call | tf_op jit(solution)/shard_map/mix/pallas_call | solution.py:485
  81.6 0.8 collective-permute-start.18
  82.4 1.2 %collective-permute-done.18.come_ref = bf16[128,1024]{1,0:T(8,128)(2,1)S(1)} collective-permute-done((bf16[128,1024]{1,0:T(8,128)(2,1)S(1)}, bf16[128,1024]{1,0:T(8,128)(2,1)S(1)}, u32[]{:S(2)}, u32[]{:S(2)}) %collective-permute-start.18) | collective-permute-done | bytes 262176 | tf_op jit(solution)/shard_map/ppermute | solution.py:408
  83.6 0.1 collective-permute-start.19
  83.7 0.8 collective-permute-start.20
  84.5 1.9 %collective-permute-start.21 = (bf16[32,1024]{1,0:T(8,128)(2,1)S(1)}, bf16[32,1024]{1,0:T(8,128)(2,1)S(1)}, u32[]{:S(2)}, u32[]{:S(2)}) collective-permute-start(bf16[32,1024]{1,0:T(8,128)(2,1)S(1)} %get-tuple-element.52), channel_id=1, source_target_pairs={{0,80},{8,88},{16,64},{24,72},{32,112},{40,120},{48,96},{56,104},{... | collective-permute-start | bytes 196616 | tf_op jit(solution)/shard_map/ppermute | solution.py:408
  86.3 0.5 collective-permute-done.19.refs_1_
  86.8 0.1 collective-permute-done.20.refs_2_
  86.9 1.6 %collective-permute-done.21.refs_3_ = bf16[32,1024]{1,0:T(8,128)(2,1)S(1)} collective-permute-done((bf16[32,1024]{1,0:T(8,128)(2,1)S(1)}, bf16[32,1024]{1,0:T(8,128)(2,1)S(1)}, u32[]{:S(2)}, u32[]{:S(2)}) %collective-permute-start.21) | collective-permute-done | bytes 65568 | tf_op jit(solution)/shard_map/ppermute | solution.py:408
  88.5 0.7 lay.1
  (2 shorter events, 0.1 us)
Async XLA Ops:
  0.0 8.9 %copy-start.2 = (s32[256]{0:T(256)S(1)}, s32[256]{0:T(256)}, u32[]{:S(2)}) copy-start(s32[256]{0:T(256)} %param.15) | copy-start | bytes 3076
  0.0 8.9 %copy-start.1 = (bf16[4096,2,1]{0,1,2:T(2,128)(2,1)S(1)}, bf16[4096,2,1]{0,1,2:T(2,128)(2,1)}, u32[]{:S(2)}) copy-start(bf16[4096,2,1]{0,1,2:T(2,128)(2,1)} %param.12) | copy-start | bytes 49156
  0.0 8.9 %copy-start = (f32[4096]{0:T(1024)S(1)}, f32[4096]{0:T(1024)}, u32[]{:S(2)}) copy-start(f32[4096]{0:T(1024)} %param.10) | copy-start | bytes 49156
  1.1 18.5 %collective-permute-start.13 = (bf16[256,1024]{1,0:T(8,128)(2,1)S(1)}, bf16[256,1024]{1,0:T(8,128)(2,1)S(1)}, u32[]{:S(2)}, u32[]{:S(2)}) collective-permute-start(bf16[256,1024]{1,0:T(8,128)(2,1)S(1)} %take.1.mine_ref), channel_id=1, source_target_pairs={{0,1},{1,2},{2,3},{3,4},{4,5},{5,6},{6,7},{7,0},{8,15},{9,8},{10,9... | collective-permute-start | bytes 1572872 | tf_op jit(solution)/shard_map/ppermute | solution.py:422
  18.0 1.6 %collective-permute-start = (bf16[256,512]{1,0:T(8,128)(2,1)S(1)}, bf16[256,512]{1,0:T(8,128)(2,1)S(1)}, u32[]{:S(2)}, u32[]{:S(2)}) collective-permute-start(bf16[256,512]{1,0:T(8,128)(2,1)S(1)} %get-tuple-element.29.own_ref), channel_id=1, source_target_pairs={{0,8},{8,0},{16,24},{24,16},{32,40},{40,32},{48,56},{56,48},{64,72... | collective-permute-start | bytes 786440 | tf_op jit(solution)/shard_map/ppermute | solution.py:408
  19.6 13.4 %collective-permute-start.14 = (bf16[256,1024]{1,0:T(8,128)(2,1)S(1)}, bf16[256,1024]{1,0:T(8,128)(2,1)S(1)}, u32[]{:S(2)}, u32[]{:S(2)}) collective-permute-start(bf16[256,1024]{1,0:T(8,128)(2,1)S(1)} %collective-permute-done.13.one_ref), channel_id=1, source_target_pairs={{0,1},{1,2},{2,3},{3,4},{4,5},{5,6},{6,7},{7,0},{8,15},{9,8},{10,9... | collective-permute-start | bytes 1572872 | tf_op jit(solution)/shard_map/ppermute | solution.py:422
  20.6 8.6 %collective-permute-start.3 = (bf16[128,512]{1,0:T(8,128)(2,1)S(1)}, bf16[128,512]{1,0:T(8,128)(2,1)S(1)}, u32[]{:S(2)}, u32[]{:S(2)}) collective-permute-start(bf16[128,512]{1,0:T(8,128)(2,1)S(1)} %get-tuple-element.31), channel_id=1, source_target_pairs={{0,48},{8,56},{16,0},{24,8},{32,16},{40,24},{48,32},{56,40},{64,11... | collective-permute-start | bytes 393224 | tf_op jit(solution)/shard_map/ppermute | solution.py:408
  23.2 6.9 %collective-permute-start.2 = (bf16[128,512]{1,0:T(8,128)(2,1)S(1)}, bf16[128,512]{1,0:T(8,128)(2,1)S(1)}, u32[]{:S(2)}, u32[]{:S(2)}) collective-permute-start(bf16[128,512]{1,0:T(8,128)(2,1)S(1)} %get-tuple-element.31), channel_id=1, source_target_pairs={{0,32},{8,40},{16,48},{24,56},{32,0},{40,8},{48,16},{56,24},{64,96... | collective-permute-start | bytes 393224 | tf_op jit(solution)/shard_map/ppermute | solution.py:408
  23.7 9.3 %collective-permute-start.1 = (bf16[128,512]{1,0:T(8,128)(2,1)S(1)}, bf16[128,512]{1,0:T(8,128)(2,1)S(1)}, u32[]{:S(2)}, u32[]{:S(2)}) collective-permute-start(bf16[128,512]{1,0:T(8,128)(2,1)S(1)} %get-tuple-element.31), channel_id=1, source_target_pairs={{0,16},{8,24},{16,32},{24,40},{32,48},{40,56},{48,0},{56,8},{64,80... | collective-permute-start | bytes 393224 | tf_op jit(solution)/shard_map/ppermute | solution.py:408
  24.3 29.4 %copy-start.3 = (f32[256]{0:T(256)S(1)}, f32[256]{0:T(256)}, u32[]{:S(2)}) copy-start(f32[256]{0:T(256)} %param.16) | copy-start | bytes 3076
  33.0 8.3 %collective-permute-start.15 = (bf16[256,1024]{1,0:T(8,128)(2,1)S(1)}, bf16[256,1024]{1,0:T(8,128)(2,1)S(1)}, u32[]{:S(2)}, u32[]{:S(2)}) collective-permute-start(bf16[256,1024]{1,0:T(8,128)(2,1)S(1)} %collective-permute-done.14.two_ref), channel_id=1, source_target_pairs={{0,1},{1,2},{2,3},{3,4},{4,5},{5,6},{6,7},{7,0},{8,15},{9,8},{10,9... | collective-permute-start | bytes 1572872 | tf_op jit(solution)/shard_map/ppermute | solution.py:422
  33.6 1.6 %collective-permute-start.4 = (bf16[128,512]{1,0:T(8,128)(2,1)S(1)}, bf16[128,512]{1,0:T(8,128)(2,1)S(1)}, u32[]{:S(2)}, u32[]{:S(2)}) collective-permute-start(bf16[128,512]{1,0:T(8,128)(2,1)S(1)} %collective-permute-done.1.refs_0_), channel_id=1, source_target_pairs={{0,8},{8,0},{16,24},{24,16},{32,40},{40,32},{48,56},{56,48},{64,72... | collective-permute-start | bytes 393224 | tf_op jit(solution)/shard_map/ppermute | solution.py:408
  34.3 1.3 %collective-permute-start.5 = (bf16[128,512]{1,0:T(8,128)(2,1)S(1)}, bf16[128,512]{1,0:T(8,128)(2,1)S(1)}, u32[]{:S(2)}, u32[]{:S(2)}) collective-permute-start(bf16[128,512]{1,0:T(8,128)(2,1)S(1)} %collective-permute-done.2.refs_1_), channel_id=1, source_target_pairs={{0,8},{8,0},{16,24},{24,16},{32,40},{40,32},{48,56},{56,48},{64,72... | collective-permute-start | bytes 393224 | tf_op jit(solution)/shard_map/ppermute | solution.py:408
  34.3 1.5 %collective-permute-start.6 = (bf16[128,512]{1,0:T(8,128)(2,1)S(1)}, bf16[128,512]{1,0:T(8,128)(2,1)S(1)}, u32[]{:S(2)}, u32[]{:S(2)}) collective-permute-start(bf16[128,512]{1,0:T(8,128)(2,1)S(1)} %collective-permute-done.3.refs_2_), channel_id=1, source_target_pairs={{0,8},{8,0},{16,24},{24,16},{32,40},{40,32},{48,56},{56,48},{64,72... | collective-permute-start | bytes 393224 | tf_op jit(solution)/shard_map/ppermute | solution.py:408
  37.0 8.3 %collective-permute-start.9 = (bf16[128,512]{1,0:T(8,128)(2,1)}, bf16[128,512]{1,0:T(8,128)(2,1)S(1)}, u32[]{:S(2)}, u32[]{:S(2)}) collective-permute-start(bf16[128,512]{1,0:T(8,128)(2,1)} %get-tuple-element.39), channel_id=1, source_target_pairs={{0,192},{8,200},{16,208},{24,216},{32,224},{40,232},{48,240},{56,2... | collective-permute-start | bytes 393224 | tf_op jit(solution)/shard_map/ppermute | solution.py:408
  39.8 6.2 %collective-permute-start.8 = (bf16[128,512]{1,0:T(8,128)(2,1)}, bf16[128,512]{1,0:T(8,128)(2,1)S(1)}, u32[]{:S(2)}, u32[]{:S(2)}) collective-permute-start(bf16[128,512]{1,0:T(8,128)(2,1)} %get-tuple-element.39), channel_id=1, source_target_pairs={{0,128},{8,136},{16,144},{24,152},{32,160},{40,168},{48,176},{56,1... | collective-permute-start | bytes 393224 | tf_op jit(solution)/shard_map/ppermute | solution.py:408
  40.1 9.6 %collective-permute-start.7 = (bf16[128,512]{1,0:T(8,128)(2,1)}, bf16[128,512]{1,0:T(8,128)(2,1)S(1)}, u32[]{:S(2)}, u32[]{:S(2)}) collective-permute-start(bf16[128,512]{1,0:T(8,128)(2,1)} %get-tuple-element.39), channel_id=1, source_target_pairs={{0,64},{8,72},{16,80},{24,88},{32,96},{40,104},{48,112},{56,120},{... | collective-permute-start | bytes 393224 | tf_op jit(solution)/shard_map/ppermute | solution.py:408
  49.7 5.5 %collective-permute-start.16 = (bf16[256,512]{1,0:T(8,128)(2,1)S(1)}, bf16[256,512]{1,0:T(8,128)(2,1)S(1)}, u32[]{:S(2)}, u32[]{:S(2)}) collective-permute-start(bf16[256,512]{1,0:T(8,128)(2,1)S(1)} %constant_dynamic-slice_fusion), channel_id=1, source_target_pairs={{0,1},{1,2},{2,3},{3,4},{4,5},{5,6},{6,7},{7,0},{8,15},{9,8},{10,9... | collective-permute-start | bytes 786440 | tf_op jit(solution)/shard_map/ppermute | solution.py:422
  51.8 1.3 %collective-permute-start.12 = (bf16[128,512]{1,0:T(8,128)(2,1)S(1)}, bf16[128,512]{1,0:T(8,128)(2,1)S(1)}, u32[]{:S(2)}, u32[]{:S(2)}) collective-permute-start(bf16[128,512]{1,0:T(8,128)(2,1)S(1)} %collective-permute-done.9.refs_2_), channel_id=1, source_target_pairs={{0,8},{8,0},{16,24},{24,16},{32,40},{40,32},{48,56},{56,48},{64,72... | collective-permute-start | bytes 393224 | tf_op jit(solution)/shard_map/ppermute | solution.py:408
  51.8 1.5 %collective-permute-start.11 = (bf16[128,512]{1,0:T(8,128)(2,1)S(1)}, bf16[128,512]{1,0:T(8,128)(2,1)S(1)}, u32[]{:S(2)}, u32[]{:S(2)}) collective-permute-start(bf16[128,512]{1,0:T(8,128)(2,1)S(1)} %collective-permute-done.8.refs_1_), channel_id=1, source_target_pairs={{0,8},{8,0},{16,24},{24,16},{32,40},{40,32},{48,56},{56,48},{64,72... | collective-permute-start | bytes 393224 | tf_op jit(solution)/shard_map/ppermute | solution.py:408
  52.3 1.3 %collective-permute-start.10 = (bf16[128,512]{1,0:T(8,128)(2,1)S(1)}, bf16[128,512]{1,0:T(8,128)(2,1)S(1)}, u32[]{:S(2)}, u32[]{:S(2)}) collective-permute-start(bf16[128,512]{1,0:T(8,128)(2,1)S(1)} %collective-permute-done.7.refs_0_), channel_id=1, source_target_pairs={{0,8},{8,0},{16,24},{24,16},{32,40},{40,32},{48,56},{56,48},{64,72... | collective-permute-start | bytes 393224 | tf_op jit(solution)/shard_map/ppermute | solution.py:408
  74.7 6.0 %collective-permute-start.17 = (bf16[4,8,32,256]{3,2,1,0:T(8,128)(2,1)S(1)}, bf16[4,8,32,256]{3,2,1,0:T(8,128)(2,1)S(1)}, u32[]{:S(2)}, u32[]{:S(2)}) collective-permute-start(bf16[4,8,32,256]{3,2,1,0:T(8,128)(2,1)S(1)} %bitcast.9), channel_id=1, source_target_pairs={{0,8},{8,0},{16,24},{24,16},{32,40},{40,32},{48,56},{56,48},{64,72... | collective-permute-start | bytes 1572872 | tf_op jit(solution)/shard_map/ppermute | solution.py:408
  81.6 1.9 %collective-permute-start.18 = (bf16[128,1024]{1,0:T(8,128)(2,1)S(1)}, bf16[128,1024]{1,0:T(8,128)(2,1)S(1)}, u32[]{:S(2)}, u32[]{:S(2)}) collective-permute-start(bf16[128,1024]{1,0:T(8,128)(2,1)S(1)} %get-tuple-element.48), channel_id=1, source_target_pairs={{0,8},{8,0},{16,24},{24,16},{32,40},{40,32},{48,56},{56,48},{64,72... | collective-permute-start | bytes 786440 | tf_op jit(solution)/shard_map/ppermute | solution.py:408
  83.6 3.2 %collective-permute-start.19 = (bf16[32,1024]{1,0:T(8,128)(2,1)S(1)}, bf16[32,1024]{1,0:T(8,128)(2,1)S(1)}, u32[]{:S(2)}, u32[]{:S(2)}) collective-permute-start(bf16[32,1024]{1,0:T(8,128)(2,1)S(1)} %get-tuple-element.50), channel_id=1, source_target_pairs={{0,16},{8,24},{16,0},{24,8},{32,48},{40,56},{48,32},{56,40},{64,80... | collective-permute-start | bytes 196616 | tf_op jit(solution)/shard_map/ppermute | solution.py:408
  83.7 3.2 %collective-permute-start.20 = (bf16[32,1024]{1,0:T(8,128)(2,1)S(1)}, bf16[32,1024]{1,0:T(8,128)(2,1)S(1)}, u32[]{:S(2)}, u32[]{:S(2)}) collective-permute-start(bf16[32,1024]{1,0:T(8,128)(2,1)S(1)} %get-tuple-element.51), channel_id=1, source_target_pairs={{0,64},{8,72},{16,80},{24,88},{32,96},{40,104},{48,112},{56,120},{... | collective-permute-start | bytes 196616 | tf_op jit(solution)/shard_map/ppermute | solution.py:408
  84.5 4.1 %collective-permute-start.21 = (bf16[32,1024]{1,0:T(8,128)(2,1)S(1)}, bf16[32,1024]{1,0:T(8,128)(2,1)S(1)}, u32[]{:S(2)}, u32[]{:S(2)}) collective-permute-start(bf16[32,1024]{1,0:T(8,128)(2,1)S(1)} %get-tuple-element.52), channel_id=1, source_target_pairs={{0,80},{8,88},{16,64},{24,72},{32,112},{40,120},{48,96},{56,104},{... | collective-permute-start | bytes 196616 | tf_op jit(solution)/shard_map/ppermute | solution.py:408

commit v13 on v11

--- a/solution.py
+++ b/solution.py
@@ -14,7 +14,7 @@
 SEQ = ("yh", "yl", "xh", "xl", "core")
 SMALL = pltpu.CompilerParams(vmem_limit_bytes=8 << 20)
 MIDDLE = pltpu.CompilerParams(vmem_limit_bytes=16 << 20)
-LARGE = pltpu.CompilerParams(vmem_limit_bytes=58 << 20)
+LARGE = pltpu.CompilerParams(vmem_limit_bytes=52 << 20)
 
 
 def mm(a, b, dims=NN):
@@ -450,7 +450,7 @@
     )(carry, other)
     near = [moved(half, along_x(s)) for s in (1, 2, 3)]
     near, looked = lax.optimization_barrier((near, look()))
-    ready = later(two, near)
+    one, ready = later((one, two), near)
     three = around(ready, 1)
     part_two = lax.dynamic_slice_in_dim(
         ready, lax.axis_index("core") * (wide // 2), wide // 2, 1

time: 92.9 us -> 86.9 us (0.935)
  blocking collectives: 0 us -> 19.7 us
  starting transfers between devices: 39.4 us -> 25.5 us
  waiting for transfers between devices: 27.2 us -> 21.9 us
  Pallas kernels: 21.8 us -> 17.6 us
  local copies, waits for them, and re-layouts: 2.02 us -> 0.03 us
    all_to_all x0 -> x1, blocking collectives: none -> 19.7 us  [per_device(): lax.all_to_all(flat.reshape(32, part, n), ('yl', 'xl', 'head'), 0, 0, til...]
    all_to_all x1 -> x0, waiting for transfers between devices: 12.1 us -> none  [per_device(): lax.all_to_all(flat.reshape(32, part, n), ('yl', 'xl', 'head'), 0, 0, til...]
    ppermute x18, waiting for transfers between devices: 12.2 us -> 21.9 us  [moved(): return lax.ppermute(value, SEQ, [(i, place_of(i)) for i in range(count)])]
    all_to_all x1 -> x0, starting transfers between devices: 7.11 us -> none  [per_device(): lax.all_to_all(flat.reshape(32, part, n), ('yl', 'xl', 'head'), 0, 0, til...]
    ppermute x18, starting transfers between devices: 20.8 us -> 16.7 us  [moved(): return lax.ppermute(value, SEQ, [(i, place_of(i)) for i in range(count)])]
    ppermute x4, waiting for transfers between devices: 2.95 us -> 0.01 us  [around(): return lax.ppermute(value, ('core', 'head'), up + down)]
    ppermute x4, starting transfers between devices: 11.5 us -> 8.78 us  [around(): return lax.ppermute(value, ('core', 'head'), up + down)]
    pallas_call x1, Pallas kernels: 6.2 us -> 4.17 us  [look(): pl.pallas_call(look_kernel, name='look', in_specs=[hbm(), vmem(), hbm()]...]
  transfers between devices with their start and end apart: 23 -> 22, of which waited for: 14 -> 18; matrix products, arithmetic and copies ran while one was open for 0% -> 0% of each run, Pallas kernels for 18% -> 16%
where the time goes in v13:
time: 86.9 us; the launch traced here: 86 us
  starting transfers between devices  25.5 us (29%)
  waiting for transfers between devices  21.9 us (25%)
  blocking collectives  19.7 us (23%)
  Pallas kernels  17.6 us (20%)
  between operations  1.41 us (2%)
    ppermute x18, waiting for transfers between devices, moved(): return lax.ppermute(value, SEQ, [(i, place_of(i)) for i in range(count)])  21.9 us
    all_to_all x1, blocking collectives, per_device(): lax.all_to_all(flat.reshape(32, part, n), ('yl', 'xl', 'head'), 0, 0, til...  19.7 us
    ppermute x18, starting transfers between devices, moved(): return lax.ppermute(value, SEQ, [(i, place_of(i)) for i in range(count)])  16.7 us
    pallas_call x1, Pallas kernels, per_device(): pl.pallas_call(fold_kernel, name='fold', in_specs=[hbm()] * 7, out_specs=...  9.06 us
    ppermute x4, starting transfers between devices, around(): return lax.ppermute(value, ('core', 'head'), up + down)  8.78 us
    pallas_call x1, Pallas kernels, look(): pl.pallas_call(look_kernel, name='look', in_specs=[hbm(), vmem(), hbm()]...  4.17 us
  transfers between devices with their start and end apart: 22, of which 18 were waited for; matrix products, arithmetic and copies ran while one was open for 0% of the time, Pallas kernels for 16%

profile of v13, /device:TPU:1, one launch (start us, length us, event | category | flops | bytes accessed | tf_op | source)
XLA Modules:
  0.0 86.0 jit_solution(12125608626226438095)
XLA Ops:
  0.0 0.0 copy-start.2
  0.0 0.0 copy-start.1
  0.0 0.0 copy-start
  0.0 1.1 %take.1.mine_ref = bf16[256,1024]{1,0:T(8,128)(2,1)S(1)} custom-call(bf16[256,4096]{1,0:T(8,128)(2,1)} %whole_ref.1), custom_call_target="tpu_custom_call" | custom-call | tf_op jit(solution)/shard_map/take/pallas_call | solution.py:428
  1.1 6.9 %collective-permute-start.11 = (bf16[256,1024]{1,0:T(8,128)(2,1)S(1)}, bf16[256,1024]{1,0:T(8,128)(2,1)S(1)}, u32[]{:S(2)}, u32[]{:S(2)}) collective-permute-start(bf16[256,1024]{1,0:T(8,128)(2,1)S(1)} %take.1.mine_ref), channel_id=1, source_target_pairs={{0,2},{1,3},{2,4},{3,5},{4,6},{5,7},{6,0},{7,1},{8,14},{9,15},{10,... | collective-permute-start | bytes 1572872 | tf_op jit(solution)/shard_map/ppermute | solution.py:422
  8.0 0.7 collective-permute-start.10
  10.1 0.0 copy-done.2
  10.1 0.0 copy-done.1
  10.1 0.0 copy-done
  10.1 9.1 %fold.1 = (bf16[256,512]{1,0:T(8,128)(2,1)S(1)}, f32[256,256]{1,0:T(8,128)S(1)}, f32[256,512]{1,0:T(8,128)S(1)}, f32[256,256]{1,0:T(8,128)S(1)}, f32[256,1]{1,0:T(8,128)S(1)}) custom-call(f32[1]{0:T(128)S(6)} %copy.10.scale_hbm, f32[1]{0:T(128)S(6)} %copy.11.rate_hbm, bf16[256,4096]{1,0:T(8,128)(2,1)} %x_hbm.3, f32[1,4096]{1,0:T(1,128)S(1)} %bitcast.12, ...), custom_call_target="tpu_custom_call" | custom-call | tf_op jit(solution)/shard_map/fold/pallas_call | solution.py:362
  19.2 0.1 collective-permute-start
  19.3 1.5 %collective-permute-done.other_ref.refs_7_ = bf16[256,512]{1,0:T(8,128)(2,1)S(1)} collective-permute-done((bf16[256,512]{1,0:T(8,128)(2,1)S(1)}, bf16[256,512]{1,0:T(8,128)(2,1)S(1)}, u32[]{:S(2)}, u32[]{:S(2)}) %collective-permute-start) | collective-permute-done | bytes 262176 | tf_op jit(solution)/shard_map/ppermute | solution.py:408
  20.8 0.3 pair.1
  21.1 2.6 %collective-permute-start.3 = (bf16[128,512]{1,0:T(8,128)(2,1)S(1)}, bf16[128,512]{1,0:T(8,128)(2,1)S(1)}, u32[]{:S(2)}, u32[]{:S(2)}) collective-permute-start(bf16[128,512]{1,0:T(8,128)(2,1)S(1)} %get-tuple-element.33), channel_id=1, source_target_pairs={{0,48},{8,56},{16,0},{24,8},{32,16},{40,24},{48,32},{56,40},{64,11... | collective-permute-start | bytes 393224 | tf_op jit(solution)/shard_map/ppermute | solution.py:408
  23.6 0.5 collective-permute-start.2
  24.2 0.6 collective-permute-start.1
  24.8 0.0 copy-start.3
  24.8 4.2 %look.1.refs_8_ = f32[256,512]{1,0:T(8,128)S(1)} custom-call(bf16[256,4096]{1,0:T(8,128)(2,1)} %x_hbm.3, f32[1,4096]{1,0:T(1,128)S(1)} %bitcast.13, bf16[3,4096,256]{2,1,0:T(8,128)(2,1)} %bitcast.18, f32[256,256]{1,0:T(8,128)S(1)} %get-tuple-element.34.key_ref, f32[256,512]{1,0:T(8,128)S(1)} %get-tuple-element.35.solved_ref, ...), custom_call_target="tpu_custom_call" | custom-call | flops 1073741824 | bytes 16777216 | tf_op jit(solution)/shard_map/look/pallas_call | solution.py:392
  28.9 0.1 collective-permute-done.3.refs_2_
  29.1 0.7 collective-permute-done.2.refs_1_
  29.8 3.6 %collective-permute-done.1.refs_0_ = bf16[128,512]{1,0:T(8,128)(2,1)S(1)} collective-permute-done((bf16[128,512]{1,0:T(8,128)(2,1)S(1)}, bf16[128,512]{1,0:T(8,128)(2,1)S(1)}, u32[]{:S(2)}, u32[]{:S(2)}) %collective-permute-start.1) | collective-permute-done | bytes 131104 | tf_op jit(solution)/shard_map/ppermute | solution.py:408
  33.4 0.0 collective-permute-done.11.two_ref
  33.4 0.0 collective-permute-done.10.one_ref
  33.4 0.7 collective-permute-start.12
  34.1 1.6 %collective-permute-start.4 = (bf16[128,512]{1,0:T(8,128)(2,1)S(1)}, bf16[128,512]{1,0:T(8,128)(2,1)S(1)}, u32[]{:S(2)}, u32[]{:S(2)}) collective-permute-start(bf16[128,512]{1,0:T(8,128)(2,1)S(1)} %collective-permute-done.1.refs_0_), channel_id=1, source_target_pairs={{0,8},{8,0},{16,24},{24,16},{32,40},{40,32},{48,56},{56,48},{64,72... | collective-permute-start | bytes 393224 | tf_op jit(solution)/shard_map/ppermute | solution.py:408
  35.7 0.0 collective-permute-start.5
  35.7 0.5 collective-permute-start.6
  36.3 0.4 collective-permute-start.13
  36.7 0.1 collective-permute-done.4.refs_3_
  36.7 0.4 collective-permute-done.5.refs_4_
  37.1 0.2 collective-permute-done.6.refs_5_
  37.3 0.6 row.1
  37.8 2.8 %collective-permute-start.9 = (bf16[128,512]{1,0:T(8,128)(2,1)S(1)}, bf16[128,512]{1,0:T(8,128)(2,1)S(1)}, u32[]{:S(2)}, u32[]{:S(2)}) collective-permute-start(bf16[128,512]{1,0:T(8,128)(2,1)S(1)} %get-tuple-element.41), channel_id=1, source_target_pairs={{0,192},{8,200},{16,208},{24,216},{32,224},{40,232},{48,240},{56,2... | collective-permute-start | bytes 393224 | tf_op jit(solution)/shard_map/ppermute | solution.py:408
  40.7 0.3 collective-permute-start.8
  41.0 0.7 collective-permute-start.7
  41.7 4.0 %collective-permute-done.9.refs_2_ = bf16[128,512]{1,0:T(8,128)(2,1)S(1)} collective-permute-done((bf16[128,512]{1,0:T(8,128)(2,1)S(1)}, bf16[128,512]{1,0:T(8,128)(2,1)S(1)}, u32[]{:S(2)}, u32[]{:S(2)}) %collective-permute-start.9) | collective-permute-done | bytes 131104 | tf_op jit(solution)/shard_map/ppermute | solution.py:408
  45.7 0.6 collective-permute-done.8.refs_1_
  46.3 4.1 %collective-permute-done.7.refs_0_ = bf16[128,512]{1,0:T(8,128)(2,1)S(1)} collective-permute-done((bf16[128,512]{1,0:T(8,128)(2,1)S(1)}, bf16[128,512]{1,0:T(8,128)(2,1)S(1)}, u32[]{:S(2)}, u32[]{:S(2)}) %collective-permute-start.7) | collective-permute-done | bytes 131104 | tf_op jit(solution)/shard_map/ppermute | solution.py:408
  50.4 0.0 collective-permute-done.13.four_ref
  50.4 0.0 collective-permute-done.12.three_ref
  50.4 0.5 collective-permute-start.14
  50.9 0.1 collective-permute-start.15
  51.0 0.4 collective-permute-start.16
  51.4 0.5 collective-permute-done.14.refs_3_
  51.9 0.4 collective-permute-done.15.refs_4_
  52.2 0.2 collective-permute-done.16.refs_5_
  52.4 0.0 copy-done.3
  52.4 0.7 read.1
  53.1 19.7 %all_to_all.5 = bf16[32,32,256]{2,1,0:T(8,128)(2,1)S(1)} all-to-all(bf16[32,32,256]{2,1,0:T(8,128)(2,1)S(1)} %bitcast.11), channel_id=1, replica_groups=mesh['yh'=2,'yl'=2,'xh'=2,'xl'=2,'core'=2,'head'=8] {'yl','xl','head'}, dimensions={0} | all-to-all | bytes 1048576 | tf_op jit(solution)/shard_map/all_to_all | solution.py:482
  72.8 2.4 %collective-permute-start.17 = (bf16[4,8,32,256]{3,2,1,0:T(8,128)(2,1)S(1)}, bf16[4,8,32,256]{3,2,1,0:T(8,128)(2,1)S(1)}, u32[]{:S(2)}, u32[]{:S(2)}) collective-permute-start(bf16[4,8,32,256]{3,2,1,0:T(8,128)(2,1)S(1)} %bitcast.9), channel_id=1, source_target_pairs={{0,8},{8,0},{16,24},{24,16},{32,40},{40,32},{48,56},{56,48},{64,72... | collective-permute-start | bytes 1572872 | tf_op jit(solution)/shard_map/ppermute | solution.py:408
  75.2 1.5 %collective-permute-done.17.other_ref = bf16[4,8,32,256]{3,2,1,0:T(8,128)(2,1)S(1)} collective-permute-done((bf16[4,8,32,256]{3,2,1,0:T(8,128)(2,1)S(1)}, bf16[4,8,32,256]{3,2,1,0:T(8,128)(2,1)S(1)}, u32[]{:S(2)}, u32[]{:S(2)}) %collective-permute-start.17) | collective-permute-done | bytes 524320 | tf_op jit(solution)/shard_map/ppermute | solution.py:408
  76.8 0.9 %mix.1 = (f32[128,1024]{1,0:T(8,128)S(1)}, bf16[128,1024]{1,0:T(8,128)(2,1)S(1)}) custom-call(bf16[4,8,32,256]{3,2,1,0:T(8,128)(2,1)S(1)} %bitcast.10, bf16[4,8,32,256]{3,2,1,0:T(8,128)(2,1)S(1)} %collective-permute-done.17.other_ref, bf16[256,1024]{1,0:T(8,128)(2,1)S(1)} %take.1.mine_ref, bf16[256,1024]{1,0:T(8,128)(2,1)S(1)} %collective-permute-done.10.one_ref, ...), custom_call_target="tpu_custom_call" | custom-call | tf_op jit(solution)/shard_map/mix/pallas_call | solution.py:486
  77.7 0.7 collective-permute-start.18
  78.4 1.2 %collective-permute-done.18.come_ref = bf16[128,1024]{1,0:T(8,128)(2,1)S(1)} collective-permute-done((bf16[128,1024]{1,0:T(8,128)(2,1)S(1)}, bf16[128,1024]{1,0:T(8,128)(2,1)S(1)}, u32[]{:S(2)}, u32[]{:S(2)}) %collective-permute-start.18) | collective-permute-done | bytes 262176 | tf_op jit(solution)/shard_map/ppermute | solution.py:408
  79.6 0.7 collective-permute-start.19
  80.3 1.0 %collective-permute-start.20 = (bf16[32,1024]{1,0:T(8,128)(2,1)S(1)}, bf16[32,1024]{1,0:T(8,128)(2,1)S(1)}, u32[]{:S(2)}, u32[]{:S(2)}) collective-permute-start(bf16[32,1024]{1,0:T(8,128)(2,1)S(1)} %get-tuple-element.55), channel_id=1, source_target_pairs={{0,64},{8,72},{16,80},{24,88},{32,96},{40,104},{48,112},{56,120},{... | collective-permute-start | bytes 196616 | tf_op jit(solution)/shard_map/ppermute | solution.py:408
  81.3 1.1 %collective-permute-start.21 = (bf16[32,1024]{1,0:T(8,128)(2,1)S(1)}, bf16[32,1024]{1,0:T(8,128)(2,1)S(1)}, u32[]{:S(2)}, u32[]{:S(2)}) collective-permute-start(bf16[32,1024]{1,0:T(8,128)(2,1)S(1)} %get-tuple-element.56), channel_id=1, source_target_pairs={{0,80},{8,88},{16,64},{24,72},{32,112},{40,120},{48,96},{56,104},{... | collective-permute-start | bytes 196616 | tf_op jit(solution)/shard_map/ppermute | solution.py:408
  82.4 0.5 collective-permute-done.19.refs_1_
  82.8 0.9 %collective-permute-done.20.refs_2_ = bf16[32,1024]{1,0:T(8,128)(2,1)S(1)} collective-permute-done((bf16[32,1024]{1,0:T(8,128)(2,1)S(1)}, bf16[32,1024]{1,0:T(8,128)(2,1)S(1)}, u32[]{:S(2)}, u32[]{:S(2)}) %collective-permute-start.20) | collective-permute-done | bytes 65568 | tf_op jit(solution)/shard_map/ppermute | solution.py:408
  83.7 1.6 %collective-permute-done.21.refs_3_ = bf16[32,1024]{1,0:T(8,128)(2,1)S(1)} collective-permute-done((bf16[32,1024]{1,0:T(8,128)(2,1)S(1)}, bf16[32,1024]{1,0:T(8,128)(2,1)S(1)}, u32[]{:S(2)}, u32[]{:S(2)}) %collective-permute-start.21) | collective-permute-done | bytes 65568 | tf_op jit(solution)/shard_map/ppermute | solution.py:408
  85.3 0.7 lay.1
  (2 shorter events, 0.1 us)
Async XLA Ops:
  0.0 10.1 %copy-start.2 = (s32[256]{0:T(256)S(1)}, s32[256]{0:T(256)}, u32[]{:S(2)}) copy-start(s32[256]{0:T(256)} %param.15) | copy-start | bytes 3076
  0.0 10.1 %copy-start.1 = (bf16[4096,2,1]{0,1,2:T(2,128)(2,1)S(1)}, bf16[4096,2,1]{0,1,2:T(2,128)(2,1)}, u32[]{:S(2)}) copy-start(bf16[4096,2,1]{0,1,2:T(2,128)(2,1)} %param.12) | copy-start | bytes 49156
  0.0 10.1 %copy-start = (f32[4096]{0:T(1024)S(1)}, f32[4096]{0:T(1024)}, u32[]{:S(2)}) copy-start(f32[4096]{0:T(1024)} %param.10) | copy-start | bytes 49156
  1.1 32.3 %collective-permute-start.11 = (bf16[256,1024]{1,0:T(8,128)(2,1)S(1)}, bf16[256,1024]{1,0:T(8,128)(2,1)S(1)}, u32[]{:S(2)}, u32[]{:S(2)}) collective-permute-start(bf16[256,1024]{1,0:T(8,128)(2,1)S(1)} %take.1.mine_ref), channel_id=1, source_target_pairs={{0,2},{1,3},{2,4},{3,5},{4,6},{5,7},{6,0},{7,1},{8,14},{9,15},{10,... | collective-permute-start | bytes 1572872 | tf_op jit(solution)/shard_map/ppermute | solution.py:422
  8.0 25.3 %collective-permute-start.10 = (bf16[256,1024]{1,0:T(8,128)(2,1)S(1)}, bf16[256,1024]{1,0:T(8,128)(2,1)S(1)}, u32[]{:S(2)}, u32[]{:S(2)}) collective-permute-start(bf16[256,1024]{1,0:T(8,128)(2,1)S(1)} %take.1.mine_ref), channel_id=1, source_target_pairs={{0,1},{1,2},{2,3},{3,4},{4,5},{5,6},{6,7},{7,0},{8,15},{9,8},{10,9... | collective-permute-start | bytes 1572872 | tf_op jit(solution)/shard_map/ppermute | solution.py:422
  19.2 1.6 %collective-permute-start = (bf16[256,512]{1,0:T(8,128)(2,1)S(1)}, bf16[256,512]{1,0:T(8,128)(2,1)S(1)}, u32[]{:S(2)}, u32[]{:S(2)}) collective-permute-start(bf16[256,512]{1,0:T(8,128)(2,1)S(1)} %get-tuple-element.31.own_ref), channel_id=1, source_target_pairs={{0,8},{8,0},{16,24},{24,16},{32,40},{40,32},{48,56},{56,48},{64,72... | collective-permute-start | bytes 786440 | tf_op jit(solution)/shard_map/ppermute | solution.py:408
  21.1 8.0 %collective-permute-start.3 = (bf16[128,512]{1,0:T(8,128)(2,1)S(1)}, bf16[128,512]{1,0:T(8,128)(2,1)S(1)}, u32[]{:S(2)}, u32[]{:S(2)}) collective-permute-start(bf16[128,512]{1,0:T(8,128)(2,1)S(1)} %get-tuple-element.33), channel_id=1, source_target_pairs={{0,48},{8,56},{16,0},{24,8},{32,16},{40,24},{48,32},{56,40},{64,11... | collective-permute-start | bytes 393224 | tf_op jit(solution)/shard_map/ppermute | solution.py:408
  23.6 6.2 %collective-permute-start.2 = (bf16[128,512]{1,0:T(8,128)(2,1)S(1)}, bf16[128,512]{1,0:T(8,128)(2,1)S(1)}, u32[]{:S(2)}, u32[]{:S(2)}) collective-permute-start(bf16[128,512]{1,0:T(8,128)(2,1)S(1)} %get-tuple-element.33), channel_id=1, source_target_pairs={{0,32},{8,40},{16,48},{24,56},{32,0},{40,8},{48,16},{56,24},{64,96... | collective-permute-start | bytes 393224 | tf_op jit(solution)/shard_map/ppermute | solution.py:408
  24.2 9.2 %collective-permute-start.1 = (bf16[128,512]{1,0:T(8,128)(2,1)S(1)}, bf16[128,512]{1,0:T(8,128)(2,1)S(1)}, u32[]{:S(2)}, u32[]{:S(2)}) collective-permute-start(bf16[128,512]{1,0:T(8,128)(2,1)S(1)} %get-tuple-element.33), channel_id=1, source_target_pairs={{0,16},{8,24},{16,32},{24,40},{32,48},{40,56},{48,0},{56,8},{64,80... | collective-permute-start | bytes 393224 | tf_op jit(solution)/shard_map/ppermute | solution.py:408
  24.8 27.7 %copy-start.3 = (f32[256]{0:T(256)S(1)}, f32[256]{0:T(256)}, u32[]{:S(2)}) copy-start(f32[256]{0:T(256)} %param.16) | copy-start | bytes 3076
  33.4 17.0 %collective-permute-start.12 = (bf16[256,1024]{1,0:T(8,128)(2,1)S(1)}, bf16[256,1024]{1,0:T(8,128)(2,1)S(1)}, u32[]{:S(2)}, u32[]{:S(2)}) collective-permute-start(bf16[256,1024]{1,0:T(8,128)(2,1)S(1)} %collective-permute-done.11.two_ref), channel_id=1, source_target_pairs={{0,1},{1,2},{2,3},{3,4},{4,5},{5,6},{6,7},{7,0},{8,15},{9,8},{10,9... | collective-permute-start | bytes 1572872 | tf_op jit(solution)/shard_map/ppermute | solution.py:422
  34.1 2.6 %collective-permute-start.4 = (bf16[128,512]{1,0:T(8,128)(2,1)S(1)}, bf16[128,512]{1,0:T(8,128)(2,1)S(1)}, u32[]{:S(2)}, u32[]{:S(2)}) collective-permute-start(bf16[128,512]{1,0:T(8,128)(2,1)S(1)} %collective-permute-done.1.refs_0_), channel_id=1, source_target_pairs={{0,8},{8,0},{16,24},{24,16},{32,40},{40,32},{48,56},{56,48},{64,72... | collective-permute-start | bytes 393224 | tf_op jit(solution)/shard_map/ppermute | solution.py:408
  35.7 1.3 %collective-permute-start.5 = (bf16[128,512]{1,0:T(8,128)(2,1)S(1)}, bf16[128,512]{1,0:T(8,128)(2,1)S(1)}, u32[]{:S(2)}, u32[]{:S(2)}) collective-permute-start(bf16[128,512]{1,0:T(8,128)(2,1)S(1)} %collective-permute-done.2.refs_1_), channel_id=1, source_target_pairs={{0,8},{8,0},{16,24},{24,16},{32,40},{40,32},{48,56},{56,48},{64,72... | collective-permute-start | bytes 393224 | tf_op jit(solution)/shard_map/ppermute | solution.py:408
  35.7 1.5 %collective-permute-start.6 = (bf16[128,512]{1,0:T(8,128)(2,1)S(1)}, bf16[128,512]{1,0:T(8,128)(2,1)S(1)}, u32[]{:S(2)}, u32[]{:S(2)}) collective-permute-start(bf16[128,512]{1,0:T(8,128)(2,1)S(1)} %collective-permute-done.3.refs_2_), channel_id=1, source_target_pairs={{0,8},{8,0},{16,24},{24,16},{32,40},{40,32},{48,56},{56,48},{64,72... | collective-permute-start | bytes 393224 | tf_op jit(solution)/shard_map/ppermute | solution.py:408
  36.3 14.1 %collective-permute-start.13 = (bf16[256,512]{1,0:T(8,128)(2,1)S(1)}, bf16[256,512]{1,0:T(8,128)(2,1)S(1)}, u32[]{:S(2)}, u32[]{:S(2)}) collective-permute-start(bf16[256,512]{1,0:T(8,128)(2,1)S(1)} %constant_dynamic-slice_fusion), channel_id=1, source_target_pairs={{0,2},{1,3},{2,4},{3,5},{4,6},{5,7},{6,0},{7,1},{8,14},{9,15},{10,... | collective-permute-start | bytes 786440 | tf_op jit(solution)/shard_map/ppermute | solution.py:422
  37.8 7.9 %collective-permute-start.9 = (bf16[128,512]{1,0:T(8,128)(2,1)S(1)}, bf16[128,512]{1,0:T(8,128)(2,1)S(1)}, u32[]{:S(2)}, u32[]{:S(2)}) collective-permute-start(bf16[128,512]{1,0:T(8,128)(2,1)S(1)} %get-tuple-element.41), channel_id=1, source_target_pairs={{0,192},{8,200},{16,208},{24,216},{32,224},{40,232},{48,240},{56,2... | collective-permute-start | bytes 393224 | tf_op jit(solution)/shard_map/ppermute | solution.py:408
  40.7 5.7 %collective-permute-start.8 = (bf16[128,512]{1,0:T(8,128)(2,1)S(1)}, bf16[128,512]{1,0:T(8,128)(2,1)S(1)}, u32[]{:S(2)}, u32[]{:S(2)}) collective-permute-start(bf16[128,512]{1,0:T(8,128)(2,1)S(1)} %get-tuple-element.41), channel_id=1, source_target_pairs={{0,128},{8,136},{16,144},{24,152},{32,160},{40,168},{48,176},{56,1... | collective-permute-start | bytes 393224 | tf_op jit(solution)/shard_map/ppermute | solution.py:408
  41.0 9.4 %collective-permute-start.7 = (bf16[128,512]{1,0:T(8,128)(2,1)S(1)}, bf16[128,512]{1,0:T(8,128)(2,1)S(1)}, u32[]{:S(2)}, u32[]{:S(2)}) collective-permute-start(bf16[128,512]{1,0:T(8,128)(2,1)S(1)} %get-tuple-element.41), channel_id=1, source_target_pairs={{0,64},{8,72},{16,80},{24,88},{32,96},{40,104},{48,112},{56,120},{... | collective-permute-start | bytes 393224 | tf_op jit(solution)/shard_map/ppermute | solution.py:408
  50.4 1.5 %collective-permute-start.14 = (bf16[128,512]{1,0:T(8,128)(2,1)S(1)}, bf16[128,512]{1,0:T(8,128)(2,1)S(1)}, u32[]{:S(2)}, u32[]{:S(2)}) collective-permute-start(bf16[128,512]{1,0:T(8,128)(2,1)S(1)} %collective-permute-done.7.refs_0_), channel_id=1, source_target_pairs={{0,8},{8,0},{16,24},{24,16},{32,40},{40,32},{48,56},{56,48},{64,72... | collective-permute-start | bytes 393224 | tf_op jit(solution)/shard_map/ppermute | solution.py:408
  50.9 1.3 %collective-permute-start.15 = (bf16[128,512]{1,0:T(8,128)(2,1)S(1)}, bf16[128,512]{1,0:T(8,128)(2,1)S(1)}, u32[]{:S(2)}, u32[]{:S(2)}) collective-permute-start(bf16[128,512]{1,0:T(8,128)(2,1)S(1)} %collective-permute-done.8.refs_1_), channel_id=1, source_target_pairs={{0,8},{8,0},{16,24},{24,16},{32,40},{40,32},{48,56},{56,48},{64,72... | collective-permute-start | bytes 393224 | tf_op jit(solution)/shard_map/ppermute | solution.py:408
  51.0 1.4 %collective-permute-start.16 = (bf16[128,512]{1,0:T(8,128)(2,1)S(1)}, bf16[128,512]{1,0:T(8,128)(2,1)S(1)}, u32[]{:S(2)}, u32[]{:S(2)}) collective-permute-start(bf16[128,512]{1,0:T(8,128)(2,1)S(1)} %collective-permute-done.9.refs_2_), channel_id=1, source_target_pairs={{0,8},{8,0},{16,24},{24,16},{32,40},{40,32},{48,56},{56,48},{64,72... | collective-permute-start | bytes 393224 | tf_op jit(solution)/shard_map/ppermute | solution.py:408
  72.8 4.0 %collective-permute-start.17 = (bf16[4,8,32,256]{3,2,1,0:T(8,128)(2,1)S(1)}, bf16[4,8,32,256]{3,2,1,0:T(8,128)(2,1)S(1)}, u32[]{:S(2)}, u32[]{:S(2)}) collective-permute-start(bf16[4,8,32,256]{3,2,1,0:T(8,128)(2,1)S(1)} %bitcast.9), channel_id=1, source_target_pairs={{0,8},{8,0},{16,24},{24,16},{32,40},{40,32},{48,56},{56,48},{64,72... | collective-permute-start | bytes 1572872 | tf_op jit(solution)/shard_map/ppermute | solution.py:408
  77.7 1.9 %collective-permute-start.18 = (bf16[128,1024]{1,0:T(8,128)(2,1)S(1)}, bf16[128,1024]{1,0:T(8,128)(2,1)S(1)}, u32[]{:S(2)}, u32[]{:S(2)}) collective-permute-start(bf16[128,1024]{1,0:T(8,128)(2,1)S(1)} %get-tuple-element.52), channel_id=1, source_target_pairs={{0,8},{8,0},{16,24},{24,16},{32,40},{40,32},{48,56},{56,48},{64,72... | collective-permute-start | bytes 786440 | tf_op jit(solution)/shard_map/ppermute | solution.py:408
  79.6 3.2 %collective-permute-start.19 = (bf16[32,1024]{1,0:T(8,128)(2,1)S(1)}, bf16[32,1024]{1,0:T(8,128)(2,1)S(1)}, u32[]{:S(2)}, u32[]{:S(2)}) collective-permute-start(bf16[32,1024]{1,0:T(8,128)(2,1)S(1)} %get-tuple-element.54), channel_id=1, source_target_pairs={{0,16},{8,24},{16,0},{24,8},{32,48},{40,56},{48,32},{56,40},{64,80... | collective-permute-start | bytes 196616 | tf_op jit(solution)/shard_map/ppermute | solution.py:408
  80.3 3.4 %collective-permute-start.20 = (bf16[32,1024]{1,0:T(8,128)(2,1)S(1)}, bf16[32,1024]{1,0:T(8,128)(2,1)S(1)}, u32[]{:S(2)}, u32[]{:S(2)}) collective-permute-start(bf16[32,1024]{1,0:T(8,128)(2,1)S(1)} %get-tuple-element.55), channel_id=1, source_target_pairs={{0,64},{8,72},{16,80},{24,88},{32,96},{40,104},{48,112},{56,120},{... | collective-permute-start | bytes 196616 | tf_op jit(solution)/shard_map/ppermute | solution.py:408
  81.3 4.0 %collective-permute-start.21 = (bf16[32,1024]{1,0:T(8,128)(2,1)S(1)}, bf16[32,1024]{1,0:T(8,128)(2,1)S(1)}, u32[]{:S(2)}, u32[]{:S(2)}) collective-permute-start(bf16[32,1024]{1,0:T(8,128)(2,1)S(1)} %get-tuple-element.56), channel_id=1, source_target_pairs={{0,80},{8,88},{16,64},{24,72},{32,112},{40,120},{48,96},{56,104},{... | collective-permute-start | bytes 196616 | tf_op jit(solution)/shard_map/ppermute | solution.py:408

commit v14 on v13

--- a/solution.py
+++ b/solution.py
@@ -467,7 +467,6 @@
         compiler_params=SMALL,
     )(pair, *near, *swapped)
     near = [moved(half, along_y(s)) for s in (1, 2, 3)]
-    near, three, four = lax.optimization_barrier((near, three, four))
     swapped = [moved(value, flip(1)) for value in near]
     flat = pl.pallas_call(
         read_kernel,
@@ -479,6 +478,7 @@
         compiler_params=SMALL,
     )(*near, *swapped, prefix, other, looked, out_gain.reshape(1, n))
     part = rows // 8
+    flat, three, four = lax.optimization_barrier((flat, three, four))
     reads = lax.all_to_all(
         flat.reshape(32, part, n), ("yl", "xl", "head"), 0, 0, tiled=True
     ).reshape(4, 8, part, n)

time: 86.9 us -> 86.7 us (level)
  starting transfers between devices: 25.5 us -> 31.9 us
  blocking collectives: 19.7 us -> 15.4 us
  waiting for transfers between devices: 21.9 us -> 18.8 us
  Pallas kernels: 17.6 us -> 18.6 us
    ppermute x18, starting transfers between devices: 16.7 us -> 23.1 us  [moved(): return lax.ppermute(value, SEQ, [(i, place_of(i)) for i in range(count)])]
    all_to_all x1, blocking collectives: 19.7 us -> 15.4 us  [per_device(): lax.all_to_all(flat.reshape(32, part, n), ('yl', 'xl', 'head'), 0, 0, til...]
    ppermute x18, waiting for transfers between devices: 21.9 us -> 18.8 us  [moved(): return lax.ppermute(value, SEQ, [(i, place_of(i)) for i in range(count)])]
    pallas_call x1, Pallas kernels: 0.57 us -> 1.6 us  [per_device(): pl.pallas_call(row_kernel, name='row', in_specs=[vmem()] * 7, out_specs=[...]
  transfers between devices with their start and end apart: 22 -> 22, of which waited for: 18 -> 15; matrix products, arithmetic and copies ran while one was open for 0% -> 0% of each run, Pallas kernels for 16% -> 18%
where the time goes in v14:
time: 86.7 us; the launch traced here: 86.1 us
  starting transfers between devices  31.9 us (37%)
  waiting for transfers between devices  18.8 us (22%)
  Pallas kernels  18.6 us (21%)
  blocking collectives  15.4 us (18%)
  between operations  1.43 us (2%)
    ppermute x18, starting transfers between devices, moved(): return lax.ppermute(value, SEQ, [(i, place_of(i)) for i in range(count)])  23.1 us
    ppermute x18, waiting for transfers between devices, moved(): return lax.ppermute(value, SEQ, [(i, place_of(i)) for i in range(count)])  18.8 us
    all_to_all x1, blocking collectives, per_device(): lax.all_to_all(flat.reshape(32, part, n), ('yl', 'xl', 'head'), 0, 0, til...  15.4 us
    pallas_call x1, Pallas kernels, per_device(): pl.pallas_call(fold_kernel, name='fold', in_specs=[hbm()] * 7, out_specs=...  9.06 us
    ppermute x4, starting transfers between devices, around(): return lax.ppermute(value, ('core', 'head'), up + down)  8.78 us
    pallas_call x1, Pallas kernels, look(): pl.pallas_call(look_kernel, name='look', in_specs=[hbm(), vmem(), hbm()]...  4.17 us
  transfers between devices with their start and end apart: 22, of which 15 were waited for; matrix products, arithmetic and copies ran while one was open for 0% of the time, Pallas kernels for 18%

profile of v14, /device:TPU:1, one launch (start us, length us, event | category | flops | bytes accessed | tf_op | source)
XLA Modules:
  0.0 86.1 jit_solution(17941831956837733505)
XLA Ops:
  0.0 0.0 copy-start.2
  0.0 0.0 copy-start.1
  0.0 0.0 copy-start
  0.0 1.1 %take.1.mine_ref = bf16[256,1024]{1,0:T(8,128)(2,1)S(1)} custom-call(bf16[256,4096]{1,0:T(8,128)(2,1)} %whole_ref.1), custom_call_target="tpu_custom_call" | custom-call | tf_op jit(solution)/shard_map/take/pallas_call | solution.py:428
  1.1 6.9 %collective-permute-start.14 = (bf16[256,1024]{1,0:T(8,128)(2,1)S(1)}, bf16[256,1024]{1,0:T(8,128)(2,1)S(1)}, u32[]{:S(2)}, u32[]{:S(2)}) collective-permute-start(bf16[256,1024]{1,0:T(8,128)(2,1)S(1)} %take.1.mine_ref), channel_id=1, source_target_pairs={{0,2},{1,3},{2,4},{3,5},{4,6},{5,7},{6,0},{7,1},{8,14},{9,15},{10,... | collective-permute-start | bytes 1572872 | tf_op jit(solution)/shard_map/ppermute | solution.py:422
  8.0 0.7 collective-permute-start.13
  10.1 0.0 copy-done.2
  10.1 0.0 copy-done.1
  10.1 0.0 copy-done
  10.1 9.1 %fold.1 = (bf16[256,512]{1,0:T(8,128)(2,1)S(1)}, f32[256,256]{1,0:T(8,128)S(1)}, f32[256,512]{1,0:T(8,128)S(1)}, f32[256,256]{1,0:T(8,128)S(1)}, f32[256,1]{1,0:T(8,128)S(1)}) custom-call(f32[1]{0:T(128)S(6)} %copy.10.scale_hbm, f32[1]{0:T(128)S(6)} %copy.11.rate_hbm, bf16[256,4096]{1,0:T(8,128)(2,1)} %x_hbm.3, f32[1,4096]{1,0:T(1,128)S(1)} %bitcast.12, ...), custom_call_target="tpu_custom_call" | custom-call | tf_op jit(solution)/shard_map/fold/pallas_call | solution.py:362
  19.2 0.1 collective-permute-start
  19.3 1.5 %collective-permute-done.other_ref.refs_7_ = bf16[256,512]{1,0:T(8,128)(2,1)S(1)} collective-permute-done((bf16[256,512]{1,0:T(8,128)(2,1)S(1)}, bf16[256,512]{1,0:T(8,128)(2,1)S(1)}, u32[]{:S(2)}, u32[]{:S(2)}) %collective-permute-start) | collective-permute-done | bytes 262176 | tf_op jit(solution)/shard_map/ppermute | solution.py:408
  20.8 0.3 pair.1
  21.1 2.6 %collective-permute-start.3 = (bf16[128,512]{1,0:T(8,128)(2,1)S(1)}, bf16[128,512]{1,0:T(8,128)(2,1)S(1)}, u32[]{:S(2)}, u32[]{:S(2)}) collective-permute-start(bf16[128,512]{1,0:T(8,128)(2,1)S(1)} %get-tuple-element.31), channel_id=1, source_target_pairs={{0,48},{8,56},{16,0},{24,8},{32,16},{40,24},{48,32},{56,40},{64,11... | collective-permute-start | bytes 393224 | tf_op jit(solution)/shard_map/ppermute | solution.py:408
  23.6 0.5 collective-permute-start.2
  24.2 0.6 collective-permute-start.1
  24.8 0.0 copy-start.3
  24.8 4.2 %look.1.refs_8_ = f32[256,512]{1,0:T(8,128)S(1)} custom-call(bf16[256,4096]{1,0:T(8,128)(2,1)} %x_hbm.3, f32[1,4096]{1,0:T(1,128)S(1)} %bitcast.13, bf16[3,4096,256]{2,1,0:T(8,128)(2,1)} %bitcast.18, f32[256,256]{1,0:T(8,128)S(1)} %get-tuple-element.32.key_ref, f32[256,512]{1,0:T(8,128)S(1)} %get-tuple-element.33.solved_ref, ...), custom_call_target="tpu_custom_call" | custom-call | flops 1073741824 | bytes 16777216 | tf_op jit(solution)/shard_map/look/pallas_call | solution.py:392
  28.9 0.1 collective-permute-done.3.refs_2_
  29.1 0.7 collective-permute-done.2.refs_1_
  29.8 3.6 %collective-permute-done.1.refs_0_ = bf16[128,512]{1,0:T(8,128)(2,1)S(1)} collective-permute-done((bf16[128,512]{1,0:T(8,128)(2,1)S(1)}, bf16[128,512]{1,0:T(8,128)(2,1)S(1)}, u32[]{:S(2)}, u32[]{:S(2)}) %collective-permute-start.1) | collective-permute-done | bytes 131104 | tf_op jit(solution)/shard_map/ppermute | solution.py:408
  33.4 0.0 collective-permute-done.14.two_ref
  33.4 0.0 collective-permute-done.13.one_ref
  33.4 0.7 collective-permute-start.15
  34.1 1.6 %collective-permute-start.4 = (bf16[128,512]{1,0:T(8,128)(2,1)S(1)}, bf16[128,512]{1,0:T(8,128)(2,1)}, u32[]{:S(2)}, u32[]{:S(2)}) collective-permute-start(bf16[128,512]{1,0:T(8,128)(2,1)S(1)} %collective-permute-done.1.refs_0_), channel_id=1, source_target_pairs={{0,8},{8,0},{16,24},{24,16},{32,40},{40,32},{48,56},{56,48},{64,72... | collective-permute-start | bytes 393224 | tf_op jit(solution)/shard_map/ppermute | solution.py:408
  35.7 0.0 collective-permute-start.5
  35.7 0.5 collective-permute-start.6
  36.2 0.6 collective-permute-done.4.refs_3_
  36.9 0.4 collective-permute-done.5.refs_4_
  37.2 0.2 collective-permute-done.6.refs_5_
  37.4 1.6 %row.1 = (bf16[128,512]{1,0:T(8,128)(2,1)S(1)}, bf16[256,512]{1,0:T(8,128)(2,1)S(1)}) custom-call(bf16[256,512]{1,0:T(8,128)(2,1)S(1)} %get-tuple-element.30.own_ref, bf16[128,512]{1,0:T(8,128)(2,1)S(1)} %collective-permute-done.1.refs_0_, bf16[128,512]{1,0:T(8,128)(2,1)S(1)} %collective-permute-done.2.refs_1_, ...), custom_call_target="tpu_custom_call" | custom-call | tf_op jit(solution)/shard_map/row/pallas_call | solution.py:460
  39.0 2.8 %collective-permute-start.9 = (bf16[128,512]{1,0:T(8,128)(2,1)S(1)}, bf16[128,512]{1,0:T(8,128)(2,1)S(1)}, u32[]{:S(2)}, u32[]{:S(2)}) collective-permute-start(bf16[128,512]{1,0:T(8,128)(2,1)S(1)} %get-tuple-element.39), channel_id=1, source_target_pairs={{0,192},{8,200},{16,208},{24,216},{32,224},{40,232},{48,240},{56,2... | collective-permute-start | bytes 393224 | tf_op jit(solution)/shard_map/ppermute | solution.py:408
  41.8 0.3 collective-permute-start.8
  42.2 0.7 collective-permute-start.7
  42.9 0.4 collective-permute-start.16
  43.3 3.8 %collective-permute-done.9.refs_2_ = bf16[128,512]{1,0:T(8,128)(2,1)S(1)} collective-permute-done((bf16[128,512]{1,0:T(8,128)(2,1)S(1)}, bf16[128,512]{1,0:T(8,128)(2,1)S(1)}, u32[]{:S(2)}, u32[]{:S(2)}) %collective-permute-start.9) | collective-permute-done | bytes 131104 | tf_op jit(solution)/shard_map/ppermute | solution.py:408
  47.1 1.3 %collective-permute-start.12 = (bf16[128,512]{1,0:T(8,128)(2,1)S(1)}, bf16[128,512]{1,0:T(8,128)(2,1)S(1)}, u32[]{:S(2)}, u32[]{:S(2)}) collective-permute-start(bf16[128,512]{1,0:T(8,128)(2,1)S(1)} %collective-permute-done.9.refs_2_), channel_id=1, source_target_pairs={{0,8},{8,0},{16,24},{24,16},{32,40},{40,32},{48,56},{56,48},{64,72... | collective-permute-start | bytes 393224 | tf_op jit(solution)/shard_map/ppermute | solution.py:408
  48.3 0.0 collective-permute-done.8.refs_1_
  48.3 2.0 %collective-permute-start.11 = (bf16[128,512]{1,0:T(8,128)(2,1)S(1)}, bf16[128,512]{1,0:T(8,128)(2,1)S(1)}, u32[]{:S(2)}, u32[]{:S(2)}) collective-permute-start(bf16[128,512]{1,0:T(8,128)(2,1)S(1)} %collective-permute-done.8.refs_1_), channel_id=1, source_target_pairs={{0,8},{8,0},{16,24},{24,16},{32,40},{40,32},{48,56},{56,48},{64,72... | collective-permute-start | bytes 393224 | tf_op jit(solution)/shard_map/ppermute | solution.py:408
  50.3 1.2 %collective-permute-done.7.refs_0_ = bf16[128,512]{1,0:T(8,128)(2,1)S(1)} collective-permute-done((bf16[128,512]{1,0:T(8,128)(2,1)S(1)}, bf16[128,512]{1,0:T(8,128)(2,1)S(1)}, u32[]{:S(2)}, u32[]{:S(2)}) %collective-permute-start.7) | collective-permute-done | bytes 131104 | tf_op jit(solution)/shard_map/ppermute | solution.py:408
  51.6 0.5 collective-permute-start.10
  52.0 0.0 collective-permute-done.12.refs_5_
  52.0 0.0 collective-permute-done.11.refs_4_
  52.1 1.0 %collective-permute-done.10.refs_3_ = bf16[128,512]{1,0:T(8,128)(2,1)S(1)} collective-permute-done((bf16[128,512]{1,0:T(8,128)(2,1)S(1)}, bf16[128,512]{1,0:T(8,128)(2,1)S(1)}, u32[]{:S(2)}, u32[]{:S(2)}) %collective-permute-start.10) | collective-permute-done | bytes 131104 | tf_op jit(solution)/shard_map/ppermute | solution.py:408
  53.0 0.0 copy-done.3
  53.0 0.7 read.1
  53.8 0.0 collective-permute-done.16.four_ref
  53.8 0.0 collective-permute-done.15.three_ref
  53.8 15.4 %all_to_all.5 = bf16[32,32,256]{2,1,0:T(8,128)(2,1)S(1)} all-to-all(bf16[32,32,256]{2,1,0:T(8,128)(2,1)S(1)} %bitcast.9), channel_id=1, replica_groups=mesh['yh'=2,'yl'=2,'xh'=2,'xl'=2,'core'=2,'head'=8] {'yl','xl','head'}, dimensions={0} | all-to-all | bytes 1048576 | tf_op jit(solution)/shard_map/all_to_all | solution.py:482
  69.2 6.1 %collective-permute-start.17 = (bf16[4,8,32,256]{3,2,1,0:T(8,128)(2,1)S(1)}, bf16[4,8,32,256]{3,2,1,0:T(8,128)(2,1)S(1)}, u32[]{:S(2)}, u32[]{:S(2)}) collective-permute-start(bf16[4,8,32,256]{3,2,1,0:T(8,128)(2,1)S(1)} %bitcast.10), channel_id=1, source_target_pairs={{0,8},{8,0},{16,24},{24,16},{32,40},{40,32},{48,56},{56,48},{64,72... | collective-permute-start | bytes 1572872 | tf_op jit(solution)/shard_map/ppermute | solution.py:408
  75.2 1.5 %collective-permute-done.17.other_ref = bf16[4,8,32,256]{3,2,1,0:T(8,128)(2,1)S(1)} collective-permute-done((bf16[4,8,32,256]{3,2,1,0:T(8,128)(2,1)S(1)}, bf16[4,8,32,256]{3,2,1,0:T(8,128)(2,1)S(1)}, u32[]{:S(2)}, u32[]{:S(2)}) %collective-permute-start.17) | collective-permute-done | bytes 524320 | tf_op jit(solution)/shard_map/ppermute | solution.py:408
  76.8 0.9 %mix.1 = (f32[128,1024]{1,0:T(8,128)S(1)}, bf16[128,1024]{1,0:T(8,128)(2,1)S(1)}) custom-call(bf16[4,8,32,256]{3,2,1,0:T(8,128)(2,1)S(1)} %bitcast.11, bf16[4,8,32,256]{3,2,1,0:T(8,128)(2,1)S(1)} %collective-permute-done.17.other_ref, bf16[256,1024]{1,0:T(8,128)(2,1)S(1)} %take.1.mine_ref, bf16[256,1024]{1,0:T(8,128)(2,1)S(1)} %collective-permute-done.13.one_ref, ...), custom_call_target="tpu_custom_call" | custom-call | tf_op jit(solution)/shard_map/mix/pallas_call | solution.py:486
  77.7 0.8 collective-permute-start.18
  78.4 1.2 %collective-permute-done.18.come_ref = bf16[128,1024]{1,0:T(8,128)(2,1)S(1)} collective-permute-done((bf16[128,1024]{1,0:T(8,128)(2,1)S(1)}, bf16[128,1024]{1,0:T(8,128)(2,1)S(1)}, u32[]{:S(2)}, u32[]{:S(2)}) %collective-permute-start.18) | collective-permute-done | bytes 262176 | tf_op jit(solution)/shard_map/ppermute | solution.py:408
  79.7 0.7 collective-permute-start.19
  80.3 1.0 %collective-permute-start.20 = (bf16[32,1024]{1,0:T(8,128)(2,1)S(1)}, bf16[32,1024]{1,0:T(8,128)(2,1)S(1)}, u32[]{:S(2)}, u32[]{:S(2)}) collective-permute-start(bf16[32,1024]{1,0:T(8,128)(2,1)S(1)} %get-tuple-element.51), channel_id=1, source_target_pairs={{0,64},{8,72},{16,80},{24,88},{32,96},{40,104},{48,112},{56,120},{... | collective-permute-start | bytes 196616 | tf_op jit(solution)/shard_map/ppermute | solution.py:408
  81.3 1.0 %collective-permute-start.21 = (bf16[32,1024]{1,0:T(8,128)(2,1)S(1)}, bf16[32,1024]{1,0:T(8,128)(2,1)S(1)}, u32[]{:S(2)}, u32[]{:S(2)}) collective-permute-start(bf16[32,1024]{1,0:T(8,128)(2,1)S(1)} %get-tuple-element.52), channel_id=1, source_target_pairs={{0,80},{8,88},{16,64},{24,72},{32,112},{40,120},{48,96},{56,104},{... | collective-permute-start | bytes 196616 | tf_op jit(solution)/shard_map/ppermute | solution.py:408
  82.4 0.5 collective-permute-done.19.refs_1_
  82.9 0.9 %collective-permute-done.20.refs_2_ = bf16[32,1024]{1,0:T(8,128)(2,1)S(1)} collective-permute-done((bf16[32,1024]{1,0:T(8,128)(2,1)S(1)}, bf16[32,1024]{1,0:T(8,128)(2,1)S(1)}, u32[]{:S(2)}, u32[]{:S(2)}) %collective-permute-start.20) | collective-permute-done | bytes 65568 | tf_op jit(solution)/shard_map/ppermute | solution.py:408
  83.7 1.6 %collective-permute-done.21.refs_3_ = bf16[32,1024]{1,0:T(8,128)(2,1)S(1)} collective-permute-done((bf16[32,1024]{1,0:T(8,128)(2,1)S(1)}, bf16[32,1024]{1,0:T(8,128)(2,1)S(1)}, u32[]{:S(2)}, u32[]{:S(2)}) %collective-permute-start.21) | collective-permute-done | bytes 65568 | tf_op jit(solution)/shard_map/ppermute | solution.py:408
  85.4 0.7 lay.1
  (2 shorter events, 0.1 us)
Async XLA Ops:
  0.0 10.1 %copy-start.2 = (s32[256]{0:T(256)S(1)}, s32[256]{0:T(256)}, u32[]{:S(2)}) copy-start(s32[256]{0:T(256)} %param.15) | copy-start | bytes 3076
  0.0 10.1 %copy-start.1 = (bf16[4096,2,1]{0,1,2:T(2,128)(2,1)S(1)}, bf16[4096,2,1]{0,1,2:T(2,128)(2,1)}, u32[]{:S(2)}) copy-start(bf16[4096,2,1]{0,1,2:T(2,128)(2,1)} %param.12) | copy-start | bytes 49156
  0.0 10.1 %copy-start = (f32[4096]{0:T(1024)S(1)}, f32[4096]{0:T(1024)}, u32[]{:S(2)}) copy-start(f32[4096]{0:T(1024)} %param.10) | copy-start | bytes 49156
  1.1 32.3 %collective-permute-start.14 = (bf16[256,1024]{1,0:T(8,128)(2,1)S(1)}, bf16[256,1024]{1,0:T(8,128)(2,1)S(1)}, u32[]{:S(2)}, u32[]{:S(2)}) collective-permute-start(bf16[256,1024]{1,0:T(8,128)(2,1)S(1)} %take.1.mine_ref), channel_id=1, source_target_pairs={{0,2},{1,3},{2,4},{3,5},{4,6},{5,7},{6,0},{7,1},{8,14},{9,15},{10,... | collective-permute-start | bytes 1572872 | tf_op jit(solution)/shard_map/ppermute | solution.py:422
  8.0 25.3 %collective-permute-start.13 = (bf16[256,1024]{1,0:T(8,128)(2,1)S(1)}, bf16[256,1024]{1,0:T(8,128)(2,1)S(1)}, u32[]{:S(2)}, u32[]{:S(2)}) collective-permute-start(bf16[256,1024]{1,0:T(8,128)(2,1)S(1)} %take.1.mine_ref), channel_id=1, source_target_pairs={{0,1},{1,2},{2,3},{3,4},{4,5},{5,6},{6,7},{7,0},{8,15},{9,8},{10,9... | collective-permute-start | bytes 1572872 | tf_op jit(solution)/shard_map/ppermute | solution.py:422
  19.2 1.6 %collective-permute-start = (bf16[256,512]{1,0:T(8,128)(2,1)S(1)}, bf16[256,512]{1,0:T(8,128)(2,1)S(1)}, u32[]{:S(2)}, u32[]{:S(2)}) collective-permute-start(bf16[256,512]{1,0:T(8,128)(2,1)S(1)} %get-tuple-element.29.own_ref), channel_id=1, source_target_pairs={{0,8},{8,0},{16,24},{24,16},{32,40},{40,32},{48,56},{56,48},{64,72... | collective-permute-start | bytes 786440 | tf_op jit(solution)/shard_map/ppermute | solution.py:408
  21.1 8.0 %collective-permute-start.3 = (bf16[128,512]{1,0:T(8,128)(2,1)S(1)}, bf16[128,512]{1,0:T(8,128)(2,1)S(1)}, u32[]{:S(2)}, u32[]{:S(2)}) collective-permute-start(bf16[128,512]{1,0:T(8,128)(2,1)S(1)} %get-tuple-element.31), channel_id=1, source_target_pairs={{0,48},{8,56},{16,0},{24,8},{32,16},{40,24},{48,32},{56,40},{64,11... | collective-permute-start | bytes 393224 | tf_op jit(solution)/shard_map/ppermute | solution.py:408
  23.6 6.2 %collective-permute-start.2 = (bf16[128,512]{1,0:T(8,128)(2,1)S(1)}, bf16[128,512]{1,0:T(8,128)(2,1)S(1)}, u32[]{:S(2)}, u32[]{:S(2)}) collective-permute-start(bf16[128,512]{1,0:T(8,128)(2,1)S(1)} %get-tuple-element.31), channel_id=1, source_target_pairs={{0,32},{8,40},{16,48},{24,56},{32,0},{40,8},{48,16},{56,24},{64,96... | collective-permute-start | bytes 393224 | tf_op jit(solution)/shard_map/ppermute | solution.py:408
  24.2 9.2 %collective-permute-start.1 = (bf16[128,512]{1,0:T(8,128)(2,1)S(1)}, bf16[128,512]{1,0:T(8,128)(2,1)S(1)}, u32[]{:S(2)}, u32[]{:S(2)}) collective-permute-start(bf16[128,512]{1,0:T(8,128)(2,1)S(1)} %get-tuple-element.31), channel_id=1, source_target_pairs={{0,16},{8,24},{16,32},{24,40},{32,48},{40,56},{48,0},{56,8},{64,80... | collective-permute-start | bytes 393224 | tf_op jit(solution)/shard_map/ppermute | solution.py:408
  24.8 28.3 %copy-start.3 = (f32[256]{0:T(256)S(1)}, f32[256]{0:T(256)}, u32[]{:S(2)}) copy-start(f32[256]{0:T(256)} %param.16) | copy-start | bytes 3076
  33.4 20.4 %collective-permute-start.15 = (bf16[256,1024]{1,0:T(8,128)(2,1)S(1)}, bf16[256,1024]{1,0:T(8,128)(2,1)S(1)}, u32[]{:S(2)}, u32[]{:S(2)}) collective-permute-start(bf16[256,1024]{1,0:T(8,128)(2,1)S(1)} %collective-permute-done.14.two_ref), channel_id=1, source_target_pairs={{0,1},{1,2},{2,3},{3,4},{4,5},{5,6},{6,7},{7,0},{8,15},{9,8},{10,9... | collective-permute-start | bytes 1572872 | tf_op jit(solution)/shard_map/ppermute | solution.py:422
  34.1 2.8 %collective-permute-start.4 = (bf16[128,512]{1,0:T(8,128)(2,1)S(1)}, bf16[128,512]{1,0:T(8,128)(2,1)}, u32[]{:S(2)}, u32[]{:S(2)}) collective-permute-start(bf16[128,512]{1,0:T(8,128)(2,1)S(1)} %collective-permute-done.1.refs_0_), channel_id=1, source_target_pairs={{0,8},{8,0},{16,24},{24,16},{32,40},{40,32},{48,56},{56,48},{64,72... | collective-permute-start | bytes 393224 | tf_op jit(solution)/shard_map/ppermute | solution.py:408
  35.7 1.5 %collective-permute-start.5 = (bf16[128,512]{1,0:T(8,128)(2,1)S(1)}, bf16[128,512]{1,0:T(8,128)(2,1)}, u32[]{:S(2)}, u32[]{:S(2)}) collective-permute-start(bf16[128,512]{1,0:T(8,128)(2,1)S(1)} %collective-permute-done.2.refs_1_), channel_id=1, source_target_pairs={{0,8},{8,0},{16,24},{24,16},{32,40},{40,32},{48,56},{56,48},{64,72... | collective-permute-start | bytes 393224 | tf_op jit(solution)/shard_map/ppermute | solution.py:408
  35.7 1.7 %collective-permute-start.6 = (bf16[128,512]{1,0:T(8,128)(2,1)S(1)}, bf16[128,512]{1,0:T(8,128)(2,1)}, u32[]{:S(2)}, u32[]{:S(2)}) collective-permute-start(bf16[128,512]{1,0:T(8,128)(2,1)S(1)} %collective-permute-done.3.refs_2_), channel_id=1, source_target_pairs={{0,8},{8,0},{16,24},{24,16},{32,40},{40,32},{48,56},{56,48},{64,72... | collective-permute-start | bytes 393224 | tf_op jit(solution)/shard_map/ppermute | solution.py:408
  39.0 8.0 %collective-permute-start.9 = (bf16[128,512]{1,0:T(8,128)(2,1)S(1)}, bf16[128,512]{1,0:T(8,128)(2,1)S(1)}, u32[]{:S(2)}, u32[]{:S(2)}) collective-permute-start(bf16[128,512]{1,0:T(8,128)(2,1)S(1)} %get-tuple-element.39), channel_id=1, source_target_pairs={{0,192},{8,200},{16,208},{24,216},{32,224},{40,232},{48,240},{56,2... | collective-permute-start | bytes 393224 | tf_op jit(solution)/shard_map/ppermute | solution.py:408
  41.8 6.5 %collective-permute-start.8 = (bf16[128,512]{1,0:T(8,128)(2,1)S(1)}, bf16[128,512]{1,0:T(8,128)(2,1)S(1)}, u32[]{:S(2)}, u32[]{:S(2)}) collective-permute-start(bf16[128,512]{1,0:T(8,128)(2,1)S(1)} %get-tuple-element.39), channel_id=1, source_target_pairs={{0,128},{8,136},{16,144},{24,152},{32,160},{40,168},{48,176},{56,1... | collective-permute-start | bytes 393224 | tf_op jit(solution)/shard_map/ppermute | solution.py:408
  42.2 9.4 %collective-permute-start.7 = (bf16[128,512]{1,0:T(8,128)(2,1)S(1)}, bf16[128,512]{1,0:T(8,128)(2,1)S(1)}, u32[]{:S(2)}, u32[]{:S(2)}) collective-permute-start(bf16[128,512]{1,0:T(8,128)(2,1)S(1)} %get-tuple-element.39), channel_id=1, source_target_pairs={{0,64},{8,72},{16,80},{24,88},{32,96},{40,104},{48,112},{56,120},{... | collective-permute-start | bytes 393224 | tf_op jit(solution)/shard_map/ppermute | solution.py:408
  42.9 10.9 %collective-permute-start.16 = (bf16[256,512]{1,0:T(8,128)(2,1)S(1)}, bf16[256,512]{1,0:T(8,128)(2,1)S(1)}, u32[]{:S(2)}, u32[]{:S(2)}) collective-permute-start(bf16[256,512]{1,0:T(8,128)(2,1)S(1)} %constant_dynamic-slice_fusion), channel_id=1, source_target_pairs={{0,2},{1,3},{2,4},{3,5},{4,6},{5,7},{6,0},{7,1},{8,14},{9,15},{10,... | collective-permute-start | bytes 786440 | tf_op jit(solution)/shard_map/ppermute | solution.py:422
  47.1 5.0 %collective-permute-start.12 = (bf16[128,512]{1,0:T(8,128)(2,1)S(1)}, bf16[128,512]{1,0:T(8,128)(2,1)S(1)}, u32[]{:S(2)}, u32[]{:S(2)}) collective-permute-start(bf16[128,512]{1,0:T(8,128)(2,1)S(1)} %collective-permute-done.9.refs_2_), channel_id=1, source_target_pairs={{0,8},{8,0},{16,24},{24,16},{32,40},{40,32},{48,56},{56,48},{64,72... | collective-permute-start | bytes 393224 | tf_op jit(solution)/shard_map/ppermute | solution.py:408
  48.3 3.7 %collective-permute-start.11 = (bf16[128,512]{1,0:T(8,128)(2,1)S(1)}, bf16[128,512]{1,0:T(8,128)(2,1)S(1)}, u32[]{:S(2)}, u32[]{:S(2)}) collective-permute-start(bf16[128,512]{1,0:T(8,128)(2,1)S(1)} %collective-permute-done.8.refs_1_), channel_id=1, source_target_pairs={{0,8},{8,0},{16,24},{24,16},{32,40},{40,32},{48,56},{56,48},{64,72... | collective-permute-start | bytes 393224 | tf_op jit(solution)/shard_map/ppermute | solution.py:408
  51.6 1.5 %collective-permute-start.10 = (bf16[128,512]{1,0:T(8,128)(2,1)S(1)}, bf16[128,512]{1,0:T(8,128)(2,1)S(1)}, u32[]{:S(2)}, u32[]{:S(2)}) collective-permute-start(bf16[128,512]{1,0:T(8,128)(2,1)S(1)} %collective-permute-done.7.refs_0_), channel_id=1, source_target_pairs={{0,8},{8,0},{16,24},{24,16},{32,40},{40,32},{48,56},{56,48},{64,72... | collective-permute-start | bytes 393224 | tf_op jit(solution)/shard_map/ppermute | solution.py:408
  69.2 7.6 %collective-permute-start.17 = (bf16[4,8,32,256]{3,2,1,0:T(8,128)(2,1)S(1)}, bf16[4,8,32,256]{3,2,1,0:T(8,128)(2,1)S(1)}, u32[]{:S(2)}, u32[]{:S(2)}) collective-permute-start(bf16[4,8,32,256]{3,2,1,0:T(8,128)(2,1)S(1)} %bitcast.10), channel_id=1, source_target_pairs={{0,8},{8,0},{16,24},{24,16},{32,40},{40,32},{48,56},{56,48},{64,72... | collective-permute-start | bytes 1572872 | tf_op jit(solution)/shard_map/ppermute | solution.py:408
  77.7 1.9 %collective-permute-start.18 = (bf16[128,1024]{1,0:T(8,128)(2,1)S(1)}, bf16[128,1024]{1,0:T(8,128)(2,1)S(1)}, u32[]{:S(2)}, u32[]{:S(2)}) collective-permute-start(bf16[128,1024]{1,0:T(8,128)(2,1)S(1)} %get-tuple-element.48), channel_id=1, source_target_pairs={{0,8},{8,0},{16,24},{24,16},{32,40},{40,32},{48,56},{56,48},{64,72... | collective-permute-start | bytes 786440 | tf_op jit(solution)/shard_map/ppermute | solution.py:408
  79.7 3.2 %collective-permute-start.19 = (bf16[32,1024]{1,0:T(8,128)(2,1)S(1)}, bf16[32,1024]{1,0:T(8,128)(2,1)S(1)}, u32[]{:S(2)}, u32[]{:S(2)}) collective-permute-start(bf16[32,1024]{1,0:T(8,128)(2,1)S(1)} %get-tuple-element.50), channel_id=1, source_target_pairs={{0,16},{8,24},{16,0},{24,8},{32,48},{40,56},{48,32},{56,40},{64,80... | collective-permute-start | bytes 196616 | tf_op jit(solution)/shard_map/ppermute | solution.py:408
  80.3 3.4 %collective-permute-start.20 = (bf16[32,1024]{1,0:T(8,128)(2,1)S(1)}, bf16[32,1024]{1,0:T(8,128)(2,1)S(1)}, u32[]{:S(2)}, u32[]{:S(2)}) collective-permute-start(bf16[32,1024]{1,0:T(8,128)(2,1)S(1)} %get-tuple-element.51), channel_id=1, source_target_pairs={{0,64},{8,72},{16,80},{24,88},{32,96},{40,104},{48,112},{56,120},{... | collective-permute-start | bytes 196616 | tf_op jit(solution)/shard_map/ppermute | solution.py:408
  81.3 4.0 %collective-permute-start.21 = (bf16[32,1024]{1,0:T(8,128)(2,1)S(1)}, bf16[32,1024]{1,0:T(8,128)(2,1)S(1)}, u32[]{:S(2)}, u32[]{:S(2)}) collective-permute-start(bf16[32,1024]{1,0:T(8,128)(2,1)S(1)} %get-tuple-element.52), channel_id=1, source_target_pairs={{0,80},{8,88},{16,64},{24,72},{32,112},{40,120},{48,96},{56,104},{... | collective-permute-start | bytes 196616 | tf_op jit(solution)/shard_map/ppermute | solution.py:408
